TPU v7x, 256 devices: a whole 4x4x8 slice. The times are simulated.
256 devices in a mesh: patch: 128 (over z, y, x), width: 2 (over core).
Axes of the slice: x: 4, y: 4, z: 8, core: 2. Of those that a mesh axis runs over, the one named last changes fastest.
Arguments:
- node_latents: bfloat16 [512, 16384], P('width', 'patch'), may hold values from -6 to 6
- edge_latents: bfloat16 [512, 131072], P('width', 'patch'), may hold values from -6 to 6
- senders: int32 [131072], P('patch'), may hold values from 0 to 16383, as said below
- receivers: int32 [131072], P('patch'), may hold values from 0 to 16383, as said below
- edge_count: int32 [128], P('patch'), may hold values from 512 to 1024, as said below
- edge_in_weight: bfloat16 [2, 512, 1536], P(None, 'width'), may hold values from -0.15625 to 0.15625
- edge_in_bias: float32 [2, 512], P(None, 'width'), may hold values from -3 to 3
- edge_out_weight: bfloat16 [2, 512, 512], P(None, 'width'), may hold values from -0.25 to 0.25
- edge_out_bias: float32 [2, 512], P(None, 'width'), may hold values from -3 to 3
- edge_gain: float32 [2, 512], P(None, 'width'), may hold values from 0.1 to 1.9
- edge_shift: float32 [2, 512], P(None, 'width'), may hold values from -3 to 3
- node_in_weight: bfloat16 [2, 512, 1024], P(None, 'width'), may hold values from -0.1875 to 0.1875
- node_in_bias: float32 [2, 512], P(None, 'width'), may hold values from -3 to 3
- node_out_weight: bfloat16 [2, 512, 512], P(None, 'width'), may hold values from -0.25 to 0.25
- node_out_bias: float32 [2, 512], P(None, 'width'), may hold values from -3 to 3
- node_gain: float32 [2, 512], P(None, 'width'), may hold values from 0.1 to 1.9
- node_shift: float32 [2, 512], P(None, 'width'), may hold values from -3 to 3
Outputs:
- nodes_out: bfloat16 [512, 16384], P('width', 'patch')
- edges_out: bfloat16 [512, 131072], P('width', 'patch')
Inputs may be any that keep to these rules, and one draw needn't show every extreme that they name: `senders`: the sender of a slot of patch p is a node of patch p, of patch p - 1 or p + 1 (counted around, modulo the number of patches), or one of the first 16 nodes of some patch. `receivers`: row r names a node of patch r // 1024, from (r // 1024) * 128 to that plus 128 - 1. Slots p * 1024 to p * 1024 + edge_count[p] - 1 of patch p are live, the rest are padding; some patch has all 1024 slots live.
All inputs are finite; a program needn't handle non-finite values.
Results may differ from a plain program's by a relative error of at most 0.014.
Values may be sent and summed in bfloat16 or wider, within the bound.
No kernel may reach another device: no remote copies, remote signals or barrier semaphores. Data moves between devices by JAX's collectives and lax.ppermute only.
A program may use at most 64 MiB of HBM per device.

v0:
```python
import jax
import jax.numpy as jnp
from jax import lax
from jax.sharding import Mesh
from jax.sharding import PartitionSpec as P

PATCH = ("patch_0", "patch_1", "patch_2")


epsilon = 1e-05


def with_halo(shard, sides, width):
    for axis, dim in sides:
        size, length = (lax.axis_size(axis), shard.shape[dim])
        up = [(i, (i + 1) % size) for i in range(size)]
        down = [(j, i) for i, j in up]
        last = lax.slice_in_dim(shard, length - width, length, axis=dim)
        initial = lax.slice_in_dim(shard, 0, width, axis=dim)
        before = lax.ppermute(last, axis, up)
        after = lax.ppermute(initial, axis, down)
        shard = jnp.concatenate([before, shard, after], axis=dim)
    return shard


def from_everyone(shard, axis):
    copies = jnp.broadcast_to(shard, (lax.axis_size(axis), *shard.shape))
    return lax.all_to_all(copies, axis, split_axis=0, concat_axis=0, tiled=True)


def joined_along(parts, dim):
    parts = jnp.moveaxis(parts, 0, dim)
    shape = parts.shape
    return parts.reshape(*shape[:dim], shape[dim] * shape[dim + 1], *shape[dim + 2 :])


def whole_of(shard, axes, dim):
    far, near = axes
    initial = from_everyone(shard, far)
    parts = jnp.swapaxes(from_everyone(initial, near), 0, 1)
    return joined_along(parts.reshape(-1, *shard.shape), dim)


def gathered_copies(shard, axis, dim):
    parts = from_everyone(shard, axis)
    return joined_along(parts, dim)


def in_blocks(shard, dim, length):
    before, after = (shard.shape[:dim], shard.shape[dim + 1 :])
    return jnp.moveaxis(shard.reshape(*before, length, -1, *after), dim, 0)


def sent_and_summed(shard, axis, dim):
    length = lax.axis_size(axis)
    parts = lax.all_to_all(in_blocks(shard, dim, length), axis, 0, 0, tiled=True)
    return jnp.sum(parts.astype(jnp.float32), axis=0)


def taken_together(shard, axis):
    return from_everyone(shard, axis).sum(axis=0)


def in_one(arrays, axis):
    ends = [0]
    for a in arrays:
        ends.append(ends[-1] + a.size)
    total = taken_together(jnp.concatenate([a.ravel() for a in arrays]), axis)
    return tuple((total[b:e].reshape(a.shape) for a, b, e in zip(arrays, ends, ends[1:])))


def normalize(values, totals, gain, shift, model_width):
    mean = totals[0][None, :] / model_width
    square = totals[1][None, :] / model_width
    return (values - mean) * lax.rsqrt(square - mean * mean + epsilon) * gain[:, None] + shift[
        :, None
    ]


def contract_first(left, right):
    return lax.dot_general(
        left, right, (((0,), (0,)), ((), ())), preferred_element_type=jnp.float32
    )


def on_device(
    node_latents,
    edge_latents,
    senders,
    receivers,
    edge_count,
    edge_in_weight,
    edge_in_bias,
    edge_out_weight,
    edge_out_bias,
    edge_gain,
    edge_shift,
    node_in_weight,
    node_in_bias,
    node_out_weight,
    node_out_bias,
    node_gain,
    node_shift,
):
    width_part, node_rows = node_latents.shape
    edge_rows = edge_latents.shape[1]
    model_width = edge_out_weight.shape[2]
    layers = edge_in_weight.shape[0]
    coarse_rows = node_rows // 8
    patch_here = lax.axis_index(PATCH)
    patch_start = patch_here * node_rows
    local_receiver = receivers - patch_start
    live = jnp.arange(edge_rows, dtype=jnp.int32) < edge_count[0]
    incidence = (
        (local_receiver[None, :] == jnp.arange(node_rows, dtype=jnp.int32)[:, None]) & live[None, :]
    ).astype(jnp.bfloat16)
    patch_count = lax.axis_size(PATCH)
    owner_patch = senders // node_rows
    within = senders - owner_patch * node_rows
    below = (patch_here + patch_count - 1) % patch_count
    above = (patch_here + 1) % patch_count
    far_index = 3 * node_rows + owner_patch * coarse_rows + within
    sender_index = jnp.where(
        owner_patch == patch_here,
        node_rows + within,
        jnp.where(
            owner_patch == below,
            within,
            jnp.where(owner_patch == above, 2 * node_rows + within, far_index),
        ),
    )
    nodes = node_latents
    edges = edge_latents
    for layer in range(layers):
        w_edge = edge_in_weight[layer]
        w_node = node_in_weight[layer]
        piece = lax.all_gather(nodes, "width", axis=0, tiled=True)
        count = piece.shape[0]

        def product(offset, weight):
            columns = lax.dynamic_slice_in_dim(weight, offset, count, 1)
            return jnp.dot(columns, piece, preferred_element_type=jnp.float32)

        sender_sum = product(model_width, w_edge)
        receiver_sum = product(2 * model_width, w_edge)
        node_first = product(0, w_node)
        sender_part = sender_sum.astype(jnp.bfloat16)
        receiver_part = receiver_sum.astype(jnp.bfloat16)
        beside_all = with_halo(sender_part, ((PATCH, 1),), node_rows)
        coarse = whole_of(sender_part[:, :coarse_rows], (("patch_0", "patch_1"), "patch_2"), 1)
        table = jnp.concatenate([beside_all, coarse], axis=1)
        edge_piece = gathered_copies(edges, "width", 0)
        edge_columns = lax.slice_in_dim(w_edge, 0, edge_piece.shape[0], axis=1)
        edge_first = jnp.dot(edge_columns, edge_piece, preferred_element_type=jnp.float32)
        before = edge_first + jnp.take(table, sender_index, axis=1).astype(jnp.float32)
        before = (
            before
            + jnp.take(receiver_part, local_receiver, axis=1).astype(jnp.float32)
            + edge_in_bias[layer][:, None]
        )
        edge_hidden = jax.nn.silu(before).astype(jnp.bfloat16)
        edge_rows_weight = edge_out_weight[layer]
        edge_partial = contract_first(edge_rows_weight, edge_hidden)
        edge_mlp = sent_and_summed(edge_partial.astype(jnp.bfloat16), "width", 0)
        edge_mlp = edge_mlp + edge_out_bias[layer][:, None]
        edge_totals = in_one(
            (jnp.sum(edge_mlp, axis=0), jnp.sum(edge_mlp * edge_mlp, axis=0)), "width"
        )
        updated = edges.astype(jnp.float32) + normalize(
            edge_mlp, edge_totals, edge_gain[layer], edge_shift[layer], model_width
        )
        edges = jnp.where(live[None, :], updated, jnp.float32(0.0)).astype(jnp.bfloat16)
        aggregate = lax.dot_general(
            edges, incidence, (((1,), (1,)), ((), ())), preferred_element_type=jnp.float32
        ).astype(jnp.bfloat16)
        aggregate_piece = lax.all_gather(aggregate, "width", axis=0, tiled=True)
        aggregate_columns = lax.dynamic_slice_in_dim(
            w_node, model_width, aggregate_piece.shape[0], 1
        )
        node_second = jnp.dot(
            aggregate_columns, aggregate_piece, preferred_element_type=jnp.float32
        )
        node_hidden = jax.nn.silu(node_first + node_second + node_in_bias[layer][:, None]).astype(
            jnp.bfloat16
        )
        node_rows_weight = node_out_weight[layer]
        node_partial = contract_first(node_rows_weight, node_hidden)
        node_mlp = sent_and_summed(node_partial.astype(jnp.bfloat16), "width", 0)
        node_mlp = node_mlp + node_out_bias[layer][:, None]
        node_totals = lax.psum(
            (jnp.sum(node_mlp, axis=0), jnp.sum(node_mlp * node_mlp, axis=0)), "width"
        )
        nodes = (
            nodes.astype(jnp.float32)
            + normalize(node_mlp, node_totals, node_gain[layer], node_shift[layer], model_width)
        ).astype(jnp.bfloat16)
    return (nodes, edges)


def solution(mesh):
    finer = Mesh(
        mesh.devices.reshape(8, 4, 4, mesh.shape["width"]),
        ("patch_0", "patch_1", "patch_2", "width"),
    )
    in_specs = (
        P("width", PATCH),
        P("width", PATCH),
        P(PATCH),
        P(PATCH),
        P(PATCH),
        P(None, "width", None),
        P(None, "width"),
        P(None, "width", None),
        P(None, "width"),
        P(None, "width"),
        P(None, "width"),
        P(None, "width", None),
        P(None, "width"),
        P(None, "width", None),
        P(None, "width"),
        P(None, "width"),
        P(None, "width"),
    )
    out_specs = (P("width", PATCH), P("width", PATCH))
    return jax.shard_map(
        on_device, mesh=finer, in_specs=in_specs, out_specs=out_specs, check_vma=False
    )
```

profile of v0, /device:TPU:1, one launch (start us, length us, event | category | flops | bytes accessed | tf_op | source)
XLA Modules:
  0.0 159.1 jit_solution(324727468950706034)
XLA Ops:
  0.6 1.5 slice_bitcast_fusion
  2.3 4.9 %all_gather.12 = bf16[512,128]{1,0:T(8,128)(2,1)S(1)} all-gather(bf16[256,128]{1,0:T(8,128)(2,1)S(1)} %copy-done.7), channel_id=1, replica_groups=mesh['patch_0'=8,'patch_1'=4,'patch_2'=4,'width'=2] {'width'}, dimensions={0}, use_global_device_ids=true | all-gather | bytes 196608 | tf_op jit(solution)/shard_map/all_gather | solution.py:137
  7.5 8.6 %collective-permute-start.1 = (bf16[256,128]{0,1:T(8,128)(2,1)S(1)}, bf16[256,128]{0,1:T(8,128)(2,1)S(1)}, u32[]{:S(2)}, u32[]{:S(2)}) collective-permute-start(bf16[256,128]{0,1:T(8,128)(2,1)S(1)} %convolution_convert_fusion.9), channel_id=1, source_target_pairs={{2,0},{4,2},{6,4},{8,6},{10,8},{12,10},{14,12},{16,14},{18,16},{20... | collective-permute-start | bytes 196616 | tf_op jit(solution)/shard_map/ppermute | solution.py:21
  16.1 0.7 broadcast_in_dim.73
  16.8 5.2 %all-to-all-start.1 = ((bf16[32,256,16]{1,2,0:T(8,128)(2,1)}), bf16[32,256,16]{1,2,0:T(8,128)(2,1)S(1)}, u32[]{:S(2)}, u32[]{:S(2)}) async-start(bf16[32,256,16]{1,2,0:T(8,128)(2,1)} %broadcast_in_dim.73), calls=%async_computation.1 | async-start | bytes 524288 | tf_op jit(solution)/shard_map/all_to_all | solution.py:28
  22.3 0.6 fusion.96
  22.9 0.5 fusion.92
  23.7 3.9 %gather_fusion.1 = bf16[1024,256]{1,0:T(8,128)(2,1)S(1)} fusion(bf16[256,128]{0,1:T(8,128)(2,1)S(1)} %copy.80, s32[1024]{0:T(1024)S(1)} %fusion.82), kind=kCustom, calls=%fused_computation.1.clone | custom fusion | bytes 1052672 | tf_op jit(solution)/shard_map/jit(_take)/gather | solution.py:158
  27.7 1.0 copy.81
  29.4 3.6 %all-to-all-done.1 = bf16[32,256,16]{1,2,0:T(8,128)(2,1)S(1)} async-done(((bf16[32,256,16]{1,2,0:T(8,128)(2,1)}), bf16[32,256,16]{1,2,0:T(8,128)(2,1)S(1)}, u32[]{:S(2)}, u32[]{:S(2)}) %all-to-all-start.1) | async-done | bytes 262176 | tf_op jit(solution)/shard_map/all_to_all | solution.py:28
  33.0 1.1 broadcast_in_dim.74
  34.0 3.5 %all-to-all-start.2 = ((bf16[4,32,256,16]{2,3,1,0:T(8,128)(2,1)}), bf16[4,32,256,16]{2,3,1,0:T(8,128)(2,1)S(1)}, u32[]{:S(2)}, u32[]{:S(2)}) async-start(bf16[4,32,256,16]{2,3,1,0:T(8,128)(2,1)} %broadcast_in_dim.74), calls=%async_computation.2 | async-start | bytes 2097152 | tf_op jit(solution)/shard_map/all_to_all | solution.py:28
  37.6 2.1 %slice_bitcast_fusion.2 = (bf16[256,1024]{1,0:T(8,128)(2,1)}, bf16[256,1024]{1,0:T(8,128)(2,1)S(1)}) fusion(bf16[2,256,1024]{2,1,0:T(8,128)(2,1)} %param.32), kind=kLoop, calls=%fused_computation.56 | loop fusion | bytes 2097152 | tf_op jit(solution)/shard_map/squeeze | solution.py:136
  39.7 0.9 fusion.46
  40.6 9.1 %all-to-all-done.2 = bf16[4,32,256,16]{2,3,1,0:T(8,128)(2,1)S(1)} async-done(((bf16[4,32,256,16]{2,3,1,0:T(8,128)(2,1)}), bf16[4,32,256,16]{2,3,1,0:T(8,128)(2,1)S(1)}, u32[]{:S(2)}, u32[]{:S(2)}) %all-to-all-start.2) | async-done | bytes 1048608 | tf_op jit(solution)/shard_map/all_to_all | solution.py:28
  49.7 1.2 broadcast_in_dim.72
  50.8 8.2 %all-to-all-start = ((bf16[2,256,1024]{2,1,0:T(8,128)(2,1)}), bf16[2,256,1024]{2,1,0:T(8,128)(2,1)}, u32[]{:S(2)}, u32[]{:S(2)}) async-start(bf16[2,256,1024]{2,1,0:T(8,128)(2,1)} %broadcast_in_dim.72), calls=%async_computation | async-start | bytes 2097152 | tf_op jit(solution)/shard_map/all_to_all | solution.py:28
  59.3 3.9 %gather_fusion = bf16[1024,256]{1,0:T(8,128)(2,1)S(1)} fusion(bf16[256,2432]{0,1:T(8,128)(2,1)S(1)} %pad_maximum_fusion, s32[1024]{0:T(1024)S(1)} %broadcast_clamp_fusion), kind=kCustom, calls=%fused_computation.clone | custom fusion | bytes 1052672 | tf_op jit(solution)/shard_map/jit(_take)/gather | solution.py:155
  63.5 2.5 %convolution_convert_fusion.1 = bf16[1024,512]{0,1:T(8,128)(2,1)S(1)} fusion(bf16[512,1024]{1,0:T(8,128)(2,1)} %bitcast.3, bf16[1024,256]{0,1:T(8,128)(2,1)} %copy.81, bf16[1024,256]{0,1:T(8,128)(2,1)S(1)} %copy.79, f32[256]{0:T(256)} %bitcast.161, pred[1024]{0:T(1024)(128)(4,1)S(1)} %get-tuple-element.26, pred[1024]{0:T(1024)(128)(4,1)S(1)} %get-tuple-element.56, ...), kind=kOutput, calls=%fused_computation.7 | convolution fusion | flops 540540928 | bytes 3673088 | tf_op jit(solution)/shard_map/dot_general | solution.py:81
  66.0 4.2 %all_to_all.62 = bf16[2,256,1024]{2,1,0:T(8,128)(2,1)S(1)} all-to-all(bf16[2,256,1024]{2,1,0:T(8,128)(2,1)S(1)} %bitcast.137), channel_id=1, replica_groups=mesh['patch_0'=8,'patch_1'=4,'patch_2'=4,'width'=2] {'width'}, dimensions={0} | all-to-all | bytes 2097152 | tf_op jit(solution)/shard_map/all_to_all | solution.py:56
  70.7 3.8 %all_to_all.63 = f32[2,1,2048]{2,1,0:T(1,128)S(1)} all-to-all(f32[2,1,2048]{2,1,0:T(1,128)S(1)} %broadcast_in_dim.75), channel_id=1, replica_groups=mesh['patch_0'=8,'patch_1'=4,'patch_2'=4,'width'=2] {'width'}, dimensions={0} | all-to-all | bytes 32768 | tf_op jit(solution)/shard_map/all_to_all | solution.py:28
  74.5 0.4 select_convert_fusion.1
  74.9 0.3 convolution_convert_fusion.7
  75.3 1.9 %all_gather.13 = bf16[512,128]{1,0:T(8,128)(2,1)S(1)} all-gather(bf16[256,128]{1,0:T(8,128)(2,1)S(1)} %convolution_convert_fusion.7), channel_id=1, replica_groups=mesh['patch_0'=8,'patch_1'=4,'patch_2'=4,'width'=2] {'width'}, dimensions={0}, use_global_device_ids=true | all-gather | bytes 196608 | tf_op jit(solution)/shard_map/all_gather | solution.py:176
  77.2 1.4 convolution_convert_fusion.3
  78.6 3.8 %all_to_all.64 = bf16[2,256,128]{1,2,0:T(8,128)(2,1)S(1)} all-to-all(bf16[2,256,128]{1,2,0:T(8,128)(2,1)S(1)} %bitcast.138), channel_id=1, replica_groups=mesh['patch_0'=8,'patch_1'=4,'patch_2'=4,'width'=2] {'width'}, dimensions={0} | all-to-all | bytes 262144 | tf_op jit(solution)/shard_map/all_to_all | solution.py:56
  82.6 2.5 %all-reduce.1 = (f32[128]{0:T(128)S(1)}, f32[128]{0:T(128)S(1)}) all-reduce(f32[128]{0:T(128)S(1)} %get-tuple-element.19, f32[128]{0:T(128)S(1)} %get-tuple-element.18), channel_id=1, replica_groups=mesh['patch_0'=8,'patch_1'=4,'patch_2'=4,'width'=2] {'width'}, use_global_device_ids=true, to_apply=%region_8.11 | all-reduce | flops 256 | bytes 2048 | tf_op jit(solution)/shard_map/psum | solution.py:190
  85.2 1.9 %all_gather.14 = bf16[512,128]{0,1:T(8,128)(2,1)S(1)} all-gather(bf16[256,128]{0,1:T(8,128)(2,1)S(1)} %add_convert_fusion.1), channel_id=1, replica_groups=mesh['patch_0'=8,'patch_1'=4,'patch_2'=4,'width'=2] {'width'}, dimensions={0}, use_global_device_ids=true | all-gather | bytes 196608 | tf_op jit(solution)/shard_map/all_gather | solution.py:137
  87.4 17.0 %all_to_all.65 = bf16[32,256,16]{1,2,0:T(8,128)(2,1)S(1)} all-to-all(bf16[32,256,16]{1,2,0:T(8,128)(2,1)S(1)} %broadcast_in_dim.78), channel_id=1, replica_groups=mesh['patch_0'=8,'patch_1'=4,'patch_2'=4,'width'=2] {'patch_0','patch_1'}, dimensions={0} | all-to-all | bytes 524288 | tf_op jit(solution)/shard_map/all_to_all | solution.py:28
  104.4 1.1 broadcast_in_dim.79
  105.5 3.5 %all-to-all-start.8 = ((bf16[4,32,256,16]{2,3,1,0:T(8,128)(2,1)}), bf16[4,32,256,16]{2,3,1,0:T(8,128)(2,1)S(1)}, u32[]{:S(2)}, u32[]{:S(2)}) async-start(bf16[4,32,256,16]{2,3,1,0:T(8,128)(2,1)} %broadcast_in_dim.79), calls=%async_computation.8 | async-start | bytes 2097152 | tf_op jit(solution)/shard_map/all_to_all | solution.py:28
  109.0 1.4 collective-permute-start.2
  110.4 5.5 %collective-permute-start.3 = (bf16[256,128]{0,1:T(8,128)(2,1)S(1)}, bf16[256,128]{0,1:T(8,128)(2,1)S(1)}, u32[]{:S(2)}, u32[]{:S(2)}) collective-permute-start(bf16[256,128]{0,1:T(8,128)(2,1)S(1)} %fusion.9), channel_id=1, source_target_pairs={{2,0},{4,2},{6,4},{8,6},{10,8},{12,10},{14,12},{16,14},{18,16},{20... | collective-permute-start | bytes 196616 | tf_op jit(solution)/shard_map/ppermute | solution.py:21
  116.4 3.9 %gather_fusion.3 = bf16[1024,256]{1,0:T(8,128)(2,1)S(1)} fusion(bf16[256,128]{0,1:T(8,128)(2,1)S(1)} %fusion.10, s32[1024]{0:T(1024)S(1)} %fusion.82), kind=kCustom, calls=%fused_computation.3.clone | custom fusion | bytes 1052672 | tf_op jit(solution)/shard_map/jit(_take)/gather | solution.py:158
  120.4 1.0 copy.89
  121.5 1.1 broadcast_in_dim.77
  122.7 8.6 %all-to-all-start.6 = ((bf16[2,256,1024]{2,1,0:T(8,128)(2,1)}), bf16[2,256,1024]{2,1,0:T(8,128)(2,1)}, u32[]{:S(2)}, u32[]{:S(2)}) async-start(bf16[2,256,1024]{2,1,0:T(8,128)(2,1)} %broadcast_in_dim.77), calls=%async_computation.6 | async-start | bytes 2097152 | tf_op jit(solution)/shard_map/all_to_all | solution.py:28
  131.5 3.9 %gather_fusion.2 = bf16[1024,256]{1,0:T(8,128)(2,1)S(1)} fusion(bf16[256,2432]{0,1:T(8,128)(2,1)S(1)} %pad_maximum_fusion.1, s32[1024]{0:T(1024)S(1)} %broadcast_clamp_fusion), kind=kCustom, calls=%fused_computation.2.clone | custom fusion | bytes 1052672 | tf_op jit(solution)/shard_map/jit(_take)/gather | solution.py:155
  135.4 1.0 copy.88
  136.4 2.6 %convolution_convert_fusion = bf16[1024,512]{0,1:T(8,128)(2,1)S(1)} fusion(bf16[512,1024]{1,0:T(8,128)(2,1)} %bitcast.25, bf16[1024,256]{0,1:T(8,128)(2,1)} %copy.89, bf16[1024,256]{0,1:T(8,128)(2,1)} %copy.88, f32[256]{0:T(256)S(1)} %bitcast.159, pred[1024]{0:T(1024)(128)(4,1)S(1)} %get-tuple-element.26, pred[1024]{0:T(1024)(128)(4,1)S(1)} %get-tuple-element.56, ...), kind=kOutput, calls=%fused_computation.6 | convolution fusion | flops 540540928 | bytes 3673088 | tf_op jit(solution)/shard_map/dot_general | solution.py:81
  139.0 4.4 %all_to_all.66 = bf16[2,256,1024]{2,1,0:T(8,128)(2,1)S(1)} all-to-all(bf16[2,256,1024]{2,1,0:T(8,128)(2,1)S(1)} %bitcast.136), channel_id=1, replica_groups=mesh['patch_0'=8,'patch_1'=4,'patch_2'=4,'width'=2] {'width'}, dimensions={0} | all-to-all | bytes 2097152 | tf_op jit(solution)/shard_map/all_to_all | solution.py:56
  143.9 3.8 %all_to_all.67 = f32[2,1,2048]{2,1,0:T(1,128)S(1)} all-to-all(f32[2,1,2048]{2,1,0:T(1,128)S(1)} %broadcast_in_dim.80), channel_id=1, replica_groups=mesh['patch_0'=8,'patch_1'=4,'patch_2'=4,'width'=2] {'width'}, dimensions={0} | all-to-all | bytes 32768 | tf_op jit(solution)/shard_map/all_to_all | solution.py:28
  147.7 0.4 select_convert_fusion
  148.5 1.9 %all_gather.15 = bf16[512,128]{1,0:T(8,128)(2,1)S(1)} all-gather(bf16[256,128]{1,0:T(8,128)(2,1)S(1)} %convolution_convert_fusion.4), channel_id=1, replica_groups=mesh['patch_0'=8,'patch_1'=4,'patch_2'=4,'width'=2] {'width'}, dimensions={0}, use_global_device_ids=true | all-gather | bytes 196608 | tf_op jit(solution)/shard_map/all_gather | solution.py:176
  150.4 1.4 convolution_convert_fusion.2
  151.8 3.8 %all_to_all.68 = bf16[2,256,128]{1,2,0:T(8,128)(2,1)S(1)} all-to-all(bf16[2,256,128]{1,2,0:T(8,128)(2,1)S(1)} %bitcast.139), channel_id=1, replica_groups=mesh['patch_0'=8,'patch_1'=4,'patch_2'=4,'width'=2] {'width'}, dimensions={0} | all-to-all | bytes 262144 | tf_op jit(solution)/shard_map/all_to_all | solution.py:56
  155.7 2.5 %all-reduce = (f32[128]{0:T(128)S(1)}, f32[128]{0:T(128)S(1)}) all-reduce(f32[128]{0:T(128)S(1)} %get-tuple-element.17, f32[128]{0:T(128)S(1)} %get-tuple-element.16), channel_id=1, replica_groups=mesh['patch_0'=8,'patch_1'=4,'patch_2'=4,'width'=2] {'width'}, use_global_device_ids=true, to_apply=%region_17.20 | all-reduce | flops 256 | bytes 2048 | tf_op jit(solution)/shard_map/psum | solution.py:190
  158.3 0.7 copy.95
  (92 shorter events, 4.1 us)
Async XLA Ops:
  0.6 1.5 copy-start.7
  2.2 21.3 %copy-start.1 = (bf16[256,1536]{1,0:T(8,128)(2,1)}, bf16[256,1536]{1,0:T(8,128)(2,1)S(1)}, u32[]{:S(2)}) copy-start(bf16[256,1536]{1,0:T(8,128)(2,1)S(1)} %get-tuple-element.29) | copy-start | bytes 2359300
  2.2 20.1 %copy-start.8 = (s32[1024]{0:T(1024)S(1)}, s32[1024]{0:T(1024)}, u32[]{:S(2)}) copy-start(s32[1024]{0:T(1024)} %param.24) | copy-start | bytes 12292
  2.2 20.1 %copy-start.9 = (s32[1024]{0:T(1024)S(1)}, s32[1024]{0:T(1024)}, u32[]{:S(2)}) copy-start(s32[1024]{0:T(1024)} %param.23) | copy-start | bytes 12292
  2.2 20.1 %copy-start.10 = (f32[2,256]{1,0:T(2,128)S(1)}, f32[2,256]{1,0:T(2,128)}, u32[]{:S(2)}) copy-start(f32[2,256]{1,0:T(2,128)} %param.27) | copy-start | bytes 6148
  2.2 20.7 %copy-start.11 = (f32[2,256]{1,0:T(2,128)S(1)}, f32[2,256]{1,0:T(2,128)}, u32[]{:S(2)}) copy-start(f32[2,256]{1,0:T(2,128)} %param.29) | copy-start | bytes 6148
  2.2 20.7 %copy-start.12 = (f32[2,256]{1,0:T(2,128)S(1)}, f32[2,256]{1,0:T(2,128)}, u32[]{:S(2)}) copy-start(f32[2,256]{1,0:T(2,128)} %param.30) | copy-start | bytes 6148
  2.2 20.7 %copy-start.13 = (f32[2,256]{1,0:T(2,128)S(1)}, f32[2,256]{1,0:T(2,128)}, u32[]{:S(2)}) copy-start(f32[2,256]{1,0:T(2,128)} %param.31) | copy-start | bytes 6148
  2.2 20.7 %copy-start.14 = (f32[2,256]{1,0:T(2,128)S(1)}, f32[2,256]{1,0:T(2,128)}, u32[]{:S(2)}) copy-start(f32[2,256]{1,0:T(2,128)} %param.33) | copy-start | bytes 6148
  2.3 21.2 %copy-start.15 = (f32[2,256]{1,0:T(2,128)S(1)}, f32[2,256]{1,0:T(2,128)}, u32[]{:S(2)}) copy-start(f32[2,256]{1,0:T(2,128)} %param.35) | copy-start | bytes 6148
  7.4 51.8 %collective-permute-start = (bf16[256,128]{0,1:T(8,128)(2,1)S(1)}, bf16[256,128]{0,1:T(8,128)(2,1)S(1)}, u32[]{:S(2)}, u32[]{:S(2)}) collective-permute-start(bf16[256,128]{0,1:T(8,128)(2,1)S(1)} %convolution_convert_fusion.9), channel_id=1, source_target_pairs={{0,2},{2,4},{4,6},{6,8},{8,10},{10,12},{12,14},{14,16},{16,18},{18... | collective-permute-start | bytes 196616 | tf_op jit(solution)/shard_map/ppermute | solution.py:20
  7.5 51.7 %collective-permute-start.1 = (bf16[256,128]{0,1:T(8,128)(2,1)S(1)}, bf16[256,128]{0,1:T(8,128)(2,1)S(1)}, u32[]{:S(2)}, u32[]{:S(2)}) collective-permute-start(bf16[256,128]{0,1:T(8,128)(2,1)S(1)} %convolution_convert_fusion.9), channel_id=1, source_target_pairs={{2,0},{4,2},{6,4},{8,6},{10,8},{12,10},{14,12},{16,14},{18,16},{20... | collective-permute-start | bytes 196616 | tf_op jit(solution)/shard_map/ppermute | solution.py:21
  16.8 16.2 %all-to-all-start.1 = ((bf16[32,256,16]{1,2,0:T(8,128)(2,1)}), bf16[32,256,16]{1,2,0:T(8,128)(2,1)S(1)}, u32[]{:S(2)}, u32[]{:S(2)}) async-start(bf16[32,256,16]{1,2,0:T(8,128)(2,1)} %broadcast_in_dim.73), calls=%async_computation.1 | async-start | bytes 524288 | tf_op jit(solution)/shard_map/all_to_all | solution.py:28
  23.7 5.6 %copy-start.16 = (f32[2,256]{1,0:T(2,128)S(1)}, f32[2,256]{1,0:T(2,128)}, u32[]{:S(2)}) copy-start(f32[2,256]{1,0:T(2,128)} %param.36) | copy-start | bytes 6148
  29.4 8.2 %copy-start.17 = (f32[2,256]{1,0:T(2,128)S(1)}, f32[2,256]{1,0:T(2,128)}, u32[]{:S(2)}) copy-start(f32[2,256]{1,0:T(2,128)} %param.37) | copy-start | bytes 6148
  34.0 15.7 %all-to-all-start.2 = ((bf16[4,32,256,16]{2,3,1,0:T(8,128)(2,1)}), bf16[4,32,256,16]{2,3,1,0:T(8,128)(2,1)S(1)}, u32[]{:S(2)}, u32[]{:S(2)}) async-start(bf16[4,32,256,16]{2,3,1,0:T(8,128)(2,1)} %broadcast_in_dim.74), calls=%async_computation.2 | async-start | bytes 2097152 | tf_op jit(solution)/shard_map/all_to_all | solution.py:28
  37.5 12.1 %copy-start = (bf16[256,1024]{1,0:T(8,128)(2,1)S(1)}, bf16[256,1024]{1,0:T(8,128)(2,1)}, u32[]{:S(2)}) copy-start(bf16[256,1024]{1,0:T(8,128)(2,1)} %param.22) | copy-start | bytes 1572868
  39.7 0.9 copy-start.4
  50.8 12.6 %all-to-all-start = ((bf16[2,256,1024]{2,1,0:T(8,128)(2,1)}), bf16[2,256,1024]{2,1,0:T(8,128)(2,1)}, u32[]{:S(2)}, u32[]{:S(2)}) async-start(bf16[2,256,1024]{2,1,0:T(8,128)(2,1)} %broadcast_in_dim.72), calls=%async_computation | async-start | bytes 2097152 | tf_op jit(solution)/shard_map/all_to_all | solution.py:28
  74.5 2.7 %copy-start.5 = (bf16[256,1024]{1,0:T(8,128)(2,1)S(1)}, bf16[256,1024]{1,0:T(8,128)(2,1)}, u32[]{:S(2)}) copy-start(bf16[256,1024]{1,0:T(8,128)(2,1)} %copy-done.4) | copy-start | bytes 1572868
  104.4 11.6 %copy-start.2 = (bf16[256,1024]{1,0:T(8,128)(2,1)S(1)}, bf16[256,1024]{1,0:T(8,128)(2,1)}, u32[]{:S(2)}) copy-start(bf16[256,1024]{1,0:T(8,128)(2,1)} %get-tuple-element.30) | copy-start | bytes 1572868
  105.5 16.0 %all-to-all-start.8 = ((bf16[4,32,256,16]{2,3,1,0:T(8,128)(2,1)}), bf16[4,32,256,16]{2,3,1,0:T(8,128)(2,1)S(1)}, u32[]{:S(2)}, u32[]{:S(2)}) async-start(bf16[4,32,256,16]{2,3,1,0:T(8,128)(2,1)} %broadcast_in_dim.79), calls=%async_computation.8 | async-start | bytes 2097152 | tf_op jit(solution)/shard_map/all_to_all | solution.py:28
  109.0 22.4 %collective-permute-start.2 = (bf16[256,128]{0,1:T(8,128)(2,1)S(1)}, bf16[256,128]{0,1:T(8,128)(2,1)S(1)}, u32[]{:S(2)}, u32[]{:S(2)}) collective-permute-start(bf16[256,128]{0,1:T(8,128)(2,1)S(1)} %fusion.9), channel_id=1, source_target_pairs={{0,2},{2,4},{4,6},{6,8},{8,10},{10,12},{12,14},{14,16},{16,18},{18... | collective-permute-start | bytes 196616 | tf_op jit(solution)/shard_map/ppermute | solution.py:20
  110.4 21.0 %collective-permute-start.3 = (bf16[256,128]{0,1:T(8,128)(2,1)S(1)}, bf16[256,128]{0,1:T(8,128)(2,1)S(1)}, u32[]{:S(2)}, u32[]{:S(2)}) collective-permute-start(bf16[256,128]{0,1:T(8,128)(2,1)S(1)} %fusion.9), channel_id=1, source_target_pairs={{2,0},{4,2},{6,4},{8,6},{10,8},{12,10},{14,12},{16,14},{18,16},{20... | collective-permute-start | bytes 196616 | tf_op jit(solution)/shard_map/ppermute | solution.py:21
  122.7 13.8 %all-to-all-start.6 = ((bf16[2,256,1024]{2,1,0:T(8,128)(2,1)}), bf16[2,256,1024]{2,1,0:T(8,128)(2,1)}, u32[]{:S(2)}, u32[]{:S(2)}) async-start(bf16[2,256,1024]{2,1,0:T(8,128)(2,1)} %broadcast_in_dim.77), calls=%async_computation.6 | async-start | bytes 2097152 | tf_op jit(solution)/shard_map/all_to_all | solution.py:28
  147.7 2.7 %copy-start.3 = (bf16[256,1024]{1,0:T(8,128)(2,1)S(1)}, bf16[256,1024]{1,0:T(8,128)(2,1)}, u32[]{:S(2)}) copy-start(bf16[256,1024]{1,0:T(8,128)(2,1)} %get-tuple-element.30) | copy-start | bytes 1572868
  148.1 7.5 %copy-start.6 = (bf16[256,1024]{1,0:T(8,128)(2,1)}, bf16[256,1024]{1,0:T(8,128)(2,1)S(1)}, u32[]{:S(2)}) copy-start(bf16[256,1024]{1,0:T(8,128)(2,1)S(1)} %select_convert_fusion) | copy-start | bytes 1572868
where the time goes:
time: 160 us; the launch traced here: 159 us
  blocking collectives  56.4 us (35%)
  starting transfers between devices  44.6 us (28%)
  local copies, waits for them, and re-layouts  30.2 us (19%)
  waiting for transfers between devices  12.8 us (8%)
  matrix products  10.6 us (7%)
  other arithmetic  2.44 us (2%)
  between operations  1.98 us (1%)
    all_to_all x5, starting transfers between devices, from_everyone(): return lax.all_to_all(copies, axis, split_axis=0, concat_axis=0, tiled=True)  29 us
    all_to_all x3, blocking collectives, from_everyone(): return lax.all_to_all(copies, axis, split_axis=0, concat_axis=0, tiled=True)  24.5 us
    all_to_all x4, blocking collectives, sent_and_summed(): lax.all_to_all(in_blocks(shard, dim, length), axis, 0, 0, tiled=True)  16.3 us
    ppermute x2, starting transfers between devices, with_halo(): after = lax.ppermute(initial, axis, down)  14.1 us
    all_to_all x5, waiting for transfers between devices, from_everyone(): return lax.all_to_all(copies, axis, split_axis=0, concat_axis=0, tiled=True)  12.8 us
    gather x4, local copies, waits for them, and re-layouts, on_device(): jnp.take(receiver_part, local_receiver, axis=1).astype(jnp.float32)  9.89 us
    gather x4, local copies, waits for them, and re-layouts, on_device(): jnp.take(table, sender_index, axis=1).astype(jnp.float32)  9.09 us
    dot_general x4, matrix products, contract_first(): lax.dot_general(left, right, (((0,), (0,)), ((), ())), preferred_element_...  7.93 us
  transfers between devices with their start and end apart: 9, of which 3 were waited for; matrix products, arithmetic and copies ran while one was open for 18% of the time, Pallas kernels for 0%

commit v1 on v0

v1 whole, which is shorter than its diff:
```python
import functools

import jax
import jax.numpy as jnp
from jax import lax
from jax.experimental import pallas as pl
from jax.experimental.pallas import tpu as pltpu
from jax.sharding import Mesh
from jax.sharding import PartitionSpec as P

Z, Y, X = "patch_0", "patch_1", "patch_2"
PATCH = (Z, Y, X)
PLANE = (Y, X)
EPSILON = 1e-05
EDGE_BLOCK = 256
VMEM_LIMIT = 48 * 1024 * 1024


def dot(left, right, contract=((1,), (0,))):
    return lax.dot_general(left, right, (contract, ((), ())), preferred_element_type=jnp.float32)


def silu(v):
    h = 0.5 * v
    return h + h * jnp.tanh(h)


def layer_norm(values, gain, shift):
    width = values.shape[0]
    mean = jnp.sum(values, axis=0, keepdims=True) * (1.0 / width)
    square = jnp.sum(values * values, axis=0, keepdims=True) * (1.0 / width)
    return (values - mean) * lax.rsqrt(square - mean * mean + EPSILON) * gain + shift


def in_order(first, mine, other):
    return jnp.concatenate([jnp.where(first, mine, other), jnp.where(first, other, mine)], axis=0)


def gather_kernel(index_ref, below_ref, here_ref, above_ref, coarse_ref, out_ref):
    index = index_ref[...]
    rows = index.shape[0]
    lane = lax.broadcasted_iota(jnp.int32, (rows, 128), 1)

    def selection(start, length):
        tiles = []
        for j in range(start, start + length, 128):
            tiles.append(jnp.where(index == lane + j, 1.0, 0.0).astype(jnp.bfloat16))
        return jnp.concatenate(tiles, axis=1) if len(tiles) > 1 else tiles[0]

    near = jnp.concatenate([below_ref[...], here_ref[...], above_ref[...]], axis=0)
    total = dot(selection(0, near.shape[0]), near)
    total = total + dot(selection(near.shape[0], coarse_ref.shape[0]), coarse_ref[...])
    out_ref[...] = total.astype(jnp.bfloat16)


def gathered(index, below, here, above, coarse):
    slots = index.shape[0]
    width = here.shape[1]
    whole = lambda a: pl.BlockSpec(a.shape, lambda i: (0, 0))
    return pl.pallas_call(
        gather_kernel,
        grid=(slots // EDGE_BLOCK,),
        in_specs=[
            pl.BlockSpec((EDGE_BLOCK, 128), lambda i: (i, 0)),
            whole(below),
            whole(here),
            whole(above),
            whole(coarse),
        ],
        out_specs=pl.BlockSpec((EDGE_BLOCK, width), lambda i: (i, 0)),
        out_shape=jax.ShapeDtypeStruct((slots, width), jnp.bfloat16),
        compiler_params=pltpu.CompilerParams(vmem_limit_bytes=VMEM_LIMIT),
        cost_estimate=pl.CostEstimate(
            flops=2 * slots * width * 2432, bytes_accessed=3 << 20, transcendentals=0
        ),
        name="gather_senders",
    )(index, below, here, above, coarse)


def update_kernel(
    first_layer,
    last_layer,
    scalar_ref,
    edge_a_ref,
    edge_b_ref,
    sent_a_ref,
    sent_b_ref,
    receiver_ref,
    node_a_ref,
    node_b_ref,
    wa_ref,
    wb_ref,
    ea_ref,
    eb_ref,
    va_ref,
    vb_ref,
    oa_ref,
    ob_ref,
    vec_a_ref,
    vec_b_ref,
    *rest,
):
    if last_layer:
        edge_out_ref, node_out_ref, part_ref, out_weight_ref, sum_ref = rest
        rows_out_ref = None
    else:
        edge_out_ref, node_out_ref, rows_out_ref, part_ref, out_weight_ref, sum_ref = rest
    step = pl.program_id(0)
    first = scalar_ref[0] == 0
    count = scalar_ref[1]
    half = vec_a_ref.shape[1]
    width = 2 * half

    def stacked(a, b):
        return jnp.concatenate([a, b], axis=0)

    def nodes_now():
        if first_layer:
            return in_order(first, node_a_ref[...], node_b_ref[...])
        return node_a_ref[...]

    w = stacked(wa_ref[0], wb_ref[0])
    vec_a, vec_b = vec_a_ref[0], vec_b_ref[0]
    hidden_vec = stacked(vec_a, vec_b)
    feature_vec = in_order(first, vec_a, vec_b)

    @pl.when(step == 0)
    def _():
        part_ref[...] = dot(w[:, 2 * width :], nodes_now()).astype(jnp.bfloat16)
        out_weight_ref[...] = stacked(ea_ref[0], eb_ref[0]).T
        sum_ref[...] = jnp.zeros_like(sum_ref)

    if first_layer:
        edges = in_order(first, edge_a_ref[...], edge_b_ref[...])
    else:
        edges = edge_a_ref[...]
    slots = edges.shape[1]
    sent_a, sent_b = sent_a_ref[...], sent_b_ref[...]
    sent = jnp.concatenate(
        [jnp.where(first, sent_a, sent_b), jnp.where(first, sent_b, sent_a)], axis=1
    )
    nodes_here = sum_ref.shape[1]
    live = lax.broadcasted_iota(jnp.int32, (1, slots), 1) + step * slots < count
    receiver = receiver_ref[...]
    incidence = jnp.where(
        (lax.broadcasted_iota(jnp.int32, (nodes_here, slots), 0) == receiver) & live, 1.0, 0.0
    ).astype(jnp.bfloat16)
    before = dot(w[:, :width], edges) + dot(w[:, width : 2 * width], sent, ((1,), (1,)))
    before = before + dot(part_ref[...], incidence) + hidden_vec[:, 0:1]
    hidden = silu(before).astype(jnp.bfloat16)
    mlp = dot(out_weight_ref[...], hidden) + feature_vec[:, 1:2]
    updated = edges.astype(jnp.float32) + layer_norm(mlp, feature_vec[:, 2:3], feature_vec[:, 3:4])
    updated = jnp.where(live, updated, 0.0).astype(jnp.bfloat16)
    sum_ref[...] += dot(updated, incidence, ((1,), (1,)))
    if last_layer:
        edge_out_ref[...] = jnp.where(first, updated[:half], updated[half:])
    else:
        edge_out_ref[...] = updated

    @pl.when(step == pl.num_programs(0) - 1)
    def _():
        nodes = nodes_now()
        v = stacked(va_ref[0], vb_ref[0])
        aggregate = sum_ref[...].astype(jnp.bfloat16)
        node_before = dot(v[:, :width], nodes) + dot(v[:, width:], aggregate)
        node_hidden = silu(node_before + hidden_vec[:, 4:5]).astype(jnp.bfloat16)
        node_weight = stacked(oa_ref[0], ob_ref[0]).T
        node_mlp = dot(node_weight, node_hidden) + feature_vec[:, 5:6]
        new = nodes.astype(jnp.float32) + layer_norm(
            node_mlp, feature_vec[:, 6:7], feature_vec[:, 7:8]
        )
        new = new.astype(jnp.bfloat16)
        mine = jnp.where(first, new[:half], new[half:])
        if last_layer:
            node_out_ref[...] = mine
        else:
            node_out_ref[...] = new
            rows_out_ref[...] = mine.T


def updated_graph(layer, layers, scalars, edges, sent, receiver, nodes, weights):
    first_layer, last_layer = layer == 0, layer == layers - 1
    slots = edges[0].shape[1]
    node_rows = nodes[0].shape[1]
    half = sent[0].shape[1]
    width = 2 * half

    def by_slot(a):
        return pl.BlockSpec((a.shape[0], EDGE_BLOCK), lambda i: (0, i))

    def by_row(a):
        return pl.BlockSpec((EDGE_BLOCK, a.shape[1]), lambda i: (i, 0))

    def whole(a):
        return pl.BlockSpec(a.shape, lambda i: (0, 0))

    def of_layer(a):
        return pl.BlockSpec((1, *a.shape[1:]), lambda i: (layer, 0, 0))

    edge_width = half if last_layer else width
    out_shape = [
        jax.ShapeDtypeStruct((edge_width, slots), jnp.bfloat16),
        jax.ShapeDtypeStruct((edge_width, node_rows), jnp.bfloat16),
    ]
    out_specs = [
        pl.BlockSpec((edge_width, EDGE_BLOCK), lambda i: (0, i)),
        pl.BlockSpec((edge_width, node_rows), lambda i: (0, 0)),
    ]
    if not last_layer:
        out_shape.append(jax.ShapeDtypeStruct((node_rows, half), jnp.bfloat16))
        out_specs.append(pl.BlockSpec((node_rows, half), lambda i: (0, 0)))
    flops = 2 * slots * width * (3 * width + 2 * node_rows)
    return pl.pallas_call(
        functools.partial(update_kernel, first_layer, last_layer),
        grid=(slots // EDGE_BLOCK,),
        in_specs=[
            pl.BlockSpec(memory_space=pltpu.SMEM),
            by_slot(edges[0]),
            by_slot(edges[1]),
            by_row(sent[0]),
            by_row(sent[1]),
            by_slot(receiver),
            whole(nodes[0]),
            whole(nodes[1]),
            *[of_layer(a) for a in weights],
        ],
        out_specs=out_specs,
        out_shape=out_shape,
        scratch_shapes=[
            pltpu.VMEM((width, node_rows), jnp.bfloat16),
            pltpu.VMEM((width, width), jnp.bfloat16),
            pltpu.VMEM((width, node_rows), jnp.float32),
        ],
        compiler_params=pltpu.CompilerParams(vmem_limit_bytes=VMEM_LIMIT),
        cost_estimate=pl.CostEstimate(
            flops=flops, bytes_accessed=8 << 20, transcendentals=slots * width
        ),
        name="update_graph",
    )(scalars, *edges, *sent, receiver, *nodes, *weights)


def from_other(a):
    return lax.ppermute(a, "width", [(0, 1), (1, 0)])


def from_everyone(shard, axes):
    copies = jnp.broadcast_to(shard, (lax.axis_size(axes), *shard.shape))
    parts = lax.all_to_all(copies, axes, split_axis=0, concat_axis=0, tiled=True)
    return parts.reshape(-1, shard.shape[-1])


def beside(rows):
    size = lax.axis_size(PATCH)
    up = [(i, (i + 1) % size) for i in range(size)]
    down = [(j, i) for i, j in up]
    return lax.ppermute(rows, PATCH, up), lax.ppermute(rows, PATCH, down)


def on_device(
    node_latents,
    edge_latents,
    senders,
    receivers,
    edge_count,
    edge_in_weight,
    edge_in_bias,
    edge_out_weight,
    edge_out_bias,
    edge_gain,
    edge_shift,
    node_in_weight,
    node_in_bias,
    node_out_weight,
    node_out_bias,
    node_gain,
    node_shift,
):
    node_rows = node_latents.shape[1]
    layers = edge_in_weight.shape[0]
    coarse_rows = node_rows // 8
    patch_here = lax.axis_index(PATCH)
    patches = lax.axis_size(PATCH)
    plane = lax.axis_size(PLANE)
    scalars = jnp.stack([lax.axis_index("width"), edge_count[0]]).astype(jnp.int32)

    rows = node_latents.T
    below, above = beside(rows)
    coarse = from_everyone(from_everyone(rows[:coarse_rows], Z), PLANE)

    vectors = jnp.stack(
        [
            edge_in_bias,
            edge_out_bias,
            edge_gain,
            edge_shift,
            node_in_bias,
            node_out_bias,
            node_gain,
            node_shift,
        ],
        axis=2,
    )
    own = (edge_in_weight, edge_out_weight, node_in_weight, node_out_weight, vectors)
    weights = []
    for a in own:
        weights += [a, from_other(a)]

    owner = senders // node_rows
    within = senders - owner * node_rows
    place = (owner % plane) * (patches // plane) + owner // plane
    index = jnp.where(
        owner == patch_here,
        node_rows + within,
        jnp.where(
            owner == (patch_here + patches - 1) % patches,
            within,
            jnp.where(
                owner == (patch_here + 1) % patches,
                2 * node_rows + within,
                3 * node_rows + place * coarse_rows + within,
            ),
        ),
    )
    index = jnp.broadcast_to(index[:, None], (index.shape[0], 128))
    receiver = (receivers - patch_here * node_rows)[None, :]

    edges = (edge_latents, from_other(edge_latents))
    nodes = (node_latents, from_other(node_latents))
    for layer in range(layers):
        sent = gathered(index, below, rows, above, coarse)
        sent = (sent, from_other(sent))
        results = updated_graph(
            layer, layers, scalars, edges, sent, receiver, nodes, weights
        )
        if layer < layers - 1:
            edges, nodes, rows = results
            edges, nodes = (edges, edges), (nodes, nodes)
            below, above = beside(rows)
            coarse = from_everyone(from_everyone(rows[:coarse_rows], Z), PLANE)
    return (results[1], results[0])


def solution(mesh):
    finer = Mesh(
        mesh.devices.reshape(8, 4, 4, mesh.shape["width"]),
        (*PATCH, "width"),
    )
    in_specs = (
        P("width", PATCH),
        P("width", PATCH),
        P(PATCH),
        P(PATCH),
        P(PATCH),
        P(None, "width", None),
        P(None, "width"),
        P(None, "width", None),
        P(None, "width"),
        P(None, "width"),
        P(None, "width"),
        P(None, "width", None),
        P(None, "width"),
        P(None, "width", None),
        P(None, "width"),
        P(None, "width"),
        P(None, "width"),
    )
    out_specs = (P("width", PATCH), P("width", PATCH))
    return jax.shard_map(
        on_device, mesh=finer, in_specs=in_specs, out_specs=out_specs, check_vma=False
    )
```

time: 160 us -> 131 us (0.82)
  blocking collectives: 56.4 us -> 25.6 us
  Pallas kernels: 0 us -> 28.8 us
  matrix products: 10.6 us -> 0 us
  starting transfers between devices: 44.6 us -> 38.2 us
  local copies, waits for them, and re-layouts: 30.2 us -> 24.2 us
  other arithmetic: 2.44 us -> 0.1 us
    pallas_call x0 -> x4, Pallas kernels: none -> 28.8 us  [the longest x2 21.3 us: updated_graph(): pl.pallas_call(functools.partial(update_kernel, first_layer, last_layer),...]
    gather x8 -> x0, local copies, waits for them, and re-layouts: 19 us -> none  [the longest x4 9.89 us: on_device(): jnp.take(receiver_part, local_receiver, axis=1).astype(jnp.float32)]
    all_to_all x7 -> x2, blocking collectives: 40.8 us -> 25.6 us  [from_everyone(): lax.all_to_all(copies, axes, split_axis=0, concat_axis=0, tiled=True)]
    all_to_all x5 -> x2, starting transfers between devices: 29 us -> 15 us  [from_everyone(): lax.all_to_all(copies, axes, split_axis=0, concat_axis=0, tiled=True)]
    unnamed x38 -> x65, local copies, waits for them, and re-layouts: 0.94 us -> 13 us
    all_to_all x5 -> x2, waiting for transfers between devices: 12.8 us -> 2.17 us  [from_everyone(): lax.all_to_all(copies, axes, split_axis=0, concat_axis=0, tiled=True)]
    all_gather x4 -> x0, blocking collectives: 10.6 us -> none  [the longest x2 6.82 us: on_device(): piece = lax.all_gather(nodes, 'width', axis=0, tiled=True)]
    dot_general x12 -> x0, matrix products: 10.6 us -> none  [the longest x4 7.93 us: contract_first(): lax.dot_general(left, right, (((0,), (0,)), ((), ())), preferred_element_...]
  transfers between devices with their start and end apart: 9 -> 15, of which waited for: 3 -> 6; matrix products, arithmetic and copies ran while one was open for 18% -> 7% of each run, Pallas kernels for 0% -> 3%
where the time goes in v1:
time: 131 us; the launch traced here: 130 us
  starting transfers between devices  38.2 us (29%)
  Pallas kernels  28.8 us (22%)
  blocking collectives  25.6 us (20%)
  local copies, waits for them, and re-layouts  24.2 us (18%)
  waiting for transfers between devices  11.4 us (9%)
  between operations  1.48 us (1%)
    all_to_all x2, blocking collectives, from_everyone(): lax.all_to_all(copies, axes, split_axis=0, concat_axis=0, tiled=True)  25.6 us
    pallas_call x2, Pallas kernels, updated_graph(): pl.pallas_call(functools.partial(update_kernel, first_layer, last_layer),...  21.3 us
    all_to_all x2, starting transfers between devices, from_everyone(): lax.all_to_all(copies, axes, split_axis=0, concat_axis=0, tiled=True)  15 us
    ppermute x4, starting transfers between devices, beside(): return (lax.ppermute(rows, PATCH, up), lax.ppermute(rows, PATCH, down))  13.9 us
    unnamed x65, local copies, waits for them, and re-layouts  13 us
    ppermute x9, starting transfers between devices, from_other(): return lax.ppermute(a, 'width', [(0, 1), (1, 0)])  9.33 us
    another operation x9, local copies, waits for them, and re-layouts, on_device(): jnp.stack([edge_in_bias, edge_out_bias, edge_gain, edge_shift, node_in_bi...  8.15 us
    pallas_call x2, Pallas kernels, gathered(): pl.pallas_call(gather_kernel, grid=(slots // EDGE_BLOCK,), in_specs=[pl.B...  7.5 us
  transfers between devices with their start and end apart: 15, of which 6 were waited for; matrix products, arithmetic and copies ran while one was open for 7% of the time, Pallas kernels for 3%

profile of v1, /device:TPU:1, one launch (start us, length us, event | category | flops | bytes accessed | tf_op | source)
XLA Modules:
  0.0 129.7 jit_solution(14753818972946929410)
XLA Ops:
  0.6 0.9 copy.41
  1.6 16.1 %all_to_all.20 = bf16[8,16,256]{2,1,0:T(8,128)(2,1)S(1)} all-to-all(bf16[8,16,256]{2,1,0:T(8,128)(2,1)S(1)} %broadcast_in_dim.22), channel_id=1, replica_groups=mesh['patch_0'=8,'patch_1'=4,'patch_2'=4,'width'=2] {'patch_0'}, dimensions={0} | all-to-all | bytes 131072 | tf_op jit(solution)/shard_map/all_to_all | solution.py:248
  17.7 1.1 broadcast_in_dim.23
  18.8 6.9 %all-to-all-start.1 = ((bf16[16,128,256]{2,1,0:T(8,128)(2,1)}), bf16[16,128,256]{2,1,0:T(8,128)(2,1)}, u32[]{:S(2)}, u32[]{:S(2)}) async-start(bf16[16,128,256]{2,1,0:T(8,128)(2,1)} %broadcast_in_dim.23), calls=%async_computation.1 | async-start | bytes 2097152 | tf_op jit(solution)/shard_map/all_to_all | solution.py:248
  25.7 2.5 %collective-permute-start.5 = (bf16[2,256,1536]{2,1,0:T(8,128)(2,1)}, bf16[2,256,1536]{2,1,0:T(8,128)(2,1)}, u32[]{:S(2)}, u32[]{:S(2)}) collective-permute-start(bf16[2,256,1536]{2,1,0:T(8,128)(2,1)} %wa_ref.3), channel_id=1, source_target_pairs={{0,1},{1,0},{2,3},{3,2},{4,5},{5,4},{6,7},{7,6},{8,9},{9,8},{10,11... | collective-permute-start | bytes 4718600 | tf_op jit(solution)/shard_map/ppermute | solution.py:243
  28.7 1.5 %collective-permute-start.1 = (bf16[128,256]{1,0:T(8,128)(2,1)S(1)}, bf16[128,256]{1,0:T(8,128)(2,1)S(1)}, u32[]{:S(2)}, u32[]{:S(2)}) collective-permute-start(bf16[128,256]{1,0:T(8,128)(2,1)S(1)} %bitcast.16), channel_id=1, source_target_pairs={{0,2},{2,4},{4,6},{6,8},{8,10},{10,12},{12,14},{14,16},{16,18},{18... | collective-permute-start | bytes 196616 | tf_op jit(solution)/shard_map/ppermute | solution.py:256
  30.4 0.9 copy.43
  31.3 0.9 copy.44
  32.2 0.9 copy.45
  33.0 0.9 copy.46
  33.9 0.9 copy.47
  34.8 0.9 copy.48
  35.7 0.9 copy.49
  36.5 1.9 %stack.43.vec_a_ref = f32[2,256,8]{2,1,0:T(8,128)S(1)} concatenate(f32[2,256,1]{2,1,0:T(8,128)S(1)} %copy.42, f32[2,256,1]{2,1,0:T(8,128)} %copy.43, f32[2,256,1]{2,1,0:T(8,128)} %copy.44, f32[2,256,1]{2,1,0:T(8,128)} %copy.45, f32[2,256,1]{2,1,0:T(8,128)} %copy.46, f32[2,256,1]{2,1,0:T(8,128)} %copy.47, f32[2,256,1]{2,1,0:T(8,128)} %copy.48, f32[2,256,1]{2,1,0:T(8,128)} %copy.49), dimensions={2} | concatenate | bytes 32768 | tf_op jit(solution)/shard_map/stack | solution.py:290
  38.9 1.2 collective-permute-done.9.vec_b_ref
  40.1 0.7 copy-done.4
  40.8 5.4 %collective-permute-start.2 = (bf16[128,256]{1,0:T(8,128)(2,1)S(1)}, bf16[128,256]{1,0:T(8,128)(2,1)S(1)}, u32[]{:S(2)}, u32[]{:S(2)}) collective-permute-start(bf16[128,256]{1,0:T(8,128)(2,1)S(1)} %bitcast.17), channel_id=1, source_target_pairs={{2,0},{4,2},{6,4},{8,6},{10,8},{12,10},{14,12},{16,14},{18,16},{20... | collective-permute-start | bytes 196616 | tf_op jit(solution)/shard_map/ppermute | solution.py:256
  46.2 0.6 copy-done.14
  46.8 0.6 collective-permute-start.4
  48.1 1.2 collective-permute-start.8
  49.4 0.6 copy-done.12
  50.2 0.9 copy-done.15
  51.1 0.8 copy-done.17
  51.9 4.1 %gather_senders.2.sent_a_ref = bf16[1024,256]{1,0:T(8,128)(2,1)} custom-call(s32[1024,128]{1,0:T(8,128)S(1)} %broadcast_in_dim.21.index_ref, bf16[128,256]{1,0:T(8,128)(2,1)S(1)} %copy-done.15, bf16[128,256]{1,0:T(8,128)(2,1)S(1)} %bitcast.18, bf16[128,256]{1,0:T(8,128)(2,1)S(1)} %copy-done.17, bf16[2048,256]{1,0:T(8,128)(2,1)} %bitcast.3.coarse_ref), custom_call_target="tpu_custom_call" | custom-call | flops 1275068416 | bytes 3145728 | tf_op jit(solution)/shard_map/gather_senders/pallas_call | solution.py:60
  57.3 1.1 collective-permute-done.3.sent_b_ref
  58.4 0.9 copy-done.5
  59.4 1.0 copy-done.7
  60.4 0.8 copy-done.11
  61.3 0.8 copy-done.13
  62.1 10.8 %update_graph.2 = (bf16[512,1024]{1,0:T(8,128)(2,1)S(1)}, bf16[512,128]{1,0:T(8,128)(2,1)S(1)}, bf16[128,256]{1,0:T(8,128)(2,1)}) custom-call(s32[2]{0:T(128)S(1)} %pad_add_fusion.scalar_ref, bf16[256,1024]{1,0:T(8,128)(2,1)S(1)} %copy-done.7, bf16[256,1024]{1,0:T(8,128)(2,1)} %collective-permute-done.edge_b_ref, ...), custom_call_target="tpu_custom_call" | custom-call | flops 1879048192 | bytes 8388608 | tf_op jit(solution)/shard_map/update_graph/pallas_call | solution.py:213
  72.9 0.7 slice.7
  73.6 9.5 %all_to_all.21 = bf16[8,16,256]{2,1,0:T(8,128)(2,1)S(1)} all-to-all(bf16[8,16,256]{2,1,0:T(8,128)(2,1)S(1)} %broadcast_in_dim.25), channel_id=1, replica_groups=mesh['patch_0'=8,'patch_1'=4,'patch_2'=4,'width'=2] {'patch_0'}, dimensions={0} | all-to-all | bytes 131072 | tf_op jit(solution)/shard_map/all_to_all | solution.py:248
  83.1 1.1 broadcast_in_dim.26
  84.2 8.0 %all-to-all-start.3 = ((bf16[16,128,256]{2,1,0:T(8,128)(2,1)}), bf16[16,128,256]{2,1,0:T(8,128)(2,1)}, u32[]{:S(2)}, u32[]{:S(2)}) async-start(bf16[16,128,256]{2,1,0:T(8,128)(2,1)} %broadcast_in_dim.26), calls=%async_computation.3 | async-start | bytes 2097152 | tf_op jit(solution)/shard_map/all_to_all | solution.py:248
  92.2 1.3 %collective-permute-start.10 = (bf16[128,256]{1,0:T(8,128)(2,1)}, bf16[128,256]{1,0:T(8,128)(2,1)S(1)}, u32[]{:S(2)}, u32[]{:S(2)}) collective-permute-start(bf16[128,256]{1,0:T(8,128)(2,1)} %get-tuple-element.8.here_ref), channel_id=1, source_target_pairs={{0,2},{2,4},{4,6},{6,8},{8,10},{10,12},{12,14},{14,16},{16,18},{18... | collective-permute-start | bytes 196616 | tf_op jit(solution)/shard_map/ppermute | solution.py:256
  93.5 5.7 %collective-permute-start.11 = (bf16[128,256]{1,0:T(8,128)(2,1)}, bf16[128,256]{1,0:T(8,128)(2,1)S(1)}, u32[]{:S(2)}, u32[]{:S(2)}) collective-permute-start(bf16[128,256]{1,0:T(8,128)(2,1)} %get-tuple-element.8.here_ref), channel_id=1, source_target_pairs={{2,0},{4,2},{6,4},{8,6},{10,8},{12,10},{14,12},{16,14},{18,16},{20... | collective-permute-start | bytes 196616 | tf_op jit(solution)/shard_map/ppermute | solution.py:256
  99.2 4.1 %collective-permute-done.10.below_ref = bf16[128,256]{1,0:T(8,128)(2,1)S(1)} collective-permute-done((bf16[128,256]{1,0:T(8,128)(2,1)}, bf16[128,256]{1,0:T(8,128)(2,1)S(1)}, u32[]{:S(2)}, u32[]{:S(2)}) %collective-permute-start.10) | collective-permute-done | bytes 65568 | tf_op jit(solution)/shard_map/ppermute | solution.py:256
  103.3 0.6 copy-done.18
  103.9 1.3 collective-permute-done.11.above_ref
  105.2 0.6 copy-done.20
  105.9 2.2 %all-to-all-done.3 = bf16[16,128,256]{2,1,0:T(8,128)(2,1)} async-done(((bf16[16,128,256]{2,1,0:T(8,128)(2,1)}), bf16[16,128,256]{2,1,0:T(8,128)(2,1)}, u32[]{:S(2)}, u32[]{:S(2)}) %all-to-all-start.3) | async-done | bytes 1048608 | tf_op jit(solution)/shard_map/all_to_all | solution.py:248
  108.0 1.0 copy-done.9
  109.1 0.8 copy-done.19
  109.9 0.8 copy-done.21
  110.8 3.4 %gather_senders.3.sent_a_ref = bf16[1024,256]{1,0:T(8,128)(2,1)S(1)} custom-call(s32[1024,128]{1,0:T(8,128)S(1)} %copy-done.9, bf16[128,256]{1,0:T(8,128)(2,1)S(1)} %copy-done.19, bf16[128,256]{1,0:T(8,128)(2,1)} %get-tuple-element.8.here_ref, bf16[128,256]{1,0:T(8,128)(2,1)S(1)} %copy-done.21, bf16[2048,256]{1,0:T(8,128)(2,1)} %bitcast.14.coarse_ref), custom_call_target="tpu_custom_call" | custom-call | flops 1275068416 | bytes 3145728 | tf_op jit(solution)/shard_map/gather_senders/pallas_call | solution.py:60
  114.2 3.5 %collective-permute-start.12 = (bf16[1024,256]{1,0:T(8,128)(2,1)S(1)}, bf16[1024,256]{1,0:T(8,128)(2,1)S(1)}, u32[]{:S(2)}, u32[]{:S(2)}) collective-permute-start(bf16[1024,256]{1,0:T(8,128)(2,1)S(1)} %gather_senders.3.sent_a_ref), channel_id=1, source_target_pairs={{0,1},{1,0},{2,3},{3,2},{4,5},{5,4},{6,7},{7,6},{8,9},{9,8},{10,11... | collective-permute-start | bytes 1572872 | tf_op jit(solution)/shard_map/ppermute | solution.py:243
  117.7 1.5 %collective-permute-done.12.sent_b_ref = bf16[1024,256]{1,0:T(8,128)(2,1)S(1)} collective-permute-done((bf16[1024,256]{1,0:T(8,128)(2,1)S(1)}, bf16[1024,256]{1,0:T(8,128)(2,1)S(1)}, u32[]{:S(2)}, u32[]{:S(2)}) %collective-permute-start.12) | collective-permute-done | bytes 524320 | tf_op jit(solution)/shard_map/ppermute | solution.py:243
  119.3 10.4 %update_graph.3 = (bf16[256,1024]{1,0:T(8,128)(2,1)}, bf16[256,128]{1,0:T(8,128)(2,1)}) custom-call(s32[2]{0:T(128)S(1)} %pad_add_fusion.scalar_ref, bf16[512,1024]{1,0:T(8,128)(2,1)S(1)} %get-tuple-element.7.edge_a_ref.edge_b_ref, bf16[512,1024]{1,0:T(8,128)(2,1)S(1)} %get-tuple-element.7.edge_a_ref.edge_b_ref, ...), custom_call_target="tpu_custom_call" | custom-call | flops 1879048192 | bytes 8388608 | tf_op jit(solution)/shard_map/update_graph/pallas_call | solution.py:213
  (72 shorter events, 2.7 us)
Async XLA Ops:
  17.7 10.5 %copy-start = (bf16[2,256,1024]{2,1,0:T(8,128)(2,1)S(1)}, bf16[2,256,1024]{2,1,0:T(8,128)(2,1)}, u32[]{:S(2)}) copy-start(bf16[2,256,1024]{2,1,0:T(8,128)(2,1)} %va_ref.3) | copy-start | bytes 3145732
  17.7 10.7 %copy-start.2 = (bf16[2,256,512]{2,1,0:T(8,128)(2,1)S(1)}, bf16[2,256,512]{2,1,0:T(8,128)(2,1)}, u32[]{:S(2)}) copy-start(bf16[2,256,512]{2,1,0:T(8,128)(2,1)} %ea_ref.3) | copy-start | bytes 1572868
  17.7 12.6 %copy-start.24 = (f32[2,256]{1,0:T(2,128)S(1)}, f32[2,256]{1,0:T(2,128)}, u32[]{:S(2)}) copy-start(f32[2,256]{1,0:T(2,128)} %param.23) | copy-start | bytes 6148
  17.7 12.7 %copy-start.25 = (f32[2,256]{1,0:T(2,128)S(1)}, f32[2,256]{1,0:T(2,128)}, u32[]{:S(2)}) copy-start(f32[2,256]{1,0:T(2,128)} %param.25) | copy-start | bytes 6148
  18.7 12.5 %copy-start.26 = (f32[2,256]{1,0:T(2,128)S(1)}, f32[2,256]{1,0:T(2,128)}, u32[]{:S(2)}) copy-start(f32[2,256]{1,0:T(2,128)} %param.26) | copy-start | bytes 6148
  18.7 13.4 %copy-start.27 = (f32[2,256]{1,0:T(2,128)S(1)}, f32[2,256]{1,0:T(2,128)}, u32[]{:S(2)}) copy-start(f32[2,256]{1,0:T(2,128)} %param.27) | copy-start | bytes 6148
  18.7 14.3 %copy-start.28 = (f32[2,256]{1,0:T(2,128)S(1)}, f32[2,256]{1,0:T(2,128)}, u32[]{:S(2)}) copy-start(f32[2,256]{1,0:T(2,128)} %param.29) | copy-start | bytes 6148
  18.7 15.2 %copy-start.29 = (f32[2,256]{1,0:T(2,128)S(1)}, f32[2,256]{1,0:T(2,128)}, u32[]{:S(2)}) copy-start(f32[2,256]{1,0:T(2,128)} %param.31) | copy-start | bytes 6148
  18.8 16.0 %copy-start.30 = (f32[2,256]{1,0:T(2,128)S(1)}, f32[2,256]{1,0:T(2,128)}, u32[]{:S(2)}) copy-start(f32[2,256]{1,0:T(2,128)} %param.32) | copy-start | bytes 6148
  18.8 16.9 %copy-start.31 = (f32[2,256]{1,0:T(2,128)S(1)}, f32[2,256]{1,0:T(2,128)}, u32[]{:S(2)}) copy-start(f32[2,256]{1,0:T(2,128)} %param.33) | copy-start | bytes 6148
  18.8 31.2 %all-to-all-start.1 = ((bf16[16,128,256]{2,1,0:T(8,128)(2,1)}), bf16[16,128,256]{2,1,0:T(8,128)(2,1)}, u32[]{:S(2)}, u32[]{:S(2)}) async-start(bf16[16,128,256]{2,1,0:T(8,128)(2,1)} %broadcast_in_dim.23), calls=%async_computation.1 | async-start | bytes 2097152 | tf_op jit(solution)/shard_map/all_to_all | solution.py:248
  25.7 31.6 %collective-permute-start.5 = (bf16[2,256,1536]{2,1,0:T(8,128)(2,1)}, bf16[2,256,1536]{2,1,0:T(8,128)(2,1)}, u32[]{:S(2)}, u32[]{:S(2)}) collective-permute-start(bf16[2,256,1536]{2,1,0:T(8,128)(2,1)} %wa_ref.3), channel_id=1, source_target_pairs={{0,1},{1,0},{2,3},{3,2},{4,5},{5,4},{6,7},{7,6},{8,9},{9,8},{10,11... | collective-permute-start | bytes 4718600 | tf_op jit(solution)/shard_map/ppermute | solution.py:243
  28.2 29.1 %collective-permute-start.7 = (bf16[2,256,1024]{2,1,0:T(8,128)(2,1)S(1)}, bf16[2,256,1024]{2,1,0:T(8,128)(2,1)}, u32[]{:S(2)}, u32[]{:S(2)}) collective-permute-start(bf16[2,256,1024]{2,1,0:T(8,128)(2,1)S(1)} %copy-done), channel_id=1, source_target_pairs={{0,1},{1,0},{2,3},{3,2},{4,5},{5,4},{6,7},{7,6},{8,9},{9,8},{10,11... | collective-permute-start | bytes 3145736 | tf_op jit(solution)/shard_map/ppermute | solution.py:243
  28.3 27.7 %collective-permute-start.6 = (bf16[2,256,512]{2,1,0:T(8,128)(2,1)S(1)}, bf16[2,256,512]{2,1,0:T(8,128)(2,1)S(1)}, u32[]{:S(2)}, u32[]{:S(2)}) collective-permute-start(bf16[2,256,512]{2,1,0:T(8,128)(2,1)S(1)} %copy-done.2), channel_id=1, source_target_pairs={{0,1},{1,0},{2,3},{3,2},{4,5},{5,4},{6,7},{7,6},{8,9},{9,8},{10,11... | collective-permute-start | bytes 1572872 | tf_op jit(solution)/shard_map/ppermute | solution.py:243
  28.7 17.5 %collective-permute-start.1 = (bf16[128,256]{1,0:T(8,128)(2,1)S(1)}, bf16[128,256]{1,0:T(8,128)(2,1)S(1)}, u32[]{:S(2)}, u32[]{:S(2)}) collective-permute-start(bf16[128,256]{1,0:T(8,128)(2,1)S(1)} %bitcast.16), channel_id=1, source_target_pairs={{0,2},{2,4},{4,6},{6,8},{8,10},{10,12},{12,14},{14,16},{16,18},{18... | collective-permute-start | bytes 196616 | tf_op jit(solution)/shard_map/ppermute | solution.py:256
  33.9 12.9 %copy-start.10 = (bf16[256,128]{1,0:T(8,128)(2,1)S(1)}, bf16[256,128]{1,0:T(8,128)(2,1)}, u32[]{:S(2)}) copy-start(bf16[256,128]{1,0:T(8,128)(2,1)} %node_a_ref.1) | copy-start | bytes 196612
  33.9 13.5 %copy-start.22 = (s32[1024]{0:T(1024)S(1)}, s32[1024]{0:T(1024)}, u32[]{:S(2)}) copy-start(s32[1024]{0:T(1024)} %param.19) | copy-start | bytes 12292
  33.9 14.2 %copy-start.3 = (bf16[2,256,512]{2,1,0:T(8,128)(2,1)S(1)}, bf16[2,256,512]{2,1,0:T(8,128)(2,1)}, u32[]{:S(2)}) copy-start(bf16[2,256,512]{2,1,0:T(8,128)(2,1)} %oa_ref.3) | copy-start | bytes 1572868
  38.5 1.6 %collective-permute-start.9 = (f32[2,256,8]{2,1,0:T(8,128)S(1)}, f32[2,256,8]{2,1,0:T(8,128)S(1)}, u32[]{:S(2)}, u32[]{:S(2)}) collective-permute-start(f32[2,256,8]{2,1,0:T(8,128)S(1)} %stack.43.vec_a_ref), channel_id=1, source_target_pairs={{0,1},{1,0},{2,3},{3,2},{4,5},{5,4},{6,7},{7,6},{8,9},{9,8},{10,11... | collective-permute-start | bytes 49160 | tf_op jit(solution)/shard_map/ppermute | solution.py:243
  40.1 0.7 copy-start.4
  40.8 6.7 %collective-permute-start.2 = (bf16[128,256]{1,0:T(8,128)(2,1)S(1)}, bf16[128,256]{1,0:T(8,128)(2,1)S(1)}, u32[]{:S(2)}, u32[]{:S(2)}) collective-permute-start(bf16[128,256]{1,0:T(8,128)(2,1)S(1)} %bitcast.17), channel_id=1, source_target_pairs={{2,0},{4,2},{6,4},{8,6},{10,8},{12,10},{14,12},{16,14},{18,16},{20... | collective-permute-start | bytes 196616 | tf_op jit(solution)/shard_map/ppermute | solution.py:256
  46.2 0.6 copy-start.14
  46.8 2.5 %collective-permute-start.4 = (bf16[256,128]{1,0:T(8,128)(2,1)S(1)}, bf16[256,128]{1,0:T(8,128)(2,1)S(1)}, u32[]{:S(2)}, u32[]{:S(2)}) collective-permute-start(bf16[256,128]{1,0:T(8,128)(2,1)S(1)} %copy-done.10), channel_id=1, source_target_pairs={{0,1},{1,0},{2,3},{3,2},{4,5},{5,4},{6,7},{7,6},{8,9},{9,8},{10,11... | collective-permute-start | bytes 196616 | tf_op jit(solution)/shard_map/ppermute | solution.py:243
  47.5 0.6 copy-start.16
  48.1 9.1 %collective-permute-start.8 = (bf16[2,256,512]{2,1,0:T(8,128)(2,1)S(1)}, bf16[2,256,512]{2,1,0:T(8,128)(2,1)S(1)}, u32[]{:S(2)}, u32[]{:S(2)}) collective-permute-start(bf16[2,256,512]{2,1,0:T(8,128)(2,1)S(1)} %copy-done.3), channel_id=1, source_target_pairs={{0,1},{1,0},{2,3},{3,2},{4,5},{5,4},{6,7},{7,6},{8,9},{9,8},{10,11... | collective-permute-start | bytes 1572872 | tf_op jit(solution)/shard_map/ppermute | solution.py:243
  49.4 0.6 copy-start.12
  50.0 7.3 %collective-permute-start = (bf16[256,1024]{1,0:T(8,128)(2,1)}, bf16[256,1024]{1,0:T(8,128)(2,1)}, u32[]{:S(2)}, u32[]{:S(2)}) collective-permute-start(bf16[256,1024]{1,0:T(8,128)(2,1)} %edge_a_ref.1), channel_id=1, source_target_pairs={{0,1},{1,0},{2,3},{3,2},{4,5},{5,4},{6,7},{7,6},{8,9},{9,8},{10,11... | collective-permute-start | bytes 1572872 | tf_op jit(solution)/shard_map/ppermute | solution.py:243
  50.2 5.8 %copy-start.8 = (s32[1024,128]{1,0:T(8,128)}, s32[1024,128]{1,0:T(8,128)S(1)}, u32[]{:S(2)}) copy-start(s32[1024,128]{1,0:T(8,128)S(1)} %broadcast_in_dim.21.index_ref) | copy-start | bytes 1572868
  50.2 0.9 copy-start.15
  51.1 0.8 copy-start.17
  51.9 5.3 %copy-start.23 = (s32[1024]{0:T(1024)S(1)}, s32[1024]{0:T(1024)}, u32[]{:S(2)}) copy-start(s32[1024]{0:T(1024)} %param.20) | copy-start | bytes 12292
  56.0 2.4 %collective-permute-start.3 = (bf16[1024,256]{1,0:T(8,128)(2,1)}, bf16[1024,256]{1,0:T(8,128)(2,1)}, u32[]{:S(2)}, u32[]{:S(2)}) collective-permute-start(bf16[1024,256]{1,0:T(8,128)(2,1)} %gather_senders.2.sent_a_ref), channel_id=1, source_target_pairs={{0,1},{1,0},{2,3},{3,2},{4,5},{5,4},{6,7},{7,6},{8,9},{9,8},{10,11... | collective-permute-start | bytes 1572872 | tf_op jit(solution)/shard_map/ppermute | solution.py:243
  58.4 0.9 copy-start.5
  59.4 1.0 copy-start.7
  60.4 0.8 copy-start.11
  61.2 0.8 copy-start.13
  84.2 23.8 %all-to-all-start.3 = ((bf16[16,128,256]{2,1,0:T(8,128)(2,1)}), bf16[16,128,256]{2,1,0:T(8,128)(2,1)}, u32[]{:S(2)}, u32[]{:S(2)}) async-start(bf16[16,128,256]{2,1,0:T(8,128)(2,1)} %broadcast_in_dim.26), calls=%async_computation.3 | async-start | bytes 2097152 | tf_op jit(solution)/shard_map/all_to_all | solution.py:248
  92.2 11.1 %collective-permute-start.10 = (bf16[128,256]{1,0:T(8,128)(2,1)}, bf16[128,256]{1,0:T(8,128)(2,1)S(1)}, u32[]{:S(2)}, u32[]{:S(2)}) collective-permute-start(bf16[128,256]{1,0:T(8,128)(2,1)} %get-tuple-element.8.here_ref), channel_id=1, source_target_pairs={{0,2},{2,4},{4,6},{6,8},{8,10},{10,12},{12,14},{14,16},{16,18},{18... | collective-permute-start | bytes 196616 | tf_op jit(solution)/shard_map/ppermute | solution.py:256
  93.5 11.7 %collective-permute-start.11 = (bf16[128,256]{1,0:T(8,128)(2,1)}, bf16[128,256]{1,0:T(8,128)(2,1)S(1)}, u32[]{:S(2)}, u32[]{:S(2)}) collective-permute-start(bf16[128,256]{1,0:T(8,128)(2,1)} %get-tuple-element.8.here_ref), channel_id=1, source_target_pairs={{2,0},{4,2},{6,4},{8,6},{10,8},{12,10},{14,12},{16,14},{18,16},{20... | collective-permute-start | bytes 196616 | tf_op jit(solution)/shard_map/ppermute | solution.py:256
  103.3 0.6 copy-start.18
  105.2 0.6 copy-start.20
  108.0 1.0 copy-start.9
  109.1 0.8 copy-start.19
  109.9 0.8 copy-start.21
  110.8 8.5 %copy-start.1 = (bf16[2,256,1024]{2,1,0:T(8,128)(2,1)S(1)}, bf16[2,256,1024]{2,1,0:T(8,128)(2,1)}, u32[]{:S(2)}) copy-start(bf16[2,256,1024]{2,1,0:T(8,128)(2,1)} %va_ref.3) | copy-start | bytes 3145732
  110.8 8.5 %copy-start.6 = (f32[2,256,8]{2,1,0:T(8,128)S(1)}, f32[2,256,8]{2,1,0:T(8,128)}, u32[]{:S(2)}) copy-start(f32[2,256,8]{2,1,0:T(8,128)} %copy-done.4) | copy-start | bytes 49156
  114.2 5.1 %collective-permute-start.12 = (bf16[1024,256]{1,0:T(8,128)(2,1)S(1)}, bf16[1024,256]{1,0:T(8,128)(2,1)S(1)}, u32[]{:S(2)}, u32[]{:S(2)}) collective-permute-start(bf16[1024,256]{1,0:T(8,128)(2,1)S(1)} %gather_senders.3.sent_a_ref), channel_id=1, source_target_pairs={{0,1},{1,0},{2,3},{3,2},{4,5},{5,4},{6,7},{7,6},{8,9},{9,8},{10,11... | collective-permute-start | bytes 1572872 | tf_op jit(solution)/shard_map/ppermute | solution.py:243

commit v2 on v1

v2 whole, which is shorter than its diff:
```python
import functools

import jax
import jax.numpy as jnp
from jax import lax
from jax.experimental import pallas as pl
from jax.experimental.pallas import tpu as pltpu
from jax.sharding import Mesh
from jax.sharding import PartitionSpec as P

Z, Y, X = "patch_0", "patch_1", "patch_2"
PATCH = (Z, Y, X)
PLANE = (Y, X)
EPSILON = 1e-05
EDGE_BLOCK = 512
VMEM_LIMIT = 32 * 1024 * 1024


def dot(left, right, contract=((1,), (0,))):
    return lax.dot_general(left, right, (contract, ((), ())), preferred_element_type=jnp.float32)


def silu(v):
    h = 0.5 * v
    return h + h * jnp.tanh(h)


def layer_norm(values, gain, shift):
    width = values.shape[0]
    mean = jnp.sum(values, axis=0, keepdims=True) * (1.0 / width)
    square = jnp.sum(values * values, axis=0, keepdims=True) * (1.0 / width)
    return (values - mean) * lax.rsqrt(square - mean * mean + EPSILON) * gain + shift


def in_order(first, mine, other):
    return jnp.concatenate([jnp.where(first, mine, other), jnp.where(first, other, mine)], axis=0)


VMEM = pl.BlockSpec(memory_space=pltpu.VMEM)
SMEM = pl.BlockSpec(memory_space=pltpu.SMEM)
HBM = pl.BlockSpec(memory_space=pltpu.HBM)


def shape(dims, dtype=jnp.bfloat16):
    return jax.ShapeDtypeStruct(dims, dtype)


def kernel_call(body, name, out_shape, inputs, in_specs, out_specs, scratch, flops):
    inputs = [
        pltpu.with_memory_space_constraint(a, pltpu.HBM) if spec is HBM else a
        for a, spec in zip(inputs, in_specs)
    ]
    if isinstance(out_specs, list):
        out_shape = [
            pltpu.HBM(a.shape, a.dtype) if spec is HBM else a
            for a, spec in zip(out_shape, out_specs)
        ]
    return pl.pallas_call(
        body,
        in_specs=in_specs,
        out_specs=out_specs,
        out_shape=out_shape,
        scratch_shapes=scratch,
        compiler_params=pltpu.CompilerParams(vmem_limit_bytes=VMEM_LIMIT),
        cost_estimate=pl.CostEstimate(flops=flops, bytes_accessed=4 << 20, transcendentals=0),
        name=name,
    )(*inputs)


def started(pairs, sems):
    copies = [pltpu.make_async_copy(a, b, sems.at[i]) for i, (a, b) in enumerate(pairs)]
    for copy in copies:
        copy.start()
    return copies


def finish(copies):
    for copy in copies:
        copy.wait()


def held(arrays):
    return [pltpu.VMEM(a.shape, a.dtype) for a in arrays]


def columns_of(ref, start, length):
    return ref.at[:, pl.ds(start, length)]


def store_rows(mine, rows_ref, copies_ref):
    rows = mine.T
    rows_ref[...] = rows
    for i in range(copies_ref.shape[0]):
        copies_ref[i] = rows[: copies_ref.shape[1]]


def rows_kernel(nodes_ref, rows_ref, copies_ref, held_ref, sem):
    copies = started([(nodes_ref, held_ref)], sem)
    finish(copies)
    store_rows(held_ref[...], rows_ref, copies_ref)


def node_rows_of(nodes, columns):
    half, node_rows = nodes.shape
    return kernel_call(
        rows_kernel,
        "node_rows",
        [shape((node_rows, half)), shape((columns, node_rows // 8, half))],
        (nodes,),
        [HBM],
        [VMEM, VMEM],
        held([nodes]) + [pltpu.SemaphoreType.DMA((1,))],
        0,
    )


def gather_kernel(
    index_in, below_in, here_in, above_in, coarse_in, out_ref, index_ref, near_ref, coarse_ref, sems
):
    rows = here_in.shape[0]
    copies = started(
        [
            (index_in, index_ref),
            (below_in, near_ref.at[pl.ds(0, rows)]),
            (here_in, near_ref.at[pl.ds(rows, rows)]),
            (above_in, near_ref.at[pl.ds(2 * rows, rows)]),
            (coarse_in, coarse_ref),
        ],
        sems,
    )
    finish(copies[:4])
    columns = index_ref[...].T
    lane = lax.broadcasted_iota(jnp.int32, (128, 128), 1)

    def selection(start, first, length):
        blocks = []
        for k in range(start // 128, (start + EDGE_BLOCK) // 128):
            index = jnp.broadcast_to(columns[:, k : k + 1], (128, 128))
            tiles = []
            for j in range(first, first + length, 128):
                tiles.append(jnp.where(index == lane + j, 1.0, 0.0).astype(jnp.bfloat16))
            blocks.append(jnp.concatenate(tiles, axis=1))
        return jnp.concatenate(blocks, axis=0)

    for start in range(0, out_ref.shape[0], EDGE_BLOCK):
        total = dot(selection(start, 0, 3 * rows), near_ref[...])
        if start == 0:
            finish(copies[4:])
        total = total + dot(selection(start, 3 * rows, coarse_ref.shape[0]), coarse_ref[...])
        out_ref[start : start + EDGE_BLOCK, :] = total.astype(jnp.bfloat16)


def gathered(index, below, here, above, coarse):
    slots = index.size
    rows, width = here.shape
    table = 3 * rows + coarse.shape[0]
    return kernel_call(
        gather_kernel,
        "gather_senders",
        shape((slots, width)),
        (index, below, here, above, coarse),
        [HBM] * 4 + [pl.BlockSpec(memory_space=pl.ANY)],
        VMEM,
        held([index, shape((3 * rows, width)), coarse]) + [pltpu.SemaphoreType.DMA((5,))],
        2 * slots * width * table,
    )


def prepare_kernel(layer, n_in, n_out, scalar_ref, *refs):
    ins, outs = refs[:n_in], refs[n_in : n_in + n_out]
    held_in = refs[n_in + n_out : 2 * n_in + n_out]
    held_out = refs[2 * n_in + n_out : 2 * (n_in + n_out)]
    in_sems, out_sems = refs[2 * (n_in + n_out) :]
    copies = started(
        [(a.at[layer] if len(a.shape) == 3 else a, b) for a, b in zip(ins, held_in)], in_sems
    )
    first = scalar_ref[0] == 0
    count = scalar_ref[1]
    sent = [pltpu.make_async_copy(held_out[i], outs[i], out_sems.at[i]) for i in range(n_out)]
    if layer == 0:
        edge_a, edge_b, receiver_ref, node_a, node_b = held_in[:5]
    else:
        edge_a, receiver_ref, node_a = held_in[:3]
        edge_b, node_b = edge_a, node_a
    wa, wb, ea, eb, va, vb, oa, ob, vec_a_ref, vec_b_ref = held_in[-10:]
    (
        before_ref,
        node_before_ref,
        incidence_ref,
        sent_weight_ref,
        out_weight_ref,
        aggregate_weight_ref,
        node_weight_ref,
        vectors_ref,
    ) = held_out[:8]
    width = out_weight_ref.shape[0]
    nodes_here, slots = incidence_ref.shape

    def stacked(a, b):
        return jnp.concatenate([a, b], axis=0)

    finish(copies)
    if layer == 0:
        edges = in_order(first, edge_a[...], edge_b[...])
        nodes = in_order(first, node_a[...], node_b[...])
        held_out[8][...] = edges
        held_out[9][...] = nodes
        sent[8].start()
        sent[9].start()
    else:
        edges, nodes = edge_a[...], node_a[...]
    w = stacked(wa[...], wb[...])
    v = stacked(va[...], vb[...])
    sent_weight_ref[...] = w[:, width : 2 * width]
    sent[3].start()
    out_weight_ref[...] = stacked(ea[...], eb[...]).T
    sent[4].start()
    aggregate_weight_ref[...] = v[:, width:]
    sent[5].start()
    node_weight_ref[...] = stacked(oa[...], ob[...]).T
    sent[6].start()
    vec_a, vec_b = vec_a_ref[...].T, vec_b_ref[...].T
    hidden_vec = stacked(vec_a, vec_b)
    vectors_ref[...] = in_order(first, vec_a, vec_b)
    sent[7].start()
    live = lax.broadcasted_iota(jnp.int32, (1, slots), 1) < count
    incidence_ref[...] = jnp.where(
        (lax.broadcasted_iota(jnp.int32, (nodes_here, slots), 0) == receiver_ref[...]) & live,
        1.0,
        0.0,
    ).astype(jnp.bfloat16)
    sent[2].start()
    node_before_ref[...] = dot(v[:, :width], nodes) + hidden_vec[:, 4:5]
    sent[1].start()
    part = dot(w[:, 2 * width :], nodes).astype(jnp.bfloat16)
    before = dot(w[:, :width], edges) + dot(part, incidence_ref[...])
    before_ref[...] = before + hidden_vec[:, 0:1]
    sent[0].start()
    finish(sent)


def prepared(layer, scalars, edges, receiver, nodes, weights):
    slots = edges[0].shape[1]
    node_rows = nodes[0].shape[1]
    width = weights[0].shape[1] * 2
    inputs = (*edges, receiver, *nodes, *weights)
    out_shape = [
        shape((width, slots), jnp.float32),
        shape((width, node_rows), jnp.float32),
        shape((node_rows, slots)),
        shape((width, width)),
        shape((width, width)),
        shape((width, width)),
        shape((width, width)),
        shape((width, 8), jnp.float32),
    ]
    if layer == 0:
        out_shape += [shape((width, slots)), shape((width, node_rows))]
    n_in, n_out = len(inputs), len(out_shape)
    one_layer = [shape(a.shape[-2:], a.dtype) for a in inputs]
    ready = kernel_call(
        functools.partial(prepare_kernel, layer, n_in, n_out),
        "prepare_layer",
        out_shape,
        (scalars, *inputs),
        [SMEM] + [HBM] * n_in,
        [HBM] * n_out,
        held(one_layer)
        + held(out_shape)
        + [pltpu.SemaphoreType.DMA((n_in,)), pltpu.SemaphoreType.DMA((n_out,))],
        2 * slots * width * (width + node_rows),
    )
    if layer == 0:
        return (ready[8], ready[9], *ready[:8])
    return (edges[0], nodes[0], *ready)


def update_kernel(last_layer, n_out, scalar_ref, sent_a_ref, sent_b_ref, *refs):
    ins, outs, held_in = refs[:10], refs[10 : 10 + n_out], refs[10 + n_out : 20 + n_out]
    held_out = refs[20 + n_out : 20 + 2 * n_out]
    in_sems, out_sems = refs[20 + 2 * n_out :]
    edges_ref, nodes_ref, before_ref, node_before_ref, incidence_ref = held_in[:5]
    sent_weight_ref, out_weight_ref, aggregate_weight_ref, node_weight_ref, vectors_ref = held_in[
        5:
    ]
    slots = edges_ref.shape[1]
    starts = range(0, slots, EDGE_BLOCK)
    early = [(ins[5], sent_weight_ref)]
    for start in starts:
        early.append(tuple(columns_of(r, start, EDGE_BLOCK) for r in (ins[2], before_ref)))
        if start == 0:
            early += [(ins[6], out_weight_ref), (ins[9], vectors_ref)]
        for i in (0, 4):
            early.append(tuple(columns_of(r, start, EDGE_BLOCK) for r in (ins[i], held_in[i])))
    late = [(ins[i], held_in[i]) for i in (1, 3, 7, 8)]
    copies = started(early + late, in_sems)
    groups = [copies[:6], copies[6:9], copies[9:]]

    first = scalar_ref[0] == 0
    count = scalar_ref[1]
    half = sent_a_ref.shape[1]
    total = None
    edge_out_ref, node_out_ref = held_out[:2]
    sent_out = []

    def send(source, target):
        copy = pltpu.make_async_copy(source, target, out_sems.at[len(sent_out)])
        copy.start()
        sent_out.append(copy)

    for turn, start in enumerate(starts):
        finish(groups[turn])
        vectors = vectors_ref[...]
        here = slice(start, start + EDGE_BLOCK)
        sent_a, sent_b = sent_a_ref[here, :], sent_b_ref[here, :]
        low = jnp.where(first, sent_a, sent_b)
        high = jnp.where(first, sent_b, sent_a)
        sent = jnp.concatenate([low, high], axis=1)
        before = before_ref[:, here] + dot(sent_weight_ref[...], sent, ((1,), (1,)))
        hidden = silu(before).astype(jnp.bfloat16)
        mlp = dot(out_weight_ref[...], hidden) + vectors[:, 1:2]
        live = lax.broadcasted_iota(jnp.int32, (1, EDGE_BLOCK), 1) + start < count
        updated = edges_ref[:, here].astype(jnp.float32) + layer_norm(
            mlp, vectors[:, 2:3], vectors[:, 3:4]
        )
        updated = jnp.where(live, updated, 0.0).astype(jnp.bfloat16)
        part = dot(updated, incidence_ref[:, here], ((1,), (1,)))
        total = part if total is None else total + part
        if last_layer:
            edge_out_ref[:, here] = jnp.where(first, updated[:half], updated[half:])
        else:
            edge_out_ref[:, here] = updated
        send(
            columns_of(edge_out_ref, start, EDGE_BLOCK), columns_of(outs[0], start, EDGE_BLOCK)
        )
    finish(groups[2])
    aggregate = total.astype(jnp.bfloat16)
    node_before = node_before_ref[...] + dot(aggregate_weight_ref[...], aggregate)
    node_hidden = silu(node_before).astype(jnp.bfloat16)
    node_mlp = dot(node_weight_ref[...], node_hidden) + vectors[:, 5:6]
    new = nodes_ref[...].astype(jnp.float32) + layer_norm(
        node_mlp, vectors[:, 6:7], vectors[:, 7:8]
    )
    new = new.astype(jnp.bfloat16)
    mine = jnp.where(first, new[:half], new[half:])
    if last_layer:
        node_out_ref[...] = mine
    else:
        store_rows(mine, *held_out[2:])
        for i in (2, 3):
            send(held_out[i], outs[i])
        node_out_ref[...] = new
    send(node_out_ref, outs[1])
    finish(sent_out)


def updated_graph(last_layer, scalars, sent, ready, copies):
    slots = ready[0].shape[1]
    node_rows = ready[1].shape[1]
    half = sent[0].shape[1]
    width = 2 * half
    out_width = half if last_layer else width
    out_shape = [shape((out_width, slots)), shape((out_width, node_rows))]
    if not last_layer:
        out_shape += [shape((node_rows, half)), shape((copies, node_rows // 8, half))]
    n_out = len(out_shape)
    blocks = slots // EDGE_BLOCK
    return kernel_call(
        functools.partial(update_kernel, last_layer, n_out),
        "update_graph",
        out_shape,
        (scalars, *sent, *ready),
        [SMEM, VMEM, VMEM] + [HBM] * 10,
        [HBM] * n_out,
        held(ready)
        + held(out_shape)
        + [
            pltpu.SemaphoreType.DMA((3 * blocks + 7,)),
            pltpu.SemaphoreType.DMA((n_out - 1 + blocks,)),
        ],
        2 * slots * width * (2 * width + node_rows),
    )


def from_other(a):
    return lax.ppermute(a, "width", [(0, 1), (1, 0)])


def exchanged(rows, copies):
    size = lax.axis_size(PATCH)
    up = [(i, (i + 1) % size) for i in range(size)]
    down = [(j, i) for i, j in up]
    below, above = lax.ppermute(rows, PATCH, up), lax.ppermute(rows, PATCH, down)
    column = lax.all_to_all(copies, Z, split_axis=0, concat_axis=0, tiled=True)
    column = column.reshape(-1, rows.shape[1])
    column, below, above = lax.optimization_barrier((column, below, above))
    plane = jnp.broadcast_to(column, (lax.axis_size(PLANE), *column.shape))
    coarse = lax.all_to_all(plane, PLANE, split_axis=0, concat_axis=0, tiled=True)
    return below, rows, above, coarse.reshape(-1, rows.shape[1])


def on_device(
    node_latents,
    edge_latents,
    senders,
    receivers,
    edge_count,
    edge_in_weight,
    edge_in_bias,
    edge_out_weight,
    edge_out_bias,
    edge_gain,
    edge_shift,
    node_in_weight,
    node_in_bias,
    node_out_weight,
    node_out_bias,
    node_gain,
    node_shift,
):
    half, node_rows = node_latents.shape
    layers = edge_in_weight.shape[0]
    coarse_rows = node_rows // 8
    patch_here = lax.axis_index(PATCH)
    patches = lax.axis_size(PATCH)
    plane = lax.axis_size(PLANE)
    columns = lax.axis_size(Z)
    scalars = jnp.stack([lax.axis_index("width"), edge_count[0]]).astype(jnp.int32)

    rows, copies = node_rows_of(node_latents, columns)
    table = exchanged(rows, copies)

    vectors = jnp.stack(
        [
            edge_in_bias,
            edge_out_bias,
            edge_gain,
            edge_shift,
            node_in_bias,
            node_out_bias,
            node_gain,
            node_shift,
        ],
        axis=1,
    )
    own = (edge_in_weight, edge_out_weight, node_in_weight, node_out_weight, vectors)
    weights = []
    for a in own:
        weights += [a, from_other(a)]

    owner = senders // node_rows
    within = senders - owner * node_rows
    place = (owner % plane) * (patches // plane) + owner // plane
    index = jnp.where(
        owner == patch_here,
        node_rows + within,
        jnp.where(
            owner == (patch_here + patches - 1) % patches,
            within,
            jnp.where(
                owner == (patch_here + 1) % patches,
                2 * node_rows + within,
                3 * node_rows + place * coarse_rows + within,
            ),
        ),
    )
    index = index.reshape(-1, 128)
    receiver = (receivers - patch_here * node_rows)[None, :]

    edges = (edge_latents, from_other(edge_latents))
    nodes = (node_latents, from_other(node_latents))
    for layer in range(layers):
        last_layer = layer == layers - 1
        ready = prepared(layer, scalars, edges, receiver, nodes, weights)
        table, ready = lax.optimization_barrier((table, ready))
        sent = gathered(index, *table)
        sent = (sent, from_other(sent))
        results = updated_graph(last_layer, scalars, sent, ready, columns)
        if not last_layer:
            edges, nodes = results[:1], results[1:2]
            table = exchanged(results[2], results[3])
    return (results[1], results[0])


def solution(mesh):
    finer = Mesh(
        mesh.devices.reshape(8, 4, 4, mesh.shape["width"]),
        (*PATCH, "width"),
    )
    in_specs = (
        P("width", PATCH),
        P("width", PATCH),
        P(PATCH),
        P(PATCH),
        P(PATCH),
        P(None, "width", None),
        P(None, "width"),
        P(None, "width", None),
        P(None, "width"),
        P(None, "width"),
        P(None, "width"),
        P(None, "width", None),
        P(None, "width"),
        P(None, "width", None),
        P(None, "width"),
        P(None, "width"),
        P(None, "width"),
    )
    out_specs = (P("width", PATCH), P("width", PATCH))
    return jax.shard_map(
        on_device, mesh=finer, in_specs=in_specs, out_specs=out_specs, check_vma=False
    )
```

time: 131 us -> 117 us (0.89)
  blocking collectives: 25.6 us -> 0 us
  local copies, waits for them, and re-layouts: 24.2 us -> 3.66 us
  waiting for transfers between devices: 11.4 us -> 29.7 us
  Pallas kernels: 28.8 us -> 35.3 us
  starting transfers between devices: 38.2 us -> 44.3 us
    all_to_all x2 -> x0, blocking collectives: 25.6 us -> none  [from_everyone(): lax.all_to_all(copies, axes, split_axis=0, concat_axis=0, tiled=True)]
    ppermute x4, waiting for transfers between devices: 5.42 us -> 17.3 us  [the longest x2 14.3 us: exchanged(): lax.ppermute(rows, PATCH, up)]
    unnamed x65 -> x46, local copies, waits for them, and re-layouts: 13 us -> 1.38 us
    another operation x9, local copies, waits for them, and re-layouts: 8.15 us -> 0.06 us  [on_device(): jnp.stack([edge_in_bias, edge_out_bias, edge_gain, edge_shift, node_in_bi...]
    pallas_call x4 -> x7, Pallas kernels: 28.8 us -> 35.3 us  [kernel_call(): pl.pallas_call(body, in_specs=in_specs, out_specs=out_specs, out_shape=ou...]
    all_to_all x2 -> x4, waiting for transfers between devices: 2.17 us -> 8.26 us  [the longest x2 8.25 us: exchanged(): lax.all_to_all(plane, PLANE, split_axis=0, concat_axis=0, tiled=True)]
    ppermute x9, starting transfers between devices: 9.33 us -> 14.7 us  [from_other(): return lax.ppermute(a, 'width', [(0, 1), (1, 0)])]
    all_to_all x2 -> x4, starting transfers between devices: 15 us -> 18 us  [the longest x2 10.7 us: exchanged(): column = lax.all_to_all(copies, Z, split_axis=0, concat_axis=0, tiled=True)]
  transfers between devices with their start and end apart: 15 -> 17, of which waited for: 6 -> 9; matrix products, arithmetic and copies ran while one was open for 7% -> 2% of each run, Pallas kernels for 3% -> 13%
where the time goes in v2:
time: 117 us; the launch traced here: 116 us
  starting transfers between devices  44.3 us (38%)
  Pallas kernels  35.3 us (30%)
  waiting for transfers between devices  29.7 us (25%)
  local copies, waits for them, and re-layouts  3.66 us (3%)
  between operations  1.88 us (2%)
  other arithmetic  1.28 us (1%)
    pallas_call x7, Pallas kernels, kernel_call(): pl.pallas_call(body, in_specs=in_specs, out_specs=out_specs, out_shape=ou...  35.3 us
    ppermute x9, starting transfers between devices, from_other(): return lax.ppermute(a, 'width', [(0, 1), (1, 0)])  14.7 us
    ppermute x2, waiting for transfers between devices, exchanged(): lax.ppermute(rows, PATCH, up)  14.3 us
    ppermute x2, starting transfers between devices, exchanged(): lax.ppermute(rows, PATCH, down)  11.6 us
    all_to_all x2, starting transfers between devices, exchanged(): column = lax.all_to_all(copies, Z, split_axis=0, concat_axis=0, tiled=True)  10.7 us
    all_to_all x2, waiting for transfers between devices, exchanged(): lax.all_to_all(plane, PLANE, split_axis=0, concat_axis=0, tiled=True)  8.25 us
    all_to_all x2, starting transfers between devices, exchanged(): lax.all_to_all(plane, PLANE, split_axis=0, concat_axis=0, tiled=True)  7.31 us
    ppermute x9, waiting for transfers between devices, from_other(): return lax.ppermute(a, 'width', [(0, 1), (1, 0)])  4.16 us
  transfers between devices with their start and end apart: 17, of which 9 were waited for; matrix products, arithmetic and copies ran while one was open for 2% of the time, Pallas kernels for 13%

profile of v2, /device:TPU:1, one launch (start us, length us, event | category | flops | bytes accessed | tf_op | source)
XLA Modules:
  0.0 116.1 jit_solution(11053423572209436627)
XLA Ops:
  0.6 0.0 copy-start.5
  0.7 0.0 copy-start.2
  0.8 3.3 %collective-permute-start.4 = (bf16[2,256,1536]{2,1,0:T(8,128)(2,1)}, bf16[2,256,1536]{2,1,0:T(8,128)(2,1)S(1)}, u32[]{:S(2)}, u32[]{:S(2)}) collective-permute-start(bf16[2,256,1536]{2,1,0:T(8,128)(2,1)} %refs_3_.3), channel_id=1, source_target_pairs={{0,1},{1,0},{2,3},{3,2},{4,5},{5,4},{6,7},{7,6},{8,9},{9,8},{10,11... | collective-permute-start | bytes 4718600 | tf_op jit(solution)/shard_map/ppermute | solution.py:386
  4.1 0.1 collective-permute-start.6
  4.2 1.5 %node_rows.1 = (bf16[128,256]{1,0:T(8,128)(2,1)S(1)}, bf16[8,16,256]{2,1,0:T(8,128)(2,1)}) custom-call(bf16[256,128]{1,0:T(8,128)(2,1)} %refs_3_.2), custom_call_target="tpu_custom_call" | custom-call | bytes 4194304 | tf_op jit(solution)/shard_map/node_rows/pallas_call | solution.py:58
  5.7 6.5 %all-to-all-start = ((bf16[8,16,256]{2,1,0:T(8,128)(2,1)}), bf16[8,16,256]{2,1,0:T(8,128)(2,1)S(1)}, u32[]{:S(2)}, u32[]{:S(2)}) async-start(bf16[8,16,256]{2,1,0:T(8,128)(2,1)} %get-tuple-element.62), calls=%async_computation | async-start | bytes 131072 | tf_op jit(solution)/shard_map/all_to_all | solution.py:394
  12.2 7.3 %collective-permute-start.1 = (bf16[128,256]{1,0:T(8,128)(2,1)S(1)}, bf16[128,256]{1,0:T(8,128)(2,1)S(1)}, u32[]{:S(2)}, u32[]{:S(2)}) collective-permute-start(bf16[128,256]{1,0:T(8,128)(2,1)S(1)} %get-tuple-element.78.here_in), channel_id=1, source_target_pairs={{2,0},{4,2},{6,4},{8,6},{10,8},{12,10},{14,12},{16,14},{18,16},{20... | collective-permute-start | bytes 196616 | tf_op jit(solution)/shard_map/ppermute | solution.py:393
  19.5 0.0 collective-permute-start
  19.5 1.3 %collective-permute-done.1.above_in = bf16[128,256]{1,0:T(8,128)(2,1)S(1)} collective-permute-done((bf16[128,256]{1,0:T(8,128)(2,1)S(1)}, bf16[128,256]{1,0:T(8,128)(2,1)S(1)}, u32[]{:S(2)}, u32[]{:S(2)}) %collective-permute-start.1) | collective-permute-done | bytes 65568 | tf_op jit(solution)/shard_map/ppermute | solution.py:393
  20.9 7.2 %collective-permute-done.below_in = bf16[128,256]{1,0:T(8,128)(2,1)S(1)} collective-permute-done((bf16[128,256]{1,0:T(8,128)(2,1)S(1)}, bf16[128,256]{1,0:T(8,128)(2,1)S(1)}, u32[]{:S(2)}, u32[]{:S(2)}) %collective-permute-start) | collective-permute-done | bytes 65568 | tf_op jit(solution)/shard_map/ppermute | solution.py:393
  28.1 0.0 all-to-all-done
  28.1 1.1 broadcast_in_dim.9
  29.2 3.7 %all-to-all-start.1 = ((bf16[16,128,256]{2,1,0:T(8,128)(2,1)}), bf16[16,128,256]{2,1,0:T(8,128)(2,1)S(1)}, u32[]{:S(2)}, u32[]{:S(2)}) async-start(bf16[16,128,256]{2,1,0:T(8,128)(2,1)} %broadcast_in_dim.9), calls=%async_computation.1 | async-start | bytes 2097152 | tf_op jit(solution)/shard_map/all_to_all | solution.py:398
  32.9 2.5 %collective-permute-start.3 = (bf16[256,128]{1,0:T(8,128)(2,1)S(1)}, bf16[256,128]{1,0:T(8,128)(2,1)S(1)}, u32[]{:S(2)}, u32[]{:S(2)}) collective-permute-start(bf16[256,128]{1,0:T(8,128)(2,1)S(1)} %copy-done.5), channel_id=1, source_target_pairs={{0,1},{1,0},{2,3},{3,2},{4,5},{5,4},{6,7},{7,6},{8,9},{9,8},{10,11... | collective-permute-start | bytes 196616 | tf_op jit(solution)/shard_map/ppermute | solution.py:386
  35.5 0.1 collective-permute-start.8
  35.7 0.5 collective-permute-start.2
  36.8 0.0 collective-permute-done.8.refs_14_.refs_12_
  36.8 0.2 collective-permute-start.5
  37.0 0.0 collective-permute-done.3.refs_4_
  37.0 0.4 collective-permute-start.7
  37.4 0.1 pad_add_fusion.scalar_ref
  37.5 0.6 broadcast_subtract_fusion
  38.1 0.6 fusion.9.index_in
  38.7 0.1 collective-permute-done.5.refs_8_.refs_6_
  38.8 1.0 collective-permute-done.7.refs_12_.refs_10_
  39.8 0.0 collective-permute-done.6.refs_10_.refs_8_
  39.8 0.0 collective-permute-done.4.refs_6_.refs_4_
  39.8 0.7 copy-done.4
  40.6 0.5 copy-done.1
  41.1 6.7 %prepare_layer.2 = (f32[512,1024]{1,0:T(8,128)}, f32[512,128]{1,0:T(8,128)}, bf16[128,1024]{1,0:T(8,128)(2,1)}, bf16[512,512]{1,0:T(8,128)(2,1)}, bf16[512,512]{...) custom-call(s32[2]{0:T(128)S(1)} %pad_add_fusion.scalar_ref, ...), custom_call_target="tpu_custom_call" | custom-call | flops 671088640 | bytes 4194304 | tf_op jit(solution)/shard_map/prepare_layer/pallas_call | solution.py:58
  47.8 0.0 all-to-all-done.1
  47.9 2.8 %gather_senders.2.sent_a_ref = bf16[1024,256]{1,0:T(8,128)(2,1)S(1)} custom-call(s32[8,128]{1,0:T(8,128)} %fusion.9.index_in, bf16[128,256]{1,0:T(8,128)(2,1)} %copy-done.20, bf16[128,256]{1,0:T(8,128)(2,1)} %copy-done, bf16[128,256]{1,0:T(8,128)(2,1)} %copy-done.19, bf16[2048,256]{1,0:T(8,128)(2,1)S(1)} %bitcast.8), custom_call_target="tpu_custom_call" | custom-call | flops 1275068416 | bytes 4194304 | tf_op jit(solution)/shard_map/gather_senders/pallas_call | solution.py:58
  50.6 3.7 %collective-permute-start.9 = (bf16[1024,256]{1,0:T(8,128)(2,1)S(1)}, bf16[1024,256]{1,0:T(8,128)(2,1)S(1)}, u32[]{:S(2)}, u32[]{:S(2)}) collective-permute-start(bf16[1024,256]{1,0:T(8,128)(2,1)S(1)} %gather_senders.2.sent_a_ref), channel_id=1, source_target_pairs={{0,1},{1,0},{2,3},{3,2},{4,5},{5,4},{6,7},{7,6},{8,9},{9,8},{10,11... | collective-permute-start | bytes 1572872 | tf_op jit(solution)/shard_map/ppermute | solution.py:386
  54.3 1.5 %collective-permute-done.9.sent_b_ref = bf16[1024,256]{1,0:T(8,128)(2,1)S(1)} collective-permute-done((bf16[1024,256]{1,0:T(8,128)(2,1)S(1)}, bf16[1024,256]{1,0:T(8,128)(2,1)S(1)}, u32[]{:S(2)}, u32[]{:S(2)}) %collective-permute-start.9) | collective-permute-done | bytes 524320 | tf_op jit(solution)/shard_map/ppermute | solution.py:386
  55.9 7.5 %update_graph.2 = (bf16[512,1024]{1,0:T(8,128)(2,1)}, bf16[512,128]{1,0:T(8,128)(2,1)}, bf16[128,256]{1,0:T(8,128)(2,1)}, bf16[8,16,256]{2,1,0:T(8,128)(2,1)}) custom-call(s32[2]{0:T(128)S(1)} %pad_add_fusion.scalar_ref, bf16[1024,256]{1,0:T(8,128)(2,1)S(1)} %gather_senders.2.sent_a_ref, bf16[1024,256]{1,0:T(8,128)(2,1)S(1)} %collective-permute-done.9.sent_b_ref, ...), custom_call_target="tpu_custom_call" | custom-call | flops 1207959552 | bytes 4194304 | tf_op jit(solution)/shard_map/update_graph/pallas_call | solution.py:58
  63.4 4.3 %all-to-all-start.2 = ((bf16[8,16,256]{2,1,0:T(8,128)(2,1)}), bf16[8,16,256]{2,1,0:T(8,128)(2,1)S(1)}, u32[]{:S(2)}, u32[]{:S(2)}) async-start(bf16[8,16,256]{2,1,0:T(8,128)(2,1)} %get-tuple-element.91), calls=%async_computation.2 | async-start | bytes 131072 | tf_op jit(solution)/shard_map/all_to_all | solution.py:394
  67.6 4.3 %collective-permute-start.11 = (bf16[128,256]{1,0:T(8,128)(2,1)}, bf16[128,256]{1,0:T(8,128)(2,1)S(1)}, u32[]{:S(2)}, u32[]{:S(2)}) collective-permute-start(bf16[128,256]{1,0:T(8,128)(2,1)} %get-tuple-element.107.here_in), channel_id=1, source_target_pairs={{2,0},{4,2},{6,4},{8,6},{10,8},{12,10},{14,12},{16,14},{18,16},{20... | collective-permute-start | bytes 196616 | tf_op jit(solution)/shard_map/ppermute | solution.py:393
  71.9 1.6 %collective-permute-done.11.above_in = bf16[128,256]{1,0:T(8,128)(2,1)S(1)} collective-permute-done((bf16[128,256]{1,0:T(8,128)(2,1)}, bf16[128,256]{1,0:T(8,128)(2,1)S(1)}, u32[]{:S(2)}, u32[]{:S(2)}) %collective-permute-start.11) | collective-permute-done | bytes 65568 | tf_op jit(solution)/shard_map/ppermute | solution.py:393
  73.5 7.1 %collective-permute-done.10.below_in = bf16[128,256]{1,0:T(8,128)(2,1)S(1)} collective-permute-done((bf16[128,256]{1,0:T(8,128)(2,1)}, bf16[128,256]{1,0:T(8,128)(2,1)S(1)}, u32[]{:S(2)}, u32[]{:S(2)}) %collective-permute-start.10) | collective-permute-done | bytes 65568 | tf_op jit(solution)/shard_map/ppermute | solution.py:393
  80.6 0.0 all-to-all-done.2
  80.6 1.1 broadcast_in_dim.11
  81.8 3.7 %all-to-all-start.3 = ((bf16[16,128,256]{2,1,0:T(8,128)(2,1)}), bf16[16,128,256]{2,1,0:T(8,128)(2,1)S(1)}, u32[]{:S(2)}, u32[]{:S(2)}) async-start(bf16[16,128,256]{2,1,0:T(8,128)(2,1)} %broadcast_in_dim.11), calls=%async_computation.3 | async-start | bytes 2097152 | tf_op jit(solution)/shard_map/all_to_all | solution.py:398
  85.4 6.6 %prepare_layer.3 = (f32[512,1024]{1,0:T(8,128)}, f32[512,128]{1,0:T(8,128)}, bf16[128,1024]{1,0:T(8,128)(2,1)}, bf16[512,512]{1,0:T(8,128)(2,1)}, bf16[512,512]{...) custom-call(s32[2]{0:T(128)S(1)} %pad_add_fusion.scalar_ref, ...), custom_call_target="tpu_custom_call" | custom-call | flops 671088640 | bytes 4194304 | tf_op jit(solution)/shard_map/prepare_layer/pallas_call | solution.py:58
  92.1 8.2 %all-to-all-done.3 = bf16[16,128,256]{2,1,0:T(8,128)(2,1)S(1)} async-done(((bf16[16,128,256]{2,1,0:T(8,128)(2,1)}), bf16[16,128,256]{2,1,0:T(8,128)(2,1)S(1)}, u32[]{:S(2)}, u32[]{:S(2)}) %all-to-all-start.3) | async-done | bytes 1048608 | tf_op jit(solution)/shard_map/all_to_all | solution.py:398
  100.3 2.8 %gather_senders.3.sent_a_ref = bf16[1024,256]{1,0:T(8,128)(2,1)S(1)} custom-call(s32[8,128]{1,0:T(8,128)} %fusion.9.index_in, bf16[128,256]{1,0:T(8,128)(2,1)} %copy-done.22, bf16[128,256]{1,0:T(8,128)(2,1)} %get-tuple-element.107.here_in, bf16[128,256]{1,0:T(8,128)(2,1)} %copy-done.21, bf16[2048,256]{1,0:T(8,128)(2,1)S(1)} %bitcast.9), custom_call_target="tpu_custom_call" | custom-call | flops 1275068416 | bytes 4194304 | tf_op jit(solution)/shard_map/gather_senders/pallas_call | solution.py:58
  103.1 3.8 %collective-permute-start.12 = (bf16[1024,256]{1,0:T(8,128)(2,1)S(1)}, bf16[1024,256]{1,0:T(8,128)(2,1)S(1)}, u32[]{:S(2)}, u32[]{:S(2)}) collective-permute-start(bf16[1024,256]{1,0:T(8,128)(2,1)S(1)} %gather_senders.3.sent_a_ref), channel_id=1, source_target_pairs={{0,1},{1,0},{2,3},{3,2},{4,5},{5,4},{6,7},{7,6},{8,9},{9,8},{10,11... | collective-permute-start | bytes 1572872 | tf_op jit(solution)/shard_map/ppermute | solution.py:386
  106.9 1.5 %collective-permute-done.12.sent_b_ref = bf16[1024,256]{1,0:T(8,128)(2,1)S(1)} collective-permute-done((bf16[1024,256]{1,0:T(8,128)(2,1)S(1)}, bf16[1024,256]{1,0:T(8,128)(2,1)S(1)}, u32[]{:S(2)}, u32[]{:S(2)}) %collective-permute-start.12) | collective-permute-done | bytes 524320 | tf_op jit(solution)/shard_map/ppermute | solution.py:386
  108.4 7.5 %update_graph.3 = (bf16[256,1024]{1,0:T(8,128)(2,1)}, bf16[256,128]{1,0:T(8,128)(2,1)}) custom-call(s32[2]{0:T(128)S(1)} %pad_add_fusion.scalar_ref, bf16[1024,256]{1,0:T(8,128)(2,1)S(1)} %gather_senders.3.sent_a_ref, bf16[1024,256]{1,0:T(8,128)(2,1)S(1)} %collective-permute-done.12.sent_b_ref, bf16[512,1024]{1,0:T(8,128)(2,1)} %get-tuple-element.110.refs_0_, ...), custom_call_target="tpu_custom_call" | custom-call | flops 1207959552 | bytes 4194304 | tf_op jit(solution)/shard_map/update_graph/pallas_call | solution.py:58
  (53 shorter events, 0.2 us)
Async XLA Ops:
  0.6 32.2 %copy-start.5 = (bf16[256,128]{1,0:T(8,128)(2,1)S(1)}, bf16[256,128]{1,0:T(8,128)(2,1)}, u32[]{:S(2)}) copy-start(bf16[256,128]{1,0:T(8,128)(2,1)} %refs_3_.2) | copy-start | bytes 196612
  0.6 34.7 %copy-start.11 = (f32[2,256]{1,0:T(2,128)S(1)}, f32[2,256]{1,0:T(2,128)}, u32[]{:S(2)}) copy-start(f32[2,256]{1,0:T(2,128)} %param.23) | copy-start | bytes 6148
  0.7 34.7 %copy-start.12 = (f32[2,256]{1,0:T(2,128)S(1)}, f32[2,256]{1,0:T(2,128)}, u32[]{:S(2)}) copy-start(f32[2,256]{1,0:T(2,128)} %param.25) | copy-start | bytes 6148
  0.7 34.7 %copy-start.13 = (f32[2,256]{1,0:T(2,128)S(1)}, f32[2,256]{1,0:T(2,128)}, u32[]{:S(2)}) copy-start(f32[2,256]{1,0:T(2,128)} %param.26) | copy-start | bytes 6148
  0.7 34.7 %copy-start.14 = (f32[2,256]{1,0:T(2,128)S(1)}, f32[2,256]{1,0:T(2,128)}, u32[]{:S(2)}) copy-start(f32[2,256]{1,0:T(2,128)} %param.27) | copy-start | bytes 6148
  0.7 34.7 %copy-start.15 = (f32[2,256]{1,0:T(2,128)S(1)}, f32[2,256]{1,0:T(2,128)}, u32[]{:S(2)}) copy-start(f32[2,256]{1,0:T(2,128)} %param.29) | copy-start | bytes 6148
  0.7 34.7 %copy-start.16 = (f32[2,256]{1,0:T(2,128)S(1)}, f32[2,256]{1,0:T(2,128)}, u32[]{:S(2)}) copy-start(f32[2,256]{1,0:T(2,128)} %param.31) | copy-start | bytes 6148
  0.7 34.7 %copy-start.17 = (f32[2,256]{1,0:T(2,128)S(1)}, f32[2,256]{1,0:T(2,128)}, u32[]{:S(2)}) copy-start(f32[2,256]{1,0:T(2,128)} %param.32) | copy-start | bytes 6148
  0.7 34.8 %copy-start.18 = (f32[2,256]{1,0:T(2,128)S(1)}, f32[2,256]{1,0:T(2,128)}, u32[]{:S(2)}) copy-start(f32[2,256]{1,0:T(2,128)} %param.33) | copy-start | bytes 6148
  0.7 36.1 %copy-start.2 = (bf16[2,256,512]{2,1,0:T(8,128)(2,1)S(1)}, bf16[2,256,512]{2,1,0:T(8,128)(2,1)}, u32[]{:S(2)}) copy-start(bf16[2,256,512]{2,1,0:T(8,128)(2,1)} %refs_5_.3) | copy-start | bytes 1572868
  0.7 36.8 %copy-start.9 = (s32[1024]{0:T(1024)S(1)}, s32[1024]{0:T(1024)}, u32[]{:S(2)}) copy-start(s32[1024]{0:T(1024)} %param.20) | copy-start | bytes 12292
  0.7 37.4 %copy-start.10 = (s32[1024]{0:T(1024)S(1)}, s32[1024]{0:T(1024)}, u32[]{:S(2)}) copy-start(s32[1024]{0:T(1024)} %param.19) | copy-start | bytes 12292
  0.8 39.0 %collective-permute-start.4 = (bf16[2,256,1536]{2,1,0:T(8,128)(2,1)}, bf16[2,256,1536]{2,1,0:T(8,128)(2,1)S(1)}, u32[]{:S(2)}, u32[]{:S(2)}) collective-permute-start(bf16[2,256,1536]{2,1,0:T(8,128)(2,1)} %refs_3_.3), channel_id=1, source_target_pairs={{0,1},{1,0},{2,3},{3,2},{4,5},{5,4},{6,7},{7,6},{8,9},{9,8},{10,11... | collective-permute-start | bytes 4718600 | tf_op jit(solution)/shard_map/ppermute | solution.py:386
  4.1 35.7 %collective-permute-start.6 = (bf16[2,256,1024]{2,1,0:T(8,128)(2,1)}, bf16[2,256,1024]{2,1,0:T(8,128)(2,1)}, u32[]{:S(2)}, u32[]{:S(2)}) collective-permute-start(bf16[2,256,1024]{2,1,0:T(8,128)(2,1)} %refs_7_.3), channel_id=1, source_target_pairs={{0,1},{1,0},{2,3},{3,2},{4,5},{5,4},{6,7},{7,6},{8,9},{9,8},{10,11... | collective-permute-start | bytes 3145736 | tf_op jit(solution)/shard_map/ppermute | solution.py:386
  5.7 42.1 %copy-start = (bf16[128,256]{1,0:T(8,128)(2,1)}, bf16[128,256]{1,0:T(8,128)(2,1)S(1)}, u32[]{:S(2)}) copy-start(bf16[128,256]{1,0:T(8,128)(2,1)S(1)} %get-tuple-element.78.here_in) | copy-start | bytes 196612
  5.7 22.3 %all-to-all-start = ((bf16[8,16,256]{2,1,0:T(8,128)(2,1)}), bf16[8,16,256]{2,1,0:T(8,128)(2,1)S(1)}, u32[]{:S(2)}, u32[]{:S(2)}) async-start(bf16[8,16,256]{2,1,0:T(8,128)(2,1)} %get-tuple-element.62), calls=%async_computation | async-start | bytes 131072 | tf_op jit(solution)/shard_map/all_to_all | solution.py:394
  12.2 8.7 %collective-permute-start.1 = (bf16[128,256]{1,0:T(8,128)(2,1)S(1)}, bf16[128,256]{1,0:T(8,128)(2,1)S(1)}, u32[]{:S(2)}, u32[]{:S(2)}) collective-permute-start(bf16[128,256]{1,0:T(8,128)(2,1)S(1)} %get-tuple-element.78.here_in), channel_id=1, source_target_pairs={{2,0},{4,2},{6,4},{8,6},{10,8},{12,10},{14,12},{16,14},{18,16},{20... | collective-permute-start | bytes 196616 | tf_op jit(solution)/shard_map/ppermute | solution.py:393
  19.5 8.5 %collective-permute-start = (bf16[128,256]{1,0:T(8,128)(2,1)S(1)}, bf16[128,256]{1,0:T(8,128)(2,1)S(1)}, u32[]{:S(2)}, u32[]{:S(2)}) collective-permute-start(bf16[128,256]{1,0:T(8,128)(2,1)S(1)} %get-tuple-element.78.here_in), channel_id=1, source_target_pairs={{0,2},{2,4},{4,6},{6,8},{8,10},{10,12},{12,14},{14,16},{16,18},{18... | collective-permute-start | bytes 196616 | tf_op jit(solution)/shard_map/ppermute | solution.py:393
  20.9 27.0 %copy-start.19 = (bf16[128,256]{1,0:T(8,128)(2,1)}, bf16[128,256]{1,0:T(8,128)(2,1)S(1)}, u32[]{:S(2)}) copy-start(bf16[128,256]{1,0:T(8,128)(2,1)S(1)} %collective-permute-done.1.above_in) | copy-start | bytes 196612
  28.1 19.8 %copy-start.20 = (bf16[128,256]{1,0:T(8,128)(2,1)}, bf16[128,256]{1,0:T(8,128)(2,1)S(1)}, u32[]{:S(2)}) copy-start(bf16[128,256]{1,0:T(8,128)(2,1)S(1)} %collective-permute-done.below_in) | copy-start | bytes 196612
  29.2 18.7 %all-to-all-start.1 = ((bf16[16,128,256]{2,1,0:T(8,128)(2,1)}), bf16[16,128,256]{2,1,0:T(8,128)(2,1)S(1)}, u32[]{:S(2)}, u32[]{:S(2)}) async-start(bf16[16,128,256]{2,1,0:T(8,128)(2,1)} %broadcast_in_dim.9), calls=%async_computation.1 | async-start | bytes 2097152 | tf_op jit(solution)/shard_map/all_to_all | solution.py:398
  32.9 4.2 %collective-permute-start.3 = (bf16[256,128]{1,0:T(8,128)(2,1)S(1)}, bf16[256,128]{1,0:T(8,128)(2,1)S(1)}, u32[]{:S(2)}, u32[]{:S(2)}) collective-permute-start(bf16[256,128]{1,0:T(8,128)(2,1)S(1)} %copy-done.5), channel_id=1, source_target_pairs={{0,1},{1,0},{2,3},{3,2},{4,5},{5,4},{6,7},{7,6},{8,9},{9,8},{10,11... | collective-permute-start | bytes 196616 | tf_op jit(solution)/shard_map/ppermute | solution.py:386
  35.5 4.3 %copy-start.6 = (f32[2,8,256]{2,1,0:T(8,128)}, f32[2,8,256]{2,1,0:T(8,128)S(1)}, u32[]{:S(2)}) copy-start(f32[2,8,256]{2,1,0:T(8,128)S(1)} %stack.43.refs_13_.refs_11_) | copy-start | bytes 49156
  35.5 1.3 %collective-permute-start.8 = (f32[2,8,256]{2,1,0:T(8,128)S(1)}, f32[2,8,256]{2,1,0:T(8,128)S(1)}, u32[]{:S(2)}, u32[]{:S(2)}) collective-permute-start(f32[2,8,256]{2,1,0:T(8,128)S(1)} %stack.43.refs_13_.refs_11_), channel_id=1, source_target_pairs={{0,1},{1,0},{2,3},{3,2},{4,5},{5,4},{6,7},{7,6},{8,9},{9,8},{10,11... | collective-permute-start | bytes 49160 | tf_op jit(solution)/shard_map/ppermute | solution.py:386
  35.7 3.0 %collective-permute-start.2 = (bf16[256,1024]{1,0:T(8,128)(2,1)}, bf16[256,1024]{1,0:T(8,128)(2,1)}, u32[]{:S(2)}, u32[]{:S(2)}) collective-permute-start(bf16[256,1024]{1,0:T(8,128)(2,1)} %refs_0_.1), channel_id=1, source_target_pairs={{0,1},{1,0},{2,3},{3,2},{4,5},{5,4},{6,7},{7,6},{8,9},{9,8},{10,11... | collective-permute-start | bytes 1572872 | tf_op jit(solution)/shard_map/ppermute | solution.py:386
  36.8 3.0 %copy-start.8 = (f32[2,8,256]{2,1,0:T(8,128)}, f32[2,8,256]{2,1,0:T(8,128)S(1)}, u32[]{:S(2)}) copy-start(f32[2,8,256]{2,1,0:T(8,128)S(1)} %collective-permute-done.8.refs_14_.refs_12_) | copy-start | bytes 49156
  36.8 2.0 %collective-permute-start.5 = (bf16[2,256,512]{2,1,0:T(8,128)(2,1)S(1)}, bf16[2,256,512]{2,1,0:T(8,128)(2,1)S(1)}, u32[]{:S(2)}, u32[]{:S(2)}) collective-permute-start(bf16[2,256,512]{2,1,0:T(8,128)(2,1)S(1)} %copy-done.2), channel_id=1, source_target_pairs={{0,1},{1,0},{2,3},{3,2},{4,5},{5,4},{6,7},{7,6},{8,9},{9,8},{10,11... | collective-permute-start | bytes 1572872 | tf_op jit(solution)/shard_map/ppermute | solution.py:386
  37.0 2.8 %copy-start.7 = (bf16[256,128]{1,0:T(8,128)(2,1)}, bf16[256,128]{1,0:T(8,128)(2,1)S(1)}, u32[]{:S(2)}) copy-start(bf16[256,128]{1,0:T(8,128)(2,1)S(1)} %collective-permute-done.3.refs_4_) | copy-start | bytes 196612
  37.0 2.8 %collective-permute-start.7 = (bf16[2,256,512]{2,1,0:T(8,128)(2,1)}, bf16[2,256,512]{2,1,0:T(8,128)(2,1)S(1)}, u32[]{:S(2)}, u32[]{:S(2)}) collective-permute-start(bf16[2,256,512]{2,1,0:T(8,128)(2,1)} %refs_9_.3), channel_id=1, source_target_pairs={{0,1},{1,0},{2,3},{3,2},{4,5},{5,4},{6,7},{7,6},{8,9},{9,8},{10,11... | collective-permute-start | bytes 1572872 | tf_op jit(solution)/shard_map/ppermute | solution.py:386
  38.8 1.0 copy-start.3
  39.8 0.8 copy-start.4
  39.8 1.3 %copy-start.1 = (bf16[2,256,1536]{2,1,0:T(8,128)(2,1)}, bf16[2,256,1536]{2,1,0:T(8,128)(2,1)S(1)}, u32[]{:S(2)}) copy-start(bf16[2,256,1536]{2,1,0:T(8,128)(2,1)S(1)} %collective-permute-done.4.refs_6_.refs_4_) | copy-start | bytes 4718596
  50.6 5.3 %collective-permute-start.9 = (bf16[1024,256]{1,0:T(8,128)(2,1)S(1)}, bf16[1024,256]{1,0:T(8,128)(2,1)S(1)}, u32[]{:S(2)}, u32[]{:S(2)}) collective-permute-start(bf16[1024,256]{1,0:T(8,128)(2,1)S(1)} %gather_senders.2.sent_a_ref), channel_id=1, source_target_pairs={{0,1},{1,0},{2,3},{3,2},{4,5},{5,4},{6,7},{7,6},{8,9},{9,8},{10,11... | collective-permute-start | bytes 1572872 | tf_op jit(solution)/shard_map/ppermute | solution.py:386
  63.4 17.3 %all-to-all-start.2 = ((bf16[8,16,256]{2,1,0:T(8,128)(2,1)}), bf16[8,16,256]{2,1,0:T(8,128)(2,1)S(1)}, u32[]{:S(2)}, u32[]{:S(2)}) async-start(bf16[8,16,256]{2,1,0:T(8,128)(2,1)} %get-tuple-element.91), calls=%async_computation.2 | async-start | bytes 131072 | tf_op jit(solution)/shard_map/all_to_all | solution.py:394
  67.6 5.9 %collective-permute-start.11 = (bf16[128,256]{1,0:T(8,128)(2,1)}, bf16[128,256]{1,0:T(8,128)(2,1)S(1)}, u32[]{:S(2)}, u32[]{:S(2)}) collective-permute-start(bf16[128,256]{1,0:T(8,128)(2,1)} %get-tuple-element.107.here_in), channel_id=1, source_target_pairs={{2,0},{4,2},{6,4},{8,6},{10,8},{12,10},{14,12},{16,14},{18,16},{20... | collective-permute-start | bytes 196616 | tf_op jit(solution)/shard_map/ppermute | solution.py:393
  71.9 8.8 %collective-permute-start.10 = (bf16[128,256]{1,0:T(8,128)(2,1)}, bf16[128,256]{1,0:T(8,128)(2,1)S(1)}, u32[]{:S(2)}, u32[]{:S(2)}) collective-permute-start(bf16[128,256]{1,0:T(8,128)(2,1)} %get-tuple-element.107.here_in), channel_id=1, source_target_pairs={{0,2},{2,4},{4,6},{6,8},{8,10},{10,12},{12,14},{14,16},{16,18},{18... | collective-permute-start | bytes 196616 | tf_op jit(solution)/shard_map/ppermute | solution.py:393
  73.5 18.5 %copy-start.21 = (bf16[128,256]{1,0:T(8,128)(2,1)}, bf16[128,256]{1,0:T(8,128)(2,1)S(1)}, u32[]{:S(2)}) copy-start(bf16[128,256]{1,0:T(8,128)(2,1)S(1)} %collective-permute-done.11.above_in) | copy-start | bytes 196612
  80.6 11.4 %copy-start.22 = (bf16[128,256]{1,0:T(8,128)(2,1)}, bf16[128,256]{1,0:T(8,128)(2,1)S(1)}, u32[]{:S(2)}) copy-start(bf16[128,256]{1,0:T(8,128)(2,1)S(1)} %collective-permute-done.10.below_in) | copy-start | bytes 196612
  81.8 18.6 %all-to-all-start.3 = ((bf16[16,128,256]{2,1,0:T(8,128)(2,1)}), bf16[16,128,256]{2,1,0:T(8,128)(2,1)S(1)}, u32[]{:S(2)}, u32[]{:S(2)}) async-start(bf16[16,128,256]{2,1,0:T(8,128)(2,1)} %broadcast_in_dim.11), calls=%async_computation.3 | async-start | bytes 2097152 | tf_op jit(solution)/shard_map/all_to_all | solution.py:398
  103.1 5.4 %collective-permute-start.12 = (bf16[1024,256]{1,0:T(8,128)(2,1)S(1)}, bf16[1024,256]{1,0:T(8,128)(2,1)S(1)}, u32[]{:S(2)}, u32[]{:S(2)}) collective-permute-start(bf16[1024,256]{1,0:T(8,128)(2,1)S(1)} %gather_senders.3.sent_a_ref), channel_id=1, source_target_pairs={{0,1},{1,0},{2,3},{3,2},{4,5},{5,4},{6,7},{7,6},{8,9},{9,8},{10,11... | collective-permute-start | bytes 1572872 | tf_op jit(solution)/shard_map/ppermute | solution.py:386

commit v3 on v2

--- a/solution.py
+++ b/solution.py
@@ -13,6 +13,7 @@
 PLANE = (Y, X)
 EPSILON = 1e-05
 EDGE_BLOCK = 512
+ROWS = 32
 VMEM_LIMIT = 32 * 1024 * 1024
 
 
@@ -166,140 +167,142 @@
     )
 
 
-def prepare_kernel(layer, n_in, n_out, scalar_ref, *refs):
-    ins, outs = refs[:n_in], refs[n_in : n_in + n_out]
-    held_in = refs[n_in + n_out : 2 * n_in + n_out]
-    held_out = refs[2 * n_in + n_out : 2 * (n_in + n_out)]
-    in_sems, out_sems = refs[2 * (n_in + n_out) :]
-    copies = started(
-        [(a.at[layer] if len(a.shape) == 3 else a, b) for a, b in zip(ins, held_in)], in_sems
-    )
+def before_kernel(layer, n_in, scalar_ref, *refs):
+    ins, outs = refs[:n_in], refs[n_in : n_in + 6]
+    edge_held, node_held, hidden_weight_ref, out_held, vec_held, receiver_ref, sems = refs[
+        n_in + 6 :
+    ]
+    before_ref, edges_ref, incidence_ref, sent_weight_ref, out_weight_ref, vectors_ref = outs
     first = scalar_ref[0] == 0
     count = scalar_ref[1]
-    sent = [pltpu.make_async_copy(held_out[i], outs[i], out_sems.at[i]) for i in range(n_out)]
+    receiver, (wa, wb, ea, eb, vec_a, vec_b) = ins[0], ins[1:7]
+    edges_in, nodes_in = ins[7 : 7 + (n_in - 7) // 2], ins[7 + (n_in - 7) // 2 :]
+    half = wa.shape[1]
+    width = 2 * half
+
+    def top(ref):
+        return ref.at[pl.ds(0, half)]
+
+    def bottom(ref):
+        return ref.at[pl.ds(half, half)]
+
+    def part(ref, start):
+        return ref.at[layer, :, pl.ds(start, width)]
+
+    def both(sources, target):
+        if len(sources) == 1:
+            return [(sources[0], target)]
+        return [(sources[0], top(target)), (sources[1], bottom(target))]
+
+    edge_target = edge_held if layer == 0 else edges_ref
+    pairs = both(nodes_in, node_held) + [(receiver, receiver_ref)]
+    pairs += [(vec_a.at[layer], vec_held.at[0]), (vec_b.at[layer], vec_held.at[1])]
+    for k, target in ((2, hidden_weight_ref.at[1]), (0, hidden_weight_ref.at[0])):
+        pairs += both((part(wa, k * width), part(wb, k * width)), target)
+    pairs += both(edges_in, edge_target)
+    split = len(pairs)
+    pairs += both((ea.at[layer], eb.at[layer]), out_held)
+    pairs += both((part(wa, width), part(wb, width)), sent_weight_ref)
+    copies = started(pairs, sems)
+    finish(copies[:split])
+
+    vec = [vec_held[0].T, vec_held[1].T]
+    hidden_vec = jnp.concatenate(vec, axis=0)
+    feature_vec = in_order(first, *vec)
+    nodes = node_held[...]
     if layer == 0:
-        edge_a, edge_b, receiver_ref, node_a, node_b = held_in[:5]
-    else:
-        edge_a, receiver_ref, node_a = held_in[:3]
-        edge_b, node_b = edge_a, node_a
-    wa, wb, ea, eb, va, vb, oa, ob, vec_a_ref, vec_b_ref = held_in[-10:]
+        nodes = in_order(first, nodes[:half], nodes[half:])
+        edges_ref[...] = in_order(first, edge_held[:half, :], edge_held[half:, :])
+    for i, column in enumerate((1, 2, 3)):
+        vectors_ref[i] = jnp.broadcast_to(feature_vec[:, column : column + 1], (width, 128))
+    vectors_ref[3] = jnp.concatenate([hidden_vec, feature_vec] + [hidden_vec] * 14, axis=1)
+    slots = incidence_ref.shape[1]
+    live = lax.broadcasted_iota(jnp.int32, (1, slots), 1) < count
+    incidence_ref[...] = jnp.where(
+        (lax.broadcasted_iota(jnp.int32, incidence_ref.shape, 0) == receiver_ref[...]) & live,
+        1.0,
+        0.0,
+    ).astype(jnp.bfloat16)
+    receiver_part = dot(hidden_weight_ref[1], nodes).astype(jnp.bfloat16)
+    before = dot(hidden_weight_ref[0], edges_ref[...]) + dot(receiver_part, incidence_ref[...])
+    before_ref[...] = before + hidden_vec[:, 0:1]
+    finish(copies[split:])
+    out_weight_ref[...] = out_held[...].T
+
+
+def before_sent(layer, scalars, edges, receiver, nodes, weights):
+    slots = edges[0].shape[1]
+    node_rows = nodes[0].shape[1]
+    width = weights[0].shape[1] * 2
+    inputs = (receiver, *weights[:4], *weights[8:], *edges, *nodes)
+    out_shape = [
+        shape((width, slots), jnp.float32),
+        shape((width, slots)),
+        shape((node_rows, slots)),
+        shape((width, width)),
+        shape((width, width)),
+        shape((4, width, 128), jnp.float32),
+    ]
+    edge_held = shape((width, slots) if layer == 0 else (16, 128))
+    return kernel_call(
+        functools.partial(before_kernel, layer, len(inputs)),
+        "before_sent",
+        out_shape,
+        (scalars, *inputs),
+        [SMEM] + [HBM] * len(inputs),
+        [VMEM] * len(out_shape),
+        held(
+            [
+                edge_held,
+                shape((width, node_rows)),
+                shape((2, width, width)),
+                shape((width, width)),
+                shape((2, *weights[8].shape[1:]), jnp.float32),
+                receiver,
+            ]
+        )
+        + [pltpu.SemaphoreType.DMA((15,))],
+        2 * slots * width * (width + node_rows),
+    )
+
+
+def update_kernel(layer, last_layer, n_nodes, n_out, scalar_ref, *refs):
     (
+        sent_a_ref,
+        sent_b_ref,
         before_ref,
-        node_before_ref,
+        edges_ref,
         incidence_ref,
         sent_weight_ref,
         out_weight_ref,
-        aggregate_weight_ref,
-        node_weight_ref,
         vectors_ref,
-    ) = held_out[:8]
-    width = out_weight_ref.shape[0]
-    nodes_here, slots = incidence_ref.shape
-
-    def stacked(a, b):
-        return jnp.concatenate([a, b], axis=0)
-
-    finish(copies)
-    if layer == 0:
-        edges = in_order(first, edge_a[...], edge_b[...])
-        nodes = in_order(first, node_a[...], node_b[...])
-        held_out[8][...] = edges
-        held_out[9][...] = nodes
-        sent[8].start()
-        sent[9].start()
-    else:
-        edges, nodes = edge_a[...], node_a[...]
-    w = stacked(wa[...], wb[...])
-    v = stacked(va[...], vb[...])
-    sent_weight_ref[...] = w[:, width : 2 * width]
-    sent[3].start()
-    out_weight_ref[...] = stacked(ea[...], eb[...]).T
-    sent[4].start()
-    aggregate_weight_ref[...] = v[:, width:]
-    sent[5].start()
-    node_weight_ref[...] = stacked(oa[...], ob[...]).T
-    sent[6].start()
-    vec_a, vec_b = vec_a_ref[...].T, vec_b_ref[...].T
-    hidden_vec = stacked(vec_a, vec_b)
-    vectors_ref[...] = in_order(first, vec_a, vec_b)
-    sent[7].start()
-    live = lax.broadcasted_iota(jnp.int32, (1, slots), 1) < count
-    incidence_ref[...] = jnp.where(
-        (lax.broadcasted_iota(jnp.int32, (nodes_here, slots), 0) == receiver_ref[...]) & live,
-        1.0,
-        0.0,
-    ).astype(jnp.bfloat16)
-    sent[2].start()
-    node_before_ref[...] = dot(v[:, :width], nodes) + hidden_vec[:, 4:5]
-    sent[1].start()
-    part = dot(w[:, 2 * width :], nodes).astype(jnp.bfloat16)
-    before = dot(w[:, :width], edges) + dot(part, incidence_ref[...])
-    before_ref[...] = before + hidden_vec[:, 0:1]
-    sent[0].start()
-    finish(sent)
-
-
-def prepared(layer, scalars, edges, receiver, nodes, weights):
-    slots = edges[0].shape[1]
-    node_rows = nodes[0].shape[1]
-    width = weights[0].shape[1] * 2
-    inputs = (*edges, receiver, *nodes, *weights)
-    out_shape = [
-        shape((width, slots), jnp.float32),
-        shape((width, node_rows), jnp.float32),
-        shape((node_rows, slots)),
-        shape((width, width)),
-        shape((width, width)),
-        shape((width, width)),
-        shape((width, width)),
-        shape((width, 8), jnp.float32),
-    ]
-    if layer == 0:
-        out_shape += [shape((width, slots)), shape((width, node_rows))]
-    n_in, n_out = len(inputs), len(out_shape)
-    one_layer = [shape(a.shape[-2:], a.dtype) for a in inputs]
-    ready = kernel_call(
-        functools.partial(prepare_kernel, layer, n_in, n_out),
-        "prepare_layer",
-        out_shape,
-        (scalars, *inputs),
-        [SMEM] + [HBM] * n_in,
-        [HBM] * n_out,
-        held(one_layer)
-        + held(out_shape)
-        + [pltpu.SemaphoreType.DMA((n_in,)), pltpu.SemaphoreType.DMA((n_out,))],
-        2 * slots * width * (width + node_rows),
-    )
-    if layer == 0:
-        return (ready[8], ready[9], *ready[:8])
-    return (edges[0], nodes[0], *ready)
-
-
-def update_kernel(last_layer, n_out, scalar_ref, sent_a_ref, sent_b_ref, *refs):
-    ins, outs, held_in = refs[:10], refs[10 : 10 + n_out], refs[10 + n_out : 20 + n_out]
-    held_out = refs[20 + n_out : 20 + 2 * n_out]
-    in_sems, out_sems = refs[20 + 2 * n_out :]
-    edges_ref, nodes_ref, before_ref, node_before_ref, incidence_ref = held_in[:5]
-    sent_weight_ref, out_weight_ref, aggregate_weight_ref, node_weight_ref, vectors_ref = held_in[
-        5:
-    ]
-    slots = edges_ref.shape[1]
-    starts = range(0, slots, EDGE_BLOCK)
-    early = [(ins[5], sent_weight_ref)]
-    for start in starts:
-        early.append(tuple(columns_of(r, start, EDGE_BLOCK) for r in (ins[2], before_ref)))
-        if start == 0:
-            early += [(ins[6], out_weight_ref), (ins[9], vectors_ref)]
-        for i in (0, 4):
-            early.append(tuple(columns_of(r, start, EDGE_BLOCK) for r in (ins[i], held_in[i])))
-    late = [(ins[i], held_in[i]) for i in (1, 3, 7, 8)]
-    copies = started(early + late, in_sems)
-    groups = [copies[:6], copies[6:9], copies[9:]]
-
+        va,
+        vb,
+        oa,
+        ob,
+    ) = refs[:12]
+    nodes_in, outs = refs[12 : 12 + n_nodes], refs[12 + n_nodes : 12 + n_nodes + n_out]
+    refs = refs[12 + n_nodes + n_out :]
+    held_out, (node_held, in_held, out_held, hidden_ref, mlp_ref) = refs[:n_out], refs[n_out:-2]
+    in_sems, out_sems = refs[-2:]
+    half = sent_a_ref.shape[1]
+    width = 2 * half
     first = scalar_ref[0] == 0
     count = scalar_ref[1]
-    half = sent_a_ref.shape[1]
-    total = None
+
+    def top(ref):
+        return ref.at[pl.ds(0, half)]
+
+    def bottom(ref):
+        return ref.at[pl.ds(half, half)]
+
+    pairs = [(va.at[layer], top(in_held)), (vb.at[layer], bottom(in_held))]
+    pairs += [(oa.at[layer], top(out_held)), (ob.at[layer], bottom(out_held))]
+    if n_nodes == 1:
+        pairs += [(nodes_in[0], node_held)]
+    else:
+        pairs += [(nodes_in[0], top(node_held)), (nodes_in[1], bottom(node_held))]
+    copies = started(pairs, in_sems)
     edge_out_ref, node_out_ref = held_out[:2]
     sent_out = []
 
@@ -308,38 +311,61 @@
         copy.start()
         sent_out.append(copy)
 
-    for turn, start in enumerate(starts):
-        finish(groups[turn])
-        vectors = vectors_ref[...]
+    slots = edges_ref.shape[1]
+    total = None
+    for start in range(0, slots, EDGE_BLOCK):
         here = slice(start, start + EDGE_BLOCK)
         sent_a, sent_b = sent_a_ref[here, :], sent_b_ref[here, :]
         low = jnp.where(first, sent_a, sent_b)
         high = jnp.where(first, sent_b, sent_a)
         sent = jnp.concatenate([low, high], axis=1)
-        before = before_ref[:, here] + dot(sent_weight_ref[...], sent, ((1,), (1,)))
-        hidden = silu(before).astype(jnp.bfloat16)
-        mlp = dot(out_weight_ref[...], hidden) + vectors[:, 1:2]
+        mlp_ref[...] = dot(sent_weight_ref[...], sent, ((1,), (1,)))
+        for row in range(0, width, ROWS):
+            rows = slice(row, row + ROWS)
+            value = silu(mlp_ref[rows, :] + before_ref[rows, here])
+            hidden_ref[rows, :] = value.astype(jnp.bfloat16)
+        mlp_ref[...] = dot(out_weight_ref[...], hidden_ref[...])
+
+        def spread(index, rows):
+            return jnp.concatenate([vectors_ref[index, rows, :]] * (EDGE_BLOCK // 128), axis=1)
+
+        new_ref = hidden_ref if last_layer else columns_of(edge_out_ref, start, EDGE_BLOCK)
+        sums = jnp.zeros((8, EDGE_BLOCK), jnp.float32)
+        squares = jnp.zeros((8, EDGE_BLOCK), jnp.float32)
+        for row in range(0, width, ROWS):
+            rows = slice(row, row + ROWS)
+            value = mlp_ref[rows, :] + spread(0, rows)
+            mlp_ref[rows, :] = value
+            sums = sums + jnp.sum(value.reshape(ROWS // 8, 8, EDGE_BLOCK), axis=0)
+            squares = squares + jnp.sum((value * value).reshape(ROWS // 8, 8, EDGE_BLOCK), axis=0)
+        mean = jnp.sum(sums, axis=0, keepdims=True) * (1.0 / width)
+        square = jnp.sum(squares, axis=0, keepdims=True) * (1.0 / width)
+        scale = lax.rsqrt(square - mean * mean + EPSILON)
         live = lax.broadcasted_iota(jnp.int32, (1, EDGE_BLOCK), 1) + start < count
-        updated = edges_ref[:, here].astype(jnp.float32) + layer_norm(
-            mlp, vectors[:, 2:3], vectors[:, 3:4]
-        )
-        updated = jnp.where(live, updated, 0.0).astype(jnp.bfloat16)
+        for row in range(0, width, ROWS):
+            rows = slice(row, row + ROWS)
+            value = (mlp_ref[rows, :] - mean) * scale * spread(1, rows) + spread(2, rows)
+            value = value + edges_ref[rows, here].astype(jnp.float32)
+            new_ref[rows, :] = jnp.where(live, value, 0.0).astype(jnp.bfloat16)
+        updated = new_ref[...]
         part = dot(updated, incidence_ref[:, here], ((1,), (1,)))
         total = part if total is None else total + part
         if last_layer:
             edge_out_ref[:, here] = jnp.where(first, updated[:half], updated[half:])
-        else:
-            edge_out_ref[:, here] = updated
-        send(
-            columns_of(edge_out_ref, start, EDGE_BLOCK), columns_of(outs[0], start, EDGE_BLOCK)
-        )
-    finish(groups[2])
+        send(new_ref if not last_layer else columns_of(edge_out_ref, start, EDGE_BLOCK),
+             columns_of(outs[0], start, EDGE_BLOCK))
+    finish(copies)
+    small = vectors_ref[3]
+    hidden_vec, feature_vec = small[:, 0:8], small[:, 8:16]
+    nodes = node_held[...]
+    if n_nodes == 2:
+        nodes = in_order(first, nodes[:half], nodes[half:])
     aggregate = total.astype(jnp.bfloat16)
-    node_before = node_before_ref[...] + dot(aggregate_weight_ref[...], aggregate)
-    node_hidden = silu(node_before).astype(jnp.bfloat16)
-    node_mlp = dot(node_weight_ref[...], node_hidden) + vectors[:, 5:6]
-    new = nodes_ref[...].astype(jnp.float32) + layer_norm(
-        node_mlp, vectors[:, 6:7], vectors[:, 7:8]
+    node_before = dot(in_held[:, :width], nodes) + dot(in_held[:, width:], aggregate)
+    node_hidden = silu(node_before + hidden_vec[:, 4:5]).astype(jnp.bfloat16)
+    node_mlp = dot(out_held[...].T, node_hidden) + feature_vec[:, 5:6]
+    new = nodes.astype(jnp.float32) + layer_norm(
+        node_mlp, feature_vec[:, 6:7], feature_vec[:, 7:8]
     )
     new = new.astype(jnp.bfloat16)
     mine = jnp.where(first, new[:half], new[half:])
@@ -354,9 +380,9 @@
     finish(sent_out)
 
 
-def updated_graph(last_layer, scalars, sent, ready, copies):
+def updated_graph(layer, last_layer, scalars, sent, ready, nodes, weights, copies):
     slots = ready[0].shape[1]
-    node_rows = ready[1].shape[1]
+    node_rows = nodes[0].shape[1]
     half = sent[0].shape[1]
     width = 2 * half
     out_width = half if last_layer else width
@@ -364,19 +390,26 @@
     if not last_layer:
         out_shape += [shape((node_rows, half)), shape((copies, node_rows // 8, half))]
     n_out = len(out_shape)
-    blocks = slots // EDGE_BLOCK
     return kernel_call(
-        functools.partial(update_kernel, last_layer, n_out),
+        functools.partial(update_kernel, layer, last_layer, len(nodes), n_out),
         "update_graph",
         out_shape,
-        (scalars, *sent, *ready),
-        [SMEM, VMEM, VMEM] + [HBM] * 10,
+        (scalars, *sent, *ready, *weights[4:8], *nodes),
+        [SMEM] + [VMEM] * (2 + len(ready)) + [HBM] * (4 + len(nodes)),
         [HBM] * n_out,
-        held(ready)
-        + held(out_shape)
+        held(out_shape)
+        + held(
+            [
+                shape((width, node_rows)),
+                shape((width, 2 * width)),
+                shape((width, width)),
+                shape((width, EDGE_BLOCK)),
+                shape((width, EDGE_BLOCK), jnp.float32),
+            ]
+        )
         + [
-            pltpu.SemaphoreType.DMA((3 * blocks + 7,)),
-            pltpu.SemaphoreType.DMA((n_out - 1 + blocks,)),
+            pltpu.SemaphoreType.DMA((6,)),
+            pltpu.SemaphoreType.DMA((n_out - 1 + slots // EDGE_BLOCK,)),
         ],
         2 * slots * width * (2 * width + node_rows),
     )
@@ -393,7 +426,6 @@
     below, above = lax.ppermute(rows, PATCH, up), lax.ppermute(rows, PATCH, down)
     column = lax.all_to_all(copies, Z, split_axis=0, concat_axis=0, tiled=True)
     column = column.reshape(-1, rows.shape[1])
-    column, below, above = lax.optimization_barrier((column, below, above))
     plane = jnp.broadcast_to(column, (lax.axis_size(PLANE), *column.shape))
     coarse = lax.all_to_all(plane, PLANE, split_axis=0, concat_axis=0, tiled=True)
     return below, rows, above, coarse.reshape(-1, rows.shape[1])
@@ -469,13 +501,15 @@
 
     edges = (edge_latents, from_other(edge_latents))
     nodes = (node_latents, from_other(node_latents))
+    table, weights, edges, nodes = lax.optimization_barrier((table, weights, edges, nodes))
     for layer in range(layers):
         last_layer = layer == layers - 1
-        ready = prepared(layer, scalars, edges, receiver, nodes, weights)
-        table, ready = lax.optimization_barrier((table, ready))
         sent = gathered(index, *table)
         sent = (sent, from_other(sent))
-        results = updated_graph(last_layer, scalars, sent, ready, columns)
+        ready = before_sent(layer, scalars, edges, receiver, nodes, weights)
+        results = updated_graph(
+            layer, last_layer, scalars, sent, ready, nodes, weights, columns
+        )
         if not last_layer:
             edges, nodes = results[:1], results[1:2]
             table = exchanged(results[2], results[3])

time: 117 us -> 113 us (0.966)
  blocking collectives: 0 us -> 11.5 us
  Pallas kernels: 35.3 us -> 28.3 us
  waiting for transfers between devices: 29.7 us -> 24.7 us
  starting transfers between devices: 44.3 us -> 42.2 us
  local copies, waits for them, and re-layouts: 3.66 us -> 2.33 us
    ppermute x2, waiting for transfers between devices: 14.3 us -> 0.51 us  [exchanged(): lax.ppermute(rows, PATCH, up)]
    all_to_all x0 -> x1, blocking collectives: none -> 11.5 us  [exchanged(): column = lax.all_to_all(copies, Z, split_axis=0, concat_axis=0, tiled=True)]
    ppermute x2, waiting for transfers between devices: 2.97 us -> 14 us  [exchanged(): lax.ppermute(rows, PATCH, down)]
    pallas_call x7, Pallas kernels: 35.3 us -> 28.3 us  [kernel_call(): pl.pallas_call(body, in_specs=in_specs, out_specs=out_specs, out_shape=ou...]
    all_to_all x2 -> x1, waiting for transfers between devices: 0.01 us -> 6.71 us  [exchanged(): column = lax.all_to_all(copies, Z, split_axis=0, concat_axis=0, tiled=True)]
    all_to_all x2, waiting for transfers between devices: 8.25 us -> 2.19 us  [exchanged(): lax.all_to_all(plane, PLANE, split_axis=0, concat_axis=0, tiled=True)]
    all_to_all x2, starting transfers between devices: 7.31 us -> 11.6 us  [exchanged(): lax.all_to_all(plane, PLANE, split_axis=0, concat_axis=0, tiled=True)]
    all_to_all x2 -> x1, starting transfers between devices: 10.7 us -> 6.46 us  [exchanged(): column = lax.all_to_all(copies, Z, split_axis=0, concat_axis=0, tiled=True)]
  transfers between devices with their start and end apart: 17 -> 16, of which waited for: 9 -> 7; matrix products, arithmetic and copies ran while one was open for 2% -> 2% of each run, Pallas kernels for 13% -> 9%
where the time goes in v3:
time: 113 us; the launch traced here: 112 us
  starting transfers between devices  42.2 us (37%)
  Pallas kernels  28.3 us (25%)
  waiting for transfers between devices  24.7 us (22%)
  blocking collectives  11.5 us (10%)
  local copies, waits for them, and re-layouts  2.33 us (2%)
  between operations  1.91 us (2%)
  other arithmetic  1.28 us (1%)
    pallas_call x7, Pallas kernels, kernel_call(): pl.pallas_call(body, in_specs=in_specs, out_specs=out_specs, out_shape=ou...  28.3 us
    ppermute x9, starting transfers between devices, from_other(): return lax.ppermute(a, 'width', [(0, 1), (1, 0)])  15 us
    ppermute x2, waiting for transfers between devices, exchanged(): lax.ppermute(rows, PATCH, down)  14 us
    all_to_all x2, starting transfers between devices, exchanged(): lax.all_to_all(plane, PLANE, split_axis=0, concat_axis=0, tiled=True)  11.6 us
    all_to_all x1, blocking collectives, exchanged(): column = lax.all_to_all(copies, Z, split_axis=0, concat_axis=0, tiled=True)  11.5 us
    ppermute x2, starting transfers between devices, exchanged(): lax.ppermute(rows, PATCH, down)  9.16 us
    all_to_all x1, waiting for transfers between devices, exchanged(): column = lax.all_to_all(copies, Z, split_axis=0, concat_axis=0, tiled=True)  6.71 us
    all_to_all x1, starting transfers between devices, exchanged(): column = lax.all_to_all(copies, Z, split_axis=0, concat_axis=0, tiled=True)  6.46 us
  transfers between devices with their start and end apart: 16, of which 7 were waited for; matrix products, arithmetic and copies ran while one was open for 2% of the time, Pallas kernels for 9%

profile of v3, /device:TPU:1, one launch (start us, length us, event | category | flops | bytes accessed | tf_op | source)
XLA Modules:
  0.0 112.1 jit_solution(3486819254957350236)
XLA Ops:
  0.6 0.0 copy-start.3
  0.7 0.0 copy-start.2
  0.7 3.3 %collective-permute-start.2 = (bf16[2,256,1536]{2,1,0:T(8,128)(2,1)}, bf16[2,256,1536]{2,1,0:T(8,128)(2,1)S(1)}, u32[]{:S(2)}, u32[]{:S(2)}) collective-permute-start(bf16[2,256,1536]{2,1,0:T(8,128)(2,1)} %refs_1_.1), channel_id=1, source_target_pairs={{0,1},{1,0},{2,3},{3,2},{4,5},{5,4},{6,7},{7,6},{8,9},{9,8},{10,11... | collective-permute-start | bytes 4718600 | tf_op jit(solution)/shard_map/ppermute | solution.py:419
  4.1 1.5 %node_rows.1 = (bf16[128,256]{1,0:T(8,128)(2,1)S(1)}, bf16[8,16,256]{2,1,0:T(8,128)(2,1)}) custom-call(bf16[256,128]{1,0:T(8,128)(2,1)} %refs_12_), custom_call_target="tpu_custom_call" | custom-call | bytes 4194304 | tf_op jit(solution)/shard_map/node_rows/pallas_call | solution.py:59
  5.6 0.0 copy-start
  5.6 6.5 %all-to-all-start = ((bf16[8,16,256]{2,1,0:T(8,128)(2,1)}), bf16[8,16,256]{2,1,0:T(8,128)(2,1)S(1)}, u32[]{:S(2)}, u32[]{:S(2)}) async-start(bf16[8,16,256]{2,1,0:T(8,128)(2,1)} %get-tuple-element.41), calls=%async_computation | async-start | bytes 131072 | tf_op jit(solution)/shard_map/all_to_all | solution.py:427
  12.1 0.4 collective-permute-start.4
  12.5 6.7 %all-to-all-done = bf16[8,16,256]{2,1,0:T(8,128)(2,1)S(1)} async-done(((bf16[8,16,256]{2,1,0:T(8,128)(2,1)}), bf16[8,16,256]{2,1,0:T(8,128)(2,1)S(1)}, u32[]{:S(2)}, u32[]{:S(2)}) %all-to-all-start) | async-done | bytes 65568 | tf_op jit(solution)/shard_map/all_to_all | solution.py:427
  19.2 1.1 broadcast_in_dim.9
  20.3 6.8 %all-to-all-start.1 = ((bf16[16,128,256]{2,1,0:T(8,128)(2,1)}), bf16[16,128,256]{2,1,0:T(8,128)(2,1)S(1)}, u32[]{:S(2)}, u32[]{:S(2)}) async-start(bf16[16,128,256]{2,1,0:T(8,128)(2,1)} %broadcast_in_dim.9), calls=%async_computation.1 | async-start | bytes 2097152 | tf_op jit(solution)/shard_map/all_to_all | solution.py:430
  27.3 2.0 %collective-permute-start.6 = (f32[2,8,256]{2,1,0:T(8,128)S(1)}, f32[2,8,256]{2,1,0:T(8,128)S(1)}, u32[]{:S(2)}, u32[]{:S(2)}) collective-permute-start(f32[2,8,256]{2,1,0:T(8,128)S(1)} %stack.43.refs_5_), channel_id=1, source_target_pairs={{0,1},{1,0},{2,3},{3,2},{4,5},{5,4},{6,7},{7,6},{8,9},{9,8},{10,11... | collective-permute-start | bytes 49160 | tf_op jit(solution)/shard_map/ppermute | solution.py:419
  29.4 0.1 collective-permute-start.8
  29.5 4.6 %collective-permute-start.1 = (bf16[128,256]{1,0:T(8,128)(2,1)S(1)}, bf16[128,256]{1,0:T(8,128)(2,1)S(1)}, u32[]{:S(2)}, u32[]{:S(2)}) collective-permute-start(bf16[128,256]{1,0:T(8,128)(2,1)S(1)} %get-tuple-element.43.here_in), channel_id=1, source_target_pairs={{2,0},{4,2},{6,4},{8,6},{10,8},{12,10},{14,12},{16,14},{18,16},{20... | collective-permute-start | bytes 196616 | tf_op jit(solution)/shard_map/ppermute | solution.py:426
  34.1 0.0 collective-permute-done.6.refs_6_
  34.1 0.0 collective-permute-start
  34.1 0.0 collective-permute-done.8.refs_10_.refs_13_
  34.1 0.8 collective-permute-start.7
  34.9 5.3 %collective-permute-done.1.above_in = bf16[128,256]{1,0:T(8,128)(2,1)S(1)} collective-permute-done((bf16[128,256]{1,0:T(8,128)(2,1)S(1)}, bf16[128,256]{1,0:T(8,128)(2,1)S(1)}, u32[]{:S(2)}, u32[]{:S(2)}) %collective-permute-start.1) | collective-permute-done | bytes 65568 | tf_op jit(solution)/shard_map/ppermute | solution.py:426
  40.2 2.8 %collective-permute-start.3 = (bf16[2,256,512]{2,1,0:T(8,128)(2,1)S(1)}, bf16[2,256,512]{2,1,0:T(8,128)(2,1)}, u32[]{:S(2)}, u32[]{:S(2)}) collective-permute-start(bf16[2,256,512]{2,1,0:T(8,128)(2,1)S(1)} %copy-done.2), channel_id=1, source_target_pairs={{0,1},{1,0},{2,3},{3,2},{4,5},{5,4},{6,7},{7,6},{8,9},{9,8},{10,11... | collective-permute-start | bytes 1572872 | tf_op jit(solution)/shard_map/ppermute | solution.py:419
  43.0 0.1 collective-permute-done.below_in
  43.1 1.4 %collective-permute-start.5 = (bf16[2,256,512]{2,1,0:T(8,128)(2,1)}, bf16[2,256,512]{2,1,0:T(8,128)(2,1)}, u32[]{:S(2)}, u32[]{:S(2)}) collective-permute-start(bf16[2,256,512]{2,1,0:T(8,128)(2,1)} %refs_10_.1), channel_id=1, source_target_pairs={{0,1},{1,0},{2,3},{3,2},{4,5},{5,4},{6,7},{7,6},{8,9},{9,8},{10,11... | collective-permute-start | bytes 1572872 | tf_op jit(solution)/shard_map/ppermute | solution.py:419
  44.5 0.6 fusion.9.index_in
  45.1 0.0 collective-permute-done.7.refs_8_
  45.1 0.0 collective-permute-done.3.refs_4_
  45.1 1.3 %collective-permute-done.5.refs_11_ = bf16[2,256,512]{2,1,0:T(8,128)(2,1)} collective-permute-done((bf16[2,256,512]{2,1,0:T(8,128)(2,1)}, bf16[2,256,512]{2,1,0:T(8,128)(2,1)}, u32[]{:S(2)}, u32[]{:S(2)}) %collective-permute-start.5) | collective-permute-done | bytes 524320 | tf_op jit(solution)/shard_map/ppermute | solution.py:419
  46.4 0.0 collective-permute-done.4.refs_9_
  46.4 0.0 collective-permute-done.2.refs_2_
  46.4 0.0 copy-start.8
  46.4 3.0 %gather_senders.2.refs_0_ = bf16[1024,256]{1,0:T(8,128)(2,1)S(1)} custom-call(s32[8,128]{1,0:T(8,128)} %fusion.9.index_in, bf16[128,256]{1,0:T(8,128)(2,1)} %copy-done.18, bf16[128,256]{1,0:T(8,128)(2,1)} %copy-done, bf16[128,256]{1,0:T(8,128)(2,1)} %copy-done.17, bf16[2048,256]{1,0:T(8,128)(2,1)S(1)} %bitcast.8), custom_call_target="tpu_custom_call" | custom-call | flops 1275068416 | bytes 4194304 | tf_op jit(solution)/shard_map/gather_senders/pallas_call | solution.py:59
  49.5 0.6 collective-permute-start.9
  50.8 0.1 pad_add_fusion.scalar_ref
  50.9 0.6 broadcast_subtract_fusion
  51.4 4.2 %before_sent.2 = (f32[512,1024]{1,0:T(8,128)S(1)}, bf16[512,1024]{1,0:T(8,128)(2,1)S(1)}, bf16[128,1024]{1,0:T(8,128)(2,1)S(1)}, bf16[512,512]{1,0:T(8,128)(2,1)...) custom-call(s32[2]{0:T(128)S(1)} %pad_add_fusion.scalar_ref, s32[1,1024]{1,0:T(1,128)} %bitcast.12, ...), custom_call_target="tpu_custom_call" | custom-call | flops 671088640 | bytes 4194304 | tf_op jit(solution)/shard_map/before_sent/pallas_call | solution.py:59
  55.7 0.0 collective-permute-done.9.refs_1_
  55.7 6.5 %update_graph.2 = (bf16[512,1024]{1,0:T(8,128)(2,1)}, bf16[512,128]{1,0:T(8,128)(2,1)}, bf16[128,256]{1,0:T(8,128)(2,1)}, bf16[8,16,256]{2,1,0:T(8,128)(2,1)}) custom-call(s32[2]{0:T(128)S(1)} %pad_add_fusion.scalar_ref, bf16[1024,256]{1,0:T(8,128)(2,1)S(1)} %gather_senders.2.refs_0_, bf16[1024,256]{1,0:T(8,128)(2,1)S(1)} %collective-permute-done.9.refs_1_, ...), custom_call_target="tpu_custom_call" | custom-call | flops 1207959552 | bytes 4194304 | tf_op jit(solution)/shard_map/update_graph/pallas_call | solution.py:59
  62.1 0.0 copy-start.19
  62.2 11.5 %all_to_all.20 = bf16[8,16,256]{2,1,0:T(8,128)(2,1)S(1)} all-to-all(bf16[8,16,256]{2,1,0:T(8,128)(2,1)} %get-tuple-element.67), channel_id=1, replica_groups=mesh['patch_0'=8,'patch_1'=4,'patch_2'=4,'width'=2] {'patch_0'}, dimensions={0} | all-to-all | bytes 131072 | tf_op jit(solution)/shard_map/all_to_all | solution.py:427
  73.6 1.1 broadcast_in_dim.11
  74.7 4.9 %all-to-all-start.3 = ((bf16[16,128,256]{2,1,0:T(8,128)(2,1)}), bf16[16,128,256]{2,1,0:T(8,128)(2,1)S(1)}, u32[]{:S(2)}, u32[]{:S(2)}) async-start(bf16[16,128,256]{2,1,0:T(8,128)(2,1)} %broadcast_in_dim.11), calls=%async_computation.3 | async-start | bytes 2097152 | tf_op jit(solution)/shard_map/all_to_all | solution.py:430
  79.6 4.5 %collective-permute-start.11 = (bf16[128,256]{1,0:T(8,128)(2,1)S(1)}, bf16[128,256]{1,0:T(8,128)(2,1)S(1)}, u32[]{:S(2)}, u32[]{:S(2)}) collective-permute-start(bf16[128,256]{1,0:T(8,128)(2,1)S(1)} %copy-done.19), channel_id=1, source_target_pairs={{2,0},{4,2},{6,4},{8,6},{10,8},{12,10},{14,12},{16,14},{18,16},{20... | collective-permute-start | bytes 196616 | tf_op jit(solution)/shard_map/ppermute | solution.py:426
  84.1 0.0 collective-permute-start.10
  84.1 8.7 %collective-permute-done.11.above_in = bf16[128,256]{1,0:T(8,128)(2,1)S(1)} collective-permute-done((bf16[128,256]{1,0:T(8,128)(2,1)S(1)}, bf16[128,256]{1,0:T(8,128)(2,1)S(1)}, u32[]{:S(2)}, u32[]{:S(2)}) %collective-permute-start.11) | collective-permute-done | bytes 65568 | tf_op jit(solution)/shard_map/ppermute | solution.py:426
  92.8 0.4 collective-permute-done.10.below_in
  93.3 2.2 %all-to-all-done.3 = bf16[16,128,256]{2,1,0:T(8,128)(2,1)S(1)} async-done(((bf16[16,128,256]{2,1,0:T(8,128)(2,1)}), bf16[16,128,256]{2,1,0:T(8,128)(2,1)S(1)}, u32[]{:S(2)}, u32[]{:S(2)}) %all-to-all-start.3) | async-done | bytes 1048608 | tf_op jit(solution)/shard_map/all_to_all | solution.py:430
  95.5 2.8 %gather_senders.3.refs_0_ = bf16[1024,256]{1,0:T(8,128)(2,1)S(1)} custom-call(s32[8,128]{1,0:T(8,128)} %fusion.9.index_in, bf16[128,256]{1,0:T(8,128)(2,1)} %copy-done.21, bf16[128,256]{1,0:T(8,128)(2,1)} %get-tuple-element.66.here_in, bf16[128,256]{1,0:T(8,128)(2,1)} %copy-done.20, bf16[2048,256]{1,0:T(8,128)(2,1)S(1)} %bitcast.9), custom_call_target="tpu_custom_call" | custom-call | flops 1275068416 | bytes 4194304 | tf_op jit(solution)/shard_map/gather_senders/pallas_call | solution.py:59
  98.2 3.4 %collective-permute-start.12 = (bf16[1024,256]{1,0:T(8,128)(2,1)S(1)}, bf16[1024,256]{1,0:T(8,128)(2,1)S(1)}, u32[]{:S(2)}, u32[]{:S(2)}) collective-permute-start(bf16[1024,256]{1,0:T(8,128)(2,1)S(1)} %gather_senders.3.refs_0_), channel_id=1, source_target_pairs={{0,1},{1,0},{2,3},{3,2},{4,5},{5,4},{6,7},{7,6},{8,9},{9,8},{10,11... | collective-permute-start | bytes 1572872 | tf_op jit(solution)/shard_map/ppermute | solution.py:419
  101.7 4.2 %before_sent.3 = (f32[512,1024]{1,0:T(8,128)S(1)}, bf16[512,1024]{1,0:T(8,128)(2,1)S(1)}, bf16[128,1024]{1,0:T(8,128)(2,1)S(1)}, bf16[512,512]{1,0:T(8,128)(2,1)...) custom-call(s32[2]{0:T(128)S(1)} %pad_add_fusion.scalar_ref, s32[1,1024]{1,0:T(1,128)} %bitcast.13, ...), custom_call_target="tpu_custom_call" | custom-call | flops 671088640 | bytes 4194304 | tf_op jit(solution)/shard_map/before_sent/pallas_call | solution.py:59
  105.9 6.0 %update_graph.3 = (bf16[256,1024]{1,0:T(8,128)(2,1)}, bf16[256,128]{1,0:T(8,128)(2,1)}) custom-call(s32[2]{0:T(128)S(1)} %pad_add_fusion.scalar_ref, bf16[1024,256]{1,0:T(8,128)(2,1)S(1)} %gather_senders.3.refs_0_, bf16[1024,256]{1,0:T(8,128)(2,1)S(1)} %collective-permute-done.12.refs_1_, f32[512,1024]{1,0:T(8,128)S(1)} %get-tuple-element.70.refs_2_, ...), custom_call_target="tpu_custom_call" | custom-call | flops 1207959552 | bytes 4194304 | tf_op jit(solution)/shard_map/update_graph/pallas_call | solution.py:59
  (50 shorter events, 0.2 us)
Async XLA Ops:
  0.6 28.7 %copy-start.3 = (bf16[256,128]{1,0:T(8,128)(2,1)S(1)}, bf16[256,128]{1,0:T(8,128)(2,1)}, u32[]{:S(2)}) copy-start(bf16[256,128]{1,0:T(8,128)(2,1)} %refs_12_) | copy-start | bytes 196612
  0.6 26.5 %copy-start.9 = (f32[2,256]{1,0:T(2,128)S(1)}, f32[2,256]{1,0:T(2,128)}, u32[]{:S(2)}) copy-start(f32[2,256]{1,0:T(2,128)} %param.23) | copy-start | bytes 6148
  0.7 26.5 %copy-start.10 = (f32[2,256]{1,0:T(2,128)S(1)}, f32[2,256]{1,0:T(2,128)}, u32[]{:S(2)}) copy-start(f32[2,256]{1,0:T(2,128)} %param.25) | copy-start | bytes 6148
  0.7 26.5 %copy-start.11 = (f32[2,256]{1,0:T(2,128)S(1)}, f32[2,256]{1,0:T(2,128)}, u32[]{:S(2)}) copy-start(f32[2,256]{1,0:T(2,128)} %param.26) | copy-start | bytes 6148
  0.7 26.5 %copy-start.12 = (f32[2,256]{1,0:T(2,128)S(1)}, f32[2,256]{1,0:T(2,128)}, u32[]{:S(2)}) copy-start(f32[2,256]{1,0:T(2,128)} %param.27) | copy-start | bytes 6148
  0.7 26.5 %copy-start.13 = (f32[2,256]{1,0:T(2,128)S(1)}, f32[2,256]{1,0:T(2,128)}, u32[]{:S(2)}) copy-start(f32[2,256]{1,0:T(2,128)} %param.29) | copy-start | bytes 6148
  0.7 26.5 %copy-start.14 = (f32[2,256]{1,0:T(2,128)S(1)}, f32[2,256]{1,0:T(2,128)}, u32[]{:S(2)}) copy-start(f32[2,256]{1,0:T(2,128)} %param.31) | copy-start | bytes 6148
  0.7 26.5 %copy-start.15 = (f32[2,256]{1,0:T(2,128)S(1)}, f32[2,256]{1,0:T(2,128)}, u32[]{:S(2)}) copy-start(f32[2,256]{1,0:T(2,128)} %param.32) | copy-start | bytes 6148
  0.7 26.5 %copy-start.16 = (f32[2,256]{1,0:T(2,128)S(1)}, f32[2,256]{1,0:T(2,128)}, u32[]{:S(2)}) copy-start(f32[2,256]{1,0:T(2,128)} %param.33) | copy-start | bytes 6148
  0.7 39.4 %copy-start.2 = (bf16[2,256,512]{2,1,0:T(8,128)(2,1)S(1)}, bf16[2,256,512]{2,1,0:T(8,128)(2,1)}, u32[]{:S(2)}) copy-start(bf16[2,256,512]{2,1,0:T(8,128)(2,1)} %refs_3_.1) | copy-start | bytes 1572868
  0.7 43.7 %copy-start.7 = (s32[1024]{0:T(1024)S(1)}, s32[1024]{0:T(1024)}, u32[]{:S(2)}) copy-start(s32[1024]{0:T(1024)} %param.19) | copy-start | bytes 12292
  0.7 45.6 %collective-permute-start.2 = (bf16[2,256,1536]{2,1,0:T(8,128)(2,1)}, bf16[2,256,1536]{2,1,0:T(8,128)(2,1)S(1)}, u32[]{:S(2)}, u32[]{:S(2)}) collective-permute-start(bf16[2,256,1536]{2,1,0:T(8,128)(2,1)} %refs_1_.1), channel_id=1, source_target_pairs={{0,1},{1,0},{2,3},{3,2},{4,5},{5,4},{6,7},{7,6},{8,9},{9,8},{10,11... | collective-permute-start | bytes 4718600 | tf_op jit(solution)/shard_map/ppermute | solution.py:419
  5.6 40.8 %copy-start = (bf16[128,256]{1,0:T(8,128)(2,1)}, bf16[128,256]{1,0:T(8,128)(2,1)S(1)}, u32[]{:S(2)}) copy-start(bf16[128,256]{1,0:T(8,128)(2,1)S(1)} %get-tuple-element.43.here_in) | copy-start | bytes 196612
  5.6 13.6 %all-to-all-start = ((bf16[8,16,256]{2,1,0:T(8,128)(2,1)}), bf16[8,16,256]{2,1,0:T(8,128)(2,1)S(1)}, u32[]{:S(2)}, u32[]{:S(2)}) async-start(bf16[8,16,256]{2,1,0:T(8,128)(2,1)} %get-tuple-element.41), calls=%async_computation | async-start | bytes 131072 | tf_op jit(solution)/shard_map/all_to_all | solution.py:427
  12.1 34.3 %collective-permute-start.4 = (bf16[2,256,1024]{2,1,0:T(8,128)(2,1)}, bf16[2,256,1024]{2,1,0:T(8,128)(2,1)}, u32[]{:S(2)}, u32[]{:S(2)}) collective-permute-start(bf16[2,256,1024]{2,1,0:T(8,128)(2,1)} %refs_8_.1), channel_id=1, source_target_pairs={{0,1},{1,0},{2,3},{3,2},{4,5},{5,4},{6,7},{7,6},{8,9},{9,8},{10,11... | collective-permute-start | bytes 3145736 | tf_op jit(solution)/shard_map/ppermute | solution.py:419
  20.3 26.0 %all-to-all-start.1 = ((bf16[16,128,256]{2,1,0:T(8,128)(2,1)}), bf16[16,128,256]{2,1,0:T(8,128)(2,1)S(1)}, u32[]{:S(2)}, u32[]{:S(2)}) async-start(bf16[16,128,256]{2,1,0:T(8,128)(2,1)} %broadcast_in_dim.9), calls=%async_computation.1 | async-start | bytes 2097152 | tf_op jit(solution)/shard_map/all_to_all | solution.py:430
  27.3 22.1 %copy-start.5 = (f32[2,8,256]{2,1,0:T(8,128)}, f32[2,8,256]{2,1,0:T(8,128)S(1)}, u32[]{:S(2)}) copy-start(f32[2,8,256]{2,1,0:T(8,128)S(1)} %stack.43.refs_5_) | copy-start | bytes 49156
  27.3 6.8 %collective-permute-start.6 = (f32[2,8,256]{2,1,0:T(8,128)S(1)}, f32[2,8,256]{2,1,0:T(8,128)S(1)}, u32[]{:S(2)}, u32[]{:S(2)}) collective-permute-start(f32[2,8,256]{2,1,0:T(8,128)S(1)} %stack.43.refs_5_), channel_id=1, source_target_pairs={{0,1},{1,0},{2,3},{3,2},{4,5},{5,4},{6,7},{7,6},{8,9},{9,8},{10,11... | collective-permute-start | bytes 49160 | tf_op jit(solution)/shard_map/ppermute | solution.py:419
  29.4 4.7 %collective-permute-start.8 = (bf16[256,128]{1,0:T(8,128)(2,1)S(1)}, bf16[256,128]{1,0:T(8,128)(2,1)S(1)}, u32[]{:S(2)}, u32[]{:S(2)}) collective-permute-start(bf16[256,128]{1,0:T(8,128)(2,1)S(1)} %copy-done.3), channel_id=1, source_target_pairs={{0,1},{1,0},{2,3},{3,2},{4,5},{5,4},{6,7},{7,6},{8,9},{9,8},{10,11... | collective-permute-start | bytes 196616 | tf_op jit(solution)/shard_map/ppermute | solution.py:419
  29.5 10.7 %collective-permute-start.1 = (bf16[128,256]{1,0:T(8,128)(2,1)S(1)}, bf16[128,256]{1,0:T(8,128)(2,1)S(1)}, u32[]{:S(2)}, u32[]{:S(2)}) collective-permute-start(bf16[128,256]{1,0:T(8,128)(2,1)S(1)} %get-tuple-element.43.here_in), channel_id=1, source_target_pairs={{2,0},{4,2},{6,4},{8,6},{10,8},{12,10},{14,12},{16,14},{18,16},{20... | collective-permute-start | bytes 196616 | tf_op jit(solution)/shard_map/ppermute | solution.py:426
  34.1 15.4 %copy-start.6 = (f32[2,8,256]{2,1,0:T(8,128)}, f32[2,8,256]{2,1,0:T(8,128)S(1)}, u32[]{:S(2)}) copy-start(f32[2,8,256]{2,1,0:T(8,128)S(1)} %collective-permute-done.6.refs_6_) | copy-start | bytes 49156
  34.1 9.0 %collective-permute-start = (bf16[128,256]{1,0:T(8,128)(2,1)S(1)}, bf16[128,256]{1,0:T(8,128)(2,1)S(1)}, u32[]{:S(2)}, u32[]{:S(2)}) collective-permute-start(bf16[128,256]{1,0:T(8,128)(2,1)S(1)} %get-tuple-element.43.here_in), channel_id=1, source_target_pairs={{0,2},{2,4},{4,6},{6,8},{8,10},{10,12},{12,14},{14,16},{16,18},{18... | collective-permute-start | bytes 196616 | tf_op jit(solution)/shard_map/ppermute | solution.py:426
  34.1 15.4 %copy-start.4 = (bf16[256,128]{1,0:T(8,128)(2,1)}, bf16[256,128]{1,0:T(8,128)(2,1)S(1)}, u32[]{:S(2)}) copy-start(bf16[256,128]{1,0:T(8,128)(2,1)S(1)} %collective-permute-done.8.refs_10_.refs_13_) | copy-start | bytes 196612
  34.1 11.0 %collective-permute-start.7 = (bf16[256,1024]{1,0:T(8,128)(2,1)}, bf16[256,1024]{1,0:T(8,128)(2,1)}, u32[]{:S(2)}, u32[]{:S(2)}) collective-permute-start(bf16[256,1024]{1,0:T(8,128)(2,1)} %refs_7_), channel_id=1, source_target_pairs={{0,1},{1,0},{2,3},{3,2},{4,5},{5,4},{6,7},{7,6},{8,9},{9,8},{10,11... | collective-permute-start | bytes 1572872 | tf_op jit(solution)/shard_map/ppermute | solution.py:419
  40.2 6.2 %copy-start.17 = (bf16[128,256]{1,0:T(8,128)(2,1)}, bf16[128,256]{1,0:T(8,128)(2,1)S(1)}, u32[]{:S(2)}) copy-start(bf16[128,256]{1,0:T(8,128)(2,1)S(1)} %collective-permute-done.1.above_in) | copy-start | bytes 196612
  40.2 4.9 %collective-permute-start.3 = (bf16[2,256,512]{2,1,0:T(8,128)(2,1)S(1)}, bf16[2,256,512]{2,1,0:T(8,128)(2,1)}, u32[]{:S(2)}, u32[]{:S(2)}) collective-permute-start(bf16[2,256,512]{2,1,0:T(8,128)(2,1)S(1)} %copy-done.2), channel_id=1, source_target_pairs={{0,1},{1,0},{2,3},{3,2},{4,5},{5,4},{6,7},{7,6},{8,9},{9,8},{10,11... | collective-permute-start | bytes 1572872 | tf_op jit(solution)/shard_map/ppermute | solution.py:419
  43.1 3.3 %copy-start.18 = (bf16[128,256]{1,0:T(8,128)(2,1)}, bf16[128,256]{1,0:T(8,128)(2,1)S(1)}, u32[]{:S(2)}) copy-start(bf16[128,256]{1,0:T(8,128)(2,1)S(1)} %collective-permute-done.below_in) | copy-start | bytes 196612
  43.1 3.3 %collective-permute-start.5 = (bf16[2,256,512]{2,1,0:T(8,128)(2,1)}, bf16[2,256,512]{2,1,0:T(8,128)(2,1)}, u32[]{:S(2)}, u32[]{:S(2)}) collective-permute-start(bf16[2,256,512]{2,1,0:T(8,128)(2,1)} %refs_10_.1), channel_id=1, source_target_pairs={{0,1},{1,0},{2,3},{3,2},{4,5},{5,4},{6,7},{7,6},{8,9},{9,8},{10,11... | collective-permute-start | bytes 1572872 | tf_op jit(solution)/shard_map/ppermute | solution.py:419
  46.4 3.1 %copy-start.1 = (bf16[2,256,1536]{2,1,0:T(8,128)(2,1)}, bf16[2,256,1536]{2,1,0:T(8,128)(2,1)S(1)}, u32[]{:S(2)}) copy-start(bf16[2,256,1536]{2,1,0:T(8,128)(2,1)S(1)} %collective-permute-done.2.refs_2_) | copy-start | bytes 4718596
  46.4 4.5 %copy-start.8 = (s32[1024]{0:T(1024)S(1)}, s32[1024]{0:T(1024)}, u32[]{:S(2)}) copy-start(s32[1024]{0:T(1024)} %param.20) | copy-start | bytes 12292
  49.5 6.2 %collective-permute-start.9 = (bf16[1024,256]{1,0:T(8,128)(2,1)S(1)}, bf16[1024,256]{1,0:T(8,128)(2,1)S(1)}, u32[]{:S(2)}, u32[]{:S(2)}) collective-permute-start(bf16[1024,256]{1,0:T(8,128)(2,1)S(1)} %gather_senders.2.refs_0_), channel_id=1, source_target_pairs={{0,1},{1,0},{2,3},{3,2},{4,5},{5,4},{6,7},{7,6},{8,9},{9,8},{10,11... | collective-permute-start | bytes 1572872 | tf_op jit(solution)/shard_map/ppermute | solution.py:419
  62.1 17.4 %copy-start.19 = (bf16[128,256]{1,0:T(8,128)(2,1)S(1)}, bf16[128,256]{1,0:T(8,128)(2,1)}, u32[]{:S(2)}) copy-start(bf16[128,256]{1,0:T(8,128)(2,1)} %get-tuple-element.66.here_in) | copy-start | bytes 196612
  74.7 20.8 %all-to-all-start.3 = ((bf16[16,128,256]{2,1,0:T(8,128)(2,1)}), bf16[16,128,256]{2,1,0:T(8,128)(2,1)S(1)}, u32[]{:S(2)}, u32[]{:S(2)}) async-start(bf16[16,128,256]{2,1,0:T(8,128)(2,1)} %broadcast_in_dim.11), calls=%async_computation.3 | async-start | bytes 2097152 | tf_op jit(solution)/shard_map/all_to_all | solution.py:430
  79.6 13.2 %collective-permute-start.11 = (bf16[128,256]{1,0:T(8,128)(2,1)S(1)}, bf16[128,256]{1,0:T(8,128)(2,1)S(1)}, u32[]{:S(2)}, u32[]{:S(2)}) collective-permute-start(bf16[128,256]{1,0:T(8,128)(2,1)S(1)} %copy-done.19), channel_id=1, source_target_pairs={{2,0},{4,2},{6,4},{8,6},{10,8},{12,10},{14,12},{16,14},{18,16},{20... | collective-permute-start | bytes 196616 | tf_op jit(solution)/shard_map/ppermute | solution.py:426
  84.1 9.1 %collective-permute-start.10 = (bf16[128,256]{1,0:T(8,128)(2,1)S(1)}, bf16[128,256]{1,0:T(8,128)(2,1)S(1)}, u32[]{:S(2)}, u32[]{:S(2)}) collective-permute-start(bf16[128,256]{1,0:T(8,128)(2,1)S(1)} %copy-done.19), channel_id=1, source_target_pairs={{0,2},{2,4},{4,6},{6,8},{8,10},{10,12},{12,14},{14,16},{16,18},{18... | collective-permute-start | bytes 196616 | tf_op jit(solution)/shard_map/ppermute | solution.py:426
  92.8 2.6 %copy-start.20 = (bf16[128,256]{1,0:T(8,128)(2,1)}, bf16[128,256]{1,0:T(8,128)(2,1)S(1)}, u32[]{:S(2)}) copy-start(bf16[128,256]{1,0:T(8,128)(2,1)S(1)} %collective-permute-done.11.above_in) | copy-start | bytes 196612
  93.3 2.2 %copy-start.21 = (bf16[128,256]{1,0:T(8,128)(2,1)}, bf16[128,256]{1,0:T(8,128)(2,1)S(1)}, u32[]{:S(2)}) copy-start(bf16[128,256]{1,0:T(8,128)(2,1)S(1)} %collective-permute-done.10.below_in) | copy-start | bytes 196612
  98.2 7.7 %collective-permute-start.12 = (bf16[1024,256]{1,0:T(8,128)(2,1)S(1)}, bf16[1024,256]{1,0:T(8,128)(2,1)S(1)}, u32[]{:S(2)}, u32[]{:S(2)}) collective-permute-start(bf16[1024,256]{1,0:T(8,128)(2,1)S(1)} %gather_senders.3.refs_0_), channel_id=1, source_target_pairs={{0,1},{1,0},{2,3},{3,2},{4,5},{5,4},{6,7},{7,6},{8,9},{9,8},{10,11... | collective-permute-start | bytes 1572872 | tf_op jit(solution)/shard_map/ppermute | solution.py:419

commit v4 on v3

--- a/solution.py
+++ b/solution.py
@@ -13,6 +13,7 @@
 PLANE = (Y, X)
 EPSILON = 1e-05
 EDGE_BLOCK = 512
+UPDATE_BLOCK = 1024
 ROWS = 32
 VMEM_LIMIT = 32 * 1024 * 1024
 
@@ -115,9 +116,9 @@
     )
 
 
-def gather_kernel(
-    index_in, below_in, here_in, above_in, coarse_in, out_ref, index_ref, near_ref, coarse_ref, sems
-):
+def gather_kernel(n, index_in, below_in, here_in, above_in, coarse_in, *refs):
+    ready_in, out_ref, ready_out = refs[:n], refs[n], refs[n + 1 : 2 * n + 1]
+    index_ref, near_ref, coarse_ref, sems, ready_sems = refs[2 * n + 1 :]
     rows = here_in.shape[0]
     copies = started(
         [
@@ -129,6 +130,7 @@
         ],
         sems,
     )
+    ready_copies = started(list(zip(ready_in, ready_out)), ready_sems)
     finish(copies[:4])
     columns = index_ref[...].T
     lane = lax.broadcasted_iota(jnp.int32, (128, 128), 1)
@@ -149,42 +151,39 @@
             finish(copies[4:])
         total = total + dot(selection(start, 3 * rows, coarse_ref.shape[0]), coarse_ref[...])
         out_ref[start : start + EDGE_BLOCK, :] = total.astype(jnp.bfloat16)
-
-
-def gathered(index, below, here, above, coarse):
+    finish(ready_copies)
+
+
+def gathered(ready, index, below, here, above, coarse):
     slots = index.size
     rows, width = here.shape
     table = 3 * rows + coarse.shape[0]
+    n = len(ready)
     return kernel_call(
-        gather_kernel,
+        functools.partial(gather_kernel, n),
         "gather_senders",
-        shape((slots, width)),
-        (index, below, here, above, coarse),
-        [HBM] * 4 + [pl.BlockSpec(memory_space=pl.ANY)],
-        VMEM,
-        held([index, shape((3 * rows, width)), coarse]) + [pltpu.SemaphoreType.DMA((5,))],
+        [shape((slots, width)), *[shape(a.shape, a.dtype) for a in ready]],
+        (index, below, here, above, coarse, *ready),
+        [HBM] * 4 + [pl.BlockSpec(memory_space=pl.ANY)] + [HBM] * n,
+        [VMEM] * (1 + n),
+        held([index, shape((3 * rows, width)), coarse])
+        + [pltpu.SemaphoreType.DMA((5,)), pltpu.SemaphoreType.DMA((n,))],
         2 * slots * width * table,
     )
 
 
-def before_kernel(layer, n_in, scalar_ref, *refs):
-    ins, outs = refs[:n_in], refs[n_in : n_in + 6]
-    edge_held, node_held, hidden_weight_ref, out_held, vec_held, receiver_ref, sems = refs[
-        n_in + 6 :
-    ]
-    before_ref, edges_ref, incidence_ref, sent_weight_ref, out_weight_ref, vectors_ref = outs
+def prepare_kernel(layer, n_in, n_out, scalar_ref, *refs):
+    ins, outs, refs = refs[:n_in], refs[n_in : n_in + n_out], refs[n_in + n_out :]
+    held_out, refs = refs[:n_out], refs[n_out:]
+    edge_held, node_held, hidden_weight_ref, out_held, vec_held, receiver_ref = refs[:6]
+    in_sems, out_sems = refs[6:]
+    before_ref, weights_ref, incidence_ref, vectors_ref = held_out[:4]
     first = scalar_ref[0] == 0
     count = scalar_ref[1]
-    receiver, (wa, wb, ea, eb, vec_a, vec_b) = ins[0], ins[1:7]
-    edges_in, nodes_in = ins[7 : 7 + (n_in - 7) // 2], ins[7 + (n_in - 7) // 2 :]
+    receiver, (wa, wb, ea, eb, va, vb, oa, ob, vec_a, vec_b) = ins[0], ins[1:11]
+    edges_in, nodes_in = ins[11 : 11 + (n_in - 11) // 2], ins[11 + (n_in - 11) // 2 :]
     half = wa.shape[1]
     width = 2 * half
-
-    def top(ref):
-        return ref.at[pl.ds(0, half)]
-
-    def bottom(ref):
-        return ref.at[pl.ds(half, half)]
 
     def part(ref, start):
         return ref.at[layer, :, pl.ds(start, width)]
@@ -192,30 +191,39 @@
     def both(sources, target):
         if len(sources) == 1:
             return [(sources[0], target)]
-        return [(sources[0], top(target)), (sources[1], bottom(target))]
-
-    edge_target = edge_held if layer == 0 else edges_ref
+        halves = (target.at[pl.ds(0, half)], target.at[pl.ds(half, half)])
+        return list(zip(sources, halves))
+
     pairs = both(nodes_in, node_held) + [(receiver, receiver_ref)]
     pairs += [(vec_a.at[layer], vec_held.at[0]), (vec_b.at[layer], vec_held.at[1])]
     for k, target in ((2, hidden_weight_ref.at[1]), (0, hidden_weight_ref.at[0])):
         pairs += both((part(wa, k * width), part(wb, k * width)), target)
-    pairs += both(edges_in, edge_target)
-    split = len(pairs)
-    pairs += both((ea.at[layer], eb.at[layer]), out_held)
-    pairs += both((part(wa, width), part(wb, width)), sent_weight_ref)
-    copies = started(pairs, sems)
-    finish(copies[:split])
+    pairs += both(edges_in, edge_held)
+    pairs += both((ea.at[layer], eb.at[layer]), out_held.at[0])
+    pairs += both((oa.at[layer], ob.at[layer]), out_held.at[1])
+    pairs += both((part(wa, width), part(wb, width)), weights_ref.at[0])
+    for k in (0, 1):
+        pairs += both((part(va, k * width), part(vb, k * width)), weights_ref.at[2 + k])
+    finish(started(pairs, in_sems))
+    sent = [pltpu.make_async_copy(held_out[i], outs[i], out_sems.at[i]) for i in range(n_out)]
 
     vec = [vec_held[0].T, vec_held[1].T]
     hidden_vec = jnp.concatenate(vec, axis=0)
     feature_vec = in_order(first, *vec)
     nodes = node_held[...]
+    edges = edge_held[...]
     if layer == 0:
         nodes = in_order(first, nodes[:half], nodes[half:])
-        edges_ref[...] = in_order(first, edge_held[:half, :], edge_held[half:, :])
-    for i, column in enumerate((1, 2, 3)):
-        vectors_ref[i] = jnp.broadcast_to(feature_vec[:, column : column + 1], (width, 128))
-    vectors_ref[3] = jnp.concatenate([hidden_vec, feature_vec] + [hidden_vec] * 14, axis=1)
+        edges = in_order(first, edges[:half], edges[half:])
+        held_out[4][...] = edges
+        sent[4].start()
+        held_out[5][...] = nodes
+        sent[5].start()
+    weights_ref[1] = out_held[0].T
+    weights_ref[4] = out_held[1].T
+    sent[1].start()
+    vectors_ref[...] = jnp.concatenate([hidden_vec, feature_vec] + [hidden_vec] * 14, axis=1)
+    sent[3].start()
     slots = incidence_ref.shape[1]
     live = lax.broadcasted_iota(jnp.int32, (1, slots), 1) < count
     incidence_ref[...] = jnp.where(
@@ -223,87 +231,62 @@
         1.0,
         0.0,
     ).astype(jnp.bfloat16)
+    sent[2].start()
     receiver_part = dot(hidden_weight_ref[1], nodes).astype(jnp.bfloat16)
-    before = dot(hidden_weight_ref[0], edges_ref[...]) + dot(receiver_part, incidence_ref[...])
+    before = dot(hidden_weight_ref[0], edges) + dot(receiver_part, incidence_ref[...])
     before_ref[...] = before + hidden_vec[:, 0:1]
-    finish(copies[split:])
-    out_weight_ref[...] = out_held[...].T
-
-
-def before_sent(layer, scalars, edges, receiver, nodes, weights):
+    sent[0].start()
+    finish(sent)
+
+
+def prepared(layer, scalars, edges, receiver, nodes, weights):
     slots = edges[0].shape[1]
     node_rows = nodes[0].shape[1]
     width = weights[0].shape[1] * 2
-    inputs = (receiver, *weights[:4], *weights[8:], *edges, *nodes)
+    inputs = (receiver, *weights, *edges, *nodes)
     out_shape = [
         shape((width, slots), jnp.float32),
-        shape((width, slots)),
+        shape((5, width, width)),
         shape((node_rows, slots)),
-        shape((width, width)),
-        shape((width, width)),
-        shape((4, width, 128), jnp.float32),
+        shape((width, 128), jnp.float32),
     ]
-    edge_held = shape((width, slots) if layer == 0 else (16, 128))
-    return kernel_call(
-        functools.partial(before_kernel, layer, len(inputs)),
-        "before_sent",
+    if layer == 0:
+        out_shape += [shape((width, slots)), shape((width, node_rows))]
+    n_in, n_out = len(inputs), len(out_shape)
+    ready = kernel_call(
+        functools.partial(prepare_kernel, layer, n_in, n_out),
+        "prepare_layer",
         out_shape,
         (scalars, *inputs),
-        [SMEM] + [HBM] * len(inputs),
-        [VMEM] * len(out_shape),
+        [SMEM] + [HBM] * n_in,
+        [HBM] * n_out,
         held(
             [
-                edge_held,
+                *out_shape,
+                shape((width, slots)),
                 shape((width, node_rows)),
                 shape((2, width, width)),
-                shape((width, width)),
+                shape((2, width, width)),
                 shape((2, *weights[8].shape[1:]), jnp.float32),
                 receiver,
             ]
         )
-        + [pltpu.SemaphoreType.DMA((15,))],
+        + [pltpu.SemaphoreType.DMA((21,)), pltpu.SemaphoreType.DMA((n_out,))],
         2 * slots * width * (width + node_rows),
     )
-
-
-def update_kernel(layer, last_layer, n_nodes, n_out, scalar_ref, *refs):
-    (
-        sent_a_ref,
-        sent_b_ref,
-        before_ref,
-        edges_ref,
-        incidence_ref,
-        sent_weight_ref,
-        out_weight_ref,
-        vectors_ref,
-        va,
-        vb,
-        oa,
-        ob,
-    ) = refs[:12]
-    nodes_in, outs = refs[12 : 12 + n_nodes], refs[12 + n_nodes : 12 + n_nodes + n_out]
-    refs = refs[12 + n_nodes + n_out :]
-    held_out, (node_held, in_held, out_held, hidden_ref, mlp_ref) = refs[:n_out], refs[n_out:-2]
-    in_sems, out_sems = refs[-2:]
+    if layer == 0:
+        return ready
+    return (*ready, *edges, *nodes)
+
+
+def update_kernel(last_layer, n_out, scalar_ref, *refs):
+    sent_a_ref, sent_b_ref, before_ref, weights_ref, incidence_ref, small_ref = refs[:6]
+    edges_ref, nodes_ref, outs, refs = refs[6], refs[7], refs[8 : 8 + n_out], refs[8 + n_out :]
+    edge_out_ref, node_out_ref, hidden_ref, mlp_ref, vectors_ref, out_sems = refs
     half = sent_a_ref.shape[1]
     width = 2 * half
     first = scalar_ref[0] == 0
     count = scalar_ref[1]
-
-    def top(ref):
-        return ref.at[pl.ds(0, half)]
-
-    def bottom(ref):
-        return ref.at[pl.ds(half, half)]
-
-    pairs = [(va.at[layer], top(in_held)), (vb.at[layer], bottom(in_held))]
-    pairs += [(oa.at[layer], top(out_held)), (ob.at[layer], bottom(out_held))]
-    if n_nodes == 1:
-        pairs += [(nodes_in[0], node_held)]
-    else:
-        pairs += [(nodes_in[0], top(node_held)), (nodes_in[1], bottom(node_held))]
-    copies = started(pairs, in_sems)
-    edge_out_ref, node_out_ref = held_out[:2]
     sent_out = []
 
     def send(source, target):
@@ -311,37 +294,41 @@
         copy.start()
         sent_out.append(copy)
 
+    small = small_ref[...]
+    hidden_vec, feature_vec = small[:, 0:8], small[:, 8:16]
+    for i, column in enumerate((1, 2, 3)):
+        vectors_ref[i] = jnp.broadcast_to(feature_vec[:, column : column + 1], (width, 128))
+
+    def spread(index, rows):
+        return jnp.concatenate([vectors_ref[index, rows, :]] * (UPDATE_BLOCK // 128), axis=1)
+
     slots = edges_ref.shape[1]
     total = None
-    for start in range(0, slots, EDGE_BLOCK):
-        here = slice(start, start + EDGE_BLOCK)
+    for start in range(0, slots, UPDATE_BLOCK):
+        here = slice(start, start + UPDATE_BLOCK)
         sent_a, sent_b = sent_a_ref[here, :], sent_b_ref[here, :]
         low = jnp.where(first, sent_a, sent_b)
         high = jnp.where(first, sent_b, sent_a)
         sent = jnp.concatenate([low, high], axis=1)
-        mlp_ref[...] = dot(sent_weight_ref[...], sent, ((1,), (1,)))
+        mlp_ref[...] = dot(weights_ref[0], sent, ((1,), (1,)))
         for row in range(0, width, ROWS):
             rows = slice(row, row + ROWS)
             value = silu(mlp_ref[rows, :] + before_ref[rows, here])
             hidden_ref[rows, :] = value.astype(jnp.bfloat16)
-        mlp_ref[...] = dot(out_weight_ref[...], hidden_ref[...])
-
-        def spread(index, rows):
-            return jnp.concatenate([vectors_ref[index, rows, :]] * (EDGE_BLOCK // 128), axis=1)
-
-        new_ref = hidden_ref if last_layer else columns_of(edge_out_ref, start, EDGE_BLOCK)
-        sums = jnp.zeros((8, EDGE_BLOCK), jnp.float32)
-        squares = jnp.zeros((8, EDGE_BLOCK), jnp.float32)
+        mlp_ref[...] = dot(weights_ref[1], hidden_ref[...])
+        new_ref = hidden_ref if last_layer else columns_of(edge_out_ref, start, UPDATE_BLOCK)
+        sums = jnp.zeros((8, UPDATE_BLOCK), jnp.float32)
+        squares = jnp.zeros((8, UPDATE_BLOCK), jnp.float32)
         for row in range(0, width, ROWS):
             rows = slice(row, row + ROWS)
             value = mlp_ref[rows, :] + spread(0, rows)
             mlp_ref[rows, :] = value
-            sums = sums + jnp.sum(value.reshape(ROWS // 8, 8, EDGE_BLOCK), axis=0)
-            squares = squares + jnp.sum((value * value).reshape(ROWS // 8, 8, EDGE_BLOCK), axis=0)
+            sums = sums + jnp.sum(value.reshape(ROWS // 8, 8, UPDATE_BLOCK), axis=0)
+            squares = squares + jnp.sum((value * value).reshape(ROWS // 8, 8, UPDATE_BLOCK), axis=0)
         mean = jnp.sum(sums, axis=0, keepdims=True) * (1.0 / width)
         square = jnp.sum(squares, axis=0, keepdims=True) * (1.0 / width)
         scale = lax.rsqrt(square - mean * mean + EPSILON)
-        live = lax.broadcasted_iota(jnp.int32, (1, EDGE_BLOCK), 1) + start < count
+        live = lax.broadcasted_iota(jnp.int32, (1, UPDATE_BLOCK), 1) + start < count
         for row in range(0, width, ROWS):
             rows = slice(row, row + ROWS)
             value = (mlp_ref[rows, :] - mean) * scale * spread(1, rows) + spread(2, rows)
@@ -352,18 +339,14 @@
         total = part if total is None else total + part
         if last_layer:
             edge_out_ref[:, here] = jnp.where(first, updated[:half], updated[half:])
-        send(new_ref if not last_layer else columns_of(edge_out_ref, start, EDGE_BLOCK),
-             columns_of(outs[0], start, EDGE_BLOCK))
-    finish(copies)
-    small = vectors_ref[3]
-    hidden_vec, feature_vec = small[:, 0:8], small[:, 8:16]
-    nodes = node_held[...]
-    if n_nodes == 2:
-        nodes = in_order(first, nodes[:half], nodes[half:])
+        send(
+            columns_of(edge_out_ref, start, UPDATE_BLOCK), columns_of(outs[0], start, UPDATE_BLOCK)
+        )
+    nodes = nodes_ref[...]
     aggregate = total.astype(jnp.bfloat16)
-    node_before = dot(in_held[:, :width], nodes) + dot(in_held[:, width:], aggregate)
+    node_before = dot(weights_ref[2], nodes) + dot(weights_ref[3], aggregate)
     node_hidden = silu(node_before + hidden_vec[:, 4:5]).astype(jnp.bfloat16)
-    node_mlp = dot(out_held[...].T, node_hidden) + feature_vec[:, 5:6]
+    node_mlp = dot(weights_ref[4], node_hidden) + feature_vec[:, 5:6]
     new = nodes.astype(jnp.float32) + layer_norm(
         node_mlp, feature_vec[:, 6:7], feature_vec[:, 7:8]
     )
@@ -371,46 +354,42 @@
     mine = jnp.where(first, new[:half], new[half:])
     if last_layer:
         node_out_ref[...] = mine
+        send(node_out_ref, outs[1])
     else:
-        store_rows(mine, *held_out[2:])
-        for i in (2, 3):
-            send(held_out[i], outs[i])
         node_out_ref[...] = new
-    send(node_out_ref, outs[1])
+        send(node_out_ref, outs[1])
+        store_rows(mine, *outs[2:])
     finish(sent_out)
 
 
-def updated_graph(layer, last_layer, scalars, sent, ready, nodes, weights, copies):
+def updated_graph(last_layer, scalars, sent, ready, copies):
     slots = ready[0].shape[1]
-    node_rows = nodes[0].shape[1]
+    node_rows = ready[5].shape[1]
     half = sent[0].shape[1]
     width = 2 * half
     out_width = half if last_layer else width
     out_shape = [shape((out_width, slots)), shape((out_width, node_rows))]
+    out_specs = [HBM, HBM]
     if not last_layer:
         out_shape += [shape((node_rows, half)), shape((copies, node_rows // 8, half))]
+        out_specs = [HBM, HBM, VMEM, VMEM]
     n_out = len(out_shape)
     return kernel_call(
-        functools.partial(update_kernel, layer, last_layer, len(nodes), n_out),
+        functools.partial(update_kernel, last_layer, n_out),
         "update_graph",
         out_shape,
-        (scalars, *sent, *ready, *weights[4:8], *nodes),
-        [SMEM] + [VMEM] * (2 + len(ready)) + [HBM] * (4 + len(nodes)),
-        [HBM] * n_out,
-        held(out_shape)
-        + held(
+        (scalars, *sent, *ready),
+        [SMEM] + [VMEM] * (2 + len(ready)),
+        out_specs,
+        held(
             [
-                shape((width, node_rows)),
-                shape((width, 2 * width)),
-                shape((width, width)),
-                shape((width, EDGE_BLOCK)),
-                shape((width, EDGE_BLOCK), jnp.float32),
+                *out_shape[:2],
+                shape((width, UPDATE_BLOCK)),
+                shape((width, UPDATE_BLOCK), jnp.float32),
+                shape((3, width, 128), jnp.float32),
             ]
         )
-        + [
-            pltpu.SemaphoreType.DMA((6,)),
-            pltpu.SemaphoreType.DMA((n_out - 1 + slots // EDGE_BLOCK,)),
-        ],
+        + [pltpu.SemaphoreType.DMA((slots // UPDATE_BLOCK + 1,))],
         2 * slots * width * (2 * width + node_rows),
     )
 
@@ -504,12 +483,11 @@
     table, weights, edges, nodes = lax.optimization_barrier((table, weights, edges, nodes))
     for layer in range(layers):
         last_layer = layer == layers - 1
-        sent = gathered(index, *table)
+        ready = prepared(layer, scalars, edges, receiver, nodes, weights)
+        table, ready = lax.optimization_barrier((table, ready))
+        sent, *ready = gathered(ready, index, *table)
         sent = (sent, from_other(sent))
-        ready = before_sent(layer, scalars, edges, receiver, nodes, weights)
-        results = updated_graph(
-            layer, last_layer, scalars, sent, ready, nodes, weights, columns
-        )
+        results = updated_graph(last_layer, scalars, sent, ready, columns)
         if not last_layer:
             edges, nodes = results[:1], results[1:2]
             table = exchanged(results[2], results[3])

time: 113 us -> 111 us (0.982)
  waiting for transfers between devices: 24.7 us -> 20 us
  local copies, waits for them, and re-layouts: 2.33 us -> 4.77 us
  Pallas kernels: 28.3 us -> 30.7 us
    ppermute x2, waiting for transfers between devices: 14 us -> 6.92 us  [exchanged(): lax.ppermute(rows, PATCH, down)]
    ppermute x9, waiting for transfers between devices: 1.28 us -> 3.89 us  [from_other(): return lax.ppermute(a, 'width', [(0, 1), (1, 0)])]
    pallas_call x7, Pallas kernels: 28.3 us -> 30.7 us  [kernel_call(): pl.pallas_call(body, in_specs=in_specs, out_specs=out_specs, out_shape=ou...]
    unnamed x44 -> x50, local copies, waits for them, and re-layouts: 0.1 us -> 2.54 us
    all_to_all x2, starting transfers between devices: 11.6 us -> 10.4 us  [exchanged(): lax.all_to_all(plane, PLANE, split_axis=0, concat_axis=0, tiled=True)]
  transfers between devices with their start and end apart: 16 -> 16, of which waited for: 7 -> 9; matrix products, arithmetic and copies ran while one was open for 2% -> 2% of each run, Pallas kernels for 9% -> 7%
where the time goes in v4:
time: 111 us
  starting transfers between devices  41.1 us (37%)
  Pallas kernels  30.7 us (28%)
  waiting for transfers between devices  20 us (18%)
  blocking collectives  11.1 us (10%)
  local copies, waits for them, and re-layouts  4.77 us (4%)
  between operations  1.93 us (2%)
  other arithmetic  1.28 us (1%)
    pallas_call x7, Pallas kernels, kernel_call(): pl.pallas_call(body, in_specs=in_specs, out_specs=out_specs, out_shape=ou...  30.7 us
    ppermute x9, starting transfers between devices, from_other(): return lax.ppermute(a, 'width', [(0, 1), (1, 0)])  15.1 us
    all_to_all x1, blocking collectives, exchanged(): column = lax.all_to_all(copies, Z, split_axis=0, concat_axis=0, tiled=True)  11.1 us
    all_to_all x2, starting transfers between devices, exchanged(): lax.all_to_all(plane, PLANE, split_axis=0, concat_axis=0, tiled=True)  10.4 us
    ppermute x2, starting transfers between devices, exchanged(): lax.ppermute(rows, PATCH, down)  9.14 us
    ppermute x2, waiting for transfers between devices, exchanged(): lax.ppermute(rows, PATCH, down)  6.92 us
    all_to_all x1, waiting for transfers between devices, exchanged(): column = lax.all_to_all(copies, Z, split_axis=0, concat_axis=0, tiled=True)  6.71 us
    all_to_all x1, starting transfers between devices, exchanged(): column = lax.all_to_all(copies, Z, split_axis=0, concat_axis=0, tiled=True)  6.46 us
  transfers between devices with their start and end apart: 16, of which 9 were waited for; matrix products, arithmetic and copies ran while one was open for 2% of the time, Pallas kernels for 7%

profile of v4, /device:TPU:1, one launch (start us, length us, event | category | flops | bytes accessed | tf_op | source)
XLA Modules:
  0.0 111.0 jit_solution(17825456791004519737)
XLA Ops:
  0.6 0.0 copy-start.7
  0.7 0.0 copy-start.3
  0.8 3.3 %collective-permute-start.2 = (bf16[2,256,1536]{2,1,0:T(8,128)(2,1)}, bf16[2,256,1536]{2,1,0:T(8,128)(2,1)S(1)}, u32[]{:S(2)}, u32[]{:S(2)}) collective-permute-start(bf16[2,256,1536]{2,1,0:T(8,128)(2,1)} %refs_1_.1), channel_id=1, source_target_pairs={{0,1},{1,0},{2,3},{3,2},{4,5},{5,4},{6,7},{7,6},{8,9},{9,8},{10,11... | collective-permute-start | bytes 4718600 | tf_op jit(solution)/shard_map/ppermute | solution.py:398
  4.1 1.5 %node_rows.1 = (bf16[128,256]{1,0:T(8,128)(2,1)S(1)}, bf16[8,16,256]{2,1,0:T(8,128)(2,1)}) custom-call(bf16[256,128]{1,0:T(8,128)(2,1)} %refs_13_), custom_call_target="tpu_custom_call" | custom-call | bytes 4194304 | tf_op jit(solution)/shard_map/node_rows/pallas_call | solution.py:60
  5.6 6.5 %all-to-all-start = ((bf16[8,16,256]{2,1,0:T(8,128)(2,1)}), bf16[8,16,256]{2,1,0:T(8,128)(2,1)S(1)}, u32[]{:S(2)}, u32[]{:S(2)}) async-start(bf16[8,16,256]{2,1,0:T(8,128)(2,1)} %get-tuple-element.73), calls=%async_computation | async-start | bytes 131072 | tf_op jit(solution)/shard_map/all_to_all | solution.py:406
  12.1 0.4 collective-permute-start.4
  12.5 6.7 %all-to-all-done = bf16[8,16,256]{2,1,0:T(8,128)(2,1)S(1)} async-done(((bf16[8,16,256]{2,1,0:T(8,128)(2,1)}), bf16[8,16,256]{2,1,0:T(8,128)(2,1)S(1)}, u32[]{:S(2)}, u32[]{:S(2)}) %all-to-all-start) | async-done | bytes 65568 | tf_op jit(solution)/shard_map/all_to_all | solution.py:406
  19.3 1.1 broadcast_in_dim.9
  20.3 6.8 %all-to-all-start.1 = ((bf16[16,128,256]{2,1,0:T(8,128)(2,1)}), bf16[16,128,256]{2,1,0:T(8,128)(2,1)S(1)}, u32[]{:S(2)}, u32[]{:S(2)}) async-start(bf16[16,128,256]{2,1,0:T(8,128)(2,1)} %broadcast_in_dim.9), calls=%async_computation.1 | async-start | bytes 2097152 | tf_op jit(solution)/shard_map/all_to_all | solution.py:409
  27.3 2.0 %collective-permute-start.6 = (f32[2,8,256]{2,1,0:T(8,128)S(1)}, f32[2,8,256]{2,1,0:T(8,128)S(1)}, u32[]{:S(2)}, u32[]{:S(2)}) collective-permute-start(f32[2,8,256]{2,1,0:T(8,128)S(1)} %stack.43.refs_9_), channel_id=1, source_target_pairs={{0,1},{1,0},{2,3},{3,2},{4,5},{5,4},{6,7},{7,6},{8,9},{9,8},{10,11... | collective-permute-start | bytes 49160 | tf_op jit(solution)/shard_map/ppermute | solution.py:398
  29.4 0.1 collective-permute-start.8
  29.5 4.6 %collective-permute-start.1 = (bf16[128,256]{1,0:T(8,128)(2,1)S(1)}, bf16[128,256]{1,0:T(8,128)(2,1)S(1)}, u32[]{:S(2)}, u32[]{:S(2)}) collective-permute-start(bf16[128,256]{1,0:T(8,128)(2,1)S(1)} %get-tuple-element.99.here_in), channel_id=1, source_target_pairs={{2,0},{4,2},{6,4},{8,6},{10,8},{12,10},{14,12},{16,14},{18,16},{20... | collective-permute-start | bytes 196616 | tf_op jit(solution)/shard_map/ppermute | solution.py:405
  34.1 0.0 collective-permute-done.6.refs_10_
  34.1 0.0 collective-permute-start
  34.8 0.0 collective-permute-done.8.refs_14_
  34.8 0.8 collective-permute-start.7
  35.6 4.6 %collective-permute-done.1.above_in = bf16[128,256]{1,0:T(8,128)(2,1)S(1)} collective-permute-done((bf16[128,256]{1,0:T(8,128)(2,1)S(1)}, bf16[128,256]{1,0:T(8,128)(2,1)S(1)}, u32[]{:S(2)}, u32[]{:S(2)}) %collective-permute-start.1) | collective-permute-done | bytes 65568 | tf_op jit(solution)/shard_map/ppermute | solution.py:405
  40.2 2.8 %collective-permute-start.3 = (bf16[2,256,512]{2,1,0:T(8,128)(2,1)S(1)}, bf16[2,256,512]{2,1,0:T(8,128)(2,1)S(1)}, u32[]{:S(2)}, u32[]{:S(2)}) collective-permute-start(bf16[2,256,512]{2,1,0:T(8,128)(2,1)S(1)} %copy-done.3), channel_id=1, source_target_pairs={{0,1},{1,0},{2,3},{3,2},{4,5},{5,4},{6,7},{7,6},{8,9},{9,8},{10,11... | collective-permute-start | bytes 1572872 | tf_op jit(solution)/shard_map/ppermute | solution.py:398
  43.0 0.1 collective-permute-done.below_in
  43.1 1.4 %collective-permute-start.5 = (bf16[2,256,512]{2,1,0:T(8,128)(2,1)}, bf16[2,256,512]{2,1,0:T(8,128)(2,1)S(1)}, u32[]{:S(2)}, u32[]{:S(2)}) collective-permute-start(bf16[2,256,512]{2,1,0:T(8,128)(2,1)} %refs_7_.1), channel_id=1, source_target_pairs={{0,1},{1,0},{2,3},{3,2},{4,5},{5,4},{6,7},{7,6},{8,9},{9,8},{10,11... | collective-permute-start | bytes 1572872 | tf_op jit(solution)/shard_map/ppermute | solution.py:398
  44.5 0.1 pad_add_fusion.scalar_ref
  44.6 0.6 broadcast_subtract_fusion
  45.2 0.6 fusion.9.index_in
  45.8 0.0 collective-permute-done.7.refs_12_
  45.8 0.0 copy-start.4
  45.8 0.4 collective-permute-done.5.refs_8_
  46.2 0.3 copy-done.6
  46.6 0.2 copy-done.4
  46.7 0.8 copy-done.5
  47.6 0.0 collective-permute-done.4.refs_6_
  47.6 1.1 %copy-done.2 = bf16[2,256,1536]{2,1,0:T(8,128)(2,1)} copy-done((bf16[2,256,1536]{2,1,0:T(8,128)(2,1)}, bf16[2,256,1536]{2,1,0:T(8,128)(2,1)S(1)}, u32[]{:S(2)}) %copy-start.2) | copy-done | bytes 1572888
  48.7 7.0 %prepare_layer.2 = (f32[512,1024]{1,0:T(8,128)}, bf16[5,512,512]{2,1,0:T(8,128)(2,1)}, bf16[128,1024]{1,0:T(8,128)(2,1)}, f32[512,128]{1,0:T(8,128)}, bf16[512,1...) custom-call(s32[2]{0:T(128)S(1)} %pad_add_fusion.scalar_ref, s32[1,1024]{1,0:T(1,128)} %bitcast.12, ...), custom_call_target="tpu_custom_call" | custom-call | flops 671088640 | bytes 4194304 | tf_op jit(solution)/shard_map/prepare_layer/pallas_call | solution.py:60
  55.8 3.0 %gather_senders.2 = (bf16[1024,256]{1,0:T(8,128)(2,1)S(1)}, f32[512,1024]{1,0:T(8,128)S(1)}, bf16[5,512,512]{2,1,0:T(8,128)(2,1)S(1)}, bf16[128,1024]{1,0:T(8,12...) custom-call(s32[8,128]{1,0:T(8,128)} %fusion.9.index_in, ...), custom_call_target="tpu_custom_call" | custom-call | flops 1275068416 | bytes 4194304 | tf_op jit(solution)/shard_map/gather_senders/pallas_call | solution.py:60
  58.8 0.3 collective-permute-start.9
  59.1 1.9 %collective-permute-done.9.refs_1_ = bf16[1024,256]{1,0:T(8,128)(2,1)S(1)} collective-permute-done((bf16[1024,256]{1,0:T(8,128)(2,1)S(1)}, bf16[1024,256]{1,0:T(8,128)(2,1)S(1)}, u32[]{:S(2)}, u32[]{:S(2)}) %collective-permute-start.9) | collective-permute-done | bytes 524320 | tf_op jit(solution)/shard_map/ppermute | solution.py:398
  61.0 5.3 %update_graph.2 = (bf16[512,1024]{1,0:T(8,128)(2,1)}, bf16[512,128]{1,0:T(8,128)(2,1)}, bf16[128,256]{1,0:T(8,128)(2,1)S(1)}, bf16[8,16,256]{2,1,0:T(8,128)(2,1)S(1)}) custom-call(s32[2]{0:T(128)S(1)} %pad_add_fusion.scalar_ref, bf16[1024,256]{1,0:T(8,128)(2,1)S(1)} %get-tuple-element.108.refs_0_, bf16[1024,256]{1,0:T(8,128)(2,1)S(1)} %collective-permute-done.9.refs_1_, ...), custom_call_target="tpu_custom_call" | custom-call | flops 1207959552 | bytes 4194304 | tf_op jit(solution)/shard_map/update_graph/pallas_call | solution.py:60
  66.3 11.1 %all_to_all.20 = bf16[8,16,256]{2,1,0:T(8,128)(2,1)S(1)} all-to-all(bf16[8,16,256]{2,1,0:T(8,128)(2,1)S(1)} %get-tuple-element.116), channel_id=1, replica_groups=mesh['patch_0'=8,'patch_1'=4,'patch_2'=4,'width'=2] {'patch_0'}, dimensions={0} | all-to-all | bytes 131072 | tf_op jit(solution)/shard_map/all_to_all | solution.py:406
  77.5 1.1 broadcast_in_dim.11
  78.5 3.7 %all-to-all-start.3 = ((bf16[16,128,256]{2,1,0:T(8,128)(2,1)}), bf16[16,128,256]{2,1,0:T(8,128)(2,1)S(1)}, u32[]{:S(2)}, u32[]{:S(2)}) async-start(bf16[16,128,256]{2,1,0:T(8,128)(2,1)} %broadcast_in_dim.11), calls=%async_computation.3 | async-start | bytes 2097152 | tf_op jit(solution)/shard_map/all_to_all | solution.py:409
  82.2 4.5 %collective-permute-start.11 = (bf16[128,256]{1,0:T(8,128)(2,1)S(1)}, bf16[128,256]{1,0:T(8,128)(2,1)S(1)}, u32[]{:S(2)}, u32[]{:S(2)}) collective-permute-start(bf16[128,256]{1,0:T(8,128)(2,1)S(1)} %get-tuple-element.124.here_in), channel_id=1, source_target_pairs={{2,0},{4,2},{6,4},{8,6},{10,8},{12,10},{14,12},{16,14},{18,16},{20... | collective-permute-start | bytes 196616 | tf_op jit(solution)/shard_map/ppermute | solution.py:405
  86.8 6.3 %prepare_layer.3 = (f32[512,1024]{1,0:T(8,128)}, bf16[5,512,512]{2,1,0:T(8,128)(2,1)}, bf16[128,1024]{1,0:T(8,128)(2,1)}, f32[512,128]{1,0:T(8,128)}) custom-call(s32[2]{0:T(128)S(1)} %pad_add_fusion.scalar_ref, s32[1,1024]{1,0:T(1,128)} %bitcast.13, bf16[2,256,1536]{2,1,0:T(8,128)(2,1)} %refs_1_.1, bf16[2,256,1536]{2,1,0:T(8,128)(2,1)} %copy-done.2, ...), custom_call_target="tpu_custom_call" | custom-call | flops 671088640 | bytes 4194304 | tf_op jit(solution)/shard_map/prepare_layer/pallas_call | solution.py:60
  93.0 2.3 %collective-permute-done.11.above_in = bf16[128,256]{1,0:T(8,128)(2,1)S(1)} collective-permute-done((bf16[128,256]{1,0:T(8,128)(2,1)S(1)}, bf16[128,256]{1,0:T(8,128)(2,1)S(1)}, u32[]{:S(2)}, u32[]{:S(2)}) %collective-permute-start.11) | collective-permute-done | bytes 65568 | tf_op jit(solution)/shard_map/ppermute | solution.py:405
  95.4 0.6 collective-permute-done.10.below_in
  95.9 1.9 %all-to-all-done.3 = bf16[16,128,256]{2,1,0:T(8,128)(2,1)S(1)} async-done(((bf16[16,128,256]{2,1,0:T(8,128)(2,1)}), bf16[16,128,256]{2,1,0:T(8,128)(2,1)S(1)}, u32[]{:S(2)}, u32[]{:S(2)}) %all-to-all-start.3) | async-done | bytes 1048608 | tf_op jit(solution)/shard_map/all_to_all | solution.py:409
  97.8 3.0 %gather_senders.3 = (bf16[1024,256]{1,0:T(8,128)(2,1)S(1)}, f32[512,1024]{1,0:T(8,128)S(1)}, bf16[5,512,512]{2,1,0:T(8,128)(2,1)S(1)}, bf16[128,1024]{1,0:T(8,12...) custom-call(s32[8,128]{1,0:T(8,128)} %fusion.9.index_in, ...), custom_call_target="tpu_custom_call" | custom-call | flops 1275068416 | bytes 4194304 | tf_op jit(solution)/shard_map/gather_senders/pallas_call | solution.py:60
  100.8 3.9 %collective-permute-start.12 = (bf16[1024,256]{1,0:T(8,128)(2,1)S(1)}, bf16[1024,256]{1,0:T(8,128)(2,1)S(1)}, u32[]{:S(2)}, u32[]{:S(2)}) collective-permute-start(bf16[1024,256]{1,0:T(8,128)(2,1)S(1)} %get-tuple-element.133.refs_0_), channel_id=1, source_target_pairs={{0,1},{1,0},{2,3},{3,2},{4,5},{5,4},{6,7},{7,6},{8,9},{9,8},{10,11... | collective-permute-start | bytes 1572872 | tf_op jit(solution)/shard_map/ppermute | solution.py:398
  104.7 1.5 %collective-permute-done.12.refs_1_ = bf16[1024,256]{1,0:T(8,128)(2,1)S(1)} collective-permute-done((bf16[1024,256]{1,0:T(8,128)(2,1)S(1)}, bf16[1024,256]{1,0:T(8,128)(2,1)S(1)}, u32[]{:S(2)}, u32[]{:S(2)}) %collective-permute-start.12) | collective-permute-done | bytes 524320 | tf_op jit(solution)/shard_map/ppermute | solution.py:398
  106.3 4.6 %update_graph.3 = (bf16[256,1024]{1,0:T(8,128)(2,1)}, bf16[256,128]{1,0:T(8,128)(2,1)}) custom-call(s32[2]{0:T(128)S(1)} %pad_add_fusion.scalar_ref, bf16[1024,256]{1,0:T(8,128)(2,1)S(1)} %get-tuple-element.133.refs_0_, bf16[1024,256]{1,0:T(8,128)(2,1)S(1)} %collective-permute-done.12.refs_1_, f32[512,1024]{1,0:T(8,128)S(1)} %get-tuple-element.134.refs_2_, ...), custom_call_target="tpu_custom_call" | custom-call | flops 1207959552 | bytes 4194304 | tf_op jit(solution)/shard_map/update_graph/pallas_call | solution.py:60
  (56 shorter events, 0.2 us)
Async XLA Ops:
  0.6 28.7 %copy-start.7 = (bf16[256,128]{1,0:T(8,128)(2,1)S(1)}, bf16[256,128]{1,0:T(8,128)(2,1)}, u32[]{:S(2)}) copy-start(bf16[256,128]{1,0:T(8,128)(2,1)} %refs_13_) | copy-start | bytes 196612
  0.6 26.5 %copy-start.17 = (f32[2,256]{1,0:T(2,128)S(1)}, f32[2,256]{1,0:T(2,128)}, u32[]{:S(2)}) copy-start(f32[2,256]{1,0:T(2,128)} %param.23) | copy-start | bytes 6148
  0.7 26.5 %copy-start.18 = (f32[2,256]{1,0:T(2,128)S(1)}, f32[2,256]{1,0:T(2,128)}, u32[]{:S(2)}) copy-start(f32[2,256]{1,0:T(2,128)} %param.25) | copy-start | bytes 6148
  0.7 26.5 %copy-start.19 = (f32[2,256]{1,0:T(2,128)S(1)}, f32[2,256]{1,0:T(2,128)}, u32[]{:S(2)}) copy-start(f32[2,256]{1,0:T(2,128)} %param.26) | copy-start | bytes 6148
  0.7 26.5 %copy-start.20 = (f32[2,256]{1,0:T(2,128)S(1)}, f32[2,256]{1,0:T(2,128)}, u32[]{:S(2)}) copy-start(f32[2,256]{1,0:T(2,128)} %param.27) | copy-start | bytes 6148
  0.7 26.5 %copy-start.21 = (f32[2,256]{1,0:T(2,128)S(1)}, f32[2,256]{1,0:T(2,128)}, u32[]{:S(2)}) copy-start(f32[2,256]{1,0:T(2,128)} %param.29) | copy-start | bytes 6148
  0.7 26.5 %copy-start.22 = (f32[2,256]{1,0:T(2,128)S(1)}, f32[2,256]{1,0:T(2,128)}, u32[]{:S(2)}) copy-start(f32[2,256]{1,0:T(2,128)} %param.31) | copy-start | bytes 6148
  0.7 26.5 %copy-start.23 = (f32[2,256]{1,0:T(2,128)S(1)}, f32[2,256]{1,0:T(2,128)}, u32[]{:S(2)}) copy-start(f32[2,256]{1,0:T(2,128)} %param.32) | copy-start | bytes 6148
  0.7 26.5 %copy-start.24 = (f32[2,256]{1,0:T(2,128)S(1)}, f32[2,256]{1,0:T(2,128)}, u32[]{:S(2)}) copy-start(f32[2,256]{1,0:T(2,128)} %param.33) | copy-start | bytes 6148
  0.7 39.5 %copy-start.3 = (bf16[2,256,512]{2,1,0:T(8,128)(2,1)S(1)}, bf16[2,256,512]{2,1,0:T(8,128)(2,1)}, u32[]{:S(2)}) copy-start(bf16[2,256,512]{2,1,0:T(8,128)(2,1)} %refs_3_.1) | copy-start | bytes 1572868
  0.7 43.8 %copy-start.15 = (s32[1024]{0:T(1024)S(1)}, s32[1024]{0:T(1024)}, u32[]{:S(2)}) copy-start(s32[1024]{0:T(1024)} %param.20) | copy-start | bytes 12292
  0.7 44.4 %copy-start.16 = (s32[1024]{0:T(1024)S(1)}, s32[1024]{0:T(1024)}, u32[]{:S(2)}) copy-start(s32[1024]{0:T(1024)} %param.19) | copy-start | bytes 12292
  0.8 46.8 %collective-permute-start.2 = (bf16[2,256,1536]{2,1,0:T(8,128)(2,1)}, bf16[2,256,1536]{2,1,0:T(8,128)(2,1)S(1)}, u32[]{:S(2)}, u32[]{:S(2)}) collective-permute-start(bf16[2,256,1536]{2,1,0:T(8,128)(2,1)} %refs_1_.1), channel_id=1, source_target_pairs={{0,1},{1,0},{2,3},{3,2},{4,5},{5,4},{6,7},{7,6},{8,9},{9,8},{10,11... | collective-permute-start | bytes 4718600 | tf_op jit(solution)/shard_map/ppermute | solution.py:398
  5.6 50.1 %copy-start = (bf16[128,256]{1,0:T(8,128)(2,1)}, bf16[128,256]{1,0:T(8,128)(2,1)S(1)}, u32[]{:S(2)}) copy-start(bf16[128,256]{1,0:T(8,128)(2,1)S(1)} %get-tuple-element.99.here_in) | copy-start | bytes 196612
  5.6 13.6 %all-to-all-start = ((bf16[8,16,256]{2,1,0:T(8,128)(2,1)}), bf16[8,16,256]{2,1,0:T(8,128)(2,1)S(1)}, u32[]{:S(2)}, u32[]{:S(2)}) async-start(bf16[8,16,256]{2,1,0:T(8,128)(2,1)} %get-tuple-element.73), calls=%async_computation | async-start | bytes 131072 | tf_op jit(solution)/shard_map/all_to_all | solution.py:406
  12.1 35.5 %collective-permute-start.4 = (bf16[2,256,1024]{2,1,0:T(8,128)(2,1)}, bf16[2,256,1024]{2,1,0:T(8,128)(2,1)}, u32[]{:S(2)}, u32[]{:S(2)}) collective-permute-start(bf16[2,256,1024]{2,1,0:T(8,128)(2,1)} %refs_5_.1), channel_id=1, source_target_pairs={{0,1},{1,0},{2,3},{3,2},{4,5},{5,4},{6,7},{7,6},{8,9},{9,8},{10,11... | collective-permute-start | bytes 3145736 | tf_op jit(solution)/shard_map/ppermute | solution.py:398
  20.3 27.2 %all-to-all-start.1 = ((bf16[16,128,256]{2,1,0:T(8,128)(2,1)}), bf16[16,128,256]{2,1,0:T(8,128)(2,1)S(1)}, u32[]{:S(2)}, u32[]{:S(2)}) async-start(bf16[16,128,256]{2,1,0:T(8,128)(2,1)} %broadcast_in_dim.9), calls=%async_computation.1 | async-start | bytes 2097152 | tf_op jit(solution)/shard_map/all_to_all | solution.py:409
  27.3 20.3 %copy-start.8 = (f32[2,8,256]{2,1,0:T(8,128)}, f32[2,8,256]{2,1,0:T(8,128)S(1)}, u32[]{:S(2)}) copy-start(f32[2,8,256]{2,1,0:T(8,128)S(1)} %stack.43.refs_9_) | copy-start | bytes 49156
  27.3 6.8 %collective-permute-start.6 = (f32[2,8,256]{2,1,0:T(8,128)S(1)}, f32[2,8,256]{2,1,0:T(8,128)S(1)}, u32[]{:S(2)}, u32[]{:S(2)}) collective-permute-start(f32[2,8,256]{2,1,0:T(8,128)S(1)} %stack.43.refs_9_), channel_id=1, source_target_pairs={{0,1},{1,0},{2,3},{3,2},{4,5},{5,4},{6,7},{7,6},{8,9},{9,8},{10,11... | collective-permute-start | bytes 49160 | tf_op jit(solution)/shard_map/ppermute | solution.py:398
  29.4 5.4 %collective-permute-start.8 = (bf16[256,128]{1,0:T(8,128)(2,1)S(1)}, bf16[256,128]{1,0:T(8,128)(2,1)S(1)}, u32[]{:S(2)}, u32[]{:S(2)}) collective-permute-start(bf16[256,128]{1,0:T(8,128)(2,1)S(1)} %copy-done.7), channel_id=1, source_target_pairs={{0,1},{1,0},{2,3},{3,2},{4,5},{5,4},{6,7},{7,6},{8,9},{9,8},{10,11... | collective-permute-start | bytes 196616 | tf_op jit(solution)/shard_map/ppermute | solution.py:398
  29.5 10.7 %collective-permute-start.1 = (bf16[128,256]{1,0:T(8,128)(2,1)S(1)}, bf16[128,256]{1,0:T(8,128)(2,1)S(1)}, u32[]{:S(2)}, u32[]{:S(2)}) collective-permute-start(bf16[128,256]{1,0:T(8,128)(2,1)S(1)} %get-tuple-element.99.here_in), channel_id=1, source_target_pairs={{2,0},{4,2},{6,4},{8,6},{10,8},{12,10},{14,12},{16,14},{18,16},{20... | collective-permute-start | bytes 196616 | tf_op jit(solution)/shard_map/ppermute | solution.py:405
  34.1 13.5 %copy-start.14 = (f32[2,8,256]{2,1,0:T(8,128)}, f32[2,8,256]{2,1,0:T(8,128)S(1)}, u32[]{:S(2)}) copy-start(f32[2,8,256]{2,1,0:T(8,128)S(1)} %collective-permute-done.6.refs_10_) | copy-start | bytes 49156
  34.1 9.0 %collective-permute-start = (bf16[128,256]{1,0:T(8,128)(2,1)S(1)}, bf16[128,256]{1,0:T(8,128)(2,1)S(1)}, u32[]{:S(2)}, u32[]{:S(2)}) collective-permute-start(bf16[128,256]{1,0:T(8,128)(2,1)S(1)} %get-tuple-element.99.here_in), channel_id=1, source_target_pairs={{0,2},{2,4},{4,6},{6,8},{8,10},{10,12},{12,14},{14,16},{16,18},{18... | collective-permute-start | bytes 196616 | tf_op jit(solution)/shard_map/ppermute | solution.py:405
  34.8 12.8 %copy-start.11 = (bf16[256,128]{1,0:T(8,128)(2,1)}, bf16[256,128]{1,0:T(8,128)(2,1)S(1)}, u32[]{:S(2)}) copy-start(bf16[256,128]{1,0:T(8,128)(2,1)S(1)} %collective-permute-done.8.refs_14_) | copy-start | bytes 196612
  34.8 11.0 %collective-permute-start.7 = (bf16[256,1024]{1,0:T(8,128)(2,1)}, bf16[256,1024]{1,0:T(8,128)(2,1)S(1)}, u32[]{:S(2)}, u32[]{:S(2)}) collective-permute-start(bf16[256,1024]{1,0:T(8,128)(2,1)} %refs_11_), channel_id=1, source_target_pairs={{0,1},{1,0},{2,3},{3,2},{4,5},{5,4},{6,7},{7,6},{8,9},{9,8},{10,11... | collective-permute-start | bytes 1572872 | tf_op jit(solution)/shard_map/ppermute | solution.py:398
  40.2 15.6 %copy-start.9 = (bf16[128,256]{1,0:T(8,128)(2,1)}, bf16[128,256]{1,0:T(8,128)(2,1)S(1)}, u32[]{:S(2)}) copy-start(bf16[128,256]{1,0:T(8,128)(2,1)S(1)} %collective-permute-done.1.above_in) | copy-start | bytes 196612
  40.2 5.6 %collective-permute-start.3 = (bf16[2,256,512]{2,1,0:T(8,128)(2,1)S(1)}, bf16[2,256,512]{2,1,0:T(8,128)(2,1)S(1)}, u32[]{:S(2)}, u32[]{:S(2)}) collective-permute-start(bf16[2,256,512]{2,1,0:T(8,128)(2,1)S(1)} %copy-done.3), channel_id=1, source_target_pairs={{0,1},{1,0},{2,3},{3,2},{4,5},{5,4},{6,7},{7,6},{8,9},{9,8},{10,11... | collective-permute-start | bytes 1572872 | tf_op jit(solution)/shard_map/ppermute | solution.py:398
  43.1 12.7 %copy-start.10 = (bf16[128,256]{1,0:T(8,128)(2,1)}, bf16[128,256]{1,0:T(8,128)(2,1)S(1)}, u32[]{:S(2)}) copy-start(bf16[128,256]{1,0:T(8,128)(2,1)S(1)} %collective-permute-done.below_in) | copy-start | bytes 196612
  43.1 3.1 %collective-permute-start.5 = (bf16[2,256,512]{2,1,0:T(8,128)(2,1)}, bf16[2,256,512]{2,1,0:T(8,128)(2,1)S(1)}, u32[]{:S(2)}, u32[]{:S(2)}) collective-permute-start(bf16[2,256,512]{2,1,0:T(8,128)(2,1)} %refs_7_.1), channel_id=1, source_target_pairs={{0,1},{1,0},{2,3},{3,2},{4,5},{5,4},{6,7},{7,6},{8,9},{9,8},{10,11... | collective-permute-start | bytes 1572872 | tf_op jit(solution)/shard_map/ppermute | solution.py:398
  45.8 0.8 copy-start.6
  45.8 1.0 copy-start.4
  46.7 0.8 copy-start.5
  47.6 1.2 %copy-start.2 = (bf16[2,256,1536]{2,1,0:T(8,128)(2,1)}, bf16[2,256,1536]{2,1,0:T(8,128)(2,1)S(1)}, u32[]{:S(2)}) copy-start(bf16[2,256,1536]{2,1,0:T(8,128)(2,1)S(1)} %collective-permute-done.2.refs_2_) | copy-start | bytes 4718596
  58.8 2.2 %collective-permute-start.9 = (bf16[1024,256]{1,0:T(8,128)(2,1)S(1)}, bf16[1024,256]{1,0:T(8,128)(2,1)S(1)}, u32[]{:S(2)}, u32[]{:S(2)}) collective-permute-start(bf16[1024,256]{1,0:T(8,128)(2,1)S(1)} %get-tuple-element.108.refs_0_), channel_id=1, source_target_pairs={{0,1},{1,0},{2,3},{3,2},{4,5},{5,4},{6,7},{7,6},{8,9},{9,8},{10,11... | collective-permute-start | bytes 1572872 | tf_op jit(solution)/shard_map/ppermute | solution.py:398
  66.3 26.7 %copy-start.1 = (bf16[128,256]{1,0:T(8,128)(2,1)}, bf16[128,256]{1,0:T(8,128)(2,1)S(1)}, u32[]{:S(2)}) copy-start(bf16[128,256]{1,0:T(8,128)(2,1)S(1)} %get-tuple-element.124.here_in) | copy-start | bytes 196612
  78.5 19.3 %all-to-all-start.3 = ((bf16[16,128,256]{2,1,0:T(8,128)(2,1)}), bf16[16,128,256]{2,1,0:T(8,128)(2,1)S(1)}, u32[]{:S(2)}, u32[]{:S(2)}) async-start(bf16[16,128,256]{2,1,0:T(8,128)(2,1)} %broadcast_in_dim.11), calls=%async_computation.3 | async-start | bytes 2097152 | tf_op jit(solution)/shard_map/all_to_all | solution.py:409
  82.2 13.1 %collective-permute-start.11 = (bf16[128,256]{1,0:T(8,128)(2,1)S(1)}, bf16[128,256]{1,0:T(8,128)(2,1)S(1)}, u32[]{:S(2)}, u32[]{:S(2)}) collective-permute-start(bf16[128,256]{1,0:T(8,128)(2,1)S(1)} %get-tuple-element.124.here_in), channel_id=1, source_target_pairs={{2,0},{4,2},{6,4},{8,6},{10,8},{12,10},{14,12},{16,14},{18,16},{20... | collective-permute-start | bytes 196616 | tf_op jit(solution)/shard_map/ppermute | solution.py:405
  86.8 9.2 %collective-permute-start.10 = (bf16[128,256]{1,0:T(8,128)(2,1)S(1)}, bf16[128,256]{1,0:T(8,128)(2,1)S(1)}, u32[]{:S(2)}, u32[]{:S(2)}) collective-permute-start(bf16[128,256]{1,0:T(8,128)(2,1)S(1)} %get-tuple-element.124.here_in), channel_id=1, source_target_pairs={{0,2},{2,4},{4,6},{6,8},{8,10},{10,12},{12,14},{14,16},{16,18},{18... | collective-permute-start | bytes 196616 | tf_op jit(solution)/shard_map/ppermute | solution.py:405
  95.4 2.5 %copy-start.12 = (bf16[128,256]{1,0:T(8,128)(2,1)}, bf16[128,256]{1,0:T(8,128)(2,1)S(1)}, u32[]{:S(2)}) copy-start(bf16[128,256]{1,0:T(8,128)(2,1)S(1)} %collective-permute-done.11.above_in) | copy-start | bytes 196612
  95.9 1.9 %copy-start.13 = (bf16[128,256]{1,0:T(8,128)(2,1)}, bf16[128,256]{1,0:T(8,128)(2,1)S(1)}, u32[]{:S(2)}) copy-start(bf16[128,256]{1,0:T(8,128)(2,1)S(1)} %collective-permute-done.10.below_in) | copy-start | bytes 196612
  100.8 5.4 %collective-permute-start.12 = (bf16[1024,256]{1,0:T(8,128)(2,1)S(1)}, bf16[1024,256]{1,0:T(8,128)(2,1)S(1)}, u32[]{:S(2)}, u32[]{:S(2)}) collective-permute-start(bf16[1024,256]{1,0:T(8,128)(2,1)S(1)} %get-tuple-element.133.refs_0_), channel_id=1, source_target_pairs={{0,1},{1,0},{2,3},{3,2},{4,5},{5,4},{6,7},{7,6},{8,9},{9,8},{10,11... | collective-permute-start | bytes 1572872 | tf_op jit(solution)/shard_map/ppermute | solution.py:398

commit v5 on v4

--- a/solution.py
+++ b/solution.py
@@ -116,9 +116,9 @@
     )
 
 
-def gather_kernel(n, index_in, below_in, here_in, above_in, coarse_in, *refs):
+def gather_kernel(n, index_in, below_in, here_in, above_in, coarse_ref, *refs):
     ready_in, out_ref, ready_out = refs[:n], refs[n], refs[n + 1 : 2 * n + 1]
-    index_ref, near_ref, coarse_ref, sems, ready_sems = refs[2 * n + 1 :]
+    index_ref, near_ref, sems, ready_sems = refs[2 * n + 1 :]
     rows = here_in.shape[0]
     copies = started(
         [
@@ -126,12 +126,11 @@
             (below_in, near_ref.at[pl.ds(0, rows)]),
             (here_in, near_ref.at[pl.ds(rows, rows)]),
             (above_in, near_ref.at[pl.ds(2 * rows, rows)]),
-            (coarse_in, coarse_ref),
         ],
         sems,
     )
     ready_copies = started(list(zip(ready_in, ready_out)), ready_sems)
-    finish(copies[:4])
+    finish(copies[:1])
     columns = index_ref[...].T
     lane = lax.broadcasted_iota(jnp.int32, (128, 128), 1)
 
@@ -146,10 +145,10 @@
         return jnp.concatenate(blocks, axis=0)
 
     for start in range(0, out_ref.shape[0], EDGE_BLOCK):
-        total = dot(selection(start, 0, 3 * rows), near_ref[...])
+        total = dot(selection(start, 3 * rows, coarse_ref.shape[0]), coarse_ref[...])
         if start == 0:
-            finish(copies[4:])
-        total = total + dot(selection(start, 3 * rows, coarse_ref.shape[0]), coarse_ref[...])
+            finish(copies[1:])
+        total = total + dot(selection(start, 0, 3 * rows), near_ref[...])
         out_ref[start : start + EDGE_BLOCK, :] = total.astype(jnp.bfloat16)
     finish(ready_copies)
 
@@ -164,10 +163,10 @@
         "gather_senders",
         [shape((slots, width)), *[shape(a.shape, a.dtype) for a in ready]],
         (index, below, here, above, coarse, *ready),
-        [HBM] * 4 + [pl.BlockSpec(memory_space=pl.ANY)] + [HBM] * n,
+        [HBM] * 4 + [VMEM] + [HBM] * n,
         [VMEM] * (1 + n),
-        held([index, shape((3 * rows, width)), coarse])
-        + [pltpu.SemaphoreType.DMA((5,)), pltpu.SemaphoreType.DMA((n,))],
+        held([index, shape((3 * rows, width))])
+        + [pltpu.SemaphoreType.DMA((4,)), pltpu.SemaphoreType.DMA((n,))],
         2 * slots * width * table,
     )
 
@@ -398,16 +397,29 @@
     return lax.ppermute(a, "width", [(0, 1), (1, 0)])
 
 
-def exchanged(rows, copies):
+def copies_kernel(rows_ref, copies_ref):
+    rows = rows_ref[...]
+    for i in range(copies_ref.shape[0]):
+        copies_ref[i] = rows
+
+
+def copied(rows, count):
+    return kernel_call(
+        copies_kernel, "copies", shape((count, *rows.shape)), (rows,), [VMEM], VMEM, [], 0
+    )
+
+
+def exchanged(rows, copies, others=()):
     size = lax.axis_size(PATCH)
     up = [(i, (i + 1) % size) for i in range(size)]
     down = [(j, i) for i, j in up]
     below, above = lax.ppermute(rows, PATCH, up), lax.ppermute(rows, PATCH, down)
     column = lax.all_to_all(copies, Z, split_axis=0, concat_axis=0, tiled=True)
     column = column.reshape(-1, rows.shape[1])
-    plane = jnp.broadcast_to(column, (lax.axis_size(PLANE), *column.shape))
+    column, others = lax.optimization_barrier((column, others))
+    plane = copied(column, lax.axis_size(PLANE))
     coarse = lax.all_to_all(plane, PLANE, split_axis=0, concat_axis=0, tiled=True)
-    return below, rows, above, coarse.reshape(-1, rows.shape[1])
+    return (below, rows, above, coarse.reshape(-1, rows.shape[1])), others
 
 
 def on_device(
@@ -439,7 +451,6 @@
     scalars = jnp.stack([lax.axis_index("width"), edge_count[0]]).astype(jnp.int32)
 
     rows, copies = node_rows_of(node_latents, columns)
-    table = exchanged(rows, copies)
 
     vectors = jnp.stack(
         [
@@ -480,7 +491,10 @@
 
     edges = (edge_latents, from_other(edge_latents))
     nodes = (node_latents, from_other(node_latents))
-    table, weights, edges, nodes = lax.optimization_barrier((table, weights, edges, nodes))
+    others = (weights[1], weights[5], edges[1], index, receiver)
+    table, others = exchanged(rows, copies, others)
+    weights[1], weights[5], other_edges, index, receiver = others
+    edges = (edges[0], other_edges)
     for layer in range(layers):
         last_layer = layer == layers - 1
         ready = prepared(layer, scalars, edges, receiver, nodes, weights)
@@ -490,7 +504,7 @@
         results = updated_graph(last_layer, scalars, sent, ready, columns)
         if not last_layer:
             edges, nodes = results[:1], results[1:2]
-            table = exchanged(results[2], results[3])
+            table, _ = exchanged(results[2], results[3])
     return (results[1], results[0])
 
 

time: 111 us -> 106 us (0.955)
  waiting for transfers between devices: 20 us -> 13.3 us
  Pallas kernels: 30.7 us -> 35.9 us
  local copies, waits for them, and re-layouts: 4.77 us -> 1.36 us
  starting transfers between devices: 41.1 us -> 39.6 us
  other arithmetic: 1.28 us -> 2.65 us
    pallas_call x7 -> x9, Pallas kernels: 30.7 us -> 35.9 us  [kernel_call(): pl.pallas_call(body, in_specs=in_specs, out_specs=out_specs, out_shape=ou...]
    ppermute x2, waiting for transfers between devices: 6.92 us -> 2.29 us  [exchanged(): lax.ppermute(rows, PATCH, down)]
    ppermute x9, starting transfers between devices: 15.1 us -> 12.8 us  [from_other(): return lax.ppermute(a, 'width', [(0, 1), (1, 0)])]
    broadcast_in_dim x2 -> x0, local copies, waits for them, and re-layouts: 2.16 us -> none  [exchanged(): plane = jnp.broadcast_to(column, (lax.axis_size(PLANE), *column.shape))]
    all_to_all x1, waiting for transfers between devices: 6.71 us -> 4.57 us  [exchanged(): column = lax.all_to_all(copies, Z, split_axis=0, concat_axis=0, tiled=True)]
    unnamed x50 -> x42, local copies, waits for them, and re-layouts: 2.54 us -> 1.3 us
  transfers between devices with their start and end apart: 16 -> 16, of which waited for: 9 -> 7; matrix products, arithmetic and copies ran while one was open for 2% -> 3% of each run, Pallas kernels for 7% -> 14%
where the time goes in v5:
time: 106 us; the launch traced here: 105 us
  starting transfers between devices  39.6 us (37%)
  Pallas kernels  35.9 us (34%)
  waiting for transfers between devices  13.3 us (13%)
  blocking collectives  10.8 us (10%)
  other arithmetic  2.65 us (2%)
  between operations  1.87 us (2%)
  local copies, waits for them, and re-layouts  1.36 us (1%)
    pallas_call x9, Pallas kernels, kernel_call(): pl.pallas_call(body, in_specs=in_specs, out_specs=out_specs, out_shape=ou...  35.9 us
    ppermute x9, starting transfers between devices, from_other(): return lax.ppermute(a, 'width', [(0, 1), (1, 0)])  12.8 us
    all_to_all x2, starting transfers between devices, exchanged(): lax.all_to_all(plane, PLANE, split_axis=0, concat_axis=0, tiled=True)  11.2 us
    all_to_all x1, blocking collectives, exchanged(): column = lax.all_to_all(copies, Z, split_axis=0, concat_axis=0, tiled=True)  10.8 us
    ppermute x2, starting transfers between devices, exchanged(): lax.ppermute(rows, PATCH, down)  8.99 us
    all_to_all x1, starting transfers between devices, exchanged(): column = lax.all_to_all(copies, Z, split_axis=0, concat_axis=0, tiled=True)  6.48 us
    all_to_all x1, waiting for transfers between devices, exchanged(): column = lax.all_to_all(copies, Z, split_axis=0, concat_axis=0, tiled=True)  4.57 us
    ppermute x9, waiting for transfers between devices, from_other(): return lax.ppermute(a, 'width', [(0, 1), (1, 0)])  3.09 us
  transfers between devices with their start and end apart: 16, of which 7 were waited for; matrix products, arithmetic and copies ran while one was open for 3% of the time, Pallas kernels for 14%

profile of v5, /device:TPU:1, one launch (start us, length us, event | category | flops | bytes accessed | tf_op | source)
XLA Modules:
  0.0 105.4 jit_solution(1574768994947644263)
XLA Ops:
  0.6 0.0 copy-start.5
  0.6 0.0 copy-start.3
  0.7 3.3 %collective-permute-start = (bf16[2,256,1536]{2,1,0:T(8,128)(2,1)}, bf16[2,256,1536]{2,1,0:T(8,128)(2,1)S(1)}, u32[]{:S(2)}, u32[]{:S(2)}) collective-permute-start(bf16[2,256,1536]{2,1,0:T(8,128)(2,1)} %refs_1_.3), channel_id=1, source_target_pairs={{0,1},{1,0},{2,3},{3,2},{4,5},{5,4},{6,7},{7,6},{8,9},{9,8},{10,11... | collective-permute-start | bytes 4718600 | tf_op jit(solution)/shard_map/ppermute | solution.py:397
  4.1 0.1 collective-permute-start.1
  4.2 0.4 collective-permute-start.2
  4.6 1.5 %node_rows.1 = (bf16[128,256]{1,0:T(8,128)(2,1)S(1)}, bf16[8,16,256]{2,1,0:T(8,128)(2,1)}) custom-call(bf16[256,128]{1,0:T(8,128)(2,1)} %refs_13_.1), custom_call_target="tpu_custom_call" | custom-call | bytes 4194304 | tf_op jit(solution)/shard_map/node_rows/pallas_call | solution.py:60
  6.1 6.5 %all-to-all-start = ((bf16[8,16,256]{2,1,0:T(8,128)(2,1)}), bf16[8,16,256]{2,1,0:T(8,128)(2,1)S(1)}, u32[]{:S(2)}, u32[]{:S(2)}) async-start(bf16[8,16,256]{2,1,0:T(8,128)(2,1)} %get-tuple-element.60), calls=%async_computation | async-start | bytes 131072 | tf_op jit(solution)/shard_map/all_to_all | solution.py:417
  12.6 1.3 %broadcast_subtract_fusion = s32[1024]{0:T(1024)} fusion(s32[1024]{0:T(1024)} %param.20, s32[]{:T(128)S(6)} %mul.28), kind=kLoop, calls=%fused_computation.26 | loop fusion | flops 1024 | bytes 8196 | tf_op jit(solution)/shard_map/sub | solution.py:490
  13.9 1.3 %fusion.9.index_in = s32[8,128]{1,0:T(8,128)} fusion(s32[1024]{0:T(1024)} %param.19, s32[]{:T(128)S(6)} %select_n.36, s32[]{:T(128)S(6)} %select_n.35, s32[]{:T(128)S(6)} %add.50), kind=kLoop, calls=%fused_computation.18 | loop fusion | flops 50176 | bytes 8204 | tf_op jit(solution)/shard_map/reshape | solution.py:489
  15.2 4.6 %all-to-all-done = bf16[8,16,256]{2,1,0:T(8,128)(2,1)S(1)} async-done(((bf16[8,16,256]{2,1,0:T(8,128)(2,1)}), bf16[8,16,256]{2,1,0:T(8,128)(2,1)S(1)}, u32[]{:S(2)}, u32[]{:S(2)}) %all-to-all-start) | async-done | bytes 65568 | tf_op jit(solution)/shard_map/all_to_all | solution.py:417
  19.8 0.0 collective-permute-done.2.refs_12_
  19.8 0.0 collective-permute-done.1.refs_6_
  19.8 0.0 collective-permute-done.refs_2_
  19.8 1.3 %copies.2 = bf16[16,128,256]{2,1,0:T(8,128)(2,1)} custom-call(bf16[128,256]{1,0:T(8,128)(2,1)S(1)} %bitcast.10), custom_call_target="tpu_custom_call" | custom-call | bytes 4194304 | tf_op jit(solution)/shard_map/copies/pallas_call | solution.py:60
  21.1 6.8 %all-to-all-start.1 = ((bf16[16,128,256]{2,1,0:T(8,128)(2,1)}), bf16[16,128,256]{2,1,0:T(8,128)(2,1)S(1)}, u32[]{:S(2)}, u32[]{:S(2)}) async-start(bf16[16,128,256]{2,1,0:T(8,128)(2,1)} %copies.2), calls=%async_computation.1 | async-start | bytes 2097152 | tf_op jit(solution)/shard_map/all_to_all | solution.py:421
  27.8 2.0 %collective-permute-start.5 = (bf16[2,256,512]{2,1,0:T(8,128)(2,1)S(1)}, bf16[2,256,512]{2,1,0:T(8,128)(2,1)}, u32[]{:S(2)}, u32[]{:S(2)}) collective-permute-start(bf16[2,256,512]{2,1,0:T(8,128)(2,1)S(1)} %copy-done.3), channel_id=1, source_target_pairs={{0,1},{1,0},{2,3},{3,2},{4,5},{5,4},{6,7},{7,6},{8,9},{9,8},{10,11... | collective-permute-start | bytes 1572872 | tf_op jit(solution)/shard_map/ppermute | solution.py:397
  29.8 0.1 collective-permute-start.6
  30.1 0.5 collective-permute-start.7
  30.6 0.1 collective-permute-start.8
  30.7 4.6 %collective-permute-start.4 = (bf16[128,256]{1,0:T(8,128)(2,1)S(1)}, bf16[128,256]{1,0:T(8,128)(2,1)S(1)}, u32[]{:S(2)}, u32[]{:S(2)}) collective-permute-start(bf16[128,256]{1,0:T(8,128)(2,1)S(1)} %get-tuple-element.75.here_in), channel_id=1, source_target_pairs={{2,0},{4,2},{6,4},{8,6},{10,8},{12,10},{14,12},{16,14},{18,16},{20... | collective-permute-start | bytes 196616 | tf_op jit(solution)/shard_map/ppermute | solution.py:416
  36.0 0.0 collective-permute-done.7.refs_10_
  36.0 0.1 collective-permute-start.3
  36.1 0.1 pad_add_fusion.scalar_ref
  36.1 0.0 collective-permute-done.8.refs_14_
  36.1 0.0 collective-permute-done.5.refs_4_
  36.2 0.4 copy-done.12
  36.6 0.2 copy-done.11
  36.8 7.0 %prepare_layer.2 = (f32[512,1024]{1,0:T(8,128)}, bf16[5,512,512]{2,1,0:T(8,128)(2,1)}, bf16[128,1024]{1,0:T(8,128)(2,1)}, f32[512,128]{1,0:T(8,128)}, bf16[512,1...) custom-call(s32[2]{0:T(128)S(1)} %pad_add_fusion.scalar_ref, s32[1,1024]{1,0:T(1,128)} %bitcast.12, ...), custom_call_target="tpu_custom_call" | custom-call | flops 671088640 | bytes 4194304 | tf_op jit(solution)/shard_map/prepare_layer/pallas_call | solution.py:60
  43.8 0.0 copy-start.7
  43.8 0.9 collective-permute-done.3.below_in
  44.7 0.0 all-to-all-done.1
  44.7 0.6 copy-done.8
  45.3 4.4 %gather_senders.2 = (bf16[1024,256]{1,0:T(8,128)(2,1)S(1)}, f32[512,1024]{1,0:T(8,128)S(1)}, bf16[5,512,512]{2,1,0:T(8,128)(2,1)S(1)}, bf16[128,1024]{1,0:T(8,12...) custom-call(s32[8,128]{1,0:T(8,128)} %fusion.9.index_in, ...), custom_call_target="tpu_custom_call" | custom-call | flops 1275068416 | bytes 4194304 | tf_op jit(solution)/shard_map/gather_senders/pallas_call | solution.py:60
  49.7 2.2 %collective-permute-start.9 = (bf16[1024,256]{1,0:T(8,128)(2,1)S(1)}, bf16[1024,256]{1,0:T(8,128)(2,1)S(1)}, u32[]{:S(2)}, u32[]{:S(2)}) collective-permute-start(bf16[1024,256]{1,0:T(8,128)(2,1)S(1)} %get-tuple-element.84.refs_0_), channel_id=1, source_target_pairs={{0,1},{1,0},{2,3},{3,2},{4,5},{5,4},{6,7},{7,6},{8,9},{9,8},{10,11... | collective-permute-start | bytes 1572872 | tf_op jit(solution)/shard_map/ppermute | solution.py:397
  51.9 1.5 %collective-permute-done.9.refs_1_ = bf16[1024,256]{1,0:T(8,128)(2,1)S(1)} collective-permute-done((bf16[1024,256]{1,0:T(8,128)(2,1)S(1)}, bf16[1024,256]{1,0:T(8,128)(2,1)S(1)}, u32[]{:S(2)}, u32[]{:S(2)}) %collective-permute-start.9) | collective-permute-done | bytes 524320 | tf_op jit(solution)/shard_map/ppermute | solution.py:397
  53.5 5.3 %update_graph.2 = (bf16[512,1024]{1,0:T(8,128)(2,1)}, bf16[512,128]{1,0:T(8,128)(2,1)}, bf16[128,256]{1,0:T(8,128)(2,1)S(1)}, bf16[8,16,256]{2,1,0:T(8,128)(2,1)S(1)}) custom-call(s32[2]{0:T(128)S(1)} %pad_add_fusion.scalar_ref, bf16[1024,256]{1,0:T(8,128)(2,1)S(1)} %get-tuple-element.84.refs_0_, bf16[1024,256]{1,0:T(8,128)(2,1)S(1)} %collective-permute-done.9.refs_1_, ...), custom_call_target="tpu_custom_call" | custom-call | flops 1207959552 | bytes 4194304 | tf_op jit(solution)/shard_map/update_graph/pallas_call | solution.py:60
  58.8 10.8 %all_to_all.20 = bf16[8,16,256]{2,1,0:T(8,128)(2,1)S(1)} all-to-all(bf16[8,16,256]{2,1,0:T(8,128)(2,1)S(1)} %get-tuple-element.92), channel_id=1, replica_groups=mesh['patch_0'=8,'patch_1'=4,'patch_2'=4,'width'=2] {'patch_0'}, dimensions={0} | all-to-all | bytes 131072 | tf_op jit(solution)/shard_map/all_to_all | solution.py:417
  69.6 1.1 %copies.3 = bf16[16,128,256]{2,1,0:T(8,128)(2,1)} custom-call(bf16[128,256]{1,0:T(8,128)(2,1)S(1)} %bitcast.11), custom_call_target="tpu_custom_call" | custom-call | bytes 4194304 | tf_op jit(solution)/shard_map/copies/pallas_call | solution.py:60
  70.7 4.5 %all-to-all-start.3 = ((bf16[16,128,256]{2,1,0:T(8,128)(2,1)}), bf16[16,128,256]{2,1,0:T(8,128)(2,1)S(1)}, u32[]{:S(2)}, u32[]{:S(2)}) async-start(bf16[16,128,256]{2,1,0:T(8,128)(2,1)} %copies.3), calls=%async_computation.3 | async-start | bytes 2097152 | tf_op jit(solution)/shard_map/all_to_all | solution.py:421
  75.2 4.4 %collective-permute-start.11 = (bf16[128,256]{1,0:T(8,128)(2,1)S(1)}, bf16[128,256]{1,0:T(8,128)(2,1)S(1)}, u32[]{:S(2)}, u32[]{:S(2)}) collective-permute-start(bf16[128,256]{1,0:T(8,128)(2,1)S(1)} %get-tuple-element.100.here_in), channel_id=1, source_target_pairs={{2,0},{4,2},{6,4},{8,6},{10,8},{12,10},{14,12},{16,14},{18,16},{20... | collective-permute-start | bytes 196616 | tf_op jit(solution)/shard_map/ppermute | solution.py:416
  79.5 6.3 %prepare_layer.3 = (f32[512,1024]{1,0:T(8,128)}, bf16[5,512,512]{2,1,0:T(8,128)(2,1)}, bf16[128,1024]{1,0:T(8,128)(2,1)}, f32[512,128]{1,0:T(8,128)}) custom-call(s32[2]{0:T(128)S(1)} %pad_add_fusion.scalar_ref, s32[1,1024]{1,0:T(1,128)} %bitcast.13, bf16[2,256,1536]{2,1,0:T(8,128)(2,1)} %refs_1_.3, bf16[2,256,1536]{2,1,0:T(8,128)(2,1)} %copy-done.2, ...), custom_call_target="tpu_custom_call" | custom-call | flops 671088640 | bytes 4194304 | tf_op jit(solution)/shard_map/prepare_layer/pallas_call | solution.py:60
  85.8 2.3 %collective-permute-done.11.above_in = bf16[128,256]{1,0:T(8,128)(2,1)S(1)} collective-permute-done((bf16[128,256]{1,0:T(8,128)(2,1)S(1)}, bf16[128,256]{1,0:T(8,128)(2,1)S(1)}, u32[]{:S(2)}, u32[]{:S(2)}) %collective-permute-start.11) | collective-permute-done | bytes 65568 | tf_op jit(solution)/shard_map/ppermute | solution.py:416
  88.1 0.7 collective-permute-done.10.below_in
  88.8 1.8 %all-to-all-done.3 = bf16[16,128,256]{2,1,0:T(8,128)(2,1)S(1)} async-done(((bf16[16,128,256]{2,1,0:T(8,128)(2,1)}), bf16[16,128,256]{2,1,0:T(8,128)(2,1)S(1)}, u32[]{:S(2)}, u32[]{:S(2)}) %all-to-all-start.3) | async-done | bytes 1048608 | tf_op jit(solution)/shard_map/all_to_all | solution.py:421
  90.6 4.5 %gather_senders.3 = (bf16[1024,256]{1,0:T(8,128)(2,1)S(1)}, f32[512,1024]{1,0:T(8,128)S(1)}, bf16[5,512,512]{2,1,0:T(8,128)(2,1)S(1)}, bf16[128,1024]{1,0:T(8,12...) custom-call(s32[8,128]{1,0:T(8,128)} %fusion.9.index_in, ...), custom_call_target="tpu_custom_call" | custom-call | flops 1275068416 | bytes 4194304 | tf_op jit(solution)/shard_map/gather_senders/pallas_call | solution.py:60
  95.1 4.0 %collective-permute-start.12 = (bf16[1024,256]{1,0:T(8,128)(2,1)S(1)}, bf16[1024,256]{1,0:T(8,128)(2,1)S(1)}, u32[]{:S(2)}, u32[]{:S(2)}) collective-permute-start(bf16[1024,256]{1,0:T(8,128)(2,1)S(1)} %get-tuple-element.109.refs_0_), channel_id=1, source_target_pairs={{0,1},{1,0},{2,3},{3,2},{4,5},{5,4},{6,7},{7,6},{8,9},{9,8},{10,11... | collective-permute-start | bytes 1572872 | tf_op jit(solution)/shard_map/ppermute | solution.py:397
  99.1 1.5 %collective-permute-done.12.refs_1_ = bf16[1024,256]{1,0:T(8,128)(2,1)S(1)} collective-permute-done((bf16[1024,256]{1,0:T(8,128)(2,1)S(1)}, bf16[1024,256]{1,0:T(8,128)(2,1)S(1)}, u32[]{:S(2)}, u32[]{:S(2)}) %collective-permute-start.12) | collective-permute-done | bytes 524320 | tf_op jit(solution)/shard_map/ppermute | solution.py:397
  100.7 4.6 %update_graph.3 = (bf16[256,1024]{1,0:T(8,128)(2,1)}, bf16[256,128]{1,0:T(8,128)(2,1)}) custom-call(s32[2]{0:T(128)S(1)} %pad_add_fusion.scalar_ref, bf16[1024,256]{1,0:T(8,128)(2,1)S(1)} %get-tuple-element.109.refs_0_, bf16[1024,256]{1,0:T(8,128)(2,1)S(1)} %collective-permute-done.12.refs_1_, f32[512,1024]{1,0:T(8,128)S(1)} %get-tuple-element.110.refs_2_, ...), custom_call_target="tpu_custom_call" | custom-call | flops 1207959552 | bytes 4194304 | tf_op jit(solution)/shard_map/update_graph/pallas_call | solution.py:60
  (48 shorter events, 0.1 us)
Async XLA Ops:
  0.6 29.9 %copy-start.5 = (bf16[256,128]{1,0:T(8,128)(2,1)S(1)}, bf16[256,128]{1,0:T(8,128)(2,1)}, u32[]{:S(2)}) copy-start(bf16[256,128]{1,0:T(8,128)(2,1)} %refs_13_.1) | copy-start | bytes 196612
  0.6 27.2 %copy-start.3 = (bf16[2,256,512]{2,1,0:T(8,128)(2,1)S(1)}, bf16[2,256,512]{2,1,0:T(8,128)(2,1)}, u32[]{:S(2)}) copy-start(bf16[2,256,512]{2,1,0:T(8,128)(2,1)} %refs_3_.3) | copy-start | bytes 1572868
  0.7 29.2 %copy-start.13 = (f32[2,256]{1,0:T(2,128)S(1)}, f32[2,256]{1,0:T(2,128)}, u32[]{:S(2)}) copy-start(f32[2,256]{1,0:T(2,128)} %param.23) | copy-start | bytes 6148
  0.7 29.2 %copy-start.14 = (f32[2,256]{1,0:T(2,128)S(1)}, f32[2,256]{1,0:T(2,128)}, u32[]{:S(2)}) copy-start(f32[2,256]{1,0:T(2,128)} %param.25) | copy-start | bytes 6148
  0.7 29.2 %copy-start.15 = (f32[2,256]{1,0:T(2,128)S(1)}, f32[2,256]{1,0:T(2,128)}, u32[]{:S(2)}) copy-start(f32[2,256]{1,0:T(2,128)} %param.26) | copy-start | bytes 6148
  0.7 29.2 %copy-start.16 = (f32[2,256]{1,0:T(2,128)S(1)}, f32[2,256]{1,0:T(2,128)}, u32[]{:S(2)}) copy-start(f32[2,256]{1,0:T(2,128)} %param.27) | copy-start | bytes 6148
  0.7 29.3 %copy-start.17 = (f32[2,256]{1,0:T(2,128)S(1)}, f32[2,256]{1,0:T(2,128)}, u32[]{:S(2)}) copy-start(f32[2,256]{1,0:T(2,128)} %param.29) | copy-start | bytes 6148
  0.7 29.3 %copy-start.18 = (f32[2,256]{1,0:T(2,128)S(1)}, f32[2,256]{1,0:T(2,128)}, u32[]{:S(2)}) copy-start(f32[2,256]{1,0:T(2,128)} %param.31) | copy-start | bytes 6148
  0.7 29.3 %copy-start.19 = (f32[2,256]{1,0:T(2,128)S(1)}, f32[2,256]{1,0:T(2,128)}, u32[]{:S(2)}) copy-start(f32[2,256]{1,0:T(2,128)} %param.32) | copy-start | bytes 6148
  0.7 29.3 %copy-start.20 = (f32[2,256]{1,0:T(2,128)S(1)}, f32[2,256]{1,0:T(2,128)}, u32[]{:S(2)}) copy-start(f32[2,256]{1,0:T(2,128)} %param.33) | copy-start | bytes 6148
  0.7 19.0 %collective-permute-start = (bf16[2,256,1536]{2,1,0:T(8,128)(2,1)}, bf16[2,256,1536]{2,1,0:T(8,128)(2,1)S(1)}, u32[]{:S(2)}, u32[]{:S(2)}) collective-permute-start(bf16[2,256,1536]{2,1,0:T(8,128)(2,1)} %refs_1_.3), channel_id=1, source_target_pairs={{0,1},{1,0},{2,3},{3,2},{4,5},{5,4},{6,7},{7,6},{8,9},{9,8},{10,11... | collective-permute-start | bytes 4718600 | tf_op jit(solution)/shard_map/ppermute | solution.py:397
  4.1 15.7 %collective-permute-start.1 = (bf16[2,256,1024]{2,1,0:T(8,128)(2,1)}, bf16[2,256,1024]{2,1,0:T(8,128)(2,1)}, u32[]{:S(2)}, u32[]{:S(2)}) collective-permute-start(bf16[2,256,1024]{2,1,0:T(8,128)(2,1)} %refs_5_.3), channel_id=1, source_target_pairs={{0,1},{1,0},{2,3},{3,2},{4,5},{5,4},{6,7},{7,6},{8,9},{9,8},{10,11... | collective-permute-start | bytes 3145736 | tf_op jit(solution)/shard_map/ppermute | solution.py:397
  4.2 15.6 %collective-permute-start.2 = (bf16[256,1024]{1,0:T(8,128)(2,1)}, bf16[256,1024]{1,0:T(8,128)(2,1)S(1)}, u32[]{:S(2)}, u32[]{:S(2)}) collective-permute-start(bf16[256,1024]{1,0:T(8,128)(2,1)} %refs_11_.1), channel_id=1, source_target_pairs={{0,1},{1,0},{2,3},{3,2},{4,5},{5,4},{6,7},{7,6},{8,9},{9,8},{10,11... | collective-permute-start | bytes 1572872 | tf_op jit(solution)/shard_map/ppermute | solution.py:397
  6.1 37.6 %copy-start = (bf16[128,256]{1,0:T(8,128)(2,1)}, bf16[128,256]{1,0:T(8,128)(2,1)S(1)}, u32[]{:S(2)}) copy-start(bf16[128,256]{1,0:T(8,128)(2,1)S(1)} %get-tuple-element.75.here_in) | copy-start | bytes 196612
  6.1 13.6 %all-to-all-start = ((bf16[8,16,256]{2,1,0:T(8,128)(2,1)}), bf16[8,16,256]{2,1,0:T(8,128)(2,1)S(1)}, u32[]{:S(2)}, u32[]{:S(2)}) async-start(bf16[8,16,256]{2,1,0:T(8,128)(2,1)} %get-tuple-element.60), calls=%async_computation | async-start | bytes 131072 | tf_op jit(solution)/shard_map/all_to_all | solution.py:417
  19.8 1.3 %copy-start.4 = (bf16[256,1024]{1,0:T(8,128)(2,1)}, bf16[256,1024]{1,0:T(8,128)(2,1)S(1)}, u32[]{:S(2)}) copy-start(bf16[256,1024]{1,0:T(8,128)(2,1)S(1)} %collective-permute-done.2.refs_12_) | copy-start | bytes 1572868
  19.8 16.4 %copy-start.2 = (bf16[2,256,1536]{2,1,0:T(8,128)(2,1)}, bf16[2,256,1536]{2,1,0:T(8,128)(2,1)S(1)}, u32[]{:S(2)}) copy-start(bf16[2,256,1536]{2,1,0:T(8,128)(2,1)S(1)} %collective-permute-done.refs_2_) | copy-start | bytes 4718596
  21.1 23.6 %all-to-all-start.1 = ((bf16[16,128,256]{2,1,0:T(8,128)(2,1)}), bf16[16,128,256]{2,1,0:T(8,128)(2,1)S(1)}, u32[]{:S(2)}, u32[]{:S(2)}) async-start(bf16[16,128,256]{2,1,0:T(8,128)(2,1)} %copies.2), calls=%async_computation.1 | async-start | bytes 2097152 | tf_op jit(solution)/shard_map/all_to_all | solution.py:421
  27.8 8.3 %collective-permute-start.5 = (bf16[2,256,512]{2,1,0:T(8,128)(2,1)S(1)}, bf16[2,256,512]{2,1,0:T(8,128)(2,1)}, u32[]{:S(2)}, u32[]{:S(2)}) collective-permute-start(bf16[2,256,512]{2,1,0:T(8,128)(2,1)S(1)} %copy-done.3), channel_id=1, source_target_pairs={{0,1},{1,0},{2,3},{3,2},{4,5},{5,4},{6,7},{7,6},{8,9},{9,8},{10,11... | collective-permute-start | bytes 1572872 | tf_op jit(solution)/shard_map/ppermute | solution.py:397
  29.8 6.4 %collective-permute-start.6 = (bf16[2,256,512]{2,1,0:T(8,128)(2,1)}, bf16[2,256,512]{2,1,0:T(8,128)(2,1)}, u32[]{:S(2)}, u32[]{:S(2)}) collective-permute-start(bf16[2,256,512]{2,1,0:T(8,128)(2,1)} %refs_7_.3), channel_id=1, source_target_pairs={{0,1},{1,0},{2,3},{3,2},{4,5},{5,4},{6,7},{7,6},{8,9},{9,8},{10,11... | collective-permute-start | bytes 1572872 | tf_op jit(solution)/shard_map/ppermute | solution.py:397
  30.1 6.1 %copy-start.6 = (f32[2,8,256]{2,1,0:T(8,128)}, f32[2,8,256]{2,1,0:T(8,128)S(1)}, u32[]{:S(2)}) copy-start(f32[2,8,256]{2,1,0:T(8,128)S(1)} %stack.43.refs_9_) | copy-start | bytes 49156
  30.1 5.9 %collective-permute-start.7 = (f32[2,8,256]{2,1,0:T(8,128)S(1)}, f32[2,8,256]{2,1,0:T(8,128)S(1)}, u32[]{:S(2)}, u32[]{:S(2)}) collective-permute-start(f32[2,8,256]{2,1,0:T(8,128)S(1)} %stack.43.refs_9_), channel_id=1, source_target_pairs={{0,1},{1,0},{2,3},{3,2},{4,5},{5,4},{6,7},{7,6},{8,9},{9,8},{10,11... | collective-permute-start | bytes 49160 | tf_op jit(solution)/shard_map/ppermute | solution.py:397
  30.6 5.6 %collective-permute-start.8 = (bf16[256,128]{1,0:T(8,128)(2,1)S(1)}, bf16[256,128]{1,0:T(8,128)(2,1)S(1)}, u32[]{:S(2)}, u32[]{:S(2)}) collective-permute-start(bf16[256,128]{1,0:T(8,128)(2,1)S(1)} %copy-done.5), channel_id=1, source_target_pairs={{0,1},{1,0},{2,3},{3,2},{4,5},{5,4},{6,7},{7,6},{8,9},{9,8},{10,11... | collective-permute-start | bytes 196616 | tf_op jit(solution)/shard_map/ppermute | solution.py:397
  30.7 13.1 %collective-permute-start.4 = (bf16[128,256]{1,0:T(8,128)(2,1)S(1)}, bf16[128,256]{1,0:T(8,128)(2,1)S(1)}, u32[]{:S(2)}, u32[]{:S(2)}) collective-permute-start(bf16[128,256]{1,0:T(8,128)(2,1)S(1)} %get-tuple-element.75.here_in), channel_id=1, source_target_pairs={{2,0},{4,2},{6,4},{8,6},{10,8},{12,10},{14,12},{16,14},{18,16},{20... | collective-permute-start | bytes 196616 | tf_op jit(solution)/shard_map/ppermute | solution.py:416
  36.0 0.6 copy-start.12
  36.0 8.7 %collective-permute-start.3 = (bf16[128,256]{1,0:T(8,128)(2,1)S(1)}, bf16[128,256]{1,0:T(8,128)(2,1)S(1)}, u32[]{:S(2)}, u32[]{:S(2)}) collective-permute-start(bf16[128,256]{1,0:T(8,128)(2,1)S(1)} %get-tuple-element.75.here_in), channel_id=1, source_target_pairs={{0,2},{2,4},{4,6},{6,8},{8,10},{10,12},{12,14},{14,16},{16,18},{18... | collective-permute-start | bytes 196616 | tf_op jit(solution)/shard_map/ppermute | solution.py:416
  36.1 0.6 copy-start.11
  43.8 0.9 copy-start.7
  44.7 0.6 copy-start.8
  49.7 3.7 %collective-permute-start.9 = (bf16[1024,256]{1,0:T(8,128)(2,1)S(1)}, bf16[1024,256]{1,0:T(8,128)(2,1)S(1)}, u32[]{:S(2)}, u32[]{:S(2)}) collective-permute-start(bf16[1024,256]{1,0:T(8,128)(2,1)S(1)} %get-tuple-element.84.refs_0_), channel_id=1, source_target_pairs={{0,1},{1,0},{2,3},{3,2},{4,5},{5,4},{6,7},{7,6},{8,9},{9,8},{10,11... | collective-permute-start | bytes 1572872 | tf_op jit(solution)/shard_map/ppermute | solution.py:397
  58.8 27.0 %copy-start.1 = (bf16[128,256]{1,0:T(8,128)(2,1)}, bf16[128,256]{1,0:T(8,128)(2,1)S(1)}, u32[]{:S(2)}) copy-start(bf16[128,256]{1,0:T(8,128)(2,1)S(1)} %get-tuple-element.100.here_in) | copy-start | bytes 196612
  70.7 20.0 %all-to-all-start.3 = ((bf16[16,128,256]{2,1,0:T(8,128)(2,1)}), bf16[16,128,256]{2,1,0:T(8,128)(2,1)S(1)}, u32[]{:S(2)}, u32[]{:S(2)}) async-start(bf16[16,128,256]{2,1,0:T(8,128)(2,1)} %copies.3), calls=%async_computation.3 | async-start | bytes 2097152 | tf_op jit(solution)/shard_map/all_to_all | solution.py:421
  75.2 12.9 %collective-permute-start.11 = (bf16[128,256]{1,0:T(8,128)(2,1)S(1)}, bf16[128,256]{1,0:T(8,128)(2,1)S(1)}, u32[]{:S(2)}, u32[]{:S(2)}) collective-permute-start(bf16[128,256]{1,0:T(8,128)(2,1)S(1)} %get-tuple-element.100.here_in), channel_id=1, source_target_pairs={{2,0},{4,2},{6,4},{8,6},{10,8},{12,10},{14,12},{16,14},{18,16},{20... | collective-permute-start | bytes 196616 | tf_op jit(solution)/shard_map/ppermute | solution.py:416
  79.5 9.3 %collective-permute-start.10 = (bf16[128,256]{1,0:T(8,128)(2,1)S(1)}, bf16[128,256]{1,0:T(8,128)(2,1)S(1)}, u32[]{:S(2)}, u32[]{:S(2)}) collective-permute-start(bf16[128,256]{1,0:T(8,128)(2,1)S(1)} %get-tuple-element.100.here_in), channel_id=1, source_target_pairs={{0,2},{2,4},{4,6},{6,8},{8,10},{10,12},{12,14},{14,16},{16,18},{18... | collective-permute-start | bytes 196616 | tf_op jit(solution)/shard_map/ppermute | solution.py:416
  88.1 2.5 %copy-start.9 = (bf16[128,256]{1,0:T(8,128)(2,1)}, bf16[128,256]{1,0:T(8,128)(2,1)S(1)}, u32[]{:S(2)}) copy-start(bf16[128,256]{1,0:T(8,128)(2,1)S(1)} %collective-permute-done.11.above_in) | copy-start | bytes 196612
  88.8 1.8 %copy-start.10 = (bf16[128,256]{1,0:T(8,128)(2,1)}, bf16[128,256]{1,0:T(8,128)(2,1)S(1)}, u32[]{:S(2)}) copy-start(bf16[128,256]{1,0:T(8,128)(2,1)S(1)} %collective-permute-done.10.below_in) | copy-start | bytes 196612
  95.1 5.6 %collective-permute-start.12 = (bf16[1024,256]{1,0:T(8,128)(2,1)S(1)}, bf16[1024,256]{1,0:T(8,128)(2,1)S(1)}, u32[]{:S(2)}, u32[]{:S(2)}) collective-permute-start(bf16[1024,256]{1,0:T(8,128)(2,1)S(1)} %get-tuple-element.109.refs_0_), channel_id=1, source_target_pairs={{0,1},{1,0},{2,3},{3,2},{4,5},{5,4},{6,7},{7,6},{8,9},{9,8},{10,11... | collective-permute-start | bytes 1572872 | tf_op jit(solution)/shard_map/ppermute | solution.py:397

commit v6 on v5

--- a/solution.py
+++ b/solution.py
@@ -41,6 +41,7 @@
 VMEM = pl.BlockSpec(memory_space=pltpu.VMEM)
 SMEM = pl.BlockSpec(memory_space=pltpu.SMEM)
 HBM = pl.BlockSpec(memory_space=pltpu.HBM)
+ANY = pl.BlockSpec(memory_space=pl.ANY)
 
 
 def shape(dims, dtype=jnp.bfloat16):
@@ -116,9 +117,9 @@
     )
 
 
-def gather_kernel(n, index_in, below_in, here_in, above_in, coarse_ref, *refs):
+def gather_kernel(n, index_in, below_in, here_in, above_in, coarse_in, *refs):
     ready_in, out_ref, ready_out = refs[:n], refs[n], refs[n + 1 : 2 * n + 1]
-    index_ref, near_ref, sems, ready_sems = refs[2 * n + 1 :]
+    index_ref, near_ref, coarse_ref, sems, ready_sems = refs[2 * n + 1 :]
     rows = here_in.shape[0]
     copies = started(
         [
@@ -126,11 +127,12 @@
             (below_in, near_ref.at[pl.ds(0, rows)]),
             (here_in, near_ref.at[pl.ds(rows, rows)]),
             (above_in, near_ref.at[pl.ds(2 * rows, rows)]),
+            (coarse_in, coarse_ref),
         ],
         sems,
     )
     ready_copies = started(list(zip(ready_in, ready_out)), ready_sems)
-    finish(copies[:1])
+    finish(copies[:4])
     columns = index_ref[...].T
     lane = lax.broadcasted_iota(jnp.int32, (128, 128), 1)
 
@@ -145,10 +147,10 @@
         return jnp.concatenate(blocks, axis=0)
 
     for start in range(0, out_ref.shape[0], EDGE_BLOCK):
-        total = dot(selection(start, 3 * rows, coarse_ref.shape[0]), coarse_ref[...])
+        total = dot(selection(start, 0, 3 * rows), near_ref[...])
         if start == 0:
-            finish(copies[1:])
-        total = total + dot(selection(start, 0, 3 * rows), near_ref[...])
+            finish(copies[4:])
+        total = total + dot(selection(start, 3 * rows, coarse_ref.shape[0]), coarse_ref[...])
         out_ref[start : start + EDGE_BLOCK, :] = total.astype(jnp.bfloat16)
     finish(ready_copies)
 
@@ -163,10 +165,10 @@
         "gather_senders",
         [shape((slots, width)), *[shape(a.shape, a.dtype) for a in ready]],
         (index, below, here, above, coarse, *ready),
-        [HBM] * 4 + [VMEM] + [HBM] * n,
+        [HBM] * 4 + [ANY] + [HBM] * n,
         [VMEM] * (1 + n),
-        held([index, shape((3 * rows, width))])
-        + [pltpu.SemaphoreType.DMA((4,)), pltpu.SemaphoreType.DMA((n,))],
+        held([index, shape((3 * rows, width)), coarse])
+        + [pltpu.SemaphoreType.DMA((5,)), pltpu.SemaphoreType.DMA((n,))],
         2 * slots * width * table,
     )
 

time: 106 us -> 103 us (0.972)
  Pallas kernels: 35.9 us -> 33 us
    pallas_call x9, Pallas kernels: 35.9 us -> 33 us  [kernel_call(): pl.pallas_call(body, in_specs=in_specs, out_specs=out_specs, out_shape=ou...]
where the time goes in v6:
time: 103 us
  starting transfers between devices  39.5 us (38%)
  Pallas kernels  33 us (32%)
  waiting for transfers between devices  13.3 us (13%)
  blocking collectives  10.8 us (10%)
  other arithmetic  2.65 us (3%)
  between operations  1.87 us (2%)
  local copies, waits for them, and re-layouts  1.36 us (1%)
    pallas_call x9, Pallas kernels, kernel_call(): pl.pallas_call(body, in_specs=in_specs, out_specs=out_specs, out_shape=ou...  33 us
    ppermute x9, starting transfers between devices, from_other(): return lax.ppermute(a, 'width', [(0, 1), (1, 0)])  12.8 us
    all_to_all x2, starting transfers between devices, exchanged(): lax.all_to_all(plane, PLANE, split_axis=0, concat_axis=0, tiled=True)  11.2 us
    all_to_all x1, blocking collectives, exchanged(): column = lax.all_to_all(copies, Z, split_axis=0, concat_axis=0, tiled=True)  10.8 us
    ppermute x2, starting transfers between devices, exchanged(): lax.ppermute(rows, PATCH, down)  8.99 us
    all_to_all x1, starting transfers between devices, exchanged(): column = lax.all_to_all(copies, Z, split_axis=0, concat_axis=0, tiled=True)  6.48 us
    all_to_all x1, waiting for transfers between devices, exchanged(): column = lax.all_to_all(copies, Z, split_axis=0, concat_axis=0, tiled=True)  4.57 us
    ppermute x9, waiting for transfers between devices, from_other(): return lax.ppermute(a, 'width', [(0, 1), (1, 0)])  3.09 us
  transfers between devices with their start and end apart: 16, of which 7 were waited for; matrix products, arithmetic and copies ran while one was open for 3% of the time, Pallas kernels for 14%

profile of v6, /device:TPU:1, one launch (start us, length us, event | category | flops | bytes accessed | tf_op | source)
XLA Modules:
  0.0 102.6 jit_solution(14830063585972425645)
XLA Ops:
  0.6 0.0 copy-start.5
  0.6 0.0 copy-start.3
  0.7 3.3 %collective-permute-start = (bf16[2,256,1536]{2,1,0:T(8,128)(2,1)}, bf16[2,256,1536]{2,1,0:T(8,128)(2,1)S(1)}, u32[]{:S(2)}, u32[]{:S(2)}) collective-permute-start(bf16[2,256,1536]{2,1,0:T(8,128)(2,1)} %refs_1_.3), channel_id=1, source_target_pairs={{0,1},{1,0},{2,3},{3,2},{4,5},{5,4},{6,7},{7,6},{8,9},{9,8},{10,11... | collective-permute-start | bytes 4718600 | tf_op jit(solution)/shard_map/ppermute | solution.py:399
  4.1 0.1 collective-permute-start.1
  4.2 0.4 collective-permute-start.2
  4.6 1.5 %node_rows.1 = (bf16[128,256]{1,0:T(8,128)(2,1)S(1)}, bf16[8,16,256]{2,1,0:T(8,128)(2,1)}) custom-call(bf16[256,128]{1,0:T(8,128)(2,1)} %refs_13_.1), custom_call_target="tpu_custom_call" | custom-call | bytes 4194304 | tf_op jit(solution)/shard_map/node_rows/pallas_call | solution.py:61
  6.1 6.5 %all-to-all-start = ((bf16[8,16,256]{2,1,0:T(8,128)(2,1)}), bf16[8,16,256]{2,1,0:T(8,128)(2,1)S(1)}, u32[]{:S(2)}, u32[]{:S(2)}) async-start(bf16[8,16,256]{2,1,0:T(8,128)(2,1)} %get-tuple-element.60), calls=%async_computation | async-start | bytes 131072 | tf_op jit(solution)/shard_map/all_to_all | solution.py:419
  12.6 1.3 %broadcast_subtract_fusion = s32[1024]{0:T(1024)} fusion(s32[1024]{0:T(1024)} %param.20, s32[]{:T(128)S(6)} %mul.28), kind=kLoop, calls=%fused_computation.26 | loop fusion | flops 1024 | bytes 8196 | tf_op jit(solution)/shard_map/sub | solution.py:492
  13.9 1.3 %fusion.9.index_in = s32[8,128]{1,0:T(8,128)} fusion(s32[1024]{0:T(1024)} %param.19, s32[]{:T(128)S(6)} %select_n.36, s32[]{:T(128)S(6)} %select_n.35, s32[]{:T(128)S(6)} %add.50), kind=kLoop, calls=%fused_computation.18 | loop fusion | flops 50176 | bytes 8204 | tf_op jit(solution)/shard_map/reshape | solution.py:491
  15.2 4.6 %all-to-all-done = bf16[8,16,256]{2,1,0:T(8,128)(2,1)S(1)} async-done(((bf16[8,16,256]{2,1,0:T(8,128)(2,1)}), bf16[8,16,256]{2,1,0:T(8,128)(2,1)S(1)}, u32[]{:S(2)}, u32[]{:S(2)}) %all-to-all-start) | async-done | bytes 65568 | tf_op jit(solution)/shard_map/all_to_all | solution.py:419
  19.8 0.0 collective-permute-done.2.refs_12_
  19.8 0.0 collective-permute-done.1.refs_6_
  19.8 0.0 collective-permute-done.refs_2_
  19.8 1.3 %copies.2 = bf16[16,128,256]{2,1,0:T(8,128)(2,1)} custom-call(bf16[128,256]{1,0:T(8,128)(2,1)S(1)} %bitcast.10), custom_call_target="tpu_custom_call" | custom-call | bytes 4194304 | tf_op jit(solution)/shard_map/copies/pallas_call | solution.py:61
  21.1 6.8 %all-to-all-start.1 = ((bf16[16,128,256]{2,1,0:T(8,128)(2,1)}), bf16[16,128,256]{2,1,0:T(8,128)(2,1)S(1)}, u32[]{:S(2)}, u32[]{:S(2)}) async-start(bf16[16,128,256]{2,1,0:T(8,128)(2,1)} %copies.2), calls=%async_computation.1 | async-start | bytes 2097152 | tf_op jit(solution)/shard_map/all_to_all | solution.py:423
  27.8 2.0 %collective-permute-start.5 = (bf16[2,256,512]{2,1,0:T(8,128)(2,1)S(1)}, bf16[2,256,512]{2,1,0:T(8,128)(2,1)}, u32[]{:S(2)}, u32[]{:S(2)}) collective-permute-start(bf16[2,256,512]{2,1,0:T(8,128)(2,1)S(1)} %copy-done.3), channel_id=1, source_target_pairs={{0,1},{1,0},{2,3},{3,2},{4,5},{5,4},{6,7},{7,6},{8,9},{9,8},{10,11... | collective-permute-start | bytes 1572872 | tf_op jit(solution)/shard_map/ppermute | solution.py:399
  29.8 0.1 collective-permute-start.6
  30.1 0.5 collective-permute-start.7
  30.6 0.1 collective-permute-start.8
  30.7 4.6 %collective-permute-start.4 = (bf16[128,256]{1,0:T(8,128)(2,1)S(1)}, bf16[128,256]{1,0:T(8,128)(2,1)S(1)}, u32[]{:S(2)}, u32[]{:S(2)}) collective-permute-start(bf16[128,256]{1,0:T(8,128)(2,1)S(1)} %get-tuple-element.75.here_in), channel_id=1, source_target_pairs={{2,0},{4,2},{6,4},{8,6},{10,8},{12,10},{14,12},{16,14},{18,16},{20... | collective-permute-start | bytes 196616 | tf_op jit(solution)/shard_map/ppermute | solution.py:418
  36.0 0.1 collective-permute-start.3
  36.1 0.1 pad_add_fusion.scalar_ref
  36.1 0.0 collective-permute-done.8.refs_14_
  36.1 0.0 collective-permute-done.5.refs_4_
  36.2 0.4 copy-done.12
  36.6 0.2 copy-done.11
  36.8 7.0 %prepare_layer.2 = (f32[512,1024]{1,0:T(8,128)}, bf16[5,512,512]{2,1,0:T(8,128)(2,1)}, bf16[128,1024]{1,0:T(8,128)(2,1)}, f32[512,128]{1,0:T(8,128)}, bf16[512,1...) custom-call(s32[2]{0:T(128)S(1)} %pad_add_fusion.scalar_ref, s32[1,1024]{1,0:T(1,128)} %bitcast.12, ...), custom_call_target="tpu_custom_call" | custom-call | flops 671088640 | bytes 4194304 | tf_op jit(solution)/shard_map/prepare_layer/pallas_call | solution.py:61
  43.8 0.0 collective-permute-done.4.above_in
  43.8 0.0 copy-start.7
  43.8 0.9 collective-permute-done.3.below_in
  44.7 0.0 all-to-all-done.1
  44.7 0.6 copy-done.8
  45.3 3.0 %gather_senders.2 = (bf16[1024,256]{1,0:T(8,128)(2,1)S(1)}, f32[512,1024]{1,0:T(8,128)S(1)}, bf16[5,512,512]{2,1,0:T(8,128)(2,1)S(1)}, bf16[128,1024]{1,0:T(8,12...) custom-call(s32[8,128]{1,0:T(8,128)} %fusion.9.index_in, ...), custom_call_target="tpu_custom_call" | custom-call | flops 1275068416 | bytes 4194304 | tf_op jit(solution)/shard_map/gather_senders/pallas_call | solution.py:61
  48.3 2.2 %collective-permute-start.9 = (bf16[1024,256]{1,0:T(8,128)(2,1)S(1)}, bf16[1024,256]{1,0:T(8,128)(2,1)S(1)}, u32[]{:S(2)}, u32[]{:S(2)}) collective-permute-start(bf16[1024,256]{1,0:T(8,128)(2,1)S(1)} %get-tuple-element.84.refs_0_), channel_id=1, source_target_pairs={{0,1},{1,0},{2,3},{3,2},{4,5},{5,4},{6,7},{7,6},{8,9},{9,8},{10,11... | collective-permute-start | bytes 1572872 | tf_op jit(solution)/shard_map/ppermute | solution.py:399
  50.5 1.5 %collective-permute-done.9.refs_1_ = bf16[1024,256]{1,0:T(8,128)(2,1)S(1)} collective-permute-done((bf16[1024,256]{1,0:T(8,128)(2,1)S(1)}, bf16[1024,256]{1,0:T(8,128)(2,1)S(1)}, u32[]{:S(2)}, u32[]{:S(2)}) %collective-permute-start.9) | collective-permute-done | bytes 524320 | tf_op jit(solution)/shard_map/ppermute | solution.py:399
  52.1 5.3 %update_graph.2 = (bf16[512,1024]{1,0:T(8,128)(2,1)}, bf16[512,128]{1,0:T(8,128)(2,1)}, bf16[128,256]{1,0:T(8,128)(2,1)S(1)}, bf16[8,16,256]{2,1,0:T(8,128)(2,1)S(1)}) custom-call(s32[2]{0:T(128)S(1)} %pad_add_fusion.scalar_ref, bf16[1024,256]{1,0:T(8,128)(2,1)S(1)} %get-tuple-element.84.refs_0_, bf16[1024,256]{1,0:T(8,128)(2,1)S(1)} %collective-permute-done.9.refs_1_, ...), custom_call_target="tpu_custom_call" | custom-call | flops 1207959552 | bytes 4194304 | tf_op jit(solution)/shard_map/update_graph/pallas_call | solution.py:61
  57.4 10.8 %all_to_all.20 = bf16[8,16,256]{2,1,0:T(8,128)(2,1)S(1)} all-to-all(bf16[8,16,256]{2,1,0:T(8,128)(2,1)S(1)} %get-tuple-element.92), channel_id=1, replica_groups=mesh['patch_0'=8,'patch_1'=4,'patch_2'=4,'width'=2] {'patch_0'}, dimensions={0} | all-to-all | bytes 131072 | tf_op jit(solution)/shard_map/all_to_all | solution.py:419
  68.2 1.1 %copies.3 = bf16[16,128,256]{2,1,0:T(8,128)(2,1)} custom-call(bf16[128,256]{1,0:T(8,128)(2,1)S(1)} %bitcast.11), custom_call_target="tpu_custom_call" | custom-call | bytes 4194304 | tf_op jit(solution)/shard_map/copies/pallas_call | solution.py:61
  69.2 4.5 %all-to-all-start.3 = ((bf16[16,128,256]{2,1,0:T(8,128)(2,1)}), bf16[16,128,256]{2,1,0:T(8,128)(2,1)S(1)}, u32[]{:S(2)}, u32[]{:S(2)}) async-start(bf16[16,128,256]{2,1,0:T(8,128)(2,1)} %copies.3), calls=%async_computation.3 | async-start | bytes 2097152 | tf_op jit(solution)/shard_map/all_to_all | solution.py:423
  73.7 4.4 %collective-permute-start.11 = (bf16[128,256]{1,0:T(8,128)(2,1)S(1)}, bf16[128,256]{1,0:T(8,128)(2,1)S(1)}, u32[]{:S(2)}, u32[]{:S(2)}) collective-permute-start(bf16[128,256]{1,0:T(8,128)(2,1)S(1)} %get-tuple-element.100.here_in), channel_id=1, source_target_pairs={{2,0},{4,2},{6,4},{8,6},{10,8},{12,10},{14,12},{16,14},{18,16},{20... | collective-permute-start | bytes 196616 | tf_op jit(solution)/shard_map/ppermute | solution.py:418
  78.1 6.3 %prepare_layer.3 = (f32[512,1024]{1,0:T(8,128)}, bf16[5,512,512]{2,1,0:T(8,128)(2,1)}, bf16[128,1024]{1,0:T(8,128)(2,1)}, f32[512,128]{1,0:T(8,128)}) custom-call(s32[2]{0:T(128)S(1)} %pad_add_fusion.scalar_ref, s32[1,1024]{1,0:T(1,128)} %bitcast.13, bf16[2,256,1536]{2,1,0:T(8,128)(2,1)} %refs_1_.3, bf16[2,256,1536]{2,1,0:T(8,128)(2,1)} %copy-done.2, ...), custom_call_target="tpu_custom_call" | custom-call | flops 671088640 | bytes 4194304 | tf_op jit(solution)/shard_map/prepare_layer/pallas_call | solution.py:61
  84.4 2.3 %collective-permute-done.11.above_in = bf16[128,256]{1,0:T(8,128)(2,1)S(1)} collective-permute-done((bf16[128,256]{1,0:T(8,128)(2,1)S(1)}, bf16[128,256]{1,0:T(8,128)(2,1)S(1)}, u32[]{:S(2)}, u32[]{:S(2)}) %collective-permute-start.11) | collective-permute-done | bytes 65568 | tf_op jit(solution)/shard_map/ppermute | solution.py:418
  86.7 0.7 collective-permute-done.10.below_in
  87.4 1.8 %all-to-all-done.3 = bf16[16,128,256]{2,1,0:T(8,128)(2,1)S(1)} async-done(((bf16[16,128,256]{2,1,0:T(8,128)(2,1)}), bf16[16,128,256]{2,1,0:T(8,128)(2,1)S(1)}, u32[]{:S(2)}, u32[]{:S(2)}) %all-to-all-start.3) | async-done | bytes 1048608 | tf_op jit(solution)/shard_map/all_to_all | solution.py:423
  89.2 3.0 %gather_senders.3 = (bf16[1024,256]{1,0:T(8,128)(2,1)S(1)}, f32[512,1024]{1,0:T(8,128)S(1)}, bf16[5,512,512]{2,1,0:T(8,128)(2,1)S(1)}, bf16[128,1024]{1,0:T(8,12...) custom-call(s32[8,128]{1,0:T(8,128)} %fusion.9.index_in, ...), custom_call_target="tpu_custom_call" | custom-call | flops 1275068416 | bytes 4194304 | tf_op jit(solution)/shard_map/gather_senders/pallas_call | solution.py:61
  92.2 4.0 %collective-permute-start.12 = (bf16[1024,256]{1,0:T(8,128)(2,1)S(1)}, bf16[1024,256]{1,0:T(8,128)(2,1)S(1)}, u32[]{:S(2)}, u32[]{:S(2)}) collective-permute-start(bf16[1024,256]{1,0:T(8,128)(2,1)S(1)} %get-tuple-element.109.refs_0_), channel_id=1, source_target_pairs={{0,1},{1,0},{2,3},{3,2},{4,5},{5,4},{6,7},{7,6},{8,9},{9,8},{10,11... | collective-permute-start | bytes 1572872 | tf_op jit(solution)/shard_map/ppermute | solution.py:399
  96.3 1.5 %collective-permute-done.12.refs_1_ = bf16[1024,256]{1,0:T(8,128)(2,1)S(1)} collective-permute-done((bf16[1024,256]{1,0:T(8,128)(2,1)S(1)}, bf16[1024,256]{1,0:T(8,128)(2,1)S(1)}, u32[]{:S(2)}, u32[]{:S(2)}) %collective-permute-start.12) | collective-permute-done | bytes 524320 | tf_op jit(solution)/shard_map/ppermute | solution.py:399
  97.8 4.6 %update_graph.3 = (bf16[256,1024]{1,0:T(8,128)(2,1)}, bf16[256,128]{1,0:T(8,128)(2,1)}) custom-call(s32[2]{0:T(128)S(1)} %pad_add_fusion.scalar_ref, bf16[1024,256]{1,0:T(8,128)(2,1)S(1)} %get-tuple-element.109.refs_0_, bf16[1024,256]{1,0:T(8,128)(2,1)S(1)} %collective-permute-done.12.refs_1_, f32[512,1024]{1,0:T(8,128)S(1)} %get-tuple-element.110.refs_2_, ...), custom_call_target="tpu_custom_call" | custom-call | flops 1207959552 | bytes 4194304 | tf_op jit(solution)/shard_map/update_graph/pallas_call | solution.py:61
  (48 shorter events, 0.1 us)
Async XLA Ops:
  0.6 29.9 %copy-start.5 = (bf16[256,128]{1,0:T(8,128)(2,1)S(1)}, bf16[256,128]{1,0:T(8,128)(2,1)}, u32[]{:S(2)}) copy-start(bf16[256,128]{1,0:T(8,128)(2,1)} %refs_13_.1) | copy-start | bytes 196612
  0.6 27.2 %copy-start.3 = (bf16[2,256,512]{2,1,0:T(8,128)(2,1)S(1)}, bf16[2,256,512]{2,1,0:T(8,128)(2,1)}, u32[]{:S(2)}) copy-start(bf16[2,256,512]{2,1,0:T(8,128)(2,1)} %refs_3_.3) | copy-start | bytes 1572868
  0.7 29.2 %copy-start.13 = (f32[2,256]{1,0:T(2,128)S(1)}, f32[2,256]{1,0:T(2,128)}, u32[]{:S(2)}) copy-start(f32[2,256]{1,0:T(2,128)} %param.23) | copy-start | bytes 6148
  0.7 29.2 %copy-start.14 = (f32[2,256]{1,0:T(2,128)S(1)}, f32[2,256]{1,0:T(2,128)}, u32[]{:S(2)}) copy-start(f32[2,256]{1,0:T(2,128)} %param.25) | copy-start | bytes 6148
  0.7 29.2 %copy-start.15 = (f32[2,256]{1,0:T(2,128)S(1)}, f32[2,256]{1,0:T(2,128)}, u32[]{:S(2)}) copy-start(f32[2,256]{1,0:T(2,128)} %param.26) | copy-start | bytes 6148
  0.7 29.2 %copy-start.16 = (f32[2,256]{1,0:T(2,128)S(1)}, f32[2,256]{1,0:T(2,128)}, u32[]{:S(2)}) copy-start(f32[2,256]{1,0:T(2,128)} %param.27) | copy-start | bytes 6148
  0.7 29.3 %copy-start.17 = (f32[2,256]{1,0:T(2,128)S(1)}, f32[2,256]{1,0:T(2,128)}, u32[]{:S(2)}) copy-start(f32[2,256]{1,0:T(2,128)} %param.29) | copy-start | bytes 6148
  0.7 29.3 %copy-start.18 = (f32[2,256]{1,0:T(2,128)S(1)}, f32[2,256]{1,0:T(2,128)}, u32[]{:S(2)}) copy-start(f32[2,256]{1,0:T(2,128)} %param.31) | copy-start | bytes 6148
  0.7 29.3 %copy-start.19 = (f32[2,256]{1,0:T(2,128)S(1)}, f32[2,256]{1,0:T(2,128)}, u32[]{:S(2)}) copy-start(f32[2,256]{1,0:T(2,128)} %param.32) | copy-start | bytes 6148
  0.7 29.3 %copy-start.20 = (f32[2,256]{1,0:T(2,128)S(1)}, f32[2,256]{1,0:T(2,128)}, u32[]{:S(2)}) copy-start(f32[2,256]{1,0:T(2,128)} %param.33) | copy-start | bytes 6148
  0.7 19.0 %collective-permute-start = (bf16[2,256,1536]{2,1,0:T(8,128)(2,1)}, bf16[2,256,1536]{2,1,0:T(8,128)(2,1)S(1)}, u32[]{:S(2)}, u32[]{:S(2)}) collective-permute-start(bf16[2,256,1536]{2,1,0:T(8,128)(2,1)} %refs_1_.3), channel_id=1, source_target_pairs={{0,1},{1,0},{2,3},{3,2},{4,5},{5,4},{6,7},{7,6},{8,9},{9,8},{10,11... | collective-permute-start | bytes 4718600 | tf_op jit(solution)/shard_map/ppermute | solution.py:399
  4.1 15.7 %collective-permute-start.1 = (bf16[2,256,1024]{2,1,0:T(8,128)(2,1)}, bf16[2,256,1024]{2,1,0:T(8,128)(2,1)}, u32[]{:S(2)}, u32[]{:S(2)}) collective-permute-start(bf16[2,256,1024]{2,1,0:T(8,128)(2,1)} %refs_5_.3), channel_id=1, source_target_pairs={{0,1},{1,0},{2,3},{3,2},{4,5},{5,4},{6,7},{7,6},{8,9},{9,8},{10,11... | collective-permute-start | bytes 3145736 | tf_op jit(solution)/shard_map/ppermute | solution.py:399
  4.2 15.6 %collective-permute-start.2 = (bf16[256,1024]{1,0:T(8,128)(2,1)}, bf16[256,1024]{1,0:T(8,128)(2,1)S(1)}, u32[]{:S(2)}, u32[]{:S(2)}) collective-permute-start(bf16[256,1024]{1,0:T(8,128)(2,1)} %refs_11_.1), channel_id=1, source_target_pairs={{0,1},{1,0},{2,3},{3,2},{4,5},{5,4},{6,7},{7,6},{8,9},{9,8},{10,11... | collective-permute-start | bytes 1572872 | tf_op jit(solution)/shard_map/ppermute | solution.py:399
  6.1 37.6 %copy-start = (bf16[128,256]{1,0:T(8,128)(2,1)}, bf16[128,256]{1,0:T(8,128)(2,1)S(1)}, u32[]{:S(2)}) copy-start(bf16[128,256]{1,0:T(8,128)(2,1)S(1)} %get-tuple-element.75.here_in) | copy-start | bytes 196612
  6.1 13.6 %all-to-all-start = ((bf16[8,16,256]{2,1,0:T(8,128)(2,1)}), bf16[8,16,256]{2,1,0:T(8,128)(2,1)S(1)}, u32[]{:S(2)}, u32[]{:S(2)}) async-start(bf16[8,16,256]{2,1,0:T(8,128)(2,1)} %get-tuple-element.60), calls=%async_computation | async-start | bytes 131072 | tf_op jit(solution)/shard_map/all_to_all | solution.py:419
  19.8 1.3 %copy-start.4 = (bf16[256,1024]{1,0:T(8,128)(2,1)}, bf16[256,1024]{1,0:T(8,128)(2,1)S(1)}, u32[]{:S(2)}) copy-start(bf16[256,1024]{1,0:T(8,128)(2,1)S(1)} %collective-permute-done.2.refs_12_) | copy-start | bytes 1572868
  19.8 16.4 %copy-start.2 = (bf16[2,256,1536]{2,1,0:T(8,128)(2,1)}, bf16[2,256,1536]{2,1,0:T(8,128)(2,1)S(1)}, u32[]{:S(2)}) copy-start(bf16[2,256,1536]{2,1,0:T(8,128)(2,1)S(1)} %collective-permute-done.refs_2_) | copy-start | bytes 4718596
  21.1 23.6 %all-to-all-start.1 = ((bf16[16,128,256]{2,1,0:T(8,128)(2,1)}), bf16[16,128,256]{2,1,0:T(8,128)(2,1)S(1)}, u32[]{:S(2)}, u32[]{:S(2)}) async-start(bf16[16,128,256]{2,1,0:T(8,128)(2,1)} %copies.2), calls=%async_computation.1 | async-start | bytes 2097152 | tf_op jit(solution)/shard_map/all_to_all | solution.py:423
  27.8 8.3 %collective-permute-start.5 = (bf16[2,256,512]{2,1,0:T(8,128)(2,1)S(1)}, bf16[2,256,512]{2,1,0:T(8,128)(2,1)}, u32[]{:S(2)}, u32[]{:S(2)}) collective-permute-start(bf16[2,256,512]{2,1,0:T(8,128)(2,1)S(1)} %copy-done.3), channel_id=1, source_target_pairs={{0,1},{1,0},{2,3},{3,2},{4,5},{5,4},{6,7},{7,6},{8,9},{9,8},{10,11... | collective-permute-start | bytes 1572872 | tf_op jit(solution)/shard_map/ppermute | solution.py:399
  29.8 6.4 %collective-permute-start.6 = (bf16[2,256,512]{2,1,0:T(8,128)(2,1)}, bf16[2,256,512]{2,1,0:T(8,128)(2,1)}, u32[]{:S(2)}, u32[]{:S(2)}) collective-permute-start(bf16[2,256,512]{2,1,0:T(8,128)(2,1)} %refs_7_.3), channel_id=1, source_target_pairs={{0,1},{1,0},{2,3},{3,2},{4,5},{5,4},{6,7},{7,6},{8,9},{9,8},{10,11... | collective-permute-start | bytes 1572872 | tf_op jit(solution)/shard_map/ppermute | solution.py:399
  30.1 6.1 %copy-start.6 = (f32[2,8,256]{2,1,0:T(8,128)}, f32[2,8,256]{2,1,0:T(8,128)S(1)}, u32[]{:S(2)}) copy-start(f32[2,8,256]{2,1,0:T(8,128)S(1)} %stack.43.refs_9_) | copy-start | bytes 49156
  30.1 5.9 %collective-permute-start.7 = (f32[2,8,256]{2,1,0:T(8,128)S(1)}, f32[2,8,256]{2,1,0:T(8,128)S(1)}, u32[]{:S(2)}, u32[]{:S(2)}) collective-permute-start(f32[2,8,256]{2,1,0:T(8,128)S(1)} %stack.43.refs_9_), channel_id=1, source_target_pairs={{0,1},{1,0},{2,3},{3,2},{4,5},{5,4},{6,7},{7,6},{8,9},{9,8},{10,11... | collective-permute-start | bytes 49160 | tf_op jit(solution)/shard_map/ppermute | solution.py:399
  30.6 5.6 %collective-permute-start.8 = (bf16[256,128]{1,0:T(8,128)(2,1)S(1)}, bf16[256,128]{1,0:T(8,128)(2,1)S(1)}, u32[]{:S(2)}, u32[]{:S(2)}) collective-permute-start(bf16[256,128]{1,0:T(8,128)(2,1)S(1)} %copy-done.5), channel_id=1, source_target_pairs={{0,1},{1,0},{2,3},{3,2},{4,5},{5,4},{6,7},{7,6},{8,9},{9,8},{10,11... | collective-permute-start | bytes 196616 | tf_op jit(solution)/shard_map/ppermute | solution.py:399
  30.7 13.1 %collective-permute-start.4 = (bf16[128,256]{1,0:T(8,128)(2,1)S(1)}, bf16[128,256]{1,0:T(8,128)(2,1)S(1)}, u32[]{:S(2)}, u32[]{:S(2)}) collective-permute-start(bf16[128,256]{1,0:T(8,128)(2,1)S(1)} %get-tuple-element.75.here_in), channel_id=1, source_target_pairs={{2,0},{4,2},{6,4},{8,6},{10,8},{12,10},{14,12},{16,14},{18,16},{20... | collective-permute-start | bytes 196616 | tf_op jit(solution)/shard_map/ppermute | solution.py:418
  36.0 0.6 copy-start.12
  36.0 8.7 %collective-permute-start.3 = (bf16[128,256]{1,0:T(8,128)(2,1)S(1)}, bf16[128,256]{1,0:T(8,128)(2,1)S(1)}, u32[]{:S(2)}, u32[]{:S(2)}) collective-permute-start(bf16[128,256]{1,0:T(8,128)(2,1)S(1)} %get-tuple-element.75.here_in), channel_id=1, source_target_pairs={{0,2},{2,4},{4,6},{6,8},{8,10},{10,12},{12,14},{14,16},{16,18},{18... | collective-permute-start | bytes 196616 | tf_op jit(solution)/shard_map/ppermute | solution.py:418
  36.1 0.6 copy-start.11
  43.8 0.9 copy-start.7
  44.7 0.6 copy-start.8
  48.3 3.7 %collective-permute-start.9 = (bf16[1024,256]{1,0:T(8,128)(2,1)S(1)}, bf16[1024,256]{1,0:T(8,128)(2,1)S(1)}, u32[]{:S(2)}, u32[]{:S(2)}) collective-permute-start(bf16[1024,256]{1,0:T(8,128)(2,1)S(1)} %get-tuple-element.84.refs_0_), channel_id=1, source_target_pairs={{0,1},{1,0},{2,3},{3,2},{4,5},{5,4},{6,7},{7,6},{8,9},{9,8},{10,11... | collective-permute-start | bytes 1572872 | tf_op jit(solution)/shard_map/ppermute | solution.py:399
  57.3 27.0 %copy-start.1 = (bf16[128,256]{1,0:T(8,128)(2,1)}, bf16[128,256]{1,0:T(8,128)(2,1)S(1)}, u32[]{:S(2)}) copy-start(bf16[128,256]{1,0:T(8,128)(2,1)S(1)} %get-tuple-element.100.here_in) | copy-start | bytes 196612
  69.2 19.9 %all-to-all-start.3 = ((bf16[16,128,256]{2,1,0:T(8,128)(2,1)}), bf16[16,128,256]{2,1,0:T(8,128)(2,1)S(1)}, u32[]{:S(2)}, u32[]{:S(2)}) async-start(bf16[16,128,256]{2,1,0:T(8,128)(2,1)} %copies.3), calls=%async_computation.3 | async-start | bytes 2097152 | tf_op jit(solution)/shard_map/all_to_all | solution.py:423
  73.7 12.9 %collective-permute-start.11 = (bf16[128,256]{1,0:T(8,128)(2,1)S(1)}, bf16[128,256]{1,0:T(8,128)(2,1)S(1)}, u32[]{:S(2)}, u32[]{:S(2)}) collective-permute-start(bf16[128,256]{1,0:T(8,128)(2,1)S(1)} %get-tuple-element.100.here_in), channel_id=1, source_target_pairs={{2,0},{4,2},{6,4},{8,6},{10,8},{12,10},{14,12},{16,14},{18,16},{20... | collective-permute-start | bytes 196616 | tf_op jit(solution)/shard_map/ppermute | solution.py:418
  78.1 9.3 %collective-permute-start.10 = (bf16[128,256]{1,0:T(8,128)(2,1)S(1)}, bf16[128,256]{1,0:T(8,128)(2,1)S(1)}, u32[]{:S(2)}, u32[]{:S(2)}) collective-permute-start(bf16[128,256]{1,0:T(8,128)(2,1)S(1)} %get-tuple-element.100.here_in), channel_id=1, source_target_pairs={{0,2},{2,4},{4,6},{6,8},{8,10},{10,12},{12,14},{14,16},{16,18},{18... | collective-permute-start | bytes 196616 | tf_op jit(solution)/shard_map/ppermute | solution.py:418
  86.7 2.5 %copy-start.9 = (bf16[128,256]{1,0:T(8,128)(2,1)}, bf16[128,256]{1,0:T(8,128)(2,1)S(1)}, u32[]{:S(2)}) copy-start(bf16[128,256]{1,0:T(8,128)(2,1)S(1)} %collective-permute-done.11.above_in) | copy-start | bytes 196612
  87.4 1.8 %copy-start.10 = (bf16[128,256]{1,0:T(8,128)(2,1)}, bf16[128,256]{1,0:T(8,128)(2,1)S(1)}, u32[]{:S(2)}) copy-start(bf16[128,256]{1,0:T(8,128)(2,1)S(1)} %collective-permute-done.10.below_in) | copy-start | bytes 196612
  92.2 5.6 %collective-permute-start.12 = (bf16[1024,256]{1,0:T(8,128)(2,1)S(1)}, bf16[1024,256]{1,0:T(8,128)(2,1)S(1)}, u32[]{:S(2)}, u32[]{:S(2)}) collective-permute-start(bf16[1024,256]{1,0:T(8,128)(2,1)S(1)} %get-tuple-element.109.refs_0_), channel_id=1, source_target_pairs={{0,1},{1,0},{2,3},{3,2},{4,5},{5,4},{6,7},{7,6},{8,9},{9,8},{10,11... | collective-permute-start | bytes 1572872 | tf_op jit(solution)/shard_map/ppermute | solution.py:399

commit v7 on v6

--- a/solution.py
+++ b/solution.py
@@ -90,17 +90,17 @@
     return ref.at[:, pl.ds(start, length)]
 
 
-def store_rows(mine, rows_ref, copies_ref):
-    rows = mine.T
+def store_rows(rows, mine, rows_ref, copies_ref):
     rows_ref[...] = rows
     for i in range(copies_ref.shape[0]):
-        copies_ref[i] = rows[: copies_ref.shape[1]]
+        copies_ref[i] = mine[: copies_ref.shape[1]]
 
 
 def rows_kernel(nodes_ref, rows_ref, copies_ref, held_ref, sem):
     copies = started([(nodes_ref, held_ref)], sem)
     finish(copies)
-    store_rows(held_ref[...], rows_ref, copies_ref)
+    rows = held_ref[...].T
+    store_rows(rows, rows, rows_ref, copies_ref)
 
 
 def node_rows_of(nodes, columns):
@@ -117,22 +117,23 @@
     )
 
 
-def gather_kernel(n, index_in, below_in, here_in, above_in, coarse_in, *refs):
+def gather_kernel(n, scalar_ref, index_in, rows_in, beside_in, coarse_in, *refs):
     ready_in, out_ref, ready_out = refs[:n], refs[n], refs[n + 1 : 2 * n + 1]
-    index_ref, near_ref, coarse_ref, sems, ready_sems = refs[2 * n + 1 :]
-    rows = here_in.shape[0]
+    index_ref, here_ref, beside_ref, coarse_ref, sems, ready_sems = refs[2 * n + 1 :]
+    core = scalar_ref[0]
+    rows, half = here_ref.shape
+    mine = pl.ds(pl.multiple_of(core * half, half), half)
     copies = started(
         [
             (index_in, index_ref),
-            (below_in, near_ref.at[pl.ds(0, rows)]),
-            (here_in, near_ref.at[pl.ds(rows, rows)]),
-            (above_in, near_ref.at[pl.ds(2 * rows, rows)]),
+            (rows_in.at[:, mine], here_ref),
+            (beside_in, beside_ref),
             (coarse_in, coarse_ref),
         ],
         sems,
     )
     ready_copies = started(list(zip(ready_in, ready_out)), ready_sems)
-    finish(copies[:4])
+    finish(copies[:3])
     columns = index_ref[...].T
     lane = lax.broadcasted_iota(jnp.int32, (128, 128), 1)
 
@@ -141,35 +142,41 @@
         for k in range(start // 128, (start + EDGE_BLOCK) // 128):
             index = jnp.broadcast_to(columns[:, k : k + 1], (128, 128))
             tiles = []
-            for j in range(first, first + length, 128):
-                tiles.append(jnp.where(index == lane + j, 1.0, 0.0).astype(jnp.bfloat16))
-            blocks.append(jnp.concatenate(tiles, axis=1))
+            for j in range(0, length, 128):
+                tiles.append(jnp.where(index == lane + (first + j), 1.0, 0.0).astype(jnp.bfloat16))
+            blocks.append(jnp.concatenate(tiles, axis=1) if len(tiles) > 1 else tiles[0])
         return jnp.concatenate(blocks, axis=0)
 
     for start in range(0, out_ref.shape[0], EDGE_BLOCK):
-        total = dot(selection(start, 0, 3 * rows), near_ref[...])
+        near = dot(selection(start, core * (2 * rows), rows), beside_ref[...])
+        total = dot(selection(start, rows, rows), here_ref[...])
         if start == 0:
-            finish(copies[4:])
+            finish(copies[3:])
         total = total + dot(selection(start, 3 * rows, coarse_ref.shape[0]), coarse_ref[...])
-        out_ref[start : start + EDGE_BLOCK, :] = total.astype(jnp.bfloat16)
+        block = slice(start, start + EDGE_BLOCK)
+        low = near[:, :half] + jnp.where(core == 0, total, 0.0)
+        high = near[:, half:] + jnp.where(core == 0, 0.0, total)
+        out_ref[block, :half] = low.astype(jnp.bfloat16)
+        out_ref[block, half:] = high.astype(jnp.bfloat16)
     finish(ready_copies)
 
 
-def gathered(ready, index, below, here, above, coarse):
+def gathered(scalars, ready, index, rows, beside, coarse):
     slots = index.size
-    rows, width = here.shape
-    table = 3 * rows + coarse.shape[0]
+    node_rows, width = rows.shape
+    half = width // 2
+    table = 3 * node_rows + coarse.shape[0]
     n = len(ready)
     return kernel_call(
         functools.partial(gather_kernel, n),
         "gather_senders",
         [shape((slots, width)), *[shape(a.shape, a.dtype) for a in ready]],
-        (index, below, here, above, coarse, *ready),
-        [HBM] * 4 + [ANY] + [HBM] * n,
+        (scalars, index, rows, beside, coarse, *ready),
+        [SMEM] + [HBM] * 3 + [ANY] + [HBM] * n,
         [VMEM] * (1 + n),
-        held([index, shape((3 * rows, width)), coarse])
-        + [pltpu.SemaphoreType.DMA((5,)), pltpu.SemaphoreType.DMA((n,))],
-        2 * slots * width * table,
+        held([index, shape((node_rows, half)), beside, coarse])
+        + [pltpu.SemaphoreType.DMA((4,)), pltpu.SemaphoreType.DMA((n,))],
+        2 * slots * half * table,
     )
 
 
@@ -284,8 +291,8 @@
     sent_a_ref, sent_b_ref, before_ref, weights_ref, incidence_ref, small_ref = refs[:6]
     edges_ref, nodes_ref, outs, refs = refs[6], refs[7], refs[8 : 8 + n_out], refs[8 + n_out :]
     edge_out_ref, node_out_ref, hidden_ref, mlp_ref, vectors_ref, out_sems = refs
-    half = sent_a_ref.shape[1]
-    width = 2 * half
+    width = sent_a_ref.shape[1]
+    half = width // 2
     first = scalar_ref[0] == 0
     count = scalar_ref[1]
     sent_out = []
@@ -307,10 +314,7 @@
     total = None
     for start in range(0, slots, UPDATE_BLOCK):
         here = slice(start, start + UPDATE_BLOCK)
-        sent_a, sent_b = sent_a_ref[here, :], sent_b_ref[here, :]
-        low = jnp.where(first, sent_a, sent_b)
-        high = jnp.where(first, sent_b, sent_a)
-        sent = jnp.concatenate([low, high], axis=1)
+        sent = sent_a_ref[here, :] + sent_b_ref[here, :]
         mlp_ref[...] = dot(weights_ref[0], sent, ((1,), (1,)))
         for row in range(0, width, ROWS):
             rows = slice(row, row + ROWS)
@@ -359,20 +363,21 @@
     else:
         node_out_ref[...] = new
         send(node_out_ref, outs[1])
-        store_rows(mine, *outs[2:])
+        rows = new.T
+        store_rows(rows, jnp.where(first, rows[:, :half], rows[:, half:]), *outs[2:])
     finish(sent_out)
 
 
 def updated_graph(last_layer, scalars, sent, ready, copies):
     slots = ready[0].shape[1]
     node_rows = ready[5].shape[1]
-    half = sent[0].shape[1]
-    width = 2 * half
+    width = sent[0].shape[1]
+    half = width // 2
     out_width = half if last_layer else width
     out_shape = [shape((out_width, slots)), shape((out_width, node_rows))]
     out_specs = [HBM, HBM]
     if not last_layer:
-        out_shape += [shape((node_rows, half)), shape((copies, node_rows // 8, half))]
+        out_shape += [shape((node_rows, width)), shape((copies, node_rows // 8, half))]
         out_specs = [HBM, HBM, VMEM, VMEM]
     n_out = len(out_shape)
     return kernel_call(
@@ -413,15 +418,16 @@
 
 def exchanged(rows, copies, others=()):
     size = lax.axis_size(PATCH)
-    up = [(i, (i + 1) % size) for i in range(size)]
-    down = [(j, i) for i, j in up]
-    below, above = lax.ppermute(rows, PATCH, up), lax.ppermute(rows, PATCH, down)
+    pairs = []
+    for i in range(size):
+        pairs += [(2 * i, (i + 1) % size * 2), (2 * i + 1, (i - 1) % size * 2 + 1)]
+    beside = lax.ppermute(rows, (*PATCH, "width"), pairs)
     column = lax.all_to_all(copies, Z, split_axis=0, concat_axis=0, tiled=True)
-    column = column.reshape(-1, rows.shape[1])
+    column = column.reshape(-1, copies.shape[2])
     column, others = lax.optimization_barrier((column, others))
     plane = copied(column, lax.axis_size(PLANE))
     coarse = lax.all_to_all(plane, PLANE, split_axis=0, concat_axis=0, tiled=True)
-    return (below, rows, above, coarse.reshape(-1, rows.shape[1])), others
+    return (rows, beside, coarse.reshape(-1, copies.shape[2])), others
 
 
 def on_device(
@@ -494,6 +500,12 @@
     edges = (edge_latents, from_other(edge_latents))
     nodes = (node_latents, from_other(node_latents))
     others = (weights[1], weights[5], edges[1], index, receiver)
+    other_rows = from_other(rows)
+    rows = jnp.where(
+        lax.axis_index("width") == 0,
+        jnp.concatenate([rows, other_rows], axis=1),
+        jnp.concatenate([other_rows, rows], axis=1),
+    )
     table, others = exchanged(rows, copies, others)
     weights[1], weights[5], other_edges, index, receiver = others
     edges = (edges[0], other_edges)
@@ -501,7 +513,7 @@
         last_layer = layer == layers - 1
         ready = prepared(layer, scalars, edges, receiver, nodes, weights)
         table, ready = lax.optimization_barrier((table, ready))
-        sent, *ready = gathered(ready, index, *table)
+        sent, *ready = gathered(scalars, ready, index, *table)
         sent = (sent, from_other(sent))
         results = updated_graph(last_layer, scalars, sent, ready, columns)
         if not last_layer:

time: 103 us -> 103 us (level)
  Pallas kernels: 33 us -> 34.6 us
  waiting for transfers between devices: 13.3 us -> 14.8 us
  blocking collectives: 10.8 us -> 9.51 us
  local copies, waits for them, and re-layouts: 1.36 us -> 0.22 us
    pallas_call x9, Pallas kernels: 33 us -> 34.6 us  [kernel_call(): pl.pallas_call(body, in_specs=in_specs, out_specs=out_specs, out_shape=ou...]
    ppermute x9 -> x10, waiting for transfers between devices: 3.09 us -> 4.59 us  [from_other(): return lax.ppermute(a, 'width', [(0, 1), (1, 0)])]
    all_to_all x1, blocking collectives: 10.8 us -> 9.51 us  [exchanged(): column = lax.all_to_all(copies, Z, split_axis=0, concat_axis=0, tiled=True)]
    unnamed x42 -> x34, local copies, waits for them, and re-layouts: 1.3 us -> 0.16 us
    ppermute x9 -> x10, starting transfers between devices: 12.8 us -> 12.1 us  [from_other(): return lax.ppermute(a, 'width', [(0, 1), (1, 0)])]
    ppermute x4 -> x2, waiting for transfers between devices: 3.87 us -> 3.96 us  [exchanged(): beside = lax.ppermute(rows, (*PATCH, 'width'), pairs)]
    ppermute x4 -> x2, starting transfers between devices: 9.07 us -> 9.15 us  [exchanged(): beside = lax.ppermute(rows, (*PATCH, 'width'), pairs)]
  transfers between devices with their start and end apart: 16 -> 15, of which waited for: 7 -> 6; matrix products, arithmetic and copies ran while one was open for 3% -> 3% of each run, Pallas kernels for 14% -> 14%
where the time goes in v7:
time: 103 us; the launch traced here: 102 us
  starting transfers between devices  38.7 us (38%)
  Pallas kernels  34.6 us (34%)
  waiting for transfers between devices  14.8 us (14%)
  blocking collectives  9.51 us (9%)
  other arithmetic  2.67 us (3%)
  between operations  1.85 us (2%)
    pallas_call x9, Pallas kernels, kernel_call(): pl.pallas_call(body, in_specs=in_specs, out_specs=out_specs, out_shape=ou...  34.6 us
    ppermute x10, starting transfers between devices, from_other(): return lax.ppermute(a, 'width', [(0, 1), (1, 0)])  12.1 us
    all_to_all x2, starting transfers between devices, exchanged(): lax.all_to_all(plane, PLANE, split_axis=0, concat_axis=0, tiled=True)  10.9 us
    all_to_all x1, blocking collectives, exchanged(): column = lax.all_to_all(copies, Z, split_axis=0, concat_axis=0, tiled=True)  9.51 us
    ppermute x2, starting transfers between devices, exchanged(): beside = lax.ppermute(rows, (*PATCH, 'width'), pairs)  9.15 us
    all_to_all x1, starting transfers between devices, exchanged(): column = lax.all_to_all(copies, Z, split_axis=0, concat_axis=0, tiled=True)  6.48 us
    ppermute x10, waiting for transfers between devices, from_other(): return lax.ppermute(a, 'width', [(0, 1), (1, 0)])  4.59 us
    all_to_all x1, waiting for transfers between devices, exchanged(): column = lax.all_to_all(copies, Z, split_axis=0, concat_axis=0, tiled=True)  4.57 us
  transfers between devices with their start and end apart: 15, of which 6 were waited for; matrix products, arithmetic and copies ran while one was open for 3% of the time, Pallas kernels for 14%

profile of v7, /device:TPU:1, one launch (start us, length us, event | category | flops | bytes accessed | tf_op | source)
XLA Modules:
  0.0 102.4 jit_solution(5507863062591121909)
XLA Ops:
  0.6 0.0 copy-start.5
  0.6 0.0 copy-start.2
  0.7 3.3 %collective-permute-start = (bf16[2,256,1536]{2,1,0:T(8,128)(2,1)}, bf16[2,256,1536]{2,1,0:T(8,128)(2,1)S(1)}, u32[]{:S(2)}, u32[]{:S(2)}) collective-permute-start(bf16[2,256,1536]{2,1,0:T(8,128)(2,1)} %refs_1_.3), channel_id=1, source_target_pairs={{0,1},{1,0},{2,3},{3,2},{4,5},{5,4},{6,7},{7,6},{8,9},{9,8},{10,11... | collective-permute-start | bytes 4718600 | tf_op jit(solution)/shard_map/ppermute | solution.py:404
  4.1 0.1 collective-permute-start.1
  4.2 0.4 collective-permute-start.2
  4.6 1.5 %node_rows.1 = (bf16[128,256]{1,0:T(8,128)(2,1)S(1)}, bf16[8,16,256]{2,1,0:T(8,128)(2,1)}) custom-call(bf16[256,128]{1,0:T(8,128)(2,1)} %refs_13_.1), custom_call_target="tpu_custom_call" | custom-call | bytes 4194304 | tf_op jit(solution)/shard_map/node_rows/pallas_call | solution.py:61
  6.1 6.5 %all-to-all-start = ((bf16[8,16,256]{2,1,0:T(8,128)(2,1)}), bf16[8,16,256]{2,1,0:T(8,128)(2,1)S(1)}, u32[]{:S(2)}, u32[]{:S(2)}) async-start(bf16[8,16,256]{2,1,0:T(8,128)(2,1)} %get-tuple-element.58), calls=%async_computation | async-start | bytes 131072 | tf_op jit(solution)/shard_map/all_to_all | solution.py:425
  12.6 1.3 %broadcast_subtract_fusion = s32[1024]{0:T(1024)} fusion(s32[1024]{0:T(1024)} %param.20, s32[]{:T(128)S(6)} %mul.28), kind=kLoop, calls=%fused_computation.27 | loop fusion | flops 1024 | bytes 8196 | tf_op jit(solution)/shard_map/sub | solution.py:498
  13.9 1.3 %fusion.9.index_in = s32[8,128]{1,0:T(8,128)} fusion(s32[1024]{0:T(1024)} %param.19, s32[]{:T(128)S(6)} %select_n.44, s32[]{:T(128)S(6)} %select_n.43, s32[]{:T(128)S(6)} %add.50), kind=kLoop, calls=%fused_computation.19 | loop fusion | flops 50176 | bytes 8204 | tf_op jit(solution)/shard_map/reshape | solution.py:497
  15.2 4.6 %all-to-all-done = bf16[8,16,256]{2,1,0:T(8,128)(2,1)S(1)} async-done(((bf16[8,16,256]{2,1,0:T(8,128)(2,1)}), bf16[8,16,256]{2,1,0:T(8,128)(2,1)S(1)}, u32[]{:S(2)}, u32[]{:S(2)}) %all-to-all-start) | async-done | bytes 65568 | tf_op jit(solution)/shard_map/all_to_all | solution.py:425
  19.7 0.0 collective-permute-done.2.refs_12_
  19.7 0.0 collective-permute-done.1.refs_6_
  19.8 0.0 collective-permute-done.refs_2_
  19.8 1.3 %copies.2 = bf16[16,128,256]{2,1,0:T(8,128)(2,1)} custom-call(bf16[128,256]{1,0:T(8,128)(2,1)S(1)} %bitcast.10), custom_call_target="tpu_custom_call" | custom-call | bytes 4194304 | tf_op jit(solution)/shard_map/copies/pallas_call | solution.py:61
  21.1 6.8 %all-to-all-start.1 = ((bf16[16,128,256]{2,1,0:T(8,128)(2,1)}), bf16[16,128,256]{2,1,0:T(8,128)(2,1)S(1)}, u32[]{:S(2)}, u32[]{:S(2)}) async-start(bf16[16,128,256]{2,1,0:T(8,128)(2,1)} %copies.2), calls=%async_computation.1 | async-start | bytes 2097152 | tf_op jit(solution)/shard_map/all_to_all | solution.py:429
  27.9 2.0 %collective-permute-start.5 = (bf16[2,256,512]{2,1,0:T(8,128)(2,1)S(1)}, bf16[2,256,512]{2,1,0:T(8,128)(2,1)}, u32[]{:S(2)}, u32[]{:S(2)}) collective-permute-start(bf16[2,256,512]{2,1,0:T(8,128)(2,1)S(1)} %copy-done.2), channel_id=1, source_target_pairs={{0,1},{1,0},{2,3},{3,2},{4,5},{5,4},{6,7},{7,6},{8,9},{9,8},{10,11... | collective-permute-start | bytes 1572872 | tf_op jit(solution)/shard_map/ppermute | solution.py:404
  29.8 0.1 collective-permute-start.6
  29.9 0.4 collective-permute-start.3
  30.4 0.1 collective-permute-start.8
  30.6 0.0 copy-start.6
  30.6 0.5 collective-permute-start.7
  31.8 0.0 collective-permute-done.3
  31.9 4.7 %collective-permute-start.4 = (bf16[128,512]{1,0:T(8,128)(2,1)S(1)}, bf16[128,512]{1,0:T(8,128)(2,1)S(1)}, u32[]{:S(2)}, u32[]{:S(2)}) collective-permute-start(bf16[128,512]{1,0:T(8,128)(2,1)S(1)} %maximum_select_fusion.rows_in), channel_id=1, source_target_pairs={{0,2},{1,255},{2,4},{3,1},{4,6},{5,3},{6,8},{7,5},{8,10},{9,7},{10... | collective-permute-start | bytes 393224 | tf_op jit(solution)/shard_map/ppermute | solution.py:424
  36.5 0.1 pad_add_fusion.scalar_ref
  36.6 0.0 collective-permute-done.7.refs_10_
  36.6 0.0 collective-permute-done.8.refs_14_
  36.6 0.0 collective-permute-done.5.refs_4_
  36.6 0.0 collective-permute-done.6.refs_8_
  36.7 7.0 %prepare_layer.2 = (f32[512,1024]{1,0:T(8,128)}, bf16[5,512,512]{2,1,0:T(8,128)(2,1)}, bf16[128,1024]{1,0:T(8,128)(2,1)}, f32[512,128]{1,0:T(8,128)}, bf16[512,1...) custom-call(s32[2]{0:T(128)S(1)} %pad_add_fusion.scalar_ref, s32[1,1024]{1,0:T(1,128)} %bitcast.12, ...), custom_call_target="tpu_custom_call" | custom-call | flops 671088640 | bytes 4194304 | tf_op jit(solution)/shard_map/prepare_layer/pallas_call | solution.py:61
  43.6 0.0 collective-permute-done.4.beside_in
  43.7 0.0 copy-start.7
  43.7 0.6 all-to-all-done.1
  44.2 0.1 copy-done.7
  44.3 3.8 %gather_senders.2 = (bf16[1024,512]{1,0:T(8,128)(2,1)S(1)}, f32[512,1024]{1,0:T(8,128)S(1)}, bf16[5,512,512]{2,1,0:T(8,128)(2,1)S(1)}, bf16[128,1024]{1,0:T(8,12...) custom-call(s32[2]{0:T(128)S(1)} %pad_add_fusion.scalar_ref, ...), custom_call_target="tpu_custom_call" | custom-call | flops 1275068416 | bytes 4194304 | tf_op jit(solution)/shard_map/gather_senders/pallas_call | solution.py:61
  48.1 2.2 %collective-permute-start.9 = (bf16[1024,512]{1,0:T(8,128)(2,1)S(1)}, bf16[1024,512]{1,0:T(8,128)(2,1)S(1)}, u32[]{:S(2)}, u32[]{:S(2)}) collective-permute-start(bf16[1024,512]{1,0:T(8,128)(2,1)S(1)} %get-tuple-element.81.refs_0_), channel_id=1, source_target_pairs={{0,1},{1,0},{2,3},{3,2},{4,5},{5,4},{6,7},{7,6},{8,9},{9,8},{10,11... | collective-permute-start | bytes 3145736 | tf_op jit(solution)/shard_map/ppermute | solution.py:404
  50.4 2.3 %collective-permute-done.9.refs_1_ = bf16[1024,512]{1,0:T(8,128)(2,1)S(1)} collective-permute-done((bf16[1024,512]{1,0:T(8,128)(2,1)S(1)}, bf16[1024,512]{1,0:T(8,128)(2,1)S(1)}, u32[]{:S(2)}, u32[]{:S(2)}) %collective-permute-start.9) | collective-permute-done | bytes 1048608 | tf_op jit(solution)/shard_map/ppermute | solution.py:404
  52.7 5.3 %update_graph.2 = (bf16[512,1024]{1,0:T(8,128)(2,1)}, bf16[512,128]{1,0:T(8,128)(2,1)}, bf16[128,512]{1,0:T(8,128)(2,1)S(1)}, bf16[8,16,256]{2,1,0:T(8,128)(2,1)S(1)}) custom-call(s32[2]{0:T(128)S(1)} %pad_add_fusion.scalar_ref, bf16[1024,512]{1,0:T(8,128)(2,1)S(1)} %get-tuple-element.81.refs_0_, bf16[1024,512]{1,0:T(8,128)(2,1)S(1)} %collective-permute-done.9.refs_1_, ...), custom_call_target="tpu_custom_call" | custom-call | flops 1207959552 | bytes 4194304 | tf_op jit(solution)/shard_map/update_graph/pallas_call | solution.py:61
  58.0 9.5 %all_to_all.20 = bf16[8,16,256]{2,1,0:T(8,128)(2,1)S(1)} all-to-all(bf16[8,16,256]{2,1,0:T(8,128)(2,1)S(1)} %get-tuple-element.89), channel_id=1, replica_groups=mesh['patch_0'=8,'patch_1'=4,'patch_2'=4,'width'=2] {'patch_0'}, dimensions={0} | all-to-all | bytes 131072 | tf_op jit(solution)/shard_map/all_to_all | solution.py:425
  67.5 1.1 %copies.3 = bf16[16,128,256]{2,1,0:T(8,128)(2,1)} custom-call(bf16[128,256]{1,0:T(8,128)(2,1)S(1)} %bitcast.11), custom_call_target="tpu_custom_call" | custom-call | bytes 4194304 | tf_op jit(solution)/shard_map/copies/pallas_call | solution.py:61
  68.6 4.2 %all-to-all-start.3 = ((bf16[16,128,256]{2,1,0:T(8,128)(2,1)}), bf16[16,128,256]{2,1,0:T(8,128)(2,1)S(1)}, u32[]{:S(2)}, u32[]{:S(2)}) async-start(bf16[16,128,256]{2,1,0:T(8,128)(2,1)} %copies.3), calls=%async_computation.3 | async-start | bytes 2097152 | tf_op jit(solution)/shard_map/all_to_all | solution.py:429
  72.8 4.5 %collective-permute-start.10 = (bf16[128,512]{1,0:T(8,128)(2,1)S(1)}, bf16[128,512]{1,0:T(8,128)(2,1)S(1)}, u32[]{:S(2)}, u32[]{:S(2)}) collective-permute-start(bf16[128,512]{1,0:T(8,128)(2,1)S(1)} %get-tuple-element.96.rows_in), channel_id=1, source_target_pairs={{0,2},{1,255},{2,4},{3,1},{4,6},{5,3},{6,8},{7,5},{8,10},{9,7},{10... | collective-permute-start | bytes 393224 | tf_op jit(solution)/shard_map/ppermute | solution.py:424
  77.3 6.2 %prepare_layer.3 = (f32[512,1024]{1,0:T(8,128)}, bf16[5,512,512]{2,1,0:T(8,128)(2,1)}, bf16[128,1024]{1,0:T(8,128)(2,1)}, f32[512,128]{1,0:T(8,128)}) custom-call(s32[2]{0:T(128)S(1)} %pad_add_fusion.scalar_ref, s32[1,1024]{1,0:T(1,128)} %bitcast.13, bf16[2,256,1536]{2,1,0:T(8,128)(2,1)} %refs_1_.3, bf16[2,256,1536]{2,1,0:T(8,128)(2,1)} %copy-done.1, ...), custom_call_target="tpu_custom_call" | custom-call | flops 671088640 | bytes 4194304 | tf_op jit(solution)/shard_map/prepare_layer/pallas_call | solution.py:61
  83.5 4.0 %collective-permute-done.10.beside_in = bf16[128,512]{1,0:T(8,128)(2,1)S(1)} collective-permute-done((bf16[128,512]{1,0:T(8,128)(2,1)S(1)}, bf16[128,512]{1,0:T(8,128)(2,1)S(1)}, u32[]{:S(2)}, u32[]{:S(2)}) %collective-permute-start.10) | collective-permute-done | bytes 131104 | tf_op jit(solution)/shard_map/ppermute | solution.py:424
  87.5 1.1 %all-to-all-done.3 = bf16[16,128,256]{2,1,0:T(8,128)(2,1)S(1)} async-done(((bf16[16,128,256]{2,1,0:T(8,128)(2,1)}), bf16[16,128,256]{2,1,0:T(8,128)(2,1)S(1)}, u32[]{:S(2)}, u32[]{:S(2)}) %all-to-all-start.3) | async-done | bytes 1048608 | tf_op jit(solution)/shard_map/all_to_all | solution.py:429
  88.5 3.8 %gather_senders.3 = (bf16[1024,512]{1,0:T(8,128)(2,1)S(1)}, f32[512,1024]{1,0:T(8,128)S(1)}, bf16[5,512,512]{2,1,0:T(8,128)(2,1)S(1)}, bf16[128,1024]{1,0:T(8,12...) custom-call(s32[2]{0:T(128)S(1)} %pad_add_fusion.scalar_ref, ...), custom_call_target="tpu_custom_call" | custom-call | flops 1275068416 | bytes 4194304 | tf_op jit(solution)/shard_map/gather_senders/pallas_call | solution.py:61
  92.4 3.0 %collective-permute-start.11 = (bf16[1024,512]{1,0:T(8,128)(2,1)S(1)}, bf16[1024,512]{1,0:T(8,128)(2,1)S(1)}, u32[]{:S(2)}, u32[]{:S(2)}) collective-permute-start(bf16[1024,512]{1,0:T(8,128)(2,1)S(1)} %get-tuple-element.105.refs_0_), channel_id=1, source_target_pairs={{0,1},{1,0},{2,3},{3,2},{4,5},{5,4},{6,7},{7,6},{8,9},{9,8},{10,11... | collective-permute-start | bytes 3145736 | tf_op jit(solution)/shard_map/ppermute | solution.py:404
  95.3 2.3 %collective-permute-done.11.refs_1_ = bf16[1024,512]{1,0:T(8,128)(2,1)S(1)} collective-permute-done((bf16[1024,512]{1,0:T(8,128)(2,1)S(1)}, bf16[1024,512]{1,0:T(8,128)(2,1)S(1)}, u32[]{:S(2)}, u32[]{:S(2)}) %collective-permute-start.11) | collective-permute-done | bytes 1048608 | tf_op jit(solution)/shard_map/ppermute | solution.py:404
  97.6 4.6 %update_graph.3 = (bf16[256,1024]{1,0:T(8,128)(2,1)}, bf16[256,128]{1,0:T(8,128)(2,1)}) custom-call(s32[2]{0:T(128)S(1)} %pad_add_fusion.scalar_ref, bf16[1024,512]{1,0:T(8,128)(2,1)S(1)} %get-tuple-element.105.refs_0_, bf16[1024,512]{1,0:T(8,128)(2,1)S(1)} %collective-permute-done.11.refs_1_, f32[512,1024]{1,0:T(8,128)S(1)} %get-tuple-element.106.refs_2_, ...), custom_call_target="tpu_custom_call" | custom-call | flops 1207959552 | bytes 4194304 | tf_op jit(solution)/shard_map/update_graph/pallas_call | solution.py:61
  (39 shorter events, 0.2 us)
Async XLA Ops:
  0.6 29.7 %copy-start.5 = (bf16[256,128]{1,0:T(8,128)(2,1)S(1)}, bf16[256,128]{1,0:T(8,128)(2,1)}, u32[]{:S(2)}) copy-start(bf16[256,128]{1,0:T(8,128)(2,1)} %refs_13_.1) | copy-start | bytes 196612
  0.6 27.2 %copy-start.2 = (bf16[2,256,512]{2,1,0:T(8,128)(2,1)S(1)}, bf16[2,256,512]{2,1,0:T(8,128)(2,1)}, u32[]{:S(2)}) copy-start(bf16[2,256,512]{2,1,0:T(8,128)(2,1)} %refs_3_.3) | copy-start | bytes 1572868
  0.7 29.8 %copy-start.9 = (f32[2,256]{1,0:T(2,128)S(1)}, f32[2,256]{1,0:T(2,128)}, u32[]{:S(2)}) copy-start(f32[2,256]{1,0:T(2,128)} %param.23) | copy-start | bytes 6148
  0.7 29.8 %copy-start.10 = (f32[2,256]{1,0:T(2,128)S(1)}, f32[2,256]{1,0:T(2,128)}, u32[]{:S(2)}) copy-start(f32[2,256]{1,0:T(2,128)} %param.25) | copy-start | bytes 6148
  0.7 29.8 %copy-start.11 = (f32[2,256]{1,0:T(2,128)S(1)}, f32[2,256]{1,0:T(2,128)}, u32[]{:S(2)}) copy-start(f32[2,256]{1,0:T(2,128)} %param.26) | copy-start | bytes 6148
  0.7 29.8 %copy-start.12 = (f32[2,256]{1,0:T(2,128)S(1)}, f32[2,256]{1,0:T(2,128)}, u32[]{:S(2)}) copy-start(f32[2,256]{1,0:T(2,128)} %param.27) | copy-start | bytes 6148
  0.7 29.8 %copy-start.13 = (f32[2,256]{1,0:T(2,128)S(1)}, f32[2,256]{1,0:T(2,128)}, u32[]{:S(2)}) copy-start(f32[2,256]{1,0:T(2,128)} %param.29) | copy-start | bytes 6148
  0.7 29.8 %copy-start.14 = (f32[2,256]{1,0:T(2,128)S(1)}, f32[2,256]{1,0:T(2,128)}, u32[]{:S(2)}) copy-start(f32[2,256]{1,0:T(2,128)} %param.31) | copy-start | bytes 6148
  0.7 29.8 %copy-start.15 = (f32[2,256]{1,0:T(2,128)S(1)}, f32[2,256]{1,0:T(2,128)}, u32[]{:S(2)}) copy-start(f32[2,256]{1,0:T(2,128)} %param.32) | copy-start | bytes 6148
  0.7 29.8 %copy-start.16 = (f32[2,256]{1,0:T(2,128)S(1)}, f32[2,256]{1,0:T(2,128)}, u32[]{:S(2)}) copy-start(f32[2,256]{1,0:T(2,128)} %param.33) | copy-start | bytes 6148
  0.7 19.0 %collective-permute-start = (bf16[2,256,1536]{2,1,0:T(8,128)(2,1)}, bf16[2,256,1536]{2,1,0:T(8,128)(2,1)S(1)}, u32[]{:S(2)}, u32[]{:S(2)}) collective-permute-start(bf16[2,256,1536]{2,1,0:T(8,128)(2,1)} %refs_1_.3), channel_id=1, source_target_pairs={{0,1},{1,0},{2,3},{3,2},{4,5},{5,4},{6,7},{7,6},{8,9},{9,8},{10,11... | collective-permute-start | bytes 4718600 | tf_op jit(solution)/shard_map/ppermute | solution.py:404
  4.1 15.7 %collective-permute-start.1 = (bf16[2,256,1024]{2,1,0:T(8,128)(2,1)}, bf16[2,256,1024]{2,1,0:T(8,128)(2,1)}, u32[]{:S(2)}, u32[]{:S(2)}) collective-permute-start(bf16[2,256,1024]{2,1,0:T(8,128)(2,1)} %refs_5_.3), channel_id=1, source_target_pairs={{0,1},{1,0},{2,3},{3,2},{4,5},{5,4},{6,7},{7,6},{8,9},{9,8},{10,11... | collective-permute-start | bytes 3145736 | tf_op jit(solution)/shard_map/ppermute | solution.py:404
  4.2 15.6 %collective-permute-start.2 = (bf16[256,1024]{1,0:T(8,128)(2,1)}, bf16[256,1024]{1,0:T(8,128)(2,1)S(1)}, u32[]{:S(2)}, u32[]{:S(2)}) collective-permute-start(bf16[256,1024]{1,0:T(8,128)(2,1)} %refs_11_.1), channel_id=1, source_target_pairs={{0,1},{1,0},{2,3},{3,2},{4,5},{5,4},{6,7},{7,6},{8,9},{9,8},{10,11... | collective-permute-start | bytes 1572872 | tf_op jit(solution)/shard_map/ppermute | solution.py:404
  6.1 13.6 %all-to-all-start = ((bf16[8,16,256]{2,1,0:T(8,128)(2,1)}), bf16[8,16,256]{2,1,0:T(8,128)(2,1)S(1)}, u32[]{:S(2)}, u32[]{:S(2)}) async-start(bf16[8,16,256]{2,1,0:T(8,128)(2,1)} %get-tuple-element.58), calls=%async_computation | async-start | bytes 131072 | tf_op jit(solution)/shard_map/all_to_all | solution.py:425
  19.7 1.4 %copy-start.4 = (bf16[256,1024]{1,0:T(8,128)(2,1)}, bf16[256,1024]{1,0:T(8,128)(2,1)S(1)}, u32[]{:S(2)}) copy-start(bf16[256,1024]{1,0:T(8,128)(2,1)S(1)} %collective-permute-done.2.refs_12_) | copy-start | bytes 1572868
  19.8 16.9 %copy-start.1 = (bf16[2,256,1536]{2,1,0:T(8,128)(2,1)}, bf16[2,256,1536]{2,1,0:T(8,128)(2,1)S(1)}, u32[]{:S(2)}) copy-start(bf16[2,256,1536]{2,1,0:T(8,128)(2,1)S(1)} %collective-permute-done.refs_2_) | copy-start | bytes 4718596
  21.1 23.1 %all-to-all-start.1 = ((bf16[16,128,256]{2,1,0:T(8,128)(2,1)}), bf16[16,128,256]{2,1,0:T(8,128)(2,1)S(1)}, u32[]{:S(2)}, u32[]{:S(2)}) async-start(bf16[16,128,256]{2,1,0:T(8,128)(2,1)} %copies.2), calls=%async_computation.1 | async-start | bytes 2097152 | tf_op jit(solution)/shard_map/all_to_all | solution.py:429
  27.9 8.8 %collective-permute-start.5 = (bf16[2,256,512]{2,1,0:T(8,128)(2,1)S(1)}, bf16[2,256,512]{2,1,0:T(8,128)(2,1)}, u32[]{:S(2)}, u32[]{:S(2)}) collective-permute-start(bf16[2,256,512]{2,1,0:T(8,128)(2,1)S(1)} %copy-done.2), channel_id=1, source_target_pairs={{0,1},{1,0},{2,3},{3,2},{4,5},{5,4},{6,7},{7,6},{8,9},{9,8},{10,11... | collective-permute-start | bytes 1572872 | tf_op jit(solution)/shard_map/ppermute | solution.py:404
  29.8 6.8 %collective-permute-start.6 = (bf16[2,256,512]{2,1,0:T(8,128)(2,1)}, bf16[2,256,512]{2,1,0:T(8,128)(2,1)}, u32[]{:S(2)}, u32[]{:S(2)}) collective-permute-start(bf16[2,256,512]{2,1,0:T(8,128)(2,1)} %refs_7_.3), channel_id=1, source_target_pairs={{0,1},{1,0},{2,3},{3,2},{4,5},{5,4},{6,7},{7,6},{8,9},{9,8},{10,11... | collective-permute-start | bytes 1572872 | tf_op jit(solution)/shard_map/ppermute | solution.py:404
  29.9 1.9 %collective-permute-start.3 = (bf16[128,256]{1,0:T(8,128)(2,1)S(1)}, bf16[128,256]{1,0:T(8,128)(2,1)S(1)}, u32[]{:S(2)}, u32[]{:S(2)}) collective-permute-start(bf16[128,256]{1,0:T(8,128)(2,1)S(1)} %get-tuple-element.60), channel_id=1, source_target_pairs={{0,1},{1,0},{2,3},{3,2},{4,5},{5,4},{6,7},{7,6},{8,9},{9,8},{10,11... | collective-permute-start | bytes 196616 | tf_op jit(solution)/shard_map/ppermute | solution.py:404
  30.4 6.3 %collective-permute-start.8 = (bf16[256,128]{1,0:T(8,128)(2,1)S(1)}, bf16[256,128]{1,0:T(8,128)(2,1)}, u32[]{:S(2)}, u32[]{:S(2)}) collective-permute-start(bf16[256,128]{1,0:T(8,128)(2,1)S(1)} %copy-done.5), channel_id=1, source_target_pairs={{0,1},{1,0},{2,3},{3,2},{4,5},{5,4},{6,7},{7,6},{8,9},{9,8},{10,11... | collective-permute-start | bytes 196616 | tf_op jit(solution)/shard_map/ppermute | solution.py:404
  30.6 6.0 %copy-start.6 = (f32[2,8,256]{2,1,0:T(8,128)}, f32[2,8,256]{2,1,0:T(8,128)S(1)}, u32[]{:S(2)}) copy-start(f32[2,8,256]{2,1,0:T(8,128)S(1)} %stack.43.refs_9_) | copy-start | bytes 49156
  30.6 6.0 %collective-permute-start.7 = (f32[2,8,256]{2,1,0:T(8,128)S(1)}, f32[2,8,256]{2,1,0:T(8,128)}, u32[]{:S(2)}, u32[]{:S(2)}) collective-permute-start(f32[2,8,256]{2,1,0:T(8,128)S(1)} %stack.43.refs_9_), channel_id=1, source_target_pairs={{0,1},{1,0},{2,3},{3,2},{4,5},{5,4},{6,7},{7,6},{8,9},{9,8},{10,11... | collective-permute-start | bytes 49160 | tf_op jit(solution)/shard_map/ppermute | solution.py:404
  31.8 11.8 %copy-start.3 = (bf16[128,512]{1,0:T(8,128)(2,1)}, bf16[128,512]{1,0:T(8,128)(2,1)S(1)}, u32[]{:S(2)}) copy-start(bf16[128,512]{1,0:T(8,128)(2,1)S(1)} %maximum_select_fusion.rows_in) | copy-start | bytes 393220
  31.9 11.8 %collective-permute-start.4 = (bf16[128,512]{1,0:T(8,128)(2,1)S(1)}, bf16[128,512]{1,0:T(8,128)(2,1)S(1)}, u32[]{:S(2)}, u32[]{:S(2)}) collective-permute-start(bf16[128,512]{1,0:T(8,128)(2,1)S(1)} %maximum_select_fusion.rows_in), channel_id=1, source_target_pairs={{0,2},{1,255},{2,4},{3,1},{4,6},{5,3},{6,8},{7,5},{8,10},{9,7},{10... | collective-permute-start | bytes 393224 | tf_op jit(solution)/shard_map/ppermute | solution.py:424
  43.7 0.7 copy-start.7
  48.1 4.5 %collective-permute-start.9 = (bf16[1024,512]{1,0:T(8,128)(2,1)S(1)}, bf16[1024,512]{1,0:T(8,128)(2,1)S(1)}, u32[]{:S(2)}, u32[]{:S(2)}) collective-permute-start(bf16[1024,512]{1,0:T(8,128)(2,1)S(1)} %get-tuple-element.81.refs_0_), channel_id=1, source_target_pairs={{0,1},{1,0},{2,3},{3,2},{4,5},{5,4},{6,7},{7,6},{8,9},{9,8},{10,11... | collective-permute-start | bytes 3145736 | tf_op jit(solution)/shard_map/ppermute | solution.py:404
  58.0 25.5 %copy-start = (bf16[128,512]{1,0:T(8,128)(2,1)}, bf16[128,512]{1,0:T(8,128)(2,1)S(1)}, u32[]{:S(2)}) copy-start(bf16[128,512]{1,0:T(8,128)(2,1)S(1)} %get-tuple-element.96.rows_in) | copy-start | bytes 393220
  68.6 19.9 %all-to-all-start.3 = ((bf16[16,128,256]{2,1,0:T(8,128)(2,1)}), bf16[16,128,256]{2,1,0:T(8,128)(2,1)S(1)}, u32[]{:S(2)}, u32[]{:S(2)}) async-start(bf16[16,128,256]{2,1,0:T(8,128)(2,1)} %copies.3), calls=%async_computation.3 | async-start | bytes 2097152 | tf_op jit(solution)/shard_map/all_to_all | solution.py:429
  72.8 14.7 %collective-permute-start.10 = (bf16[128,512]{1,0:T(8,128)(2,1)S(1)}, bf16[128,512]{1,0:T(8,128)(2,1)S(1)}, u32[]{:S(2)}, u32[]{:S(2)}) collective-permute-start(bf16[128,512]{1,0:T(8,128)(2,1)S(1)} %get-tuple-element.96.rows_in), channel_id=1, source_target_pairs={{0,2},{1,255},{2,4},{3,1},{4,6},{5,3},{6,8},{7,5},{8,10},{9,7},{10... | collective-permute-start | bytes 393224 | tf_op jit(solution)/shard_map/ppermute | solution.py:424
  87.5 1.1 %copy-start.8 = (bf16[128,512]{1,0:T(8,128)(2,1)}, bf16[128,512]{1,0:T(8,128)(2,1)S(1)}, u32[]{:S(2)}) copy-start(bf16[128,512]{1,0:T(8,128)(2,1)S(1)} %collective-permute-done.10.beside_in) | copy-start | bytes 393220
  92.4 5.3 %collective-permute-start.11 = (bf16[1024,512]{1,0:T(8,128)(2,1)S(1)}, bf16[1024,512]{1,0:T(8,128)(2,1)S(1)}, u32[]{:S(2)}, u32[]{:S(2)}) collective-permute-start(bf16[1024,512]{1,0:T(8,128)(2,1)S(1)} %get-tuple-element.105.refs_0_), channel_id=1, source_target_pairs={{0,1},{1,0},{2,3},{3,2},{4,5},{5,4},{6,7},{7,6},{8,9},{9,8},{10,11... | collective-permute-start | bytes 3145736 | tf_op jit(solution)/shard_map/ppermute | solution.py:404

commit v8 on v7

--- a/solution.py
+++ b/solution.py
@@ -509,16 +509,17 @@
     table, others = exchanged(rows, copies, others)
     weights[1], weights[5], other_edges, index, receiver = others
     edges = (edges[0], other_edges)
+    ready = prepared(0, scalars, edges, receiver, nodes, weights)
+    table, ready = lax.optimization_barrier((table, ready))
     for layer in range(layers):
         last_layer = layer == layers - 1
-        ready = prepared(layer, scalars, edges, receiver, nodes, weights)
-        table, ready = lax.optimization_barrier((table, ready))
         sent, *ready = gathered(scalars, ready, index, *table)
         sent = (sent, from_other(sent))
         results = updated_graph(last_layer, scalars, sent, ready, columns)
         if not last_layer:
             edges, nodes = results[:1], results[1:2]
-            table, _ = exchanged(results[2], results[3])
+            ready = prepared(layer + 1, scalars, edges, receiver, nodes, weights)
+            table, ready = exchanged(results[2], results[3], ready)
     return (results[1], results[0])
 
 

time: 103 us -> 104 us (level)
  blocking collectives: 9.51 us -> 0 us
  waiting for transfers between devices: 14.8 us -> 20 us
  starting transfers between devices: 38.7 us -> 43.9 us
    all_to_all x1 -> x0, blocking collectives: 9.51 us -> none  [exchanged(): column = lax.all_to_all(copies, Z, split_axis=0, concat_axis=0, tiled=True)]
    ppermute x2, waiting for transfers between devices: 3.96 us -> 8.35 us  [exchanged(): beside = lax.ppermute(rows, (*PATCH, 'width'), pairs)]
    all_to_all x1 -> x2, starting transfers between devices: 6.48 us -> 9.85 us  [exchanged(): column = lax.all_to_all(copies, Z, split_axis=0, concat_axis=0, tiled=True)]
    ppermute x2, starting transfers between devices: 9.15 us -> 11 us  [exchanged(): beside = lax.ppermute(rows, (*PATCH, 'width'), pairs)]
    all_to_all x1 -> x2, waiting for transfers between devices: 4.57 us -> 5.35 us  [exchanged(): column = lax.all_to_all(copies, Z, split_axis=0, concat_axis=0, tiled=True)]
  transfers between devices with their start and end apart: 15 -> 16, of which waited for: 6 -> 7; matrix products, arithmetic and copies ran while one was open for 3% -> 3% of each run, Pallas kernels for 14% -> 14%
where the time goes in v8:
time: 104 us
  starting transfers between devices  43.9 us (42%)
  Pallas kernels  35.2 us (34%)
  waiting for transfers between devices  20 us (19%)
  other arithmetic  2.68 us (3%)
  between operations  1.86 us (2%)
    pallas_call x9, Pallas kernels, kernel_call(): pl.pallas_call(body, in_specs=in_specs, out_specs=out_specs, out_shape=ou...  35.2 us
    ppermute x10, starting transfers between devices, from_other(): return lax.ppermute(a, 'width', [(0, 1), (1, 0)])  12.1 us
    ppermute x2, starting transfers between devices, exchanged(): beside = lax.ppermute(rows, (*PATCH, 'width'), pairs)  11 us
    all_to_all x2, starting transfers between devices, exchanged(): lax.all_to_all(plane, PLANE, split_axis=0, concat_axis=0, tiled=True)  10.9 us
    all_to_all x2, starting transfers between devices, exchanged(): column = lax.all_to_all(copies, Z, split_axis=0, concat_axis=0, tiled=True)  9.85 us
    ppermute x2, waiting for transfers between devices, exchanged(): beside = lax.ppermute(rows, (*PATCH, 'width'), pairs)  8.35 us
    all_to_all x2, waiting for transfers between devices, exchanged(): column = lax.all_to_all(copies, Z, split_axis=0, concat_axis=0, tiled=True)  5.35 us
    ppermute x10, waiting for transfers between devices, from_other(): return lax.ppermute(a, 'width', [(0, 1), (1, 0)])  4.59 us
  transfers between devices with their start and end apart: 16, of which 7 were waited for; matrix products, arithmetic and copies ran while one was open for 3% of the time, Pallas kernels for 14%

profile of v8, /device:TPU:1, one launch (start us, length us, event | category | flops | bytes accessed | tf_op | source)
XLA Modules:
  0.0 103.8 jit_solution(12396083813611590275)
XLA Ops:
  0.6 0.0 copy-start.5
  0.6 0.0 copy-start.2
  0.7 3.3 %collective-permute-start = (bf16[2,256,1536]{2,1,0:T(8,128)(2,1)}, bf16[2,256,1536]{2,1,0:T(8,128)(2,1)S(1)}, u32[]{:S(2)}, u32[]{:S(2)}) collective-permute-start(bf16[2,256,1536]{2,1,0:T(8,128)(2,1)} %refs_1_.3), channel_id=1, source_target_pairs={{0,1},{1,0},{2,3},{3,2},{4,5},{5,4},{6,7},{7,6},{8,9},{9,8},{10,11... | collective-permute-start | bytes 4718600 | tf_op jit(solution)/shard_map/ppermute | solution.py:404
  4.1 0.1 collective-permute-start.1
  4.2 0.4 collective-permute-start.2
  4.6 1.5 %node_rows.1 = (bf16[128,256]{1,0:T(8,128)(2,1)S(1)}, bf16[8,16,256]{2,1,0:T(8,128)(2,1)}) custom-call(bf16[256,128]{1,0:T(8,128)(2,1)} %refs_13_.1), custom_call_target="tpu_custom_call" | custom-call | bytes 4194304 | tf_op jit(solution)/shard_map/node_rows/pallas_call | solution.py:61
  6.1 6.5 %all-to-all-start = ((bf16[8,16,256]{2,1,0:T(8,128)(2,1)}), bf16[8,16,256]{2,1,0:T(8,128)(2,1)S(1)}, u32[]{:S(2)}, u32[]{:S(2)}) async-start(bf16[8,16,256]{2,1,0:T(8,128)(2,1)} %get-tuple-element.56), calls=%async_computation | async-start | bytes 131072 | tf_op jit(solution)/shard_map/all_to_all | solution.py:425
  12.6 1.3 %broadcast_subtract_fusion = s32[1024]{0:T(1024)} fusion(s32[1024]{0:T(1024)} %param.20, s32[]{:T(128)S(6)} %mul.28), kind=kLoop, calls=%fused_computation.27 | loop fusion | flops 1024 | bytes 8196 | tf_op jit(solution)/shard_map/sub | solution.py:498
  13.9 1.3 %fusion.9.index_in = s32[8,128]{1,0:T(8,128)} fusion(s32[1024]{0:T(1024)} %param.19, s32[]{:T(128)S(6)} %select_n.44, s32[]{:T(128)S(6)} %select_n.43, s32[]{:T(128)S(6)} %add.50), kind=kLoop, calls=%fused_computation.19 | loop fusion | flops 50176 | bytes 8204 | tf_op jit(solution)/shard_map/reshape | solution.py:497
  15.2 4.6 %all-to-all-done = bf16[8,16,256]{2,1,0:T(8,128)(2,1)S(1)} async-done(((bf16[8,16,256]{2,1,0:T(8,128)(2,1)}), bf16[8,16,256]{2,1,0:T(8,128)(2,1)S(1)}, u32[]{:S(2)}, u32[]{:S(2)}) %all-to-all-start) | async-done | bytes 65568 | tf_op jit(solution)/shard_map/all_to_all | solution.py:425
  19.7 0.0 collective-permute-done.2.refs_12_
  19.7 0.0 collective-permute-done.1.refs_6_
  19.8 0.0 collective-permute-done.refs_2_
  19.8 1.3 %copies.2 = bf16[16,128,256]{2,1,0:T(8,128)(2,1)} custom-call(bf16[128,256]{1,0:T(8,128)(2,1)S(1)} %bitcast.10), custom_call_target="tpu_custom_call" | custom-call | bytes 4194304 | tf_op jit(solution)/shard_map/copies/pallas_call | solution.py:61
  21.1 6.8 %all-to-all-start.1 = ((bf16[16,128,256]{2,1,0:T(8,128)(2,1)}), bf16[16,128,256]{2,1,0:T(8,128)(2,1)S(1)}, u32[]{:S(2)}, u32[]{:S(2)}) async-start(bf16[16,128,256]{2,1,0:T(8,128)(2,1)} %copies.2), calls=%async_computation.1 | async-start | bytes 2097152 | tf_op jit(solution)/shard_map/all_to_all | solution.py:429
  27.8 2.0 %collective-permute-start.5 = (bf16[2,256,512]{2,1,0:T(8,128)(2,1)S(1)}, bf16[2,256,512]{2,1,0:T(8,128)(2,1)}, u32[]{:S(2)}, u32[]{:S(2)}) collective-permute-start(bf16[2,256,512]{2,1,0:T(8,128)(2,1)S(1)} %copy-done.2), channel_id=1, source_target_pairs={{0,1},{1,0},{2,3},{3,2},{4,5},{5,4},{6,7},{7,6},{8,9},{9,8},{10,11... | collective-permute-start | bytes 1572872 | tf_op jit(solution)/shard_map/ppermute | solution.py:404
  29.8 0.1 collective-permute-start.6
  29.9 0.4 collective-permute-start.3
  30.3 0.1 collective-permute-start.8
  30.6 0.5 collective-permute-start.7
  31.8 0.0 collective-permute-done.3
  31.8 4.7 %collective-permute-start.4 = (bf16[128,512]{1,0:T(8,128)(2,1)S(1)}, bf16[128,512]{1,0:T(8,128)(2,1)S(1)}, u32[]{:S(2)}, u32[]{:S(2)}) collective-permute-start(bf16[128,512]{1,0:T(8,128)(2,1)S(1)} %maximum_select_fusion.rows_in), channel_id=1, source_target_pairs={{0,2},{1,255},{2,4},{3,1},{4,6},{5,3},{6,8},{7,5},{8,10},{9,7},{10... | collective-permute-start | bytes 393224 | tf_op jit(solution)/shard_map/ppermute | solution.py:424
  36.5 0.1 pad_add_fusion.scalar_ref
  36.6 0.0 collective-permute-done.7.refs_10_
  36.6 0.0 collective-permute-done.8.refs_14_
  36.6 0.0 collective-permute-done.5.refs_4_
  36.6 0.0 collective-permute-done.6.refs_8_
  36.6 7.0 %prepare_layer.2 = (f32[512,1024]{1,0:T(8,128)}, bf16[5,512,512]{2,1,0:T(8,128)(2,1)}, bf16[128,1024]{1,0:T(8,128)(2,1)}, f32[512,128]{1,0:T(8,128)}, bf16[512,1...) custom-call(s32[2]{0:T(128)S(1)} %pad_add_fusion.scalar_ref, s32[1,1024]{1,0:T(1,128)} %bitcast.12, ...), custom_call_target="tpu_custom_call" | custom-call | flops 671088640 | bytes 4194304 | tf_op jit(solution)/shard_map/prepare_layer/pallas_call | solution.py:61
  43.6 0.0 collective-permute-done.4.beside_in
  43.6 0.0 copy-start.7
  43.6 0.6 all-to-all-done.1
  44.2 0.1 copy-done.7
  44.3 3.8 %gather_senders.2 = (bf16[1024,512]{1,0:T(8,128)(2,1)S(1)}, f32[512,1024]{1,0:T(8,128)S(1)}, bf16[5,512,512]{2,1,0:T(8,128)(2,1)S(1)}, bf16[128,1024]{1,0:T(8,12...) custom-call(s32[2]{0:T(128)S(1)} %pad_add_fusion.scalar_ref, ...), custom_call_target="tpu_custom_call" | custom-call | flops 1275068416 | bytes 4194304 | tf_op jit(solution)/shard_map/gather_senders/pallas_call | solution.py:61
  48.1 2.3 %collective-permute-start.9 = (bf16[1024,512]{1,0:T(8,128)(2,1)S(1)}, bf16[1024,512]{1,0:T(8,128)(2,1)S(1)}, u32[]{:S(2)}, u32[]{:S(2)}) collective-permute-start(bf16[1024,512]{1,0:T(8,128)(2,1)S(1)} %get-tuple-element.79.refs_0_), channel_id=1, source_target_pairs={{0,1},{1,0},{2,3},{3,2},{4,5},{5,4},{6,7},{7,6},{8,9},{9,8},{10,11... | collective-permute-start | bytes 3145736 | tf_op jit(solution)/shard_map/ppermute | solution.py:404
  50.3 2.3 %collective-permute-done.9.refs_1_ = bf16[1024,512]{1,0:T(8,128)(2,1)S(1)} collective-permute-done((bf16[1024,512]{1,0:T(8,128)(2,1)S(1)}, bf16[1024,512]{1,0:T(8,128)(2,1)S(1)}, u32[]{:S(2)}, u32[]{:S(2)}) %collective-permute-start.9) | collective-permute-done | bytes 1048608 | tf_op jit(solution)/shard_map/ppermute | solution.py:404
  52.6 5.9 %update_graph.2 = (bf16[512,1024]{1,0:T(8,128)(2,1)}, bf16[512,128]{1,0:T(8,128)(2,1)}, bf16[128,512]{1,0:T(8,128)(2,1)S(1)}, bf16[8,16,256]{2,1,0:T(8,128)(2,1)}) custom-call(s32[2]{0:T(128)S(1)} %pad_add_fusion.scalar_ref, bf16[1024,512]{1,0:T(8,128)(2,1)S(1)} %get-tuple-element.79.refs_0_, bf16[1024,512]{1,0:T(8,128)(2,1)S(1)} %collective-permute-done.9.refs_1_, ...), custom_call_target="tpu_custom_call" | custom-call | flops 1207959552 | bytes 4194304 | tf_op jit(solution)/shard_map/update_graph/pallas_call | solution.py:61
  58.6 3.4 %all-to-all-start.2 = ((bf16[8,16,256]{2,1,0:T(8,128)(2,1)}), bf16[8,16,256]{2,1,0:T(8,128)(2,1)S(1)}, u32[]{:S(2)}, u32[]{:S(2)}) async-start(bf16[8,16,256]{2,1,0:T(8,128)(2,1)} %get-tuple-element.87), calls=%async_computation.2 | async-start | bytes 131072 | tf_op jit(solution)/shard_map/all_to_all | solution.py:425
  62.0 6.3 %prepare_layer.3 = (f32[512,1024]{1,0:T(8,128)}, bf16[5,512,512]{2,1,0:T(8,128)(2,1)}, bf16[128,1024]{1,0:T(8,128)(2,1)}, f32[512,128]{1,0:T(8,128)}) custom-call(s32[2]{0:T(128)S(1)} %pad_add_fusion.scalar_ref, s32[1,1024]{1,0:T(1,128)} %bitcast.13, bf16[2,256,1536]{2,1,0:T(8,128)(2,1)} %refs_1_.3, bf16[2,256,1536]{2,1,0:T(8,128)(2,1)} %copy-done.1, ...), custom_call_target="tpu_custom_call" | custom-call | flops 671088640 | bytes 4194304 | tf_op jit(solution)/shard_map/prepare_layer/pallas_call | solution.py:61
  68.2 0.8 all-to-all-done.2
  69.0 1.1 %copies.3 = bf16[16,128,256]{2,1,0:T(8,128)(2,1)} custom-call(bf16[128,256]{1,0:T(8,128)(2,1)S(1)} %bitcast.11), custom_call_target="tpu_custom_call" | custom-call | bytes 4194304 | tf_op jit(solution)/shard_map/copies/pallas_call | solution.py:61
  70.1 4.2 %all-to-all-start.3 = ((bf16[16,128,256]{2,1,0:T(8,128)(2,1)}), bf16[16,128,256]{2,1,0:T(8,128)(2,1)S(1)}, u32[]{:S(2)}, u32[]{:S(2)}) async-start(bf16[16,128,256]{2,1,0:T(8,128)(2,1)} %copies.3), calls=%async_computation.3 | async-start | bytes 2097152 | tf_op jit(solution)/shard_map/all_to_all | solution.py:429
  74.3 6.3 %collective-permute-start.10 = (bf16[128,512]{1,0:T(8,128)(2,1)S(1)}, bf16[128,512]{1,0:T(8,128)(2,1)S(1)}, u32[]{:S(2)}, u32[]{:S(2)}) collective-permute-start(bf16[128,512]{1,0:T(8,128)(2,1)S(1)} %get-tuple-element.86.rows_in), channel_id=1, source_target_pairs={{0,2},{1,255},{2,4},{3,1},{4,6},{5,3},{6,8},{7,5},{8,10},{9,7},{10... | collective-permute-start | bytes 393224 | tf_op jit(solution)/shard_map/ppermute | solution.py:424
  80.6 8.3 %collective-permute-done.10.beside_in = bf16[128,512]{1,0:T(8,128)(2,1)S(1)} collective-permute-done((bf16[128,512]{1,0:T(8,128)(2,1)S(1)}, bf16[128,512]{1,0:T(8,128)(2,1)S(1)}, u32[]{:S(2)}, u32[]{:S(2)}) %collective-permute-start.10) | collective-permute-done | bytes 131104 | tf_op jit(solution)/shard_map/ppermute | solution.py:424
  89.0 1.1 %all-to-all-done.3 = bf16[16,128,256]{2,1,0:T(8,128)(2,1)S(1)} async-done(((bf16[16,128,256]{2,1,0:T(8,128)(2,1)}), bf16[16,128,256]{2,1,0:T(8,128)(2,1)S(1)}, u32[]{:S(2)}, u32[]{:S(2)}) %all-to-all-start.3) | async-done | bytes 1048608 | tf_op jit(solution)/shard_map/all_to_all | solution.py:429
  90.0 3.8 %gather_senders.3 = (bf16[1024,512]{1,0:T(8,128)(2,1)S(1)}, f32[512,1024]{1,0:T(8,128)S(1)}, bf16[5,512,512]{2,1,0:T(8,128)(2,1)S(1)}, bf16[128,1024]{1,0:T(8,12...) custom-call(s32[2]{0:T(128)S(1)} %pad_add_fusion.scalar_ref, ...), custom_call_target="tpu_custom_call" | custom-call | flops 1275068416 | bytes 4194304 | tf_op jit(solution)/shard_map/gather_senders/pallas_call | solution.py:61
  93.9 3.0 %collective-permute-start.11 = (bf16[1024,512]{1,0:T(8,128)(2,1)S(1)}, bf16[1024,512]{1,0:T(8,128)(2,1)S(1)}, u32[]{:S(2)}, u32[]{:S(2)}) collective-permute-start(bf16[1024,512]{1,0:T(8,128)(2,1)S(1)} %get-tuple-element.101.refs_0_), channel_id=1, source_target_pairs={{0,1},{1,0},{2,3},{3,2},{4,5},{5,4},{6,7},{7,6},{8,9},{9,8},{10,11... | collective-permute-start | bytes 3145736 | tf_op jit(solution)/shard_map/ppermute | solution.py:404
  96.8 2.3 %collective-permute-done.11.refs_1_ = bf16[1024,512]{1,0:T(8,128)(2,1)S(1)} collective-permute-done((bf16[1024,512]{1,0:T(8,128)(2,1)S(1)}, bf16[1024,512]{1,0:T(8,128)(2,1)S(1)}, u32[]{:S(2)}, u32[]{:S(2)}) %collective-permute-start.11) | collective-permute-done | bytes 1048608 | tf_op jit(solution)/shard_map/ppermute | solution.py:404
  99.1 4.6 %update_graph.3 = (bf16[256,1024]{1,0:T(8,128)(2,1)}, bf16[256,128]{1,0:T(8,128)(2,1)}) custom-call(s32[2]{0:T(128)S(1)} %pad_add_fusion.scalar_ref, bf16[1024,512]{1,0:T(8,128)(2,1)S(1)} %get-tuple-element.101.refs_0_, bf16[1024,512]{1,0:T(8,128)(2,1)S(1)} %collective-permute-done.11.refs_1_, f32[512,1024]{1,0:T(8,128)S(1)} %get-tuple-element.102.refs_2_, ...), custom_call_target="tpu_custom_call" | custom-call | flops 1207959552 | bytes 4194304 | tf_op jit(solution)/shard_map/update_graph/pallas_call | solution.py:61
  (40 shorter events, 0.2 us)
Async XLA Ops:
  0.6 29.7 %copy-start.5 = (bf16[256,128]{1,0:T(8,128)(2,1)S(1)}, bf16[256,128]{1,0:T(8,128)(2,1)}, u32[]{:S(2)}) copy-start(bf16[256,128]{1,0:T(8,128)(2,1)} %refs_13_.1) | copy-start | bytes 196612
  0.6 27.2 %copy-start.2 = (bf16[2,256,512]{2,1,0:T(8,128)(2,1)S(1)}, bf16[2,256,512]{2,1,0:T(8,128)(2,1)}, u32[]{:S(2)}) copy-start(bf16[2,256,512]{2,1,0:T(8,128)(2,1)} %refs_3_.3) | copy-start | bytes 1572868
  0.7 29.8 %copy-start.9 = (f32[2,256]{1,0:T(2,128)S(1)}, f32[2,256]{1,0:T(2,128)}, u32[]{:S(2)}) copy-start(f32[2,256]{1,0:T(2,128)} %param.23) | copy-start | bytes 6148
  0.7 29.8 %copy-start.10 = (f32[2,256]{1,0:T(2,128)S(1)}, f32[2,256]{1,0:T(2,128)}, u32[]{:S(2)}) copy-start(f32[2,256]{1,0:T(2,128)} %param.25) | copy-start | bytes 6148
  0.7 29.8 %copy-start.11 = (f32[2,256]{1,0:T(2,128)S(1)}, f32[2,256]{1,0:T(2,128)}, u32[]{:S(2)}) copy-start(f32[2,256]{1,0:T(2,128)} %param.26) | copy-start | bytes 6148
  0.7 29.8 %copy-start.12 = (f32[2,256]{1,0:T(2,128)S(1)}, f32[2,256]{1,0:T(2,128)}, u32[]{:S(2)}) copy-start(f32[2,256]{1,0:T(2,128)} %param.27) | copy-start | bytes 6148
  0.7 29.8 %copy-start.13 = (f32[2,256]{1,0:T(2,128)S(1)}, f32[2,256]{1,0:T(2,128)}, u32[]{:S(2)}) copy-start(f32[2,256]{1,0:T(2,128)} %param.29) | copy-start | bytes 6148
  0.7 29.8 %copy-start.14 = (f32[2,256]{1,0:T(2,128)S(1)}, f32[2,256]{1,0:T(2,128)}, u32[]{:S(2)}) copy-start(f32[2,256]{1,0:T(2,128)} %param.31) | copy-start | bytes 6148
  0.7 29.8 %copy-start.15 = (f32[2,256]{1,0:T(2,128)S(1)}, f32[2,256]{1,0:T(2,128)}, u32[]{:S(2)}) copy-start(f32[2,256]{1,0:T(2,128)} %param.32) | copy-start | bytes 6148
  0.7 29.8 %copy-start.16 = (f32[2,256]{1,0:T(2,128)S(1)}, f32[2,256]{1,0:T(2,128)}, u32[]{:S(2)}) copy-start(f32[2,256]{1,0:T(2,128)} %param.33) | copy-start | bytes 6148
  0.7 19.0 %collective-permute-start = (bf16[2,256,1536]{2,1,0:T(8,128)(2,1)}, bf16[2,256,1536]{2,1,0:T(8,128)(2,1)S(1)}, u32[]{:S(2)}, u32[]{:S(2)}) collective-permute-start(bf16[2,256,1536]{2,1,0:T(8,128)(2,1)} %refs_1_.3), channel_id=1, source_target_pairs={{0,1},{1,0},{2,3},{3,2},{4,5},{5,4},{6,7},{7,6},{8,9},{9,8},{10,11... | collective-permute-start | bytes 4718600 | tf_op jit(solution)/shard_map/ppermute | solution.py:404
  4.1 15.7 %collective-permute-start.1 = (bf16[2,256,1024]{2,1,0:T(8,128)(2,1)}, bf16[2,256,1024]{2,1,0:T(8,128)(2,1)}, u32[]{:S(2)}, u32[]{:S(2)}) collective-permute-start(bf16[2,256,1024]{2,1,0:T(8,128)(2,1)} %refs_5_.3), channel_id=1, source_target_pairs={{0,1},{1,0},{2,3},{3,2},{4,5},{5,4},{6,7},{7,6},{8,9},{9,8},{10,11... | collective-permute-start | bytes 3145736 | tf_op jit(solution)/shard_map/ppermute | solution.py:404
  4.2 15.6 %collective-permute-start.2 = (bf16[256,1024]{1,0:T(8,128)(2,1)}, bf16[256,1024]{1,0:T(8,128)(2,1)S(1)}, u32[]{:S(2)}, u32[]{:S(2)}) collective-permute-start(bf16[256,1024]{1,0:T(8,128)(2,1)} %refs_11_.1), channel_id=1, source_target_pairs={{0,1},{1,0},{2,3},{3,2},{4,5},{5,4},{6,7},{7,6},{8,9},{9,8},{10,11... | collective-permute-start | bytes 1572872 | tf_op jit(solution)/shard_map/ppermute | solution.py:404
  6.1 13.6 %all-to-all-start = ((bf16[8,16,256]{2,1,0:T(8,128)(2,1)}), bf16[8,16,256]{2,1,0:T(8,128)(2,1)S(1)}, u32[]{:S(2)}, u32[]{:S(2)}) async-start(bf16[8,16,256]{2,1,0:T(8,128)(2,1)} %get-tuple-element.56), calls=%async_computation | async-start | bytes 131072 | tf_op jit(solution)/shard_map/all_to_all | solution.py:425
  19.7 1.3 %copy-start.4 = (bf16[256,1024]{1,0:T(8,128)(2,1)}, bf16[256,1024]{1,0:T(8,128)(2,1)S(1)}, u32[]{:S(2)}) copy-start(bf16[256,1024]{1,0:T(8,128)(2,1)S(1)} %collective-permute-done.2.refs_12_) | copy-start | bytes 1572868
  19.8 16.8 %copy-start.1 = (bf16[2,256,1536]{2,1,0:T(8,128)(2,1)}, bf16[2,256,1536]{2,1,0:T(8,128)(2,1)S(1)}, u32[]{:S(2)}) copy-start(bf16[2,256,1536]{2,1,0:T(8,128)(2,1)S(1)} %collective-permute-done.refs_2_) | copy-start | bytes 4718596
  21.1 23.1 %all-to-all-start.1 = ((bf16[16,128,256]{2,1,0:T(8,128)(2,1)}), bf16[16,128,256]{2,1,0:T(8,128)(2,1)S(1)}, u32[]{:S(2)}, u32[]{:S(2)}) async-start(bf16[16,128,256]{2,1,0:T(8,128)(2,1)} %copies.2), calls=%async_computation.1 | async-start | bytes 2097152 | tf_op jit(solution)/shard_map/all_to_all | solution.py:429
  27.8 8.8 %collective-permute-start.5 = (bf16[2,256,512]{2,1,0:T(8,128)(2,1)S(1)}, bf16[2,256,512]{2,1,0:T(8,128)(2,1)}, u32[]{:S(2)}, u32[]{:S(2)}) collective-permute-start(bf16[2,256,512]{2,1,0:T(8,128)(2,1)S(1)} %copy-done.2), channel_id=1, source_target_pairs={{0,1},{1,0},{2,3},{3,2},{4,5},{5,4},{6,7},{7,6},{8,9},{9,8},{10,11... | collective-permute-start | bytes 1572872 | tf_op jit(solution)/shard_map/ppermute | solution.py:404
  29.8 6.8 %collective-permute-start.6 = (bf16[2,256,512]{2,1,0:T(8,128)(2,1)}, bf16[2,256,512]{2,1,0:T(8,128)(2,1)}, u32[]{:S(2)}, u32[]{:S(2)}) collective-permute-start(bf16[2,256,512]{2,1,0:T(8,128)(2,1)} %refs_7_.3), channel_id=1, source_target_pairs={{0,1},{1,0},{2,3},{3,2},{4,5},{5,4},{6,7},{7,6},{8,9},{9,8},{10,11... | collective-permute-start | bytes 1572872 | tf_op jit(solution)/shard_map/ppermute | solution.py:404
  29.9 1.9 %collective-permute-start.3 = (bf16[128,256]{1,0:T(8,128)(2,1)S(1)}, bf16[128,256]{1,0:T(8,128)(2,1)S(1)}, u32[]{:S(2)}, u32[]{:S(2)}) collective-permute-start(bf16[128,256]{1,0:T(8,128)(2,1)S(1)} %get-tuple-element.58), channel_id=1, source_target_pairs={{0,1},{1,0},{2,3},{3,2},{4,5},{5,4},{6,7},{7,6},{8,9},{9,8},{10,11... | collective-permute-start | bytes 196616 | tf_op jit(solution)/shard_map/ppermute | solution.py:404
  30.3 6.3 %collective-permute-start.8 = (bf16[256,128]{1,0:T(8,128)(2,1)S(1)}, bf16[256,128]{1,0:T(8,128)(2,1)}, u32[]{:S(2)}, u32[]{:S(2)}) collective-permute-start(bf16[256,128]{1,0:T(8,128)(2,1)S(1)} %copy-done.5), channel_id=1, source_target_pairs={{0,1},{1,0},{2,3},{3,2},{4,5},{5,4},{6,7},{7,6},{8,9},{9,8},{10,11... | collective-permute-start | bytes 196616 | tf_op jit(solution)/shard_map/ppermute | solution.py:404
  30.6 6.0 %copy-start.6 = (f32[2,8,256]{2,1,0:T(8,128)}, f32[2,8,256]{2,1,0:T(8,128)S(1)}, u32[]{:S(2)}) copy-start(f32[2,8,256]{2,1,0:T(8,128)S(1)} %stack.43.refs_9_) | copy-start | bytes 49156
  30.6 6.0 %collective-permute-start.7 = (f32[2,8,256]{2,1,0:T(8,128)S(1)}, f32[2,8,256]{2,1,0:T(8,128)}, u32[]{:S(2)}, u32[]{:S(2)}) collective-permute-start(f32[2,8,256]{2,1,0:T(8,128)S(1)} %stack.43.refs_9_), channel_id=1, source_target_pairs={{0,1},{1,0},{2,3},{3,2},{4,5},{5,4},{6,7},{7,6},{8,9},{9,8},{10,11... | collective-permute-start | bytes 49160 | tf_op jit(solution)/shard_map/ppermute | solution.py:404
  31.8 11.8 %copy-start.3 = (bf16[128,512]{1,0:T(8,128)(2,1)}, bf16[128,512]{1,0:T(8,128)(2,1)S(1)}, u32[]{:S(2)}) copy-start(bf16[128,512]{1,0:T(8,128)(2,1)S(1)} %maximum_select_fusion.rows_in) | copy-start | bytes 393220
  31.8 11.8 %collective-permute-start.4 = (bf16[128,512]{1,0:T(8,128)(2,1)S(1)}, bf16[128,512]{1,0:T(8,128)(2,1)S(1)}, u32[]{:S(2)}, u32[]{:S(2)}) collective-permute-start(bf16[128,512]{1,0:T(8,128)(2,1)S(1)} %maximum_select_fusion.rows_in), channel_id=1, source_target_pairs={{0,2},{1,255},{2,4},{3,1},{4,6},{5,3},{6,8},{7,5},{8,10},{9,7},{10... | collective-permute-start | bytes 393224 | tf_op jit(solution)/shard_map/ppermute | solution.py:424
  43.6 0.7 copy-start.7
  48.1 4.5 %collective-permute-start.9 = (bf16[1024,512]{1,0:T(8,128)(2,1)S(1)}, bf16[1024,512]{1,0:T(8,128)(2,1)S(1)}, u32[]{:S(2)}, u32[]{:S(2)}) collective-permute-start(bf16[1024,512]{1,0:T(8,128)(2,1)S(1)} %get-tuple-element.79.refs_0_), channel_id=1, source_target_pairs={{0,1},{1,0},{2,3},{3,2},{4,5},{5,4},{6,7},{7,6},{8,9},{9,8},{10,11... | collective-permute-start | bytes 3145736 | tf_op jit(solution)/shard_map/ppermute | solution.py:404
  58.6 15.7 %copy-start = (bf16[128,512]{1,0:T(8,128)(2,1)}, bf16[128,512]{1,0:T(8,128)(2,1)S(1)}, u32[]{:S(2)}) copy-start(bf16[128,512]{1,0:T(8,128)(2,1)S(1)} %get-tuple-element.86.rows_in) | copy-start | bytes 393220
  58.6 10.4 %all-to-all-start.2 = ((bf16[8,16,256]{2,1,0:T(8,128)(2,1)}), bf16[8,16,256]{2,1,0:T(8,128)(2,1)S(1)}, u32[]{:S(2)}, u32[]{:S(2)}) async-start(bf16[8,16,256]{2,1,0:T(8,128)(2,1)} %get-tuple-element.87), calls=%async_computation.2 | async-start | bytes 131072 | tf_op jit(solution)/shard_map/all_to_all | solution.py:425
  70.1 19.9 %all-to-all-start.3 = ((bf16[16,128,256]{2,1,0:T(8,128)(2,1)}), bf16[16,128,256]{2,1,0:T(8,128)(2,1)S(1)}, u32[]{:S(2)}, u32[]{:S(2)}) async-start(bf16[16,128,256]{2,1,0:T(8,128)(2,1)} %copies.3), calls=%async_computation.3 | async-start | bytes 2097152 | tf_op jit(solution)/shard_map/all_to_all | solution.py:429
  74.3 14.6 %collective-permute-start.10 = (bf16[128,512]{1,0:T(8,128)(2,1)S(1)}, bf16[128,512]{1,0:T(8,128)(2,1)S(1)}, u32[]{:S(2)}, u32[]{:S(2)}) collective-permute-start(bf16[128,512]{1,0:T(8,128)(2,1)S(1)} %get-tuple-element.86.rows_in), channel_id=1, source_target_pairs={{0,2},{1,255},{2,4},{3,1},{4,6},{5,3},{6,8},{7,5},{8,10},{9,7},{10... | collective-permute-start | bytes 393224 | tf_op jit(solution)/shard_map/ppermute | solution.py:424
  89.0 1.1 %copy-start.8 = (bf16[128,512]{1,0:T(8,128)(2,1)}, bf16[128,512]{1,0:T(8,128)(2,1)S(1)}, u32[]{:S(2)}) copy-start(bf16[128,512]{1,0:T(8,128)(2,1)S(1)} %collective-permute-done.10.beside_in) | copy-start | bytes 393220
  93.9 5.3 %collective-permute-start.11 = (bf16[1024,512]{1,0:T(8,128)(2,1)S(1)}, bf16[1024,512]{1,0:T(8,128)(2,1)S(1)}, u32[]{:S(2)}, u32[]{:S(2)}) collective-permute-start(bf16[1024,512]{1,0:T(8,128)(2,1)S(1)} %get-tuple-element.101.refs_0_), channel_id=1, source_target_pairs={{0,1},{1,0},{2,3},{3,2},{4,5},{5,4},{6,7},{7,6},{8,9},{9,8},{10,11... | collective-permute-start | bytes 3145736 | tf_op jit(solution)/shard_map/ppermute | solution.py:404

commit v9 on v7

--- a/solution.py
+++ b/solution.py
@@ -117,23 +117,28 @@
     )
 
 
-def gather_kernel(n, scalar_ref, index_in, rows_in, beside_in, coarse_in, *refs):
+def gather_kernel(n, scalar_ref, index_in, rows_in, beside_in, other_in, coarse_in, *refs):
     ready_in, out_ref, ready_out = refs[:n], refs[n], refs[n + 1 : 2 * n + 1]
-    index_ref, here_ref, beside_ref, coarse_ref, sems, ready_sems = refs[2 * n + 1 :]
+    index_ref, near_ref, coarse_ref, sems, ready_sems = refs[2 * n + 1 :]
     core = scalar_ref[0]
-    rows, half = here_ref.shape
+    rows, half = other_in.shape
     mine = pl.ds(pl.multiple_of(core * half, half), half)
+
+    def slot(i):
+        return near_ref.at[pl.ds(pl.multiple_of(i * rows, rows), rows)]
+
     copies = started(
         [
             (index_in, index_ref),
-            (rows_in.at[:, mine], here_ref),
-            (beside_in, beside_ref),
+            (rows_in.at[:, mine], slot(1)),
+            (beside_in.at[:, mine], slot(2 * core)),
+            (other_in, slot(2 - 2 * core)),
             (coarse_in, coarse_ref),
         ],
         sems,
     )
     ready_copies = started(list(zip(ready_in, ready_out)), ready_sems)
-    finish(copies[:3])
+    finish(copies[:4])
     columns = index_ref[...].T
     lane = lax.broadcasted_iota(jnp.int32, (128, 128), 1)
 
@@ -142,40 +147,34 @@
         for k in range(start // 128, (start + EDGE_BLOCK) // 128):
             index = jnp.broadcast_to(columns[:, k : k + 1], (128, 128))
             tiles = []
-            for j in range(0, length, 128):
-                tiles.append(jnp.where(index == lane + (first + j), 1.0, 0.0).astype(jnp.bfloat16))
-            blocks.append(jnp.concatenate(tiles, axis=1) if len(tiles) > 1 else tiles[0])
+            for j in range(first, first + length, 128):
+                tiles.append(jnp.where(index == lane + j, 1.0, 0.0).astype(jnp.bfloat16))
+            blocks.append(jnp.concatenate(tiles, axis=1))
         return jnp.concatenate(blocks, axis=0)
 
     for start in range(0, out_ref.shape[0], EDGE_BLOCK):
-        near = dot(selection(start, core * (2 * rows), rows), beside_ref[...])
-        total = dot(selection(start, rows, rows), here_ref[...])
+        total = dot(selection(start, 0, 3 * rows), near_ref[...])
         if start == 0:
-            finish(copies[3:])
+            finish(copies[4:])
         total = total + dot(selection(start, 3 * rows, coarse_ref.shape[0]), coarse_ref[...])
-        block = slice(start, start + EDGE_BLOCK)
-        low = near[:, :half] + jnp.where(core == 0, total, 0.0)
-        high = near[:, half:] + jnp.where(core == 0, 0.0, total)
-        out_ref[block, :half] = low.astype(jnp.bfloat16)
-        out_ref[block, half:] = high.astype(jnp.bfloat16)
+        out_ref[start : start + EDGE_BLOCK, :] = total.astype(jnp.bfloat16)
     finish(ready_copies)
 
 
-def gathered(scalars, ready, index, rows, beside, coarse):
+def gathered(scalars, ready, index, rows, beside, other, coarse):
     slots = index.size
-    node_rows, width = rows.shape
-    half = width // 2
+    node_rows, half = other.shape
     table = 3 * node_rows + coarse.shape[0]
     n = len(ready)
     return kernel_call(
         functools.partial(gather_kernel, n),
         "gather_senders",
-        [shape((slots, width)), *[shape(a.shape, a.dtype) for a in ready]],
-        (scalars, index, rows, beside, coarse, *ready),
-        [SMEM] + [HBM] * 3 + [ANY] + [HBM] * n,
+        [shape((slots, half)), *[shape(a.shape, a.dtype) for a in ready]],
+        (scalars, index, rows, beside, other, coarse, *ready),
+        [SMEM] + [HBM] * 4 + [ANY] + [HBM] * n,
         [VMEM] * (1 + n),
-        held([index, shape((node_rows, half)), beside, coarse])
-        + [pltpu.SemaphoreType.DMA((4,)), pltpu.SemaphoreType.DMA((n,))],
+        held([index, shape((3 * node_rows, half)), coarse])
+        + [pltpu.SemaphoreType.DMA((5,)), pltpu.SemaphoreType.DMA((n,))],
         2 * slots * half * table,
     )
 
@@ -291,8 +290,8 @@
     sent_a_ref, sent_b_ref, before_ref, weights_ref, incidence_ref, small_ref = refs[:6]
     edges_ref, nodes_ref, outs, refs = refs[6], refs[7], refs[8 : 8 + n_out], refs[8 + n_out :]
     edge_out_ref, node_out_ref, hidden_ref, mlp_ref, vectors_ref, out_sems = refs
-    width = sent_a_ref.shape[1]
-    half = width // 2
+    half = sent_a_ref.shape[1]
+    width = 2 * half
     first = scalar_ref[0] == 0
     count = scalar_ref[1]
     sent_out = []
@@ -314,7 +313,10 @@
     total = None
     for start in range(0, slots, UPDATE_BLOCK):
         here = slice(start, start + UPDATE_BLOCK)
-        sent = sent_a_ref[here, :] + sent_b_ref[here, :]
+        sent_a, sent_b = sent_a_ref[here, :], sent_b_ref[here, :]
+        low = jnp.where(first, sent_a, sent_b)
+        high = jnp.where(first, sent_b, sent_a)
+        sent = jnp.concatenate([low, high], axis=1)
         mlp_ref[...] = dot(weights_ref[0], sent, ((1,), (1,)))
         for row in range(0, width, ROWS):
             rows = slice(row, row + ROWS)
@@ -371,8 +373,8 @@
 def updated_graph(last_layer, scalars, sent, ready, copies):
     slots = ready[0].shape[1]
     node_rows = ready[5].shape[1]
-    width = sent[0].shape[1]
-    half = width // 2
+    half = sent[0].shape[1]
+    width = 2 * half
     out_width = half if last_layer else width
     out_shape = [shape((out_width, slots)), shape((out_width, node_rows))]
     out_specs = [HBM, HBM]
@@ -428,6 +430,15 @@
     plane = copied(column, lax.axis_size(PLANE))
     coarse = lax.all_to_all(plane, PLANE, split_axis=0, concat_axis=0, tiled=True)
     return (rows, beside, coarse.reshape(-1, copies.shape[2])), others
+
+
+def completed(table, ready):
+    rows, beside, coarse = table
+    beside, ready = lax.optimization_barrier((beside, ready))
+    half = coarse.shape[1]
+    theirs = (1 - lax.axis_index("width")) * half
+    other = from_other(lax.dynamic_slice_in_dim(beside, theirs, half, 1))
+    return (rows, beside, other, coarse), ready
 
 
 def on_device(
@@ -512,6 +523,7 @@
     for layer in range(layers):
         last_layer = layer == layers - 1
         ready = prepared(layer, scalars, edges, receiver, nodes, weights)
+        table, ready = completed(table, ready)
         table, ready = lax.optimization_barrier((table, ready))
         sent, *ready = gathered(scalars, ready, index, *table)
         sent = (sent, from_other(sent))

time: 103 us -> 102 us (level)
  starting transfers between devices: 38.7 us -> 37.1 us
  local copies, waits for them, and re-layouts: 0.22 us -> 1.4 us
  blocking collectives: 9.51 us -> 10.6 us
    ppermute x10 -> x12, starting transfers between devices: 12.1 us -> 10.3 us  [from_other(): return lax.ppermute(a, 'width', [(0, 1), (1, 0)])]
    all_to_all x2, waiting for transfers between devices: 1.63 us -> 0.01 us  [exchanged(): lax.all_to_all(plane, PLANE, split_axis=0, concat_axis=0, tiled=True)]
    unnamed x34 -> x38, local copies, waits for them, and re-layouts: 0.16 us -> 1.32 us
    all_to_all x1, blocking collectives: 9.51 us -> 10.6 us  [exchanged(): column = lax.all_to_all(copies, Z, split_axis=0, concat_axis=0, tiled=True)]
    ppermute x10 -> x12, waiting for transfers between devices: 4.59 us -> 5.34 us  [from_other(): return lax.ppermute(a, 'width', [(0, 1), (1, 0)])]
  transfers between devices with their start and end apart: 15 -> 17, of which waited for: 6 -> 6; matrix products, arithmetic and copies ran while one was open for 3% -> 3% of each run, Pallas kernels for 14% -> 15%
where the time goes in v9:
time: 102 us
  starting transfers between devices  37.1 us (36%)
  Pallas kernels  34.1 us (33%)
  waiting for transfers between devices  13.8 us (14%)
  blocking collectives  10.6 us (10%)
  other arithmetic  2.69 us (3%)
  between operations  1.88 us (2%)
  local copies, waits for them, and re-layouts  1.4 us (1%)
    pallas_call x9, Pallas kernels, kernel_call(): pl.pallas_call(body, in_specs=in_specs, out_specs=out_specs, out_shape=ou...  34.1 us
    all_to_all x2, starting transfers between devices, exchanged(): lax.all_to_all(plane, PLANE, split_axis=0, concat_axis=0, tiled=True)  11.1 us
    all_to_all x1, blocking collectives, exchanged(): column = lax.all_to_all(copies, Z, split_axis=0, concat_axis=0, tiled=True)  10.6 us
    ppermute x12, starting transfers between devices, from_other(): return lax.ppermute(a, 'width', [(0, 1), (1, 0)])  10.3 us
    ppermute x2, starting transfers between devices, exchanged(): beside = lax.ppermute(rows, (*PATCH, 'width'), pairs)  9.16 us
    all_to_all x1, starting transfers between devices, exchanged(): column = lax.all_to_all(copies, Z, split_axis=0, concat_axis=0, tiled=True)  6.48 us
    ppermute x12, waiting for transfers between devices, from_other(): return lax.ppermute(a, 'width', [(0, 1), (1, 0)])  5.34 us
    all_to_all x1, waiting for transfers between devices, exchanged(): column = lax.all_to_all(copies, Z, split_axis=0, concat_axis=0, tiled=True)  4.56 us
  transfers between devices with their start and end apart: 17, of which 6 were waited for; matrix products, arithmetic and copies ran while one was open for 3% of the time, Pallas kernels for 15%

profile of v9, /device:TPU:1, one launch (start us, length us, event | category | flops | bytes accessed | tf_op | source)
XLA Modules:
  0.0 101.6 jit_solution(4472482108423217787)
XLA Ops:
  0.6 0.0 copy-start.7
  0.6 0.0 copy-start.2
  0.7 3.3 %collective-permute-start = (bf16[2,256,1536]{2,1,0:T(8,128)(2,1)}, bf16[2,256,1536]{2,1,0:T(8,128)(2,1)S(1)}, u32[]{:S(2)}, u32[]{:S(2)}) collective-permute-start(bf16[2,256,1536]{2,1,0:T(8,128)(2,1)} %refs_1_.3), channel_id=1, source_target_pairs={{0,1},{1,0},{2,3},{3,2},{4,5},{5,4},{6,7},{7,6},{8,9},{9,8},{10,11... | collective-permute-start | bytes 4718600 | tf_op jit(solution)/shard_map/ppermute | solution.py:406
  4.1 0.1 collective-permute-start.1
  4.2 0.4 collective-permute-start.2
  4.6 1.5 %node_rows.1 = (bf16[128,256]{1,0:T(8,128)(2,1)S(1)}, bf16[8,16,256]{2,1,0:T(8,128)(2,1)}) custom-call(bf16[256,128]{1,0:T(8,128)(2,1)} %refs_13_.1), custom_call_target="tpu_custom_call" | custom-call | bytes 4194304 | tf_op jit(solution)/shard_map/node_rows/pallas_call | solution.py:61
  6.1 6.5 %all-to-all-start = ((bf16[8,16,256]{2,1,0:T(8,128)(2,1)}), bf16[8,16,256]{2,1,0:T(8,128)(2,1)S(1)}, u32[]{:S(2)}, u32[]{:S(2)}) async-start(bf16[8,16,256]{2,1,0:T(8,128)(2,1)} %get-tuple-element.74), calls=%async_computation | async-start | bytes 131072 | tf_op jit(solution)/shard_map/all_to_all | solution.py:427
  12.6 1.3 %broadcast_subtract_fusion = s32[1024]{0:T(1024)} fusion(s32[1024]{0:T(1024)} %param.20, s32[]{:T(128)S(6)} %mul.32), kind=kLoop, calls=%fused_computation.27 | loop fusion | flops 1024 | bytes 8196 | tf_op jit(solution)/shard_map/sub | solution.py:509
  13.9 1.3 %fusion.9.index_in = s32[8,128]{1,0:T(8,128)} fusion(s32[1024]{0:T(1024)} %param.19, s32[]{:T(128)S(6)} %select_n.48, s32[]{:T(128)S(6)} %select_n.47, s32[]{:T(128)S(6)} %add.54), kind=kLoop, calls=%fused_computation.19 | loop fusion | flops 50176 | bytes 8204 | tf_op jit(solution)/shard_map/reshape | solution.py:508
  15.2 4.6 %all-to-all-done = bf16[8,16,256]{2,1,0:T(8,128)(2,1)S(1)} async-done(((bf16[8,16,256]{2,1,0:T(8,128)(2,1)}), bf16[8,16,256]{2,1,0:T(8,128)(2,1)S(1)}, u32[]{:S(2)}, u32[]{:S(2)}) %all-to-all-start) | async-done | bytes 65568 | tf_op jit(solution)/shard_map/all_to_all | solution.py:427
  19.8 0.0 collective-permute-done.refs_2_
  19.8 1.3 %copies.2 = bf16[16,128,256]{2,1,0:T(8,128)(2,1)} custom-call(bf16[128,256]{1,0:T(8,128)(2,1)S(1)} %bitcast.10), custom_call_target="tpu_custom_call" | custom-call | bytes 4194304 | tf_op jit(solution)/shard_map/copies/pallas_call | solution.py:61
  21.0 6.8 %all-to-all-start.1 = ((bf16[16,128,256]{2,1,0:T(8,128)(2,1)}), bf16[16,128,256]{2,1,0:T(8,128)(2,1)S(1)}, u32[]{:S(2)}, u32[]{:S(2)}) async-start(bf16[16,128,256]{2,1,0:T(8,128)(2,1)} %copies.2), calls=%async_computation.1 | async-start | bytes 2097152 | tf_op jit(solution)/shard_map/all_to_all | solution.py:431
  27.8 2.0 %collective-permute-start.5 = (bf16[2,256,512]{2,1,0:T(8,128)(2,1)S(1)}, bf16[2,256,512]{2,1,0:T(8,128)(2,1)}, u32[]{:S(2)}, u32[]{:S(2)}) collective-permute-start(bf16[2,256,512]{2,1,0:T(8,128)(2,1)S(1)} %copy-done.2), channel_id=1, source_target_pairs={{0,1},{1,0},{2,3},{3,2},{4,5},{5,4},{6,7},{7,6},{8,9},{9,8},{10,11... | collective-permute-start | bytes 1572872 | tf_op jit(solution)/shard_map/ppermute | solution.py:406
  29.8 0.1 collective-permute-start.6
  29.9 0.4 collective-permute-start.3
  30.3 0.1 collective-permute-start.8
  30.6 0.5 collective-permute-start.7
  31.7 0.0 collective-permute-done.3
  31.8 4.7 %collective-permute-start.4 = (bf16[128,512]{1,0:T(8,128)(2,1)S(1)}, bf16[128,512]{1,0:T(8,128)(2,1)S(1)}, u32[]{:S(2)}, u32[]{:S(2)}) collective-permute-start(bf16[128,512]{1,0:T(8,128)(2,1)S(1)} %maximum_select_fusion.rows_in), channel_id=1, source_target_pairs={{0,2},{1,255},{2,4},{3,1},{4,6},{5,3},{6,8},{7,5},{8,10},{9,7},{10... | collective-permute-start | bytes 393224 | tf_op jit(solution)/shard_map/ppermute | solution.py:426
  36.5 0.1 pad_add_fusion.scalar_ref
  36.6 0.0 collective-permute-done.7.refs_10_
  36.6 0.0 collective-permute-done.8.refs_14_
  36.6 0.0 collective-permute-done.5.refs_4_
  36.6 7.0 %prepare_layer.2 = (f32[512,1024]{1,0:T(8,128)}, bf16[5,512,512]{2,1,0:T(8,128)(2,1)}, bf16[128,1024]{1,0:T(8,128)(2,1)}, f32[512,128]{1,0:T(8,128)}, bf16[512,1...) custom-call(s32[2]{0:T(128)S(1)} %pad_add_fusion.scalar_ref, s32[1,1024]{1,0:T(1,128)} %bitcast.12, ...), custom_call_target="tpu_custom_call" | custom-call | flops 671088640 | bytes 4194304 | tf_op jit(solution)/shard_map/prepare_layer/pallas_call | solution.py:61
  43.6 0.0 collective-permute-done.4.beside_in
  43.6 0.0 copy-start.5
  43.7 0.3 collective-permute-start.9
  44.0 1.0 collective-permute-done.9.other_in
  45.0 0.6 copy-done.10
  45.6 3.6 %gather_senders.2 = (bf16[1024,256]{1,0:T(8,128)(2,1)S(1)}, f32[512,1024]{1,0:T(8,128)S(1)}, bf16[5,512,512]{2,1,0:T(8,128)(2,1)S(1)}, bf16[128,1024]{1,0:T(8,12...) custom-call(s32[2]{0:T(128)S(1)} %pad_add_fusion.scalar_ref, ...), custom_call_target="tpu_custom_call" | custom-call | flops 1275068416 | bytes 4194304 | tf_op jit(solution)/shard_map/gather_senders/pallas_call | solution.py:61
  49.2 0.9 collective-permute-start.10
  50.1 1.5 %collective-permute-done.10.refs_1_ = bf16[1024,256]{1,0:T(8,128)(2,1)S(1)} collective-permute-done((bf16[1024,256]{1,0:T(8,128)(2,1)S(1)}, bf16[1024,256]{1,0:T(8,128)(2,1)S(1)}, u32[]{:S(2)}, u32[]{:S(2)}) %collective-permute-start.10) | collective-permute-done | bytes 524320 | tf_op jit(solution)/shard_map/ppermute | solution.py:406
  51.6 5.3 %update_graph.2 = (bf16[512,1024]{1,0:T(8,128)(2,1)}, bf16[512,128]{1,0:T(8,128)(2,1)}, bf16[128,512]{1,0:T(8,128)(2,1)S(1)}, bf16[8,16,256]{2,1,0:T(8,128)(2,1)S(1)}) custom-call(s32[2]{0:T(128)S(1)} %pad_add_fusion.scalar_ref, bf16[1024,256]{1,0:T(8,128)(2,1)S(1)} %get-tuple-element.105.refs_0_, bf16[1024,256]{1,0:T(8,128)(2,1)S(1)} %collective-permute-done.10.refs_1_, ...), custom_call_target="tpu_custom_call" | custom-call | flops 1207959552 | bytes 4194304 | tf_op jit(solution)/shard_map/update_graph/pallas_call | solution.py:61
  56.9 10.6 %all_to_all.20 = bf16[8,16,256]{2,1,0:T(8,128)(2,1)S(1)} all-to-all(bf16[8,16,256]{2,1,0:T(8,128)(2,1)S(1)} %get-tuple-element.120), channel_id=1, replica_groups=mesh['patch_0'=8,'patch_1'=4,'patch_2'=4,'width'=2] {'patch_0'}, dimensions={0} | all-to-all | bytes 131072 | tf_op jit(solution)/shard_map/all_to_all | solution.py:427
  67.6 1.1 %copies.3 = bf16[16,128,256]{2,1,0:T(8,128)(2,1)} custom-call(bf16[128,256]{1,0:T(8,128)(2,1)S(1)} %bitcast.11), custom_call_target="tpu_custom_call" | custom-call | bytes 4194304 | tf_op jit(solution)/shard_map/copies/pallas_call | solution.py:61
  68.7 4.4 %all-to-all-start.3 = ((bf16[16,128,256]{2,1,0:T(8,128)(2,1)}), bf16[16,128,256]{2,1,0:T(8,128)(2,1)S(1)}, u32[]{:S(2)}, u32[]{:S(2)}) async-start(bf16[16,128,256]{2,1,0:T(8,128)(2,1)} %copies.3), calls=%async_computation.3 | async-start | bytes 2097152 | tf_op jit(solution)/shard_map/all_to_all | solution.py:431
  73.0 4.5 %collective-permute-start.11 = (bf16[128,512]{1,0:T(8,128)(2,1)S(1)}, bf16[128,512]{1,0:T(8,128)(2,1)S(1)}, u32[]{:S(2)}, u32[]{:S(2)}) collective-permute-start(bf16[128,512]{1,0:T(8,128)(2,1)S(1)} %get-tuple-element.127.rows_in), channel_id=1, source_target_pairs={{0,2},{1,255},{2,4},{3,1},{4,6},{5,3},{6,8},{7,5},{8,10},{9,7},{10... | collective-permute-start | bytes 393224 | tf_op jit(solution)/shard_map/ppermute | solution.py:426
  77.5 6.3 %prepare_layer.3 = (f32[512,1024]{1,0:T(8,128)}, bf16[5,512,512]{2,1,0:T(8,128)(2,1)}, bf16[128,1024]{1,0:T(8,128)(2,1)}, f32[512,128]{1,0:T(8,128)}) custom-call(s32[2]{0:T(128)S(1)} %pad_add_fusion.scalar_ref, s32[1,1024]{1,0:T(1,128)} %bitcast.13, bf16[2,256,1536]{2,1,0:T(8,128)(2,1)} %refs_1_.3, bf16[2,256,1536]{2,1,0:T(8,128)(2,1)} %copy-done.1, ...), custom_call_target="tpu_custom_call" | custom-call | flops 671088640 | bytes 4194304 | tf_op jit(solution)/shard_map/prepare_layer/pallas_call | solution.py:61
  83.8 3.9 %collective-permute-done.11.beside_in = bf16[128,512]{1,0:T(8,128)(2,1)S(1)} collective-permute-done((bf16[128,512]{1,0:T(8,128)(2,1)S(1)}, bf16[128,512]{1,0:T(8,128)(2,1)S(1)}, u32[]{:S(2)}, u32[]{:S(2)}) %collective-permute-start.11) | collective-permute-done | bytes 131104 | tf_op jit(solution)/shard_map/ppermute | solution.py:426
  87.7 0.1 collective-permute-start.12
  87.8 1.2 %collective-permute-done.12.other_in = bf16[128,256]{1,0:T(8,128)(2,1)S(1)} collective-permute-done((bf16[128,256]{1,0:T(8,128)(2,1)S(1)}, bf16[128,256]{1,0:T(8,128)(2,1)S(1)}, u32[]{:S(2)}, u32[]{:S(2)}) %collective-permute-start.12) | collective-permute-done | bytes 65568 | tf_op jit(solution)/shard_map/ppermute | solution.py:406
  89.0 0.0 all-to-all-done.3
  89.1 0.6 copy-done.9
  89.7 3.6 %gather_senders.3 = (bf16[1024,256]{1,0:T(8,128)(2,1)S(1)}, f32[512,1024]{1,0:T(8,128)S(1)}, bf16[5,512,512]{2,1,0:T(8,128)(2,1)S(1)}, bf16[128,1024]{1,0:T(8,12...) custom-call(s32[2]{0:T(128)S(1)} %pad_add_fusion.scalar_ref, ...), custom_call_target="tpu_custom_call" | custom-call | flops 1275068416 | bytes 4194304 | tf_op jit(solution)/shard_map/gather_senders/pallas_call | solution.py:61
  93.2 2.1 %collective-permute-start.13 = (bf16[1024,256]{1,0:T(8,128)(2,1)S(1)}, bf16[1024,256]{1,0:T(8,128)(2,1)S(1)}, u32[]{:S(2)}, u32[]{:S(2)}) collective-permute-start(bf16[1024,256]{1,0:T(8,128)(2,1)S(1)} %get-tuple-element.137.refs_0_), channel_id=1, source_target_pairs={{0,1},{1,0},{2,3},{3,2},{4,5},{5,4},{6,7},{7,6},{8,9},{9,8},{10,11... | collective-permute-start | bytes 1572872 | tf_op jit(solution)/shard_map/ppermute | solution.py:406
  95.3 1.5 %collective-permute-done.13.refs_1_ = bf16[1024,256]{1,0:T(8,128)(2,1)S(1)} collective-permute-done((bf16[1024,256]{1,0:T(8,128)(2,1)S(1)}, bf16[1024,256]{1,0:T(8,128)(2,1)S(1)}, u32[]{:S(2)}, u32[]{:S(2)}) %collective-permute-start.13) | collective-permute-done | bytes 524320 | tf_op jit(solution)/shard_map/ppermute | solution.py:406
  96.8 4.6 %update_graph.3 = (bf16[256,1024]{1,0:T(8,128)(2,1)}, bf16[256,128]{1,0:T(8,128)(2,1)}) custom-call(s32[2]{0:T(128)S(1)} %pad_add_fusion.scalar_ref, bf16[1024,256]{1,0:T(8,128)(2,1)S(1)} %get-tuple-element.137.refs_0_, bf16[1024,256]{1,0:T(8,128)(2,1)S(1)} %collective-permute-done.13.refs_1_, f32[512,1024]{1,0:T(8,128)S(1)} %get-tuple-element.138.refs_2_, ...), custom_call_target="tpu_custom_call" | custom-call | flops 1207959552 | bytes 4194304 | tf_op jit(solution)/shard_map/update_graph/pallas_call | solution.py:61
  (49 shorter events, 0.2 us)
Async XLA Ops:
  0.6 29.7 %copy-start.7 = (bf16[256,128]{1,0:T(8,128)(2,1)S(1)}, bf16[256,128]{1,0:T(8,128)(2,1)}, u32[]{:S(2)}) copy-start(bf16[256,128]{1,0:T(8,128)(2,1)} %refs_13_.1) | copy-start | bytes 196612
  0.6 27.2 %copy-start.2 = (bf16[2,256,512]{2,1,0:T(8,128)(2,1)S(1)}, bf16[2,256,512]{2,1,0:T(8,128)(2,1)}, u32[]{:S(2)}) copy-start(bf16[2,256,512]{2,1,0:T(8,128)(2,1)} %refs_3_.3) | copy-start | bytes 1572868
  0.7 29.7 %copy-start.11 = (f32[2,256]{1,0:T(2,128)S(1)}, f32[2,256]{1,0:T(2,128)}, u32[]{:S(2)}) copy-start(f32[2,256]{1,0:T(2,128)} %param.23) | copy-start | bytes 6148
  0.7 29.7 %copy-start.12 = (f32[2,256]{1,0:T(2,128)S(1)}, f32[2,256]{1,0:T(2,128)}, u32[]{:S(2)}) copy-start(f32[2,256]{1,0:T(2,128)} %param.25) | copy-start | bytes 6148
  0.7 29.7 %copy-start.13 = (f32[2,256]{1,0:T(2,128)S(1)}, f32[2,256]{1,0:T(2,128)}, u32[]{:S(2)}) copy-start(f32[2,256]{1,0:T(2,128)} %param.26) | copy-start | bytes 6148
  0.7 29.8 %copy-start.14 = (f32[2,256]{1,0:T(2,128)S(1)}, f32[2,256]{1,0:T(2,128)}, u32[]{:S(2)}) copy-start(f32[2,256]{1,0:T(2,128)} %param.27) | copy-start | bytes 6148
  0.7 29.8 %copy-start.15 = (f32[2,256]{1,0:T(2,128)S(1)}, f32[2,256]{1,0:T(2,128)}, u32[]{:S(2)}) copy-start(f32[2,256]{1,0:T(2,128)} %param.29) | copy-start | bytes 6148
  0.7 29.8 %copy-start.16 = (f32[2,256]{1,0:T(2,128)S(1)}, f32[2,256]{1,0:T(2,128)}, u32[]{:S(2)}) copy-start(f32[2,256]{1,0:T(2,128)} %param.31) | copy-start | bytes 6148
  0.7 29.8 %copy-start.17 = (f32[2,256]{1,0:T(2,128)S(1)}, f32[2,256]{1,0:T(2,128)}, u32[]{:S(2)}) copy-start(f32[2,256]{1,0:T(2,128)} %param.32) | copy-start | bytes 6148
  0.7 29.8 %copy-start.18 = (f32[2,256]{1,0:T(2,128)S(1)}, f32[2,256]{1,0:T(2,128)}, u32[]{:S(2)}) copy-start(f32[2,256]{1,0:T(2,128)} %param.33) | copy-start | bytes 6148
  0.7 19.0 %collective-permute-start = (bf16[2,256,1536]{2,1,0:T(8,128)(2,1)}, bf16[2,256,1536]{2,1,0:T(8,128)(2,1)S(1)}, u32[]{:S(2)}, u32[]{:S(2)}) collective-permute-start(bf16[2,256,1536]{2,1,0:T(8,128)(2,1)} %refs_1_.3), channel_id=1, source_target_pairs={{0,1},{1,0},{2,3},{3,2},{4,5},{5,4},{6,7},{7,6},{8,9},{9,8},{10,11... | collective-permute-start | bytes 4718600 | tf_op jit(solution)/shard_map/ppermute | solution.py:406
  4.1 15.7 %collective-permute-start.1 = (bf16[2,256,1024]{2,1,0:T(8,128)(2,1)}, bf16[2,256,1024]{2,1,0:T(8,128)(2,1)}, u32[]{:S(2)}, u32[]{:S(2)}) collective-permute-start(bf16[2,256,1024]{2,1,0:T(8,128)(2,1)} %refs_5_.3), channel_id=1, source_target_pairs={{0,1},{1,0},{2,3},{3,2},{4,5},{5,4},{6,7},{7,6},{8,9},{9,8},{10,11... | collective-permute-start | bytes 3145736 | tf_op jit(solution)/shard_map/ppermute | solution.py:406
  4.2 15.6 %collective-permute-start.2 = (bf16[256,1024]{1,0:T(8,128)(2,1)}, bf16[256,1024]{1,0:T(8,128)(2,1)S(1)}, u32[]{:S(2)}, u32[]{:S(2)}) collective-permute-start(bf16[256,1024]{1,0:T(8,128)(2,1)} %refs_11_.1), channel_id=1, source_target_pairs={{0,1},{1,0},{2,3},{3,2},{4,5},{5,4},{6,7},{7,6},{8,9},{9,8},{10,11... | collective-permute-start | bytes 1572872 | tf_op jit(solution)/shard_map/ppermute | solution.py:406
  6.1 13.6 %all-to-all-start = ((bf16[8,16,256]{2,1,0:T(8,128)(2,1)}), bf16[8,16,256]{2,1,0:T(8,128)(2,1)S(1)}, u32[]{:S(2)}, u32[]{:S(2)}) async-start(bf16[8,16,256]{2,1,0:T(8,128)(2,1)} %get-tuple-element.74), calls=%async_computation | async-start | bytes 131072 | tf_op jit(solution)/shard_map/all_to_all | solution.py:427
  19.7 1.3 %copy-start.4 = (bf16[256,1024]{1,0:T(8,128)(2,1)}, bf16[256,1024]{1,0:T(8,128)(2,1)S(1)}, u32[]{:S(2)}) copy-start(bf16[256,1024]{1,0:T(8,128)(2,1)S(1)} %collective-permute-done.2.refs_12_) | copy-start | bytes 1572868
  19.8 16.8 %copy-start.1 = (bf16[2,256,1536]{2,1,0:T(8,128)(2,1)}, bf16[2,256,1536]{2,1,0:T(8,128)(2,1)S(1)}, u32[]{:S(2)}) copy-start(bf16[2,256,1536]{2,1,0:T(8,128)(2,1)S(1)} %collective-permute-done.refs_2_) | copy-start | bytes 4718596
  21.0 24.0 %all-to-all-start.1 = ((bf16[16,128,256]{2,1,0:T(8,128)(2,1)}), bf16[16,128,256]{2,1,0:T(8,128)(2,1)S(1)}, u32[]{:S(2)}, u32[]{:S(2)}) async-start(bf16[16,128,256]{2,1,0:T(8,128)(2,1)} %copies.2), calls=%async_computation.1 | async-start | bytes 2097152 | tf_op jit(solution)/shard_map/all_to_all | solution.py:431
  27.8 8.8 %collective-permute-start.5 = (bf16[2,256,512]{2,1,0:T(8,128)(2,1)S(1)}, bf16[2,256,512]{2,1,0:T(8,128)(2,1)}, u32[]{:S(2)}, u32[]{:S(2)}) collective-permute-start(bf16[2,256,512]{2,1,0:T(8,128)(2,1)S(1)} %copy-done.2), channel_id=1, source_target_pairs={{0,1},{1,0},{2,3},{3,2},{4,5},{5,4},{6,7},{7,6},{8,9},{9,8},{10,11... | collective-permute-start | bytes 1572872 | tf_op jit(solution)/shard_map/ppermute | solution.py:406
  29.8 6.8 %collective-permute-start.6 = (bf16[2,256,512]{2,1,0:T(8,128)(2,1)}, bf16[2,256,512]{2,1,0:T(8,128)(2,1)}, u32[]{:S(2)}, u32[]{:S(2)}) collective-permute-start(bf16[2,256,512]{2,1,0:T(8,128)(2,1)} %refs_7_.3), channel_id=1, source_target_pairs={{0,1},{1,0},{2,3},{3,2},{4,5},{5,4},{6,7},{7,6},{8,9},{9,8},{10,11... | collective-permute-start | bytes 1572872 | tf_op jit(solution)/shard_map/ppermute | solution.py:406
  29.9 1.9 %collective-permute-start.3 = (bf16[128,256]{1,0:T(8,128)(2,1)S(1)}, bf16[128,256]{1,0:T(8,128)(2,1)S(1)}, u32[]{:S(2)}, u32[]{:S(2)}) collective-permute-start(bf16[128,256]{1,0:T(8,128)(2,1)S(1)} %get-tuple-element.76), channel_id=1, source_target_pairs={{0,1},{1,0},{2,3},{3,2},{4,5},{5,4},{6,7},{7,6},{8,9},{9,8},{10,11... | collective-permute-start | bytes 196616 | tf_op jit(solution)/shard_map/ppermute | solution.py:406
  30.3 6.3 %collective-permute-start.8 = (bf16[256,128]{1,0:T(8,128)(2,1)S(1)}, bf16[256,128]{1,0:T(8,128)(2,1)}, u32[]{:S(2)}, u32[]{:S(2)}) collective-permute-start(bf16[256,128]{1,0:T(8,128)(2,1)S(1)} %copy-done.7), channel_id=1, source_target_pairs={{0,1},{1,0},{2,3},{3,2},{4,5},{5,4},{6,7},{7,6},{8,9},{9,8},{10,11... | collective-permute-start | bytes 196616 | tf_op jit(solution)/shard_map/ppermute | solution.py:406
  30.6 6.0 %copy-start.8 = (f32[2,8,256]{2,1,0:T(8,128)}, f32[2,8,256]{2,1,0:T(8,128)S(1)}, u32[]{:S(2)}) copy-start(f32[2,8,256]{2,1,0:T(8,128)S(1)} %stack.43.refs_9_) | copy-start | bytes 49156
  30.6 6.0 %collective-permute-start.7 = (f32[2,8,256]{2,1,0:T(8,128)S(1)}, f32[2,8,256]{2,1,0:T(8,128)}, u32[]{:S(2)}, u32[]{:S(2)}) collective-permute-start(f32[2,8,256]{2,1,0:T(8,128)S(1)} %stack.43.refs_9_), channel_id=1, source_target_pairs={{0,1},{1,0},{2,3},{3,2},{4,5},{5,4},{6,7},{7,6},{8,9},{9,8},{10,11... | collective-permute-start | bytes 49160 | tf_op jit(solution)/shard_map/ppermute | solution.py:406
  31.8 11.8 %copy-start.3 = (bf16[128,512]{1,0:T(8,128)(2,1)}, bf16[128,512]{1,0:T(8,128)(2,1)S(1)}, u32[]{:S(2)}) copy-start(bf16[128,512]{1,0:T(8,128)(2,1)S(1)} %maximum_select_fusion.rows_in) | copy-start | bytes 393220
  31.8 11.8 %collective-permute-start.4 = (bf16[128,512]{1,0:T(8,128)(2,1)S(1)}, bf16[128,512]{1,0:T(8,128)(2,1)S(1)}, u32[]{:S(2)}, u32[]{:S(2)}) collective-permute-start(bf16[128,512]{1,0:T(8,128)(2,1)S(1)} %maximum_select_fusion.rows_in), channel_id=1, source_target_pairs={{0,2},{1,255},{2,4},{3,1},{4,6},{5,3},{6,8},{7,5},{8,10},{9,7},{10... | collective-permute-start | bytes 393224 | tf_op jit(solution)/shard_map/ppermute | solution.py:426
  43.6 1.4 %copy-start.5 = (bf16[128,512]{1,0:T(8,128)(2,1)}, bf16[128,512]{1,0:T(8,128)(2,1)S(1)}, u32[]{:S(2)}) copy-start(bf16[128,512]{1,0:T(8,128)(2,1)S(1)} %collective-permute-done.4.beside_in) | copy-start | bytes 393220
  43.7 1.3 %collective-permute-start.9 = (bf16[128,256]{1,0:T(8,128)(2,1)S(1)}, bf16[128,256]{1,0:T(8,128)(2,1)S(1)}, u32[]{:S(2)}, u32[]{:S(2)}) collective-permute-start(bf16[128,256]{1,0:T(8,128)(2,1)S(1)} %constant_dynamic-slice_fusion.1), channel_id=1, source_target_pairs={{0,1},{1,0},{2,3},{3,2},{4,5},{5,4},{6,7},{7,6},{8,9},{9,8},{10,11... | collective-permute-start | bytes 196616 | tf_op jit(solution)/shard_map/ppermute | solution.py:406
  45.0 0.6 copy-start.10
  49.2 2.4 %collective-permute-start.10 = (bf16[1024,256]{1,0:T(8,128)(2,1)S(1)}, bf16[1024,256]{1,0:T(8,128)(2,1)S(1)}, u32[]{:S(2)}, u32[]{:S(2)}) collective-permute-start(bf16[1024,256]{1,0:T(8,128)(2,1)S(1)} %get-tuple-element.105.refs_0_), channel_id=1, source_target_pairs={{0,1},{1,0},{2,3},{3,2},{4,5},{5,4},{6,7},{7,6},{8,9},{9,8},{10,11... | collective-permute-start | bytes 1572872 | tf_op jit(solution)/shard_map/ppermute | solution.py:406
  56.9 26.8 %copy-start = (bf16[128,512]{1,0:T(8,128)(2,1)}, bf16[128,512]{1,0:T(8,128)(2,1)S(1)}, u32[]{:S(2)}) copy-start(bf16[128,512]{1,0:T(8,128)(2,1)S(1)} %get-tuple-element.127.rows_in) | copy-start | bytes 393220
  68.7 20.4 %all-to-all-start.3 = ((bf16[16,128,256]{2,1,0:T(8,128)(2,1)}), bf16[16,128,256]{2,1,0:T(8,128)(2,1)S(1)}, u32[]{:S(2)}, u32[]{:S(2)}) async-start(bf16[16,128,256]{2,1,0:T(8,128)(2,1)} %copies.3), calls=%async_computation.3 | async-start | bytes 2097152 | tf_op jit(solution)/shard_map/all_to_all | solution.py:431
  73.0 14.7 %collective-permute-start.11 = (bf16[128,512]{1,0:T(8,128)(2,1)S(1)}, bf16[128,512]{1,0:T(8,128)(2,1)S(1)}, u32[]{:S(2)}, u32[]{:S(2)}) collective-permute-start(bf16[128,512]{1,0:T(8,128)(2,1)S(1)} %get-tuple-element.127.rows_in), channel_id=1, source_target_pairs={{0,2},{1,255},{2,4},{3,1},{4,6},{5,3},{6,8},{7,5},{8,10},{9,7},{10... | collective-permute-start | bytes 393224 | tf_op jit(solution)/shard_map/ppermute | solution.py:426
  87.7 1.4 %copy-start.6 = (bf16[128,512]{1,0:T(8,128)(2,1)}, bf16[128,512]{1,0:T(8,128)(2,1)S(1)}, u32[]{:S(2)}) copy-start(bf16[128,512]{1,0:T(8,128)(2,1)S(1)} %collective-permute-done.11.beside_in) | copy-start | bytes 393220
  87.7 1.3 %collective-permute-start.12 = (bf16[128,256]{1,0:T(8,128)(2,1)S(1)}, bf16[128,256]{1,0:T(8,128)(2,1)S(1)}, u32[]{:S(2)}, u32[]{:S(2)}) collective-permute-start(bf16[128,256]{1,0:T(8,128)(2,1)S(1)} %constant_dynamic-slice_fusion), channel_id=1, source_target_pairs={{0,1},{1,0},{2,3},{3,2},{4,5},{5,4},{6,7},{7,6},{8,9},{9,8},{10,11... | collective-permute-start | bytes 196616 | tf_op jit(solution)/shard_map/ppermute | solution.py:406
  89.0 0.6 copy-start.9
  93.2 3.6 %collective-permute-start.13 = (bf16[1024,256]{1,0:T(8,128)(2,1)S(1)}, bf16[1024,256]{1,0:T(8,128)(2,1)S(1)}, u32[]{:S(2)}, u32[]{:S(2)}) collective-permute-start(bf16[1024,256]{1,0:T(8,128)(2,1)S(1)} %get-tuple-element.137.refs_0_), channel_id=1, source_target_pairs={{0,1},{1,0},{2,3},{3,2},{4,5},{5,4},{6,7},{7,6},{8,9},{9,8},{10,11... | collective-permute-start | bytes 1572872 | tf_op jit(solution)/shard_map/ppermute | solution.py:406

commit v10 on v9

--- a/solution.py
+++ b/solution.py
@@ -286,7 +286,7 @@
     return (*ready, *edges, *nodes)
 
 
-def update_kernel(last_layer, n_out, scalar_ref, *refs):
+def update_kernel(last_layer, block, n_out, scalar_ref, *refs):
     sent_a_ref, sent_b_ref, before_ref, weights_ref, incidence_ref, small_ref = refs[:6]
     edges_ref, nodes_ref, outs, refs = refs[6], refs[7], refs[8 : 8 + n_out], refs[8 + n_out :]
     edge_out_ref, node_out_ref, hidden_ref, mlp_ref, vectors_ref, out_sems = refs
@@ -307,12 +307,12 @@
         vectors_ref[i] = jnp.broadcast_to(feature_vec[:, column : column + 1], (width, 128))
 
     def spread(index, rows):
-        return jnp.concatenate([vectors_ref[index, rows, :]] * (UPDATE_BLOCK // 128), axis=1)
+        return jnp.concatenate([vectors_ref[index, rows, :]] * (block // 128), axis=1)
 
     slots = edges_ref.shape[1]
     total = None
-    for start in range(0, slots, UPDATE_BLOCK):
-        here = slice(start, start + UPDATE_BLOCK)
+    for start in range(0, slots, block):
+        here = slice(start, start + block)
         sent_a, sent_b = sent_a_ref[here, :], sent_b_ref[here, :]
         low = jnp.where(first, sent_a, sent_b)
         high = jnp.where(first, sent_b, sent_a)
@@ -323,19 +323,19 @@
             value = silu(mlp_ref[rows, :] + before_ref[rows, here])
             hidden_ref[rows, :] = value.astype(jnp.bfloat16)
         mlp_ref[...] = dot(weights_ref[1], hidden_ref[...])
-        new_ref = hidden_ref if last_layer else columns_of(edge_out_ref, start, UPDATE_BLOCK)
-        sums = jnp.zeros((8, UPDATE_BLOCK), jnp.float32)
-        squares = jnp.zeros((8, UPDATE_BLOCK), jnp.float32)
+        new_ref = hidden_ref if last_layer else columns_of(edge_out_ref, start, block)
+        sums = jnp.zeros((8, block), jnp.float32)
+        squares = jnp.zeros((8, block), jnp.float32)
         for row in range(0, width, ROWS):
             rows = slice(row, row + ROWS)
             value = mlp_ref[rows, :] + spread(0, rows)
             mlp_ref[rows, :] = value
-            sums = sums + jnp.sum(value.reshape(ROWS // 8, 8, UPDATE_BLOCK), axis=0)
-            squares = squares + jnp.sum((value * value).reshape(ROWS // 8, 8, UPDATE_BLOCK), axis=0)
+            sums = sums + jnp.sum(value.reshape(ROWS // 8, 8, block), axis=0)
+            squares = squares + jnp.sum((value * value).reshape(ROWS // 8, 8, block), axis=0)
         mean = jnp.sum(sums, axis=0, keepdims=True) * (1.0 / width)
         square = jnp.sum(squares, axis=0, keepdims=True) * (1.0 / width)
         scale = lax.rsqrt(square - mean * mean + EPSILON)
-        live = lax.broadcasted_iota(jnp.int32, (1, UPDATE_BLOCK), 1) + start < count
+        live = lax.broadcasted_iota(jnp.int32, (1, block), 1) + start < count
         for row in range(0, width, ROWS):
             rows = slice(row, row + ROWS)
             value = (mlp_ref[rows, :] - mean) * scale * spread(1, rows) + spread(2, rows)
@@ -347,7 +347,7 @@
         if last_layer:
             edge_out_ref[:, here] = jnp.where(first, updated[:half], updated[half:])
         send(
-            columns_of(edge_out_ref, start, UPDATE_BLOCK), columns_of(outs[0], start, UPDATE_BLOCK)
+            columns_of(edge_out_ref, start, block), columns_of(outs[0], start, block)
         )
     nodes = nodes_ref[...]
     aggregate = total.astype(jnp.bfloat16)
@@ -371,6 +371,7 @@
 
 
 def updated_graph(last_layer, scalars, sent, ready, copies):
+    block = UPDATE_BLOCK if last_layer else UPDATE_BLOCK // 2
     slots = ready[0].shape[1]
     node_rows = ready[5].shape[1]
     half = sent[0].shape[1]
@@ -383,7 +384,7 @@
         out_specs = [HBM, HBM, VMEM, VMEM]
     n_out = len(out_shape)
     return kernel_call(
-        functools.partial(update_kernel, last_layer, n_out),
+        functools.partial(update_kernel, last_layer, block, n_out),
         "update_graph",
         out_shape,
         (scalars, *sent, *ready),
@@ -392,12 +393,12 @@
         held(
             [
                 *out_shape[:2],
-                shape((width, UPDATE_BLOCK)),
-                shape((width, UPDATE_BLOCK), jnp.float32),
+                shape((width, block)),
+                shape((width, block), jnp.float32),
                 shape((3, width, 128), jnp.float32),
             ]
         )
-        + [pltpu.SemaphoreType.DMA((slots // UPDATE_BLOCK + 1,))],
+        + [pltpu.SemaphoreType.DMA((slots // block + 1,))],
         2 * slots * width * (2 * width + node_rows),
     )
 
@@ -406,16 +407,15 @@
     return lax.ppermute(a, "width", [(0, 1), (1, 0)])
 
 
-def copies_kernel(rows_ref, copies_ref):
-    rows = rows_ref[...]
-    for i in range(copies_ref.shape[0]):
-        copies_ref[i] = rows
+def copies_kernel(rows_ref, copies_ref, sems):
+    finish(started([(rows_ref, copies_ref.at[i]) for i in range(copies_ref.shape[0])], sems))
 
 
 def copied(rows, count):
+    sems = [pltpu.SemaphoreType.DMA((count,))]
     return kernel_call(
-        copies_kernel, "copies", shape((count, *rows.shape)), (rows,), [VMEM], VMEM, [], 0
-    )
+        copies_kernel, "copies", [shape((count, *rows.shape))], (rows,), [VMEM], [HBM], sems, 0
+    )[0]
 
 
 def exchanged(rows, copies, others=()):

time: 102 us -> 102 us (level)
  no operation moved by 1% of the time
where the time goes in v10:
time: 102 us; the launch traced here: 101 us
  starting transfers between devices  36.8 us (36%)
  Pallas kernels  33.9 us (33%)
  waiting for transfers between devices  13.9 us (14%)
  blocking collectives  10.7 us (10%)
  other arithmetic  2.68 us (3%)
  between operations  1.89 us (2%)
  local copies, waits for them, and re-layouts  1.48 us (1%)
    pallas_call x9, Pallas kernels, kernel_call(): pl.pallas_call(body, in_specs=in_specs, out_specs=out_specs, out_shape=ou...  33.9 us
    all_to_all x2, starting transfers between devices, exchanged(): lax.all_to_all(plane, PLANE, split_axis=0, concat_axis=0, tiled=True)  11 us
    all_to_all x1, blocking collectives, exchanged(): column = lax.all_to_all(copies, Z, split_axis=0, concat_axis=0, tiled=True)  10.7 us
    ppermute x12, starting transfers between devices, from_other(): return lax.ppermute(a, 'width', [(0, 1), (1, 0)])  10.1 us
    ppermute x2, starting transfers between devices, exchanged(): beside = lax.ppermute(rows, (*PATCH, 'width'), pairs)  9.16 us
    all_to_all x1, starting transfers between devices, exchanged(): column = lax.all_to_all(copies, Z, split_axis=0, concat_axis=0, tiled=True)  6.48 us
    ppermute x12, waiting for transfers between devices, from_other(): return lax.ppermute(a, 'width', [(0, 1), (1, 0)])  5.44 us
    all_to_all x1, waiting for transfers between devices, exchanged(): column = lax.all_to_all(copies, Z, split_axis=0, concat_axis=0, tiled=True)  4.56 us
  transfers between devices with their start and end apart: 17, of which 6 were waited for; matrix products, arithmetic and copies ran while one was open for 3% of the time, Pallas kernels for 15%

profile of v10, /device:TPU:1, one launch (start us, length us, event | category | flops | bytes accessed | tf_op | source)
XLA Modules:
  0.0 101.5 jit_solution(16334119931994294548)
XLA Ops:
  0.6 0.0 copy-start.7
  0.6 0.0 copy-start.3
  0.7 3.3 %collective-permute-start = (bf16[2,256,1536]{2,1,0:T(8,128)(2,1)}, bf16[2,256,1536]{2,1,0:T(8,128)(2,1)S(1)}, u32[]{:S(2)}, u32[]{:S(2)}) collective-permute-start(bf16[2,256,1536]{2,1,0:T(8,128)(2,1)} %refs_1_.3), channel_id=1, source_target_pairs={{0,1},{1,0},{2,3},{3,2},{4,5},{5,4},{6,7},{7,6},{8,9},{9,8},{10,11... | collective-permute-start | bytes 4718600 | tf_op jit(solution)/shard_map/ppermute | solution.py:407
  4.1 0.1 collective-permute-start.1
  4.2 0.4 collective-permute-start.2
  4.6 1.5 %node_rows.1 = (bf16[128,256]{1,0:T(8,128)(2,1)S(1)}, bf16[8,16,256]{2,1,0:T(8,128)(2,1)}) custom-call(bf16[256,128]{1,0:T(8,128)(2,1)} %refs_13_.1), custom_call_target="tpu_custom_call" | custom-call | bytes 4194304 | tf_op jit(solution)/shard_map/node_rows/pallas_call | solution.py:61
  6.1 6.5 %all-to-all-start = ((bf16[8,16,256]{2,1,0:T(8,128)(2,1)}), bf16[8,16,256]{2,1,0:T(8,128)(2,1)S(1)}, u32[]{:S(2)}, u32[]{:S(2)}) async-start(bf16[8,16,256]{2,1,0:T(8,128)(2,1)} %get-tuple-element.74), calls=%async_computation | async-start | bytes 131072 | tf_op jit(solution)/shard_map/all_to_all | solution.py:427
  12.6 1.3 %broadcast_subtract_fusion = s32[1024]{0:T(1024)} fusion(s32[1024]{0:T(1024)} %param.20, s32[]{:T(128)S(6)} %mul.32), kind=kLoop, calls=%fused_computation.27 | loop fusion | flops 1024 | bytes 8196 | tf_op jit(solution)/shard_map/sub | solution.py:509
  13.9 1.3 %fusion.9.index_in = s32[8,128]{1,0:T(8,128)} fusion(s32[1024]{0:T(1024)} %param.19, s32[]{:T(128)S(6)} %select_n.48, s32[]{:T(128)S(6)} %select_n.47, s32[]{:T(128)S(6)} %add.54), kind=kLoop, calls=%fused_computation.19 | loop fusion | flops 50176 | bytes 8204 | tf_op jit(solution)/shard_map/reshape | solution.py:508
  15.2 4.6 %all-to-all-done = bf16[8,16,256]{2,1,0:T(8,128)(2,1)S(1)} async-done(((bf16[8,16,256]{2,1,0:T(8,128)(2,1)}), bf16[8,16,256]{2,1,0:T(8,128)(2,1)S(1)}, u32[]{:S(2)}, u32[]{:S(2)}) %all-to-all-start) | async-done | bytes 65568 | tf_op jit(solution)/shard_map/all_to_all | solution.py:427
  19.7 0.0 collective-permute-done.2.refs_12_
  19.7 0.0 collective-permute-done.1.refs_6_
  19.8 0.0 collective-permute-done.refs_2_
  19.8 1.2 %copies.2 = bf16[16,128,256]{2,1,0:T(8,128)(2,1)} custom-call(bf16[128,256]{1,0:T(8,128)(2,1)S(1)} %bitcast.10), custom_call_target="tpu_custom_call" | custom-call | bytes 4194304 | tf_op jit(solution)/shard_map/copies/pallas_call | solution.py:61
  21.0 0.1 copy-done.2
  21.1 6.8 %all-to-all-start.1 = ((bf16[16,128,256]{2,1,0:T(8,128)(2,1)}), bf16[16,128,256]{2,1,0:T(8,128)(2,1)S(1)}, u32[]{:S(2)}, u32[]{:S(2)}) async-start(bf16[16,128,256]{2,1,0:T(8,128)(2,1)} %copies.2), calls=%async_computation.1 | async-start | bytes 2097152 | tf_op jit(solution)/shard_map/all_to_all | solution.py:431
  27.9 2.0 %collective-permute-start.5 = (bf16[2,256,512]{2,1,0:T(8,128)(2,1)S(1)}, bf16[2,256,512]{2,1,0:T(8,128)(2,1)}, u32[]{:S(2)}, u32[]{:S(2)}) collective-permute-start(bf16[2,256,512]{2,1,0:T(8,128)(2,1)S(1)} %copy-done.3), channel_id=1, source_target_pairs={{0,1},{1,0},{2,3},{3,2},{4,5},{5,4},{6,7},{7,6},{8,9},{9,8},{10,11... | collective-permute-start | bytes 1572872 | tf_op jit(solution)/shard_map/ppermute | solution.py:407
  29.8 0.1 collective-permute-start.6
  29.9 0.4 collective-permute-start.3
  30.4 0.1 collective-permute-start.8
  30.6 0.5 collective-permute-start.7
  31.9 4.7 %collective-permute-start.4 = (bf16[128,512]{1,0:T(8,128)(2,1)S(1)}, bf16[128,512]{1,0:T(8,128)(2,1)S(1)}, u32[]{:S(2)}, u32[]{:S(2)}) collective-permute-start(bf16[128,512]{1,0:T(8,128)(2,1)S(1)} %maximum_select_fusion.rows_in), channel_id=1, source_target_pairs={{0,2},{1,255},{2,4},{3,1},{4,6},{5,3},{6,8},{7,5},{8,10},{9,7},{10... | collective-permute-start | bytes 393224 | tf_op jit(solution)/shard_map/ppermute | solution.py:426
  36.5 0.1 pad_add_fusion.scalar_ref
  36.6 0.0 collective-permute-done.7.refs_10_
  36.6 0.0 collective-permute-done.8.refs_14_
  36.6 0.0 collective-permute-done.6.refs_8_
  36.7 7.1 %prepare_layer.2 = (f32[512,1024]{1,0:T(8,128)}, bf16[5,512,512]{2,1,0:T(8,128)(2,1)}, bf16[128,1024]{1,0:T(8,128)(2,1)}, f32[512,128]{1,0:T(8,128)}, bf16[512,1...) custom-call(s32[2]{0:T(128)S(1)} %pad_add_fusion.scalar_ref, s32[1,1024]{1,0:T(1,128)} %bitcast.12, ...), custom_call_target="tpu_custom_call" | custom-call | flops 671088640 | bytes 4194304 | tf_op jit(solution)/shard_map/prepare_layer/pallas_call | solution.py:61
  43.8 0.2 collective-permute-start.9
  44.0 1.1 %collective-permute-done.9.other_in = bf16[128,256]{1,0:T(8,128)(2,1)S(1)} collective-permute-done((bf16[128,256]{1,0:T(8,128)(2,1)S(1)}, bf16[128,256]{1,0:T(8,128)(2,1)S(1)}, u32[]{:S(2)}, u32[]{:S(2)}) %collective-permute-start.9) | collective-permute-done | bytes 65568 | tf_op jit(solution)/shard_map/ppermute | solution.py:407
  45.2 0.6 copy-done.10
  45.8 3.6 %gather_senders.2 = (bf16[1024,256]{1,0:T(8,128)(2,1)S(1)}, f32[512,1024]{1,0:T(8,128)S(1)}, bf16[5,512,512]{2,1,0:T(8,128)(2,1)S(1)}, bf16[128,1024]{1,0:T(8,12...) custom-call(s32[2]{0:T(128)S(1)} %pad_add_fusion.scalar_ref, ...), custom_call_target="tpu_custom_call" | custom-call | flops 1275068416 | bytes 4194304 | tf_op jit(solution)/shard_map/gather_senders/pallas_call | solution.py:61
  49.3 0.8 collective-permute-start.10
  50.1 1.5 %collective-permute-done.10.refs_1_ = bf16[1024,256]{1,0:T(8,128)(2,1)S(1)} collective-permute-done((bf16[1024,256]{1,0:T(8,128)(2,1)S(1)}, bf16[1024,256]{1,0:T(8,128)(2,1)S(1)}, u32[]{:S(2)}, u32[]{:S(2)}) %collective-permute-start.10) | collective-permute-done | bytes 524320 | tf_op jit(solution)/shard_map/ppermute | solution.py:407
  51.7 5.0 %update_graph.2 = (bf16[512,1024]{1,0:T(8,128)(2,1)}, bf16[512,128]{1,0:T(8,128)(2,1)}, bf16[128,512]{1,0:T(8,128)(2,1)S(1)}, bf16[8,16,256]{2,1,0:T(8,128)(2,1)S(1)}) custom-call(s32[2]{0:T(128)S(1)} %pad_add_fusion.scalar_ref, bf16[1024,256]{1,0:T(8,128)(2,1)S(1)} %get-tuple-element.105.refs_0_, bf16[1024,256]{1,0:T(8,128)(2,1)S(1)} %collective-permute-done.10.refs_1_, ...), custom_call_target="tpu_custom_call" | custom-call | flops 1207959552 | bytes 4194304 | tf_op jit(solution)/shard_map/update_graph/pallas_call | solution.py:61
  56.7 10.7 %all_to_all.20 = bf16[8,16,256]{2,1,0:T(8,128)(2,1)S(1)} all-to-all(bf16[8,16,256]{2,1,0:T(8,128)(2,1)S(1)} %get-tuple-element.120), channel_id=1, replica_groups=mesh['patch_0'=8,'patch_1'=4,'patch_2'=4,'width'=2] {'patch_0'}, dimensions={0} | all-to-all | bytes 131072 | tf_op jit(solution)/shard_map/all_to_all | solution.py:427
  67.5 1.1 %copies.3 = bf16[16,128,256]{2,1,0:T(8,128)(2,1)} custom-call(bf16[128,256]{1,0:T(8,128)(2,1)S(1)} %bitcast.11), custom_call_target="tpu_custom_call" | custom-call | bytes 4194304 | tf_op jit(solution)/shard_map/copies/pallas_call | solution.py:61
  68.6 4.3 %all-to-all-start.3 = ((bf16[16,128,256]{2,1,0:T(8,128)(2,1)}), bf16[16,128,256]{2,1,0:T(8,128)(2,1)S(1)}, u32[]{:S(2)}, u32[]{:S(2)}) async-start(bf16[16,128,256]{2,1,0:T(8,128)(2,1)} %copies.3), calls=%async_computation.3 | async-start | bytes 2097152 | tf_op jit(solution)/shard_map/all_to_all | solution.py:431
  72.9 4.5 %collective-permute-start.11 = (bf16[128,512]{1,0:T(8,128)(2,1)S(1)}, bf16[128,512]{1,0:T(8,128)(2,1)S(1)}, u32[]{:S(2)}, u32[]{:S(2)}) collective-permute-start(bf16[128,512]{1,0:T(8,128)(2,1)S(1)} %get-tuple-element.127.rows_in), channel_id=1, source_target_pairs={{0,2},{1,255},{2,4},{3,1},{4,6},{5,3},{6,8},{7,5},{8,10},{9,7},{10... | collective-permute-start | bytes 393224 | tf_op jit(solution)/shard_map/ppermute | solution.py:426
  77.4 6.3 %prepare_layer.3 = (f32[512,1024]{1,0:T(8,128)}, bf16[5,512,512]{2,1,0:T(8,128)(2,1)}, bf16[128,1024]{1,0:T(8,128)(2,1)}, f32[512,128]{1,0:T(8,128)}) custom-call(s32[2]{0:T(128)S(1)} %pad_add_fusion.scalar_ref, s32[1,1024]{1,0:T(1,128)} %bitcast.13, bf16[2,256,1536]{2,1,0:T(8,128)(2,1)} %refs_1_.3, bf16[2,256,1536]{2,1,0:T(8,128)(2,1)} %copy-done.1, ...), custom_call_target="tpu_custom_call" | custom-call | flops 671088640 | bytes 4194304 | tf_op jit(solution)/shard_map/prepare_layer/pallas_call | solution.py:61
  83.6 3.9 %collective-permute-done.11.beside_in = bf16[128,512]{1,0:T(8,128)(2,1)S(1)} collective-permute-done((bf16[128,512]{1,0:T(8,128)(2,1)S(1)}, bf16[128,512]{1,0:T(8,128)(2,1)S(1)}, u32[]{:S(2)}, u32[]{:S(2)}) %collective-permute-start.11) | collective-permute-done | bytes 131104 | tf_op jit(solution)/shard_map/ppermute | solution.py:426
  87.5 0.1 collective-permute-start.12
  87.6 1.2 %collective-permute-done.12.other_in = bf16[128,256]{1,0:T(8,128)(2,1)S(1)} collective-permute-done((bf16[128,256]{1,0:T(8,128)(2,1)S(1)}, bf16[128,256]{1,0:T(8,128)(2,1)S(1)}, u32[]{:S(2)}, u32[]{:S(2)}) %collective-permute-start.12) | collective-permute-done | bytes 65568 | tf_op jit(solution)/shard_map/ppermute | solution.py:407
  88.9 0.0 all-to-all-done.3
  88.9 0.6 copy-done.9
  89.5 3.6 %gather_senders.3 = (bf16[1024,256]{1,0:T(8,128)(2,1)S(1)}, f32[512,1024]{1,0:T(8,128)S(1)}, bf16[5,512,512]{2,1,0:T(8,128)(2,1)S(1)}, bf16[128,1024]{1,0:T(8,12...) custom-call(s32[2]{0:T(128)S(1)} %pad_add_fusion.scalar_ref, ...), custom_call_target="tpu_custom_call" | custom-call | flops 1275068416 | bytes 4194304 | tf_op jit(solution)/shard_map/gather_senders/pallas_call | solution.py:61
  93.1 2.1 %collective-permute-start.13 = (bf16[1024,256]{1,0:T(8,128)(2,1)S(1)}, bf16[1024,256]{1,0:T(8,128)(2,1)S(1)}, u32[]{:S(2)}, u32[]{:S(2)}) collective-permute-start(bf16[1024,256]{1,0:T(8,128)(2,1)S(1)} %get-tuple-element.137.refs_0_), channel_id=1, source_target_pairs={{0,1},{1,0},{2,3},{3,2},{4,5},{5,4},{6,7},{7,6},{8,9},{9,8},{10,11... | collective-permute-start | bytes 1572872 | tf_op jit(solution)/shard_map/ppermute | solution.py:407
  95.2 1.5 %collective-permute-done.13.refs_1_ = bf16[1024,256]{1,0:T(8,128)(2,1)S(1)} collective-permute-done((bf16[1024,256]{1,0:T(8,128)(2,1)S(1)}, bf16[1024,256]{1,0:T(8,128)(2,1)S(1)}, u32[]{:S(2)}, u32[]{:S(2)}) %collective-permute-start.13) | collective-permute-done | bytes 524320 | tf_op jit(solution)/shard_map/ppermute | solution.py:407
  96.7 4.6 %update_graph.3 = (bf16[256,1024]{1,0:T(8,128)(2,1)}, bf16[256,128]{1,0:T(8,128)(2,1)}) custom-call(s32[2]{0:T(128)S(1)} %pad_add_fusion.scalar_ref, bf16[1024,256]{1,0:T(8,128)(2,1)S(1)} %get-tuple-element.137.refs_0_, bf16[1024,256]{1,0:T(8,128)(2,1)S(1)} %collective-permute-done.13.refs_1_, f32[512,1024]{1,0:T(8,128)S(1)} %get-tuple-element.138.refs_2_, ...), custom_call_target="tpu_custom_call" | custom-call | flops 1207959552 | bytes 4194304 | tf_op jit(solution)/shard_map/update_graph/pallas_call | solution.py:61
  (49 shorter events, 0.2 us)
Async XLA Ops:
  0.6 29.7 %copy-start.7 = (bf16[256,128]{1,0:T(8,128)(2,1)S(1)}, bf16[256,128]{1,0:T(8,128)(2,1)}, u32[]{:S(2)}) copy-start(bf16[256,128]{1,0:T(8,128)(2,1)} %refs_13_.1) | copy-start | bytes 196612
  0.6 27.2 %copy-start.3 = (bf16[2,256,512]{2,1,0:T(8,128)(2,1)S(1)}, bf16[2,256,512]{2,1,0:T(8,128)(2,1)}, u32[]{:S(2)}) copy-start(bf16[2,256,512]{2,1,0:T(8,128)(2,1)} %refs_3_.3) | copy-start | bytes 1572868
  0.7 29.8 %copy-start.11 = (f32[2,256]{1,0:T(2,128)S(1)}, f32[2,256]{1,0:T(2,128)}, u32[]{:S(2)}) copy-start(f32[2,256]{1,0:T(2,128)} %param.23) | copy-start | bytes 6148
  0.7 29.8 %copy-start.12 = (f32[2,256]{1,0:T(2,128)S(1)}, f32[2,256]{1,0:T(2,128)}, u32[]{:S(2)}) copy-start(f32[2,256]{1,0:T(2,128)} %param.25) | copy-start | bytes 6148
  0.7 29.8 %copy-start.13 = (f32[2,256]{1,0:T(2,128)S(1)}, f32[2,256]{1,0:T(2,128)}, u32[]{:S(2)}) copy-start(f32[2,256]{1,0:T(2,128)} %param.26) | copy-start | bytes 6148
  0.7 29.8 %copy-start.14 = (f32[2,256]{1,0:T(2,128)S(1)}, f32[2,256]{1,0:T(2,128)}, u32[]{:S(2)}) copy-start(f32[2,256]{1,0:T(2,128)} %param.27) | copy-start | bytes 6148
  0.7 29.8 %copy-start.15 = (f32[2,256]{1,0:T(2,128)S(1)}, f32[2,256]{1,0:T(2,128)}, u32[]{:S(2)}) copy-start(f32[2,256]{1,0:T(2,128)} %param.29) | copy-start | bytes 6148
  0.7 29.8 %copy-start.16 = (f32[2,256]{1,0:T(2,128)S(1)}, f32[2,256]{1,0:T(2,128)}, u32[]{:S(2)}) copy-start(f32[2,256]{1,0:T(2,128)} %param.31) | copy-start | bytes 6148
  0.7 29.8 %copy-start.17 = (f32[2,256]{1,0:T(2,128)S(1)}, f32[2,256]{1,0:T(2,128)}, u32[]{:S(2)}) copy-start(f32[2,256]{1,0:T(2,128)} %param.32) | copy-start | bytes 6148
  0.7 29.9 %copy-start.18 = (f32[2,256]{1,0:T(2,128)S(1)}, f32[2,256]{1,0:T(2,128)}, u32[]{:S(2)}) copy-start(f32[2,256]{1,0:T(2,128)} %param.33) | copy-start | bytes 6148
  0.7 19.0 %collective-permute-start = (bf16[2,256,1536]{2,1,0:T(8,128)(2,1)}, bf16[2,256,1536]{2,1,0:T(8,128)(2,1)S(1)}, u32[]{:S(2)}, u32[]{:S(2)}) collective-permute-start(bf16[2,256,1536]{2,1,0:T(8,128)(2,1)} %refs_1_.3), channel_id=1, source_target_pairs={{0,1},{1,0},{2,3},{3,2},{4,5},{5,4},{6,7},{7,6},{8,9},{9,8},{10,11... | collective-permute-start | bytes 4718600 | tf_op jit(solution)/shard_map/ppermute | solution.py:407
  4.1 15.7 %collective-permute-start.1 = (bf16[2,256,1024]{2,1,0:T(8,128)(2,1)}, bf16[2,256,1024]{2,1,0:T(8,128)(2,1)S(1)}, u32[]{:S(2)}, u32[]{:S(2)}) collective-permute-start(bf16[2,256,1024]{2,1,0:T(8,128)(2,1)} %refs_5_.3), channel_id=1, source_target_pairs={{0,1},{1,0},{2,3},{3,2},{4,5},{5,4},{6,7},{7,6},{8,9},{9,8},{10,11... | collective-permute-start | bytes 3145736 | tf_op jit(solution)/shard_map/ppermute | solution.py:407
  4.2 15.6 %collective-permute-start.2 = (bf16[256,1024]{1,0:T(8,128)(2,1)}, bf16[256,1024]{1,0:T(8,128)(2,1)}, u32[]{:S(2)}, u32[]{:S(2)}) collective-permute-start(bf16[256,1024]{1,0:T(8,128)(2,1)} %refs_11_.1), channel_id=1, source_target_pairs={{0,1},{1,0},{2,3},{3,2},{4,5},{5,4},{6,7},{7,6},{8,9},{9,8},{10,11... | collective-permute-start | bytes 1572872 | tf_op jit(solution)/shard_map/ppermute | solution.py:407
  6.1 13.6 %all-to-all-start = ((bf16[8,16,256]{2,1,0:T(8,128)(2,1)}), bf16[8,16,256]{2,1,0:T(8,128)(2,1)S(1)}, u32[]{:S(2)}, u32[]{:S(2)}) async-start(bf16[8,16,256]{2,1,0:T(8,128)(2,1)} %get-tuple-element.74), calls=%async_computation | async-start | bytes 131072 | tf_op jit(solution)/shard_map/all_to_all | solution.py:427
  19.8 1.4 %copy-start.2 = (bf16[2,256,1024]{2,1,0:T(8,128)(2,1)}, bf16[2,256,1024]{2,1,0:T(8,128)(2,1)S(1)}, u32[]{:S(2)}) copy-start(bf16[2,256,1024]{2,1,0:T(8,128)(2,1)S(1)} %collective-permute-done.1.refs_6_) | copy-start | bytes 3145732
  19.8 16.9 %copy-start.1 = (bf16[2,256,1536]{2,1,0:T(8,128)(2,1)}, bf16[2,256,1536]{2,1,0:T(8,128)(2,1)S(1)}, u32[]{:S(2)}) copy-start(bf16[2,256,1536]{2,1,0:T(8,128)(2,1)S(1)} %collective-permute-done.refs_2_) | copy-start | bytes 4718596
  21.1 24.0 %all-to-all-start.1 = ((bf16[16,128,256]{2,1,0:T(8,128)(2,1)}), bf16[16,128,256]{2,1,0:T(8,128)(2,1)S(1)}, u32[]{:S(2)}, u32[]{:S(2)}) async-start(bf16[16,128,256]{2,1,0:T(8,128)(2,1)} %copies.2), calls=%async_computation.1 | async-start | bytes 2097152 | tf_op jit(solution)/shard_map/all_to_all | solution.py:431
  27.9 8.8 %collective-permute-start.5 = (bf16[2,256,512]{2,1,0:T(8,128)(2,1)S(1)}, bf16[2,256,512]{2,1,0:T(8,128)(2,1)}, u32[]{:S(2)}, u32[]{:S(2)}) collective-permute-start(bf16[2,256,512]{2,1,0:T(8,128)(2,1)S(1)} %copy-done.3), channel_id=1, source_target_pairs={{0,1},{1,0},{2,3},{3,2},{4,5},{5,4},{6,7},{7,6},{8,9},{9,8},{10,11... | collective-permute-start | bytes 1572872 | tf_op jit(solution)/shard_map/ppermute | solution.py:407
  29.8 6.8 %collective-permute-start.6 = (bf16[2,256,512]{2,1,0:T(8,128)(2,1)}, bf16[2,256,512]{2,1,0:T(8,128)(2,1)}, u32[]{:S(2)}, u32[]{:S(2)}) collective-permute-start(bf16[2,256,512]{2,1,0:T(8,128)(2,1)} %refs_7_.3), channel_id=1, source_target_pairs={{0,1},{1,0},{2,3},{3,2},{4,5},{5,4},{6,7},{7,6},{8,9},{9,8},{10,11... | collective-permute-start | bytes 1572872 | tf_op jit(solution)/shard_map/ppermute | solution.py:407
  29.9 1.9 %collective-permute-start.3 = (bf16[128,256]{1,0:T(8,128)(2,1)S(1)}, bf16[128,256]{1,0:T(8,128)(2,1)S(1)}, u32[]{:S(2)}, u32[]{:S(2)}) collective-permute-start(bf16[128,256]{1,0:T(8,128)(2,1)S(1)} %get-tuple-element.76), channel_id=1, source_target_pairs={{0,1},{1,0},{2,3},{3,2},{4,5},{5,4},{6,7},{7,6},{8,9},{9,8},{10,11... | collective-permute-start | bytes 196616 | tf_op jit(solution)/shard_map/ppermute | solution.py:407
  30.4 6.3 %collective-permute-start.8 = (bf16[256,128]{1,0:T(8,128)(2,1)S(1)}, bf16[256,128]{1,0:T(8,128)(2,1)}, u32[]{:S(2)}, u32[]{:S(2)}) collective-permute-start(bf16[256,128]{1,0:T(8,128)(2,1)S(1)} %copy-done.7), channel_id=1, source_target_pairs={{0,1},{1,0},{2,3},{3,2},{4,5},{5,4},{6,7},{7,6},{8,9},{9,8},{10,11... | collective-permute-start | bytes 196616 | tf_op jit(solution)/shard_map/ppermute | solution.py:407
  30.6 6.0 %copy-start.8 = (f32[2,8,256]{2,1,0:T(8,128)}, f32[2,8,256]{2,1,0:T(8,128)S(1)}, u32[]{:S(2)}) copy-start(f32[2,8,256]{2,1,0:T(8,128)S(1)} %stack.43.refs_9_) | copy-start | bytes 49156
  30.6 6.0 %collective-permute-start.7 = (f32[2,8,256]{2,1,0:T(8,128)S(1)}, f32[2,8,256]{2,1,0:T(8,128)}, u32[]{:S(2)}, u32[]{:S(2)}) collective-permute-start(f32[2,8,256]{2,1,0:T(8,128)S(1)} %stack.43.refs_9_), channel_id=1, source_target_pairs={{0,1},{1,0},{2,3},{3,2},{4,5},{5,4},{6,7},{7,6},{8,9},{9,8},{10,11... | collective-permute-start | bytes 49160 | tf_op jit(solution)/shard_map/ppermute | solution.py:407
  31.8 11.9 %copy-start.4 = (bf16[128,512]{1,0:T(8,128)(2,1)}, bf16[128,512]{1,0:T(8,128)(2,1)S(1)}, u32[]{:S(2)}) copy-start(bf16[128,512]{1,0:T(8,128)(2,1)S(1)} %maximum_select_fusion.rows_in) | copy-start | bytes 393220
  31.9 11.9 %collective-permute-start.4 = (bf16[128,512]{1,0:T(8,128)(2,1)S(1)}, bf16[128,512]{1,0:T(8,128)(2,1)S(1)}, u32[]{:S(2)}, u32[]{:S(2)}) collective-permute-start(bf16[128,512]{1,0:T(8,128)(2,1)S(1)} %maximum_select_fusion.rows_in), channel_id=1, source_target_pairs={{0,2},{1,255},{2,4},{3,1},{4,6},{5,3},{6,8},{7,5},{8,10},{9,7},{10... | collective-permute-start | bytes 393224 | tf_op jit(solution)/shard_map/ppermute | solution.py:426
  43.8 1.4 %copy-start.5 = (bf16[128,512]{1,0:T(8,128)(2,1)}, bf16[128,512]{1,0:T(8,128)(2,1)S(1)}, u32[]{:S(2)}) copy-start(bf16[128,512]{1,0:T(8,128)(2,1)S(1)} %collective-permute-done.4.beside_in) | copy-start | bytes 393220
  43.8 1.3 %collective-permute-start.9 = (bf16[128,256]{1,0:T(8,128)(2,1)S(1)}, bf16[128,256]{1,0:T(8,128)(2,1)S(1)}, u32[]{:S(2)}, u32[]{:S(2)}) collective-permute-start(bf16[128,256]{1,0:T(8,128)(2,1)S(1)} %constant_dynamic-slice_fusion.1), channel_id=1, source_target_pairs={{0,1},{1,0},{2,3},{3,2},{4,5},{5,4},{6,7},{7,6},{8,9},{9,8},{10,11... | collective-permute-start | bytes 196616 | tf_op jit(solution)/shard_map/ppermute | solution.py:407
  45.1 0.6 copy-start.10
  49.3 2.3 %collective-permute-start.10 = (bf16[1024,256]{1,0:T(8,128)(2,1)S(1)}, bf16[1024,256]{1,0:T(8,128)(2,1)S(1)}, u32[]{:S(2)}, u32[]{:S(2)}) collective-permute-start(bf16[1024,256]{1,0:T(8,128)(2,1)S(1)} %get-tuple-element.105.refs_0_), channel_id=1, source_target_pairs={{0,1},{1,0},{2,3},{3,2},{4,5},{5,4},{6,7},{7,6},{8,9},{9,8},{10,11... | collective-permute-start | bytes 1572872 | tf_op jit(solution)/shard_map/ppermute | solution.py:407
  56.7 26.9 %copy-start = (bf16[128,512]{1,0:T(8,128)(2,1)}, bf16[128,512]{1,0:T(8,128)(2,1)S(1)}, u32[]{:S(2)}) copy-start(bf16[128,512]{1,0:T(8,128)(2,1)S(1)} %get-tuple-element.127.rows_in) | copy-start | bytes 393220
  68.6 20.3 %all-to-all-start.3 = ((bf16[16,128,256]{2,1,0:T(8,128)(2,1)}), bf16[16,128,256]{2,1,0:T(8,128)(2,1)S(1)}, u32[]{:S(2)}, u32[]{:S(2)}) async-start(bf16[16,128,256]{2,1,0:T(8,128)(2,1)} %copies.3), calls=%async_computation.3 | async-start | bytes 2097152 | tf_op jit(solution)/shard_map/all_to_all | solution.py:431
  72.9 14.6 %collective-permute-start.11 = (bf16[128,512]{1,0:T(8,128)(2,1)S(1)}, bf16[128,512]{1,0:T(8,128)(2,1)S(1)}, u32[]{:S(2)}, u32[]{:S(2)}) collective-permute-start(bf16[128,512]{1,0:T(8,128)(2,1)S(1)} %get-tuple-element.127.rows_in), channel_id=1, source_target_pairs={{0,2},{1,255},{2,4},{3,1},{4,6},{5,3},{6,8},{7,5},{8,10},{9,7},{10... | collective-permute-start | bytes 393224 | tf_op jit(solution)/shard_map/ppermute | solution.py:426
  87.5 1.4 %copy-start.6 = (bf16[128,512]{1,0:T(8,128)(2,1)}, bf16[128,512]{1,0:T(8,128)(2,1)S(1)}, u32[]{:S(2)}) copy-start(bf16[128,512]{1,0:T(8,128)(2,1)S(1)} %collective-permute-done.11.beside_in) | copy-start | bytes 393220
  87.5 1.3 %collective-permute-start.12 = (bf16[128,256]{1,0:T(8,128)(2,1)S(1)}, bf16[128,256]{1,0:T(8,128)(2,1)S(1)}, u32[]{:S(2)}, u32[]{:S(2)}) collective-permute-start(bf16[128,256]{1,0:T(8,128)(2,1)S(1)} %constant_dynamic-slice_fusion), channel_id=1, source_target_pairs={{0,1},{1,0},{2,3},{3,2},{4,5},{5,4},{6,7},{7,6},{8,9},{9,8},{10,11... | collective-permute-start | bytes 196616 | tf_op jit(solution)/shard_map/ppermute | solution.py:407
  88.9 0.6 copy-start.9
  93.1 3.6 %collective-permute-start.13 = (bf16[1024,256]{1,0:T(8,128)(2,1)S(1)}, bf16[1024,256]{1,0:T(8,128)(2,1)S(1)}, u32[]{:S(2)}, u32[]{:S(2)}) collective-permute-start(bf16[1024,256]{1,0:T(8,128)(2,1)S(1)} %get-tuple-element.137.refs_0_), channel_id=1, source_target_pairs={{0,1},{1,0},{2,3},{3,2},{4,5},{5,4},{6,7},{7,6},{8,9},{9,8},{10,11... | collective-permute-start | bytes 1572872 | tf_op jit(solution)/shard_map/ppermute | solution.py:407

commit v11 on v10

--- a/solution.py
+++ b/solution.py
@@ -241,7 +241,7 @@
     sent[2].start()
     receiver_part = dot(hidden_weight_ref[1], nodes).astype(jnp.bfloat16)
     before = dot(hidden_weight_ref[0], edges) + dot(receiver_part, incidence_ref[...])
-    before_ref[...] = before + hidden_vec[:, 0:1]
+    before_ref[...] = (before + hidden_vec[:, 0:1]).astype(jnp.bfloat16)
     sent[0].start()
     finish(sent)
 
@@ -252,7 +252,7 @@
     width = weights[0].shape[1] * 2
     inputs = (receiver, *weights, *edges, *nodes)
     out_shape = [
-        shape((width, slots), jnp.float32),
+        shape((width, slots)),
         shape((5, width, width)),
         shape((node_rows, slots)),
         shape((width, 128), jnp.float32),
@@ -320,7 +320,7 @@
         mlp_ref[...] = dot(weights_ref[0], sent, ((1,), (1,)))
         for row in range(0, width, ROWS):
             rows = slice(row, row + ROWS)
-            value = silu(mlp_ref[rows, :] + before_ref[rows, here])
+            value = silu(mlp_ref[rows, :] + before_ref[rows, here].astype(jnp.float32))
             hidden_ref[rows, :] = value.astype(jnp.bfloat16)
         mlp_ref[...] = dot(weights_ref[1], hidden_ref[...])
         new_ref = hidden_ref if last_layer else columns_of(edge_out_ref, start, block)

time: 102 us -> 102 us (level)
    pallas_call x9, Pallas kernels: 33.9 us -> 32.9 us  [kernel_call(): pl.pallas_call(body, in_specs=in_specs, out_specs=out_specs, out_shape=ou...]
  transfers between devices with their start and end apart: 17 -> 17, of which waited for: 6 -> 6; matrix products, arithmetic and copies ran while one was open for 3% -> 3% of each run, Pallas kernels for 15% -> 14%
where the time goes in v11:
time: 102 us; the launch traced here: 101 us
  starting transfers between devices  37.8 us (37%)
  Pallas kernels  32.9 us (32%)
  waiting for transfers between devices  14.1 us (14%)
  blocking collectives  10.4 us (10%)
  other arithmetic  2.69 us (3%)
  between operations  1.89 us (2%)
  local copies, waits for them, and re-layouts  1.56 us (2%)
    pallas_call x9, Pallas kernels, kernel_call(): pl.pallas_call(body, in_specs=in_specs, out_specs=out_specs, out_shape=ou...  32.9 us
    all_to_all x2, starting transfers between devices, exchanged(): lax.all_to_all(plane, PLANE, split_axis=0, concat_axis=0, tiled=True)  11.4 us
    ppermute x12, starting transfers between devices, from_other(): return lax.ppermute(a, 'width', [(0, 1), (1, 0)])  10.7 us
    all_to_all x1, blocking collectives, exchanged(): column = lax.all_to_all(copies, Z, split_axis=0, concat_axis=0, tiled=True)  10.4 us
    ppermute x2, starting transfers between devices, exchanged(): beside = lax.ppermute(rows, (*PATCH, 'width'), pairs)  9.16 us
    all_to_all x1, starting transfers between devices, exchanged(): column = lax.all_to_all(copies, Z, split_axis=0, concat_axis=0, tiled=True)  6.48 us
    ppermute x12, waiting for transfers between devices, from_other(): return lax.ppermute(a, 'width', [(0, 1), (1, 0)])  5.24 us
    all_to_all x1, waiting for transfers between devices, exchanged(): column = lax.all_to_all(copies, Z, split_axis=0, concat_axis=0, tiled=True)  4.56 us
  transfers between devices with their start and end apart: 17, of which 6 were waited for; matrix products, arithmetic and copies ran while one was open for 3% of the time, Pallas kernels for 14%

profile of v11, /device:TPU:1, one launch (start us, length us, event | category | flops | bytes accessed | tf_op | source)
XLA Modules:
  0.0 101.3 jit_solution(3228174581549514774)
XLA Ops:
  0.6 0.0 copy-start.7
  0.6 0.0 copy-start.3
  0.7 3.3 %collective-permute-start = (bf16[2,256,1536]{2,1,0:T(8,128)(2,1)}, bf16[2,256,1536]{2,1,0:T(8,128)(2,1)S(1)}, u32[]{:S(2)}, u32[]{:S(2)}) collective-permute-start(bf16[2,256,1536]{2,1,0:T(8,128)(2,1)} %refs_1_.3), channel_id=1, source_target_pairs={{0,1},{1,0},{2,3},{3,2},{4,5},{5,4},{6,7},{7,6},{8,9},{9,8},{10,11... | collective-permute-start | bytes 4718600 | tf_op jit(solution)/shard_map/ppermute | solution.py:407
  4.1 0.1 collective-permute-start.1
  4.2 0.4 collective-permute-start.2
  4.6 1.5 %node_rows.1 = (bf16[128,256]{1,0:T(8,128)(2,1)S(1)}, bf16[8,16,256]{2,1,0:T(8,128)(2,1)}) custom-call(bf16[256,128]{1,0:T(8,128)(2,1)} %refs_13_.1), custom_call_target="tpu_custom_call" | custom-call | bytes 4194304 | tf_op jit(solution)/shard_map/node_rows/pallas_call | solution.py:61
  6.1 6.5 %all-to-all-start = ((bf16[8,16,256]{2,1,0:T(8,128)(2,1)}), bf16[8,16,256]{2,1,0:T(8,128)(2,1)S(1)}, u32[]{:S(2)}, u32[]{:S(2)}) async-start(bf16[8,16,256]{2,1,0:T(8,128)(2,1)} %get-tuple-element.74), calls=%async_computation | async-start | bytes 131072 | tf_op jit(solution)/shard_map/all_to_all | solution.py:427
  12.6 1.3 %broadcast_subtract_fusion = s32[1024]{0:T(1024)} fusion(s32[1024]{0:T(1024)} %param.20, s32[]{:T(128)S(6)} %mul.32), kind=kLoop, calls=%fused_computation.27 | loop fusion | flops 1024 | bytes 8196 | tf_op jit(solution)/shard_map/sub | solution.py:509
  13.9 1.3 %fusion.9.index_in = s32[8,128]{1,0:T(8,128)} fusion(s32[1024]{0:T(1024)} %param.19, s32[]{:T(128)S(6)} %select_n.48, s32[]{:T(128)S(6)} %select_n.47, s32[]{:T(128)S(6)} %add.54), kind=kLoop, calls=%fused_computation.19 | loop fusion | flops 50176 | bytes 8204 | tf_op jit(solution)/shard_map/reshape | solution.py:508
  15.2 4.6 %all-to-all-done = bf16[8,16,256]{2,1,0:T(8,128)(2,1)S(1)} async-done(((bf16[8,16,256]{2,1,0:T(8,128)(2,1)}), bf16[8,16,256]{2,1,0:T(8,128)(2,1)S(1)}, u32[]{:S(2)}, u32[]{:S(2)}) %all-to-all-start) | async-done | bytes 65568 | tf_op jit(solution)/shard_map/all_to_all | solution.py:427
  19.7 0.0 collective-permute-done.2.refs_12_
  19.7 0.0 collective-permute-done.1.refs_6_
  19.8 0.0 collective-permute-done.refs_2_
  19.8 1.2 %copies.2 = bf16[16,128,256]{2,1,0:T(8,128)(2,1)} custom-call(bf16[128,256]{1,0:T(8,128)(2,1)S(1)} %bitcast.10), custom_call_target="tpu_custom_call" | custom-call | bytes 4194304 | tf_op jit(solution)/shard_map/copies/pallas_call | solution.py:61
  20.9 0.2 copy-done.2
  21.1 6.8 %all-to-all-start.1 = ((bf16[16,128,256]{2,1,0:T(8,128)(2,1)}), bf16[16,128,256]{2,1,0:T(8,128)(2,1)S(1)}, u32[]{:S(2)}, u32[]{:S(2)}) async-start(bf16[16,128,256]{2,1,0:T(8,128)(2,1)} %copies.2), calls=%async_computation.1 | async-start | bytes 2097152 | tf_op jit(solution)/shard_map/all_to_all | solution.py:431
  27.9 2.0 %collective-permute-start.5 = (bf16[2,256,512]{2,1,0:T(8,128)(2,1)S(1)}, bf16[2,256,512]{2,1,0:T(8,128)(2,1)}, u32[]{:S(2)}, u32[]{:S(2)}) collective-permute-start(bf16[2,256,512]{2,1,0:T(8,128)(2,1)S(1)} %copy-done.3), channel_id=1, source_target_pairs={{0,1},{1,0},{2,3},{3,2},{4,5},{5,4},{6,7},{7,6},{8,9},{9,8},{10,11... | collective-permute-start | bytes 1572872 | tf_op jit(solution)/shard_map/ppermute | solution.py:407
  29.8 0.1 collective-permute-start.6
  29.9 0.4 collective-permute-start.3
  30.4 0.1 collective-permute-start.8
  30.7 0.5 collective-permute-start.7
  31.8 0.0 collective-permute-done.3
  31.9 4.7 %collective-permute-start.4 = (bf16[128,512]{1,0:T(8,128)(2,1)S(1)}, bf16[128,512]{1,0:T(8,128)(2,1)S(1)}, u32[]{:S(2)}, u32[]{:S(2)}) collective-permute-start(bf16[128,512]{1,0:T(8,128)(2,1)S(1)} %maximum_select_fusion.rows_in), channel_id=1, source_target_pairs={{0,2},{1,255},{2,4},{3,1},{4,6},{5,3},{6,8},{7,5},{8,10},{9,7},{10... | collective-permute-start | bytes 393224 | tf_op jit(solution)/shard_map/ppermute | solution.py:426
  36.6 0.1 pad_add_fusion.scalar_ref
  36.6 0.0 collective-permute-done.7.refs_10_
  36.6 0.0 collective-permute-done.8.refs_14_
  36.6 0.0 collective-permute-done.5.refs_4_
  36.7 6.7 %prepare_layer.2 = (bf16[512,1024]{1,0:T(8,128)(2,1)}, bf16[5,512,512]{2,1,0:T(8,128)(2,1)}, bf16[128,1024]{1,0:T(8,128)(2,1)}, f32[512,128]{1,0:T(8,128)}, bf16...) custom-call(s32[2]{0:T(128)S(1)} %pad_add_fusion.scalar_ref, s32[1,1024]{1,0:T(1,128)} %bitcast.12, ...), custom_call_target="tpu_custom_call" | custom-call | flops 671088640 | bytes 4194304 | tf_op jit(solution)/shard_map/prepare_layer/pallas_call | solution.py:61
  43.4 0.6 collective-permute-start.9
  44.1 0.9 collective-permute-done.9.other_in
  45.0 0.6 copy-done.10
  45.6 3.4 %gather_senders.2 = (bf16[1024,256]{1,0:T(8,128)(2,1)S(1)}, bf16[512,1024]{1,0:T(8,128)(2,1)S(1)}, bf16[5,512,512]{2,1,0:T(8,128)(2,1)S(1)}, bf16[128,1024]{1,0:...) custom-call(s32[2]{0:T(128)S(1)} %pad_add_fusion.scalar_ref, ...), custom_call_target="tpu_custom_call" | custom-call | flops 1275068416 | bytes 4194304 | tf_op jit(solution)/shard_map/gather_senders/pallas_call | solution.py:61
  49.0 1.0 collective-permute-start.10
  49.9 1.5 %collective-permute-done.10.refs_1_ = bf16[1024,256]{1,0:T(8,128)(2,1)S(1)} collective-permute-done((bf16[1024,256]{1,0:T(8,128)(2,1)S(1)}, bf16[1024,256]{1,0:T(8,128)(2,1)S(1)}, u32[]{:S(2)}, u32[]{:S(2)}) %collective-permute-start.10) | collective-permute-done | bytes 524320 | tf_op jit(solution)/shard_map/ppermute | solution.py:407
  51.5 5.1 %update_graph.2 = (bf16[512,1024]{1,0:T(8,128)(2,1)}, bf16[512,128]{1,0:T(8,128)(2,1)}, bf16[128,512]{1,0:T(8,128)(2,1)S(1)}, bf16[8,16,256]{2,1,0:T(8,128)(2,1)S(1)}) custom-call(s32[2]{0:T(128)S(1)} %pad_add_fusion.scalar_ref, bf16[1024,256]{1,0:T(8,128)(2,1)S(1)} %get-tuple-element.105.refs_0_, bf16[1024,256]{1,0:T(8,128)(2,1)S(1)} %collective-permute-done.10.refs_1_, ...), custom_call_target="tpu_custom_call" | custom-call | flops 1207959552 | bytes 4194304 | tf_op jit(solution)/shard_map/update_graph/pallas_call | solution.py:61
  56.6 10.4 %all_to_all.20 = bf16[8,16,256]{2,1,0:T(8,128)(2,1)S(1)} all-to-all(bf16[8,16,256]{2,1,0:T(8,128)(2,1)S(1)} %get-tuple-element.120), channel_id=1, replica_groups=mesh['patch_0'=8,'patch_1'=4,'patch_2'=4,'width'=2] {'patch_0'}, dimensions={0} | all-to-all | bytes 131072 | tf_op jit(solution)/shard_map/all_to_all | solution.py:427
  66.9 1.2 %copies.3 = bf16[16,128,256]{2,1,0:T(8,128)(2,1)} custom-call(bf16[128,256]{1,0:T(8,128)(2,1)S(1)} %bitcast.11), custom_call_target="tpu_custom_call" | custom-call | bytes 4194304 | tf_op jit(solution)/shard_map/copies/pallas_call | solution.py:61
  68.1 4.7 %all-to-all-start.3 = ((bf16[16,128,256]{2,1,0:T(8,128)(2,1)}), bf16[16,128,256]{2,1,0:T(8,128)(2,1)S(1)}, u32[]{:S(2)}, u32[]{:S(2)}) async-start(bf16[16,128,256]{2,1,0:T(8,128)(2,1)} %copies.3), calls=%async_computation.3 | async-start | bytes 2097152 | tf_op jit(solution)/shard_map/all_to_all | solution.py:431
  72.8 4.5 %collective-permute-start.11 = (bf16[128,512]{1,0:T(8,128)(2,1)S(1)}, bf16[128,512]{1,0:T(8,128)(2,1)S(1)}, u32[]{:S(2)}, u32[]{:S(2)}) collective-permute-start(bf16[128,512]{1,0:T(8,128)(2,1)S(1)} %get-tuple-element.127.rows_in), channel_id=1, source_target_pairs={{0,2},{1,255},{2,4},{3,1},{4,6},{5,3},{6,8},{7,5},{8,10},{9,7},{10... | collective-permute-start | bytes 393224 | tf_op jit(solution)/shard_map/ppermute | solution.py:426
  77.3 5.9 %prepare_layer.3 = (bf16[512,1024]{1,0:T(8,128)(2,1)}, bf16[5,512,512]{2,1,0:T(8,128)(2,1)}, bf16[128,1024]{1,0:T(8,128)(2,1)}, f32[512,128]{1,0:T(8,128)}) custom-call(s32[2]{0:T(128)S(1)} %pad_add_fusion.scalar_ref, s32[1,1024]{1,0:T(1,128)} %bitcast.13, bf16[2,256,1536]{2,1,0:T(8,128)(2,1)} %refs_1_.3, bf16[2,256,1536]{2,1,0:T(8,128)(2,1)} %copy-done.1, ...), custom_call_target="tpu_custom_call" | custom-call | flops 671088640 | bytes 4194304 | tf_op jit(solution)/shard_map/prepare_layer/pallas_call | solution.py:61
  83.2 4.3 %collective-permute-done.11.beside_in = bf16[128,512]{1,0:T(8,128)(2,1)S(1)} collective-permute-done((bf16[128,512]{1,0:T(8,128)(2,1)S(1)}, bf16[128,512]{1,0:T(8,128)(2,1)S(1)}, u32[]{:S(2)}, u32[]{:S(2)}) %collective-permute-start.11) | collective-permute-done | bytes 131104 | tf_op jit(solution)/shard_map/ppermute | solution.py:426
  87.5 0.1 collective-permute-start.12
  87.6 1.2 %collective-permute-done.12.other_in = bf16[128,256]{1,0:T(8,128)(2,1)S(1)} collective-permute-done((bf16[128,256]{1,0:T(8,128)(2,1)S(1)}, bf16[128,256]{1,0:T(8,128)(2,1)S(1)}, u32[]{:S(2)}, u32[]{:S(2)}) %collective-permute-start.12) | collective-permute-done | bytes 65568 | tf_op jit(solution)/shard_map/ppermute | solution.py:407
  88.8 0.6 copy-done.9
  89.4 3.4 %gather_senders.3 = (bf16[1024,256]{1,0:T(8,128)(2,1)S(1)}, bf16[512,1024]{1,0:T(8,128)(2,1)S(1)}, bf16[5,512,512]{2,1,0:T(8,128)(2,1)S(1)}, bf16[128,1024]{1,0:...) custom-call(s32[2]{0:T(128)S(1)} %pad_add_fusion.scalar_ref, ...), custom_call_target="tpu_custom_call" | custom-call | flops 1275068416 | bytes 4194304 | tf_op jit(solution)/shard_map/gather_senders/pallas_call | solution.py:61
  92.8 2.1 %collective-permute-start.13 = (bf16[1024,256]{1,0:T(8,128)(2,1)S(1)}, bf16[1024,256]{1,0:T(8,128)(2,1)S(1)}, u32[]{:S(2)}, u32[]{:S(2)}) collective-permute-start(bf16[1024,256]{1,0:T(8,128)(2,1)S(1)} %get-tuple-element.137.refs_0_), channel_id=1, source_target_pairs={{0,1},{1,0},{2,3},{3,2},{4,5},{5,4},{6,7},{7,6},{8,9},{9,8},{10,11... | collective-permute-start | bytes 1572872 | tf_op jit(solution)/shard_map/ppermute | solution.py:407
  94.9 1.5 %collective-permute-done.13.refs_1_ = bf16[1024,256]{1,0:T(8,128)(2,1)S(1)} collective-permute-done((bf16[1024,256]{1,0:T(8,128)(2,1)S(1)}, bf16[1024,256]{1,0:T(8,128)(2,1)S(1)}, u32[]{:S(2)}, u32[]{:S(2)}) %collective-permute-start.13) | collective-permute-done | bytes 524320 | tf_op jit(solution)/shard_map/ppermute | solution.py:407
  96.4 4.6 %update_graph.3 = (bf16[256,1024]{1,0:T(8,128)(2,1)}, bf16[256,128]{1,0:T(8,128)(2,1)}) custom-call(s32[2]{0:T(128)S(1)} %pad_add_fusion.scalar_ref, bf16[1024,256]{1,0:T(8,128)(2,1)S(1)} %get-tuple-element.137.refs_0_, bf16[1024,256]{1,0:T(8,128)(2,1)S(1)} %collective-permute-done.13.refs_1_, bf16[512,1024]{1,0:T(8,128)(2,1)S(1)} %get-tuple-element.138.refs_2_, ...), custom_call_target="tpu_custom_call" | custom-call | flops 1207959552 | bytes 4194304 | tf_op jit(solution)/shard_map/update_graph/pallas_call | solution.py:61
  (49 shorter events, 0.2 us)
Async XLA Ops:
  0.6 29.7 %copy-start.7 = (bf16[256,128]{1,0:T(8,128)(2,1)S(1)}, bf16[256,128]{1,0:T(8,128)(2,1)}, u32[]{:S(2)}) copy-start(bf16[256,128]{1,0:T(8,128)(2,1)} %refs_13_.1) | copy-start | bytes 196612
  0.6 27.2 %copy-start.3 = (bf16[2,256,512]{2,1,0:T(8,128)(2,1)S(1)}, bf16[2,256,512]{2,1,0:T(8,128)(2,1)}, u32[]{:S(2)}) copy-start(bf16[2,256,512]{2,1,0:T(8,128)(2,1)} %refs_3_.3) | copy-start | bytes 1572868
  0.7 29.8 %copy-start.11 = (f32[2,256]{1,0:T(2,128)S(1)}, f32[2,256]{1,0:T(2,128)}, u32[]{:S(2)}) copy-start(f32[2,256]{1,0:T(2,128)} %param.23) | copy-start | bytes 6148
  0.7 29.8 %copy-start.12 = (f32[2,256]{1,0:T(2,128)S(1)}, f32[2,256]{1,0:T(2,128)}, u32[]{:S(2)}) copy-start(f32[2,256]{1,0:T(2,128)} %param.25) | copy-start | bytes 6148
  0.7 29.8 %copy-start.13 = (f32[2,256]{1,0:T(2,128)S(1)}, f32[2,256]{1,0:T(2,128)}, u32[]{:S(2)}) copy-start(f32[2,256]{1,0:T(2,128)} %param.26) | copy-start | bytes 6148
  0.7 29.8 %copy-start.14 = (f32[2,256]{1,0:T(2,128)S(1)}, f32[2,256]{1,0:T(2,128)}, u32[]{:S(2)}) copy-start(f32[2,256]{1,0:T(2,128)} %param.27) | copy-start | bytes 6148
  0.7 29.8 %copy-start.15 = (f32[2,256]{1,0:T(2,128)S(1)}, f32[2,256]{1,0:T(2,128)}, u32[]{:S(2)}) copy-start(f32[2,256]{1,0:T(2,128)} %param.29) | copy-start | bytes 6148
  0.7 29.8 %copy-start.16 = (f32[2,256]{1,0:T(2,128)S(1)}, f32[2,256]{1,0:T(2,128)}, u32[]{:S(2)}) copy-start(f32[2,256]{1,0:T(2,128)} %param.31) | copy-start | bytes 6148
  0.7 29.8 %copy-start.17 = (f32[2,256]{1,0:T(2,128)S(1)}, f32[2,256]{1,0:T(2,128)}, u32[]{:S(2)}) copy-start(f32[2,256]{1,0:T(2,128)} %param.32) | copy-start | bytes 6148
  0.7 29.9 %copy-start.18 = (f32[2,256]{1,0:T(2,128)S(1)}, f32[2,256]{1,0:T(2,128)}, u32[]{:S(2)}) copy-start(f32[2,256]{1,0:T(2,128)} %param.33) | copy-start | bytes 6148
  0.7 19.0 %collective-permute-start = (bf16[2,256,1536]{2,1,0:T(8,128)(2,1)}, bf16[2,256,1536]{2,1,0:T(8,128)(2,1)S(1)}, u32[]{:S(2)}, u32[]{:S(2)}) collective-permute-start(bf16[2,256,1536]{2,1,0:T(8,128)(2,1)} %refs_1_.3), channel_id=1, source_target_pairs={{0,1},{1,0},{2,3},{3,2},{4,5},{5,4},{6,7},{7,6},{8,9},{9,8},{10,11... | collective-permute-start | bytes 4718600 | tf_op jit(solution)/shard_map/ppermute | solution.py:407
  4.1 15.7 %collective-permute-start.1 = (bf16[2,256,1024]{2,1,0:T(8,128)(2,1)}, bf16[2,256,1024]{2,1,0:T(8,128)(2,1)S(1)}, u32[]{:S(2)}, u32[]{:S(2)}) collective-permute-start(bf16[2,256,1024]{2,1,0:T(8,128)(2,1)} %refs_5_.3), channel_id=1, source_target_pairs={{0,1},{1,0},{2,3},{3,2},{4,5},{5,4},{6,7},{7,6},{8,9},{9,8},{10,11... | collective-permute-start | bytes 3145736 | tf_op jit(solution)/shard_map/ppermute | solution.py:407
  4.2 15.6 %collective-permute-start.2 = (bf16[256,1024]{1,0:T(8,128)(2,1)}, bf16[256,1024]{1,0:T(8,128)(2,1)}, u32[]{:S(2)}, u32[]{:S(2)}) collective-permute-start(bf16[256,1024]{1,0:T(8,128)(2,1)} %refs_11_.1), channel_id=1, source_target_pairs={{0,1},{1,0},{2,3},{3,2},{4,5},{5,4},{6,7},{7,6},{8,9},{9,8},{10,11... | collective-permute-start | bytes 1572872 | tf_op jit(solution)/shard_map/ppermute | solution.py:407
  6.1 13.6 %all-to-all-start = ((bf16[8,16,256]{2,1,0:T(8,128)(2,1)}), bf16[8,16,256]{2,1,0:T(8,128)(2,1)S(1)}, u32[]{:S(2)}, u32[]{:S(2)}) async-start(bf16[8,16,256]{2,1,0:T(8,128)(2,1)} %get-tuple-element.74), calls=%async_computation | async-start | bytes 131072 | tf_op jit(solution)/shard_map/all_to_all | solution.py:427
  19.8 1.4 %copy-start.2 = (bf16[2,256,1024]{2,1,0:T(8,128)(2,1)}, bf16[2,256,1024]{2,1,0:T(8,128)(2,1)S(1)}, u32[]{:S(2)}) copy-start(bf16[2,256,1024]{2,1,0:T(8,128)(2,1)S(1)} %collective-permute-done.1.refs_6_) | copy-start | bytes 3145732
  19.8 16.9 %copy-start.1 = (bf16[2,256,1536]{2,1,0:T(8,128)(2,1)}, bf16[2,256,1536]{2,1,0:T(8,128)(2,1)S(1)}, u32[]{:S(2)}) copy-start(bf16[2,256,1536]{2,1,0:T(8,128)(2,1)S(1)} %collective-permute-done.refs_2_) | copy-start | bytes 4718596
  21.1 23.9 %all-to-all-start.1 = ((bf16[16,128,256]{2,1,0:T(8,128)(2,1)}), bf16[16,128,256]{2,1,0:T(8,128)(2,1)S(1)}, u32[]{:S(2)}, u32[]{:S(2)}) async-start(bf16[16,128,256]{2,1,0:T(8,128)(2,1)} %copies.2), calls=%async_computation.1 | async-start | bytes 2097152 | tf_op jit(solution)/shard_map/all_to_all | solution.py:431
  27.9 8.8 %collective-permute-start.5 = (bf16[2,256,512]{2,1,0:T(8,128)(2,1)S(1)}, bf16[2,256,512]{2,1,0:T(8,128)(2,1)}, u32[]{:S(2)}, u32[]{:S(2)}) collective-permute-start(bf16[2,256,512]{2,1,0:T(8,128)(2,1)S(1)} %copy-done.3), channel_id=1, source_target_pairs={{0,1},{1,0},{2,3},{3,2},{4,5},{5,4},{6,7},{7,6},{8,9},{9,8},{10,11... | collective-permute-start | bytes 1572872 | tf_op jit(solution)/shard_map/ppermute | solution.py:407
  29.8 6.8 %collective-permute-start.6 = (bf16[2,256,512]{2,1,0:T(8,128)(2,1)}, bf16[2,256,512]{2,1,0:T(8,128)(2,1)}, u32[]{:S(2)}, u32[]{:S(2)}) collective-permute-start(bf16[2,256,512]{2,1,0:T(8,128)(2,1)} %refs_7_.3), channel_id=1, source_target_pairs={{0,1},{1,0},{2,3},{3,2},{4,5},{5,4},{6,7},{7,6},{8,9},{9,8},{10,11... | collective-permute-start | bytes 1572872 | tf_op jit(solution)/shard_map/ppermute | solution.py:407
  29.9 1.9 %collective-permute-start.3 = (bf16[128,256]{1,0:T(8,128)(2,1)S(1)}, bf16[128,256]{1,0:T(8,128)(2,1)S(1)}, u32[]{:S(2)}, u32[]{:S(2)}) collective-permute-start(bf16[128,256]{1,0:T(8,128)(2,1)S(1)} %get-tuple-element.76), channel_id=1, source_target_pairs={{0,1},{1,0},{2,3},{3,2},{4,5},{5,4},{6,7},{7,6},{8,9},{9,8},{10,11... | collective-permute-start | bytes 196616 | tf_op jit(solution)/shard_map/ppermute | solution.py:407
  30.4 6.3 %collective-permute-start.8 = (bf16[256,128]{1,0:T(8,128)(2,1)S(1)}, bf16[256,128]{1,0:T(8,128)(2,1)}, u32[]{:S(2)}, u32[]{:S(2)}) collective-permute-start(bf16[256,128]{1,0:T(8,128)(2,1)S(1)} %copy-done.7), channel_id=1, source_target_pairs={{0,1},{1,0},{2,3},{3,2},{4,5},{5,4},{6,7},{7,6},{8,9},{9,8},{10,11... | collective-permute-start | bytes 196616 | tf_op jit(solution)/shard_map/ppermute | solution.py:407
  30.6 6.0 %copy-start.8 = (f32[2,8,256]{2,1,0:T(8,128)}, f32[2,8,256]{2,1,0:T(8,128)S(1)}, u32[]{:S(2)}) copy-start(f32[2,8,256]{2,1,0:T(8,128)S(1)} %stack.43.refs_9_) | copy-start | bytes 49156
  30.7 6.0 %collective-permute-start.7 = (f32[2,8,256]{2,1,0:T(8,128)S(1)}, f32[2,8,256]{2,1,0:T(8,128)}, u32[]{:S(2)}, u32[]{:S(2)}) collective-permute-start(f32[2,8,256]{2,1,0:T(8,128)S(1)} %stack.43.refs_9_), channel_id=1, source_target_pairs={{0,1},{1,0},{2,3},{3,2},{4,5},{5,4},{6,7},{7,6},{8,9},{9,8},{10,11... | collective-permute-start | bytes 49160 | tf_op jit(solution)/shard_map/ppermute | solution.py:407
  31.9 11.5 %copy-start.4 = (bf16[128,512]{1,0:T(8,128)(2,1)}, bf16[128,512]{1,0:T(8,128)(2,1)S(1)}, u32[]{:S(2)}) copy-start(bf16[128,512]{1,0:T(8,128)(2,1)S(1)} %maximum_select_fusion.rows_in) | copy-start | bytes 393220
  31.9 11.5 %collective-permute-start.4 = (bf16[128,512]{1,0:T(8,128)(2,1)S(1)}, bf16[128,512]{1,0:T(8,128)(2,1)S(1)}, u32[]{:S(2)}, u32[]{:S(2)}) collective-permute-start(bf16[128,512]{1,0:T(8,128)(2,1)S(1)} %maximum_select_fusion.rows_in), channel_id=1, source_target_pairs={{0,2},{1,255},{2,4},{3,1},{4,6},{5,3},{6,8},{7,5},{8,10},{9,7},{10... | collective-permute-start | bytes 393224 | tf_op jit(solution)/shard_map/ppermute | solution.py:426
  43.4 1.6 %copy-start.5 = (bf16[128,512]{1,0:T(8,128)(2,1)}, bf16[128,512]{1,0:T(8,128)(2,1)S(1)}, u32[]{:S(2)}) copy-start(bf16[128,512]{1,0:T(8,128)(2,1)S(1)} %collective-permute-done.4.beside_in) | copy-start | bytes 393220
  43.4 1.5 %collective-permute-start.9 = (bf16[128,256]{1,0:T(8,128)(2,1)S(1)}, bf16[128,256]{1,0:T(8,128)(2,1)S(1)}, u32[]{:S(2)}, u32[]{:S(2)}) collective-permute-start(bf16[128,256]{1,0:T(8,128)(2,1)S(1)} %constant_dynamic-slice_fusion.1), channel_id=1, source_target_pairs={{0,1},{1,0},{2,3},{3,2},{4,5},{5,4},{6,7},{7,6},{8,9},{9,8},{10,11... | collective-permute-start | bytes 196616 | tf_op jit(solution)/shard_map/ppermute | solution.py:407
  45.0 0.6 copy-start.10
  49.0 2.5 %collective-permute-start.10 = (bf16[1024,256]{1,0:T(8,128)(2,1)S(1)}, bf16[1024,256]{1,0:T(8,128)(2,1)S(1)}, u32[]{:S(2)}, u32[]{:S(2)}) collective-permute-start(bf16[1024,256]{1,0:T(8,128)(2,1)S(1)} %get-tuple-element.105.refs_0_), channel_id=1, source_target_pairs={{0,1},{1,0},{2,3},{3,2},{4,5},{5,4},{6,7},{7,6},{8,9},{9,8},{10,11... | collective-permute-start | bytes 1572872 | tf_op jit(solution)/shard_map/ppermute | solution.py:407
  56.6 26.6 %copy-start = (bf16[128,512]{1,0:T(8,128)(2,1)}, bf16[128,512]{1,0:T(8,128)(2,1)S(1)}, u32[]{:S(2)}) copy-start(bf16[128,512]{1,0:T(8,128)(2,1)S(1)} %get-tuple-element.127.rows_in) | copy-start | bytes 393220
  68.1 20.7 %all-to-all-start.3 = ((bf16[16,128,256]{2,1,0:T(8,128)(2,1)}), bf16[16,128,256]{2,1,0:T(8,128)(2,1)S(1)}, u32[]{:S(2)}, u32[]{:S(2)}) async-start(bf16[16,128,256]{2,1,0:T(8,128)(2,1)} %copies.3), calls=%async_computation.3 | async-start | bytes 2097152 | tf_op jit(solution)/shard_map/all_to_all | solution.py:431
  72.8 14.6 %collective-permute-start.11 = (bf16[128,512]{1,0:T(8,128)(2,1)S(1)}, bf16[128,512]{1,0:T(8,128)(2,1)S(1)}, u32[]{:S(2)}, u32[]{:S(2)}) collective-permute-start(bf16[128,512]{1,0:T(8,128)(2,1)S(1)} %get-tuple-element.127.rows_in), channel_id=1, source_target_pairs={{0,2},{1,255},{2,4},{3,1},{4,6},{5,3},{6,8},{7,5},{8,10},{9,7},{10... | collective-permute-start | bytes 393224 | tf_op jit(solution)/shard_map/ppermute | solution.py:426
  87.5 1.4 %copy-start.6 = (bf16[128,512]{1,0:T(8,128)(2,1)}, bf16[128,512]{1,0:T(8,128)(2,1)S(1)}, u32[]{:S(2)}) copy-start(bf16[128,512]{1,0:T(8,128)(2,1)S(1)} %collective-permute-done.11.beside_in) | copy-start | bytes 393220
  87.5 1.3 %collective-permute-start.12 = (bf16[128,256]{1,0:T(8,128)(2,1)S(1)}, bf16[128,256]{1,0:T(8,128)(2,1)S(1)}, u32[]{:S(2)}, u32[]{:S(2)}) collective-permute-start(bf16[128,256]{1,0:T(8,128)(2,1)S(1)} %constant_dynamic-slice_fusion), channel_id=1, source_target_pairs={{0,1},{1,0},{2,3},{3,2},{4,5},{5,4},{6,7},{7,6},{8,9},{9,8},{10,11... | collective-permute-start | bytes 196616 | tf_op jit(solution)/shard_map/ppermute | solution.py:407
  88.8 0.6 copy-start.9
  92.8 3.6 %collective-permute-start.13 = (bf16[1024,256]{1,0:T(8,128)(2,1)S(1)}, bf16[1024,256]{1,0:T(8,128)(2,1)S(1)}, u32[]{:S(2)}, u32[]{:S(2)}) collective-permute-start(bf16[1024,256]{1,0:T(8,128)(2,1)S(1)} %get-tuple-element.137.refs_0_), channel_id=1, source_target_pairs={{0,1},{1,0},{2,3},{3,2},{4,5},{5,4},{6,7},{7,6},{8,9},{9,8},{10,11... | collective-permute-start | bytes 1572872 | tf_op jit(solution)/shard_map/ppermute | solution.py:407
